TPU v7x, 32 devices: a whole 2x2x4 slice. The times are simulated.
32 devices in a mesh: narrow: 4 (over x, core), wide: 8 (over z, y).
Axes of the slice: x: 2, y: 2, z: 4, core: 2. Of those that a mesh axis runs over, the one named last changes fastest.
Arguments:
- block_input: bfloat16 [2, 4096, 2048], P(None, ('narrow', 'wide')), may hold values from -6 to 6
- segment_ids: int32 [2, 4096], P(None, ('narrow', 'wide')), may hold values from 0 to 15, never falling along the last dimension, each value on 1 to 512 neighbouring positions
- cotangent: bfloat16 [2, 4096, 2048], P(None, ('narrow', 'wide')), may hold values from -6 to 6
- attn_gain: bfloat16 [2048], P(('narrow', 'wide')), may hold values from 0.099609375 to 1.8984375
- attn_shift: bfloat16 [2048], P(('narrow', 'wide')), may hold values from -3 to 3
- query_weight: bfloat16 [2048, 2048], P(('narrow', 'wide')), may hold values from -0.125 to 0.125
- query_bias: bfloat16 [2048], P(('narrow', 'wide')), may hold values from -3 to 3
- key_weight: bfloat16 [2048, 2048], P(('narrow', 'wide')), may hold values from -0.125 to 0.125
- value_weight: bfloat16 [2048, 2048], P(('narrow', 'wide')), may hold values from -0.125 to 0.125
- value_bias: bfloat16 [2048], P(('narrow', 'wide')), may hold values from -3 to 3
- out_weight: bfloat16 [2048, 2048], P(('narrow', 'wide')), may hold values from -1 to 1
- out_bias: bfloat16 [2048], P(('narrow', 'wide')), may hold values from -3 to 3
- mlp_gain: bfloat16 [2048], P(('narrow', 'wide')), may hold values from 0.099609375 to 1.8984375
- mlp_shift: bfloat16 [2048], P(('narrow', 'wide')), may hold values from -3 to 3
- up_weight: bfloat16 [2048, 8192], P(('narrow', 'wide')), may hold values from -0.125 to 0.125
- up_bias: bfloat16 [8192], P(('narrow', 'wide')), may hold values from -3 to 3
- down_weight: bfloat16 [8192, 2048], P(('narrow', 'wide')), may hold values from -0.0625 to 0.0625
- down_bias: bfloat16 [2048], P(('narrow', 'wide')), may hold values from -3 to 3
Outputs:
- block_output: bfloat16 [2, 4096, 2048], P(None, ('narrow', 'wide'))
- input_grad: float32 [2, 4096, 2048], P(None, ('narrow', 'wide'))
- attn_gain_grad: float32 [2048], P(('narrow', 'wide'))
- attn_shift_grad: float32 [2048], P(('narrow', 'wide'))
- query_weight_grad: float32 [2048, 2048], P(('narrow', 'wide'))
- query_bias_grad: float32 [2048], P(('narrow', 'wide'))
- key_weight_grad: float32 [2048, 2048], P(('narrow', 'wide'))
- value_weight_grad: float32 [2048, 2048], P(('narrow', 'wide'))
- value_bias_grad: float32 [2048], P(('narrow', 'wide'))
- out_weight_grad: float32 [2048, 2048], P(('narrow', 'wide'))
- out_bias_grad: float32 [2048], P(('narrow', 'wide'))
- mlp_gain_grad: float32 [2048], P(('narrow', 'wide'))
- mlp_shift_grad: float32 [2048], P(('narrow', 'wide'))
- up_weight_grad: float32 [2048, 8192], P(('narrow', 'wide'))
- up_bias_grad: float32 [8192], P(('narrow', 'wide'))
- down_weight_grad: float32 [8192, 2048], P(('narrow', 'wide'))
- down_bias_grad: float32 [2048], P(('narrow', 'wide'))
Inputs may be any that keep to these rules, and one draw needn't show every extreme that they name: `segment_ids`: in each sequence the document numbers never fall, every number is used, each document has 1 to 512 tokens and the longest has exactly 512.
All inputs are finite; a program needn't handle non-finite values.
Results may differ from a plain program's by a relative error of at most 0.019.
Values may be sent and summed in bfloat16 or wider, within the bound.
No kernel may reach another device: no remote copies, remote signals or barrier semaphores. Data moves between devices by JAX's collectives and lax.ppermute only.
A program may use at most 448 MiB of HBM per device.

v0:
```python
import math

import jax
import jax.numpy as jnp
from jax import lax
from jax.sharding import PartitionSpec as P

HEADS = 16
REACH = 4


eps = 1e-05
neg_big = -1e30


def shifted(value, axis, by):
    devices = lax.axis_size(axis)
    return lax.ppermute(value, axis, [(i, (i + by) % devices) for i in range(devices)])


def as_sent(value):

    def short(part):
        return part.astype(jnp.bfloat16) if part.dtype == jnp.float32 else part

    return jax.tree.map(short, value)


def normalize(values, gain, shift):
    center = jnp.mean(values, axis=-1, keepdims=True)
    centered = values - center
    spread = jnp.mean(centered * centered, axis=-1, keepdims=True)
    return centered * lax.rsqrt(spread + eps) * gain + shift


def gelu_exact(values):
    return jax.nn.gelu(values, approximate=False)


def matmul(left, right):
    return jnp.dot(left, right, preferred_element_type=jnp.float32)


def outer_sum(left, right):
    return lax.dot_general(
        left, right, (((0,), (0,)), ((), ())), preferred_element_type=jnp.float32
    )


def times_transpose(left, right):
    return lax.dot_general(
        left, right, (((1,), (1,)), ((), ())), preferred_element_type=jnp.float32
    )


def key_positions(first_row, row_count, tokens, narrow_size, wide_size):
    row_ids = first_row + jnp.arange(row_count, dtype=jnp.int32)
    source_wide = row_ids // (tokens * narrow_size)
    source_narrow = row_ids // tokens % narrow_size
    return (source_narrow * wide_size + source_wide) * tokens + row_ids % tokens


def block_mask(query_segs, query_pos, key_segs, key_pos):
    same_doc = query_segs[:, :, None] == key_segs[:, None, :]
    causal = key_pos[None, None, :] <= query_pos[None, :, None]
    return jnp.logical_and(same_doc, causal)


def raw_scores(query_rows, key_rows, score_scale, allowed):
    scores = (
        jnp.einsum("bqhd,bkhd->bhqk", query_rows, key_rows, preferred_element_type=jnp.float32)
        * score_scale
    )
    return jnp.where(allowed[:, None], scores, neg_big)


def forward_block(running, query_heads, key_block, value_block, allowed, score_scale):
    row_max, row_total, weighted = running
    scores = raw_scores(query_heads, key_block, score_scale, allowed)
    new_max = jnp.maximum(row_max, jnp.max(scores, axis=-1))
    rescale = jnp.exp(row_max - new_max)
    exp_terms = jnp.where(allowed[:, None], jnp.exp(scores - new_max[..., None]), 0.0)
    row_total = row_total * rescale + jnp.sum(exp_terms, axis=-1)
    added = jnp.einsum(
        "bhqk,bkhd->bqhd",
        exp_terms.astype(jnp.bfloat16),
        value_block,
        preferred_element_type=jnp.float32,
    )
    weighted = weighted * jnp.transpose(rescale, (0, 2, 1))[..., None] + added
    return (new_max, row_total, weighted)


def backward_block(
    query_grad,
    query_heads,
    dout_heads,
    key_block,
    value_block,
    allowed,
    delta,
    log_total,
    score_scale,
):
    scores = raw_scores(query_heads, key_block, score_scale, allowed)
    attn_probs = jnp.where(allowed[:, None], jnp.exp(scores - log_total[..., None]), 0.0)
    prob_grad = jnp.einsum(
        "bqhd,bkhd->bhqk", dout_heads, value_block, preferred_element_type=jnp.float32
    )
    score_grad = (attn_probs * (prob_grad - delta[..., None])).astype(jnp.bfloat16)
    query_grad = query_grad + score_scale * jnp.einsum(
        "bhqk,bkhd->bqhd", score_grad, key_block, preferred_element_type=jnp.float32
    )
    key_grad = score_scale * jnp.einsum(
        "bhqk,bqhd->bkhd", score_grad, query_heads, preferred_element_type=jnp.float32
    )
    value_grad = jnp.einsum(
        "bhqk,bqhd->bkhd",
        attn_probs.astype(jnp.bfloat16),
        dout_heads,
        preferred_element_type=jnp.float32,
    )
    return (query_grad, key_grad, value_grad)


def on_device(
    block_input,
    segment_ids,
    cotangent,
    attn_gain,
    attn_shift,
    query_weight,
    query_bias,
    key_weight,
    value_weight,
    value_bias,
    out_weight,
    out_bias,
    mlp_gain,
    mlp_shift,
    up_weight,
    up_bias,
    down_weight,
    down_bias,
):
    batch, tokens, model_width = block_input.shape
    narrow_size = lax.axis_size("narrow")
    wide_size = lax.axis_size("wide")
    wide_index = lax.axis_index("wide")
    group_rows = tokens * narrow_size
    heads_local = HEADS // narrow_size
    head_dim = model_width // HEADS
    score_scale = 1.0 / math.sqrt(head_dim)
    f32 = jnp.float32
    bf16 = jnp.bfloat16
    attn_set = (
        lax.all_gather(attn_gain, ("narrow", "wide"), axis=0, tiled=True),
        lax.all_gather(attn_shift, ("narrow", "wide"), axis=0, tiled=True),
        lax.all_gather(query_weight, ("narrow", "wide"), axis=0, tiled=True),
        lax.all_gather(query_bias, ("narrow", "wide"), axis=0, tiled=True),
        lax.all_gather(key_weight, ("narrow", "wide"), axis=0, tiled=True),
        lax.all_gather(value_weight, ("narrow", "wide"), axis=0, tiled=True),
        lax.all_gather(value_bias, ("narrow", "wide"), axis=0, tiled=True),
        lax.all_gather(out_weight, ("narrow", "wide"), axis=0, tiled=True),
        lax.all_gather(out_bias, ("narrow", "wide"), axis=0, tiled=True),
    )
    (
        gain_attn,
        shift_attn,
        query_full,
        qbias_full,
        key_full,
        value_full,
        vbias_full,
        out_full,
        obias_full,
    ) = attn_set
    inputs = block_input.astype(f32).reshape(-1, model_width)
    first_norm = normalize(inputs, gain_attn.astype(f32), shift_attn.astype(f32)).astype(bf16)
    split_shape = (batch, tokens, HEADS, head_dim)
    queries = (
        (matmul(first_norm, query_full) + qbias_full.astype(f32)).astype(bf16).reshape(split_shape)
    )
    key_rows = matmul(first_norm, key_full).astype(bf16).reshape(split_shape)
    value_rows = (
        (matmul(first_norm, value_full) + vbias_full.astype(f32)).astype(bf16).reshape(split_shape)
    )
    query_heads, key_heads, value_heads = (
        lax.all_to_all(queries, "narrow", split_axis=2, concat_axis=1, tiled=True),
        lax.all_to_all(key_rows, "narrow", split_axis=2, concat_axis=1, tiled=True),
        lax.all_to_all(value_rows, "narrow", split_axis=2, concat_axis=1, tiled=True),
    )
    query_segs = lax.all_gather(segment_ids, "narrow", axis=1, tiled=True)
    query_pos = key_positions(wide_index * group_rows, group_rows, tokens, narrow_size, wide_size)

    def block_allowed(cycle_step, seg_block):
        source = (wide_index - cycle_step) % wide_size
        key_pos = key_positions(source * group_rows, group_rows, tokens, narrow_size, wide_size)
        return block_mask(query_segs, query_pos, seg_block, key_pos)

    running = (
        jnp.full((batch, heads_local, group_rows), neg_big, f32),
        jnp.zeros((batch, heads_local, group_rows), f32),
        jnp.zeros((batch, group_rows, heads_local, head_dim), f32),
    )
    travelling = (key_heads, value_heads, query_segs)
    received = []
    for cycle_step in range(REACH + 1):
        if cycle_step > 0:
            travelling = shifted((travelling[0], travelling[1], travelling[2]), "wide", 1)
        received.append(travelling)
        key_block, value_block, seg_block = travelling
        allowed = block_allowed(cycle_step, seg_block)
        running = forward_block(running, query_heads, key_block, value_block, allowed, score_scale)
    row_max, row_total, weighted = running
    attn_out = weighted / jnp.transpose(row_total, (0, 2, 1))[..., None]
    log_total = row_max + jnp.log(row_total)
    mixed = lax.all_to_all(
        attn_out.astype(bf16), "narrow", split_axis=1, concat_axis=2, tiled=True
    ).reshape(-1, model_width)
    middle = inputs + matmul(mixed, out_full) + obias_full.astype(f32)
    mlp_set = (
        lax.all_gather(mlp_gain, ("narrow", "wide"), axis=0, tiled=True),
        lax.all_gather(mlp_shift, ("narrow", "wide"), axis=0, tiled=True),
        lax.all_gather(up_weight, ("narrow", "wide"), axis=0, tiled=True),
        lax.all_gather(up_bias, ("narrow", "wide"), axis=0, tiled=True),
        lax.all_gather(down_weight, ("narrow", "wide"), axis=0, tiled=True),
        lax.all_gather(down_bias, ("narrow", "wide"), axis=0, tiled=True),
    )
    gain_mlp, shift_mlp, up_full, ubias_full, down_full, dbias_full = mlp_set
    second_norm = normalize(middle, gain_mlp.astype(f32), shift_mlp.astype(f32)).astype(bf16)
    inner = matmul(second_norm, up_full) + ubias_full.astype(f32)
    hidden = gelu_exact(inner).astype(bf16)
    output = middle + matmul(hidden, down_full) + dbias_full.astype(f32)
    block_output = output.astype(bf16).reshape(batch, tokens, model_width)
    mlp_set = (
        lax.all_gather(mlp_gain, ("narrow", "wide"), axis=0, tiled=True),
        lax.all_gather(mlp_shift, ("narrow", "wide"), axis=0, tiled=True),
        lax.all_gather(up_weight, ("narrow", "wide"), axis=0, tiled=True),
        lax.all_gather(up_bias, ("narrow", "wide"), axis=0, tiled=True),
        lax.all_gather(down_weight, ("narrow", "wide"), axis=0, tiled=True),
        lax.all_gather(down_bias, ("narrow", "wide"), axis=0, tiled=True),
    )
    gain_mlp, shift_mlp, up_full, ubias_full, down_full, dbias_full = mlp_set
    cotan_rows = cotangent.reshape(-1, model_width)
    down_grad = outer_sum(hidden, cotan_rows)
    dbias_grad = jnp.sum(cotan_rows.astype(f32), axis=0)
    hidden_grad = times_transpose(cotan_rows, down_full)
    gelu_pull = jax.vjp(gelu_exact, inner)[1]
    inner_grad = gelu_pull(hidden_grad)[0].astype(bf16)
    up_grad = outer_sum(second_norm, inner_grad)
    ubias_grad = jnp.sum(inner_grad.astype(f32), axis=0)
    second_grad = times_transpose(inner_grad, up_full)
    mlp_pull = jax.vjp(normalize, middle, gain_mlp.astype(f32), shift_mlp.astype(f32))[1]
    middle_part, mgain_grad, mshift_grad = mlp_pull(second_grad)
    middle_grad = cotan_rows.astype(f32) + middle_part
    mlp_shards = (
        lax.psum_scatter(mgain_grad, ("narrow", "wide"), scatter_dimension=0, tiled=True),
        lax.psum_scatter(mshift_grad, ("narrow", "wide"), scatter_dimension=0, tiled=True),
        lax.psum_scatter(up_grad, ("narrow", "wide"), scatter_dimension=0, tiled=True),
        lax.psum_scatter(ubias_grad, ("narrow", "wide"), scatter_dimension=0, tiled=True),
        lax.psum_scatter(down_grad, ("narrow", "wide"), scatter_dimension=0, tiled=True),
        lax.psum_scatter(dbias_grad, ("narrow", "wide"), scatter_dimension=0, tiled=True),
    )
    attn_set = (
        lax.all_gather(attn_gain, ("narrow", "wide"), axis=0, tiled=True),
        lax.all_gather(attn_shift, ("narrow", "wide"), axis=0, tiled=True),
        lax.all_gather(query_weight, ("narrow", "wide"), axis=0, tiled=True),
        lax.all_gather(query_bias, ("narrow", "wide"), axis=0, tiled=True),
        lax.all_gather(key_weight, ("narrow", "wide"), axis=0, tiled=True),
        lax.all_gather(value_weight, ("narrow", "wide"), axis=0, tiled=True),
        lax.all_gather(value_bias, ("narrow", "wide"), axis=0, tiled=True),
        lax.all_gather(out_weight, ("narrow", "wide"), axis=0, tiled=True),
        lax.all_gather(out_bias, ("narrow", "wide"), axis=0, tiled=True),
    )
    (
        gain_attn,
        shift_attn,
        query_full,
        qbias_full,
        key_full,
        value_full,
        vbias_full,
        out_full,
        obias_full,
    ) = attn_set
    branch_grad = middle_grad.astype(bf16)
    out_grad = outer_sum(mixed, branch_grad)
    obias_grad = jnp.sum(branch_grad.astype(f32), axis=0)
    mixed_grad = times_transpose(branch_grad, out_full).astype(bf16).reshape(split_shape)
    dout_heads = lax.all_to_all(mixed_grad, "narrow", split_axis=2, concat_axis=1, tiled=True)
    delta = jnp.transpose(jnp.sum(dout_heads.astype(f32) * attn_out, axis=-1), (0, 2, 1))
    travelling = (key_heads, value_heads, query_segs)
    received = []
    for cycle_step in range(REACH + 1):
        if cycle_step > 0:
            travelling = shifted((travelling[0], travelling[1], travelling[2]), "wide", 1)
        received.append(travelling)
    query_grad = jnp.zeros((batch, group_rows, heads_local, head_dim), f32)
    key_terms = []
    value_terms = []
    for cycle_step in range(REACH + 1):
        key_block, value_block, seg_block = received[cycle_step]
        allowed = block_allowed(cycle_step, seg_block)
        query_grad, key_term, value_term = backward_block(
            query_grad,
            query_heads,
            dout_heads,
            key_block,
            value_block,
            allowed,
            delta,
            log_total,
            score_scale,
        )
        key_terms.append(key_term)
        value_terms.append(value_term)
    carried = (key_terms[REACH], value_terms[REACH])
    for cycle_step in range(REACH - 1, -1, -1):
        arrived = shifted((as_sent(carried[0]), as_sent(carried[1])), "wide", -1)
        carried = (arrived[0] + key_terms[cycle_step], arrived[1] + value_terms[cycle_step])
    key_sum, value_sum = carried
    query_back, key_back, value_back = (
        lax.all_to_all(query_grad.astype(bf16), "narrow", split_axis=1, concat_axis=2, tiled=True),
        lax.all_to_all(key_sum.astype(bf16), "narrow", split_axis=1, concat_axis=2, tiled=True),
        lax.all_to_all(value_sum.astype(bf16), "narrow", split_axis=1, concat_axis=2, tiled=True),
    )
    query_back = query_back.reshape(-1, model_width)
    key_back = key_back.reshape(-1, model_width)
    value_back = value_back.reshape(-1, model_width)
    query_wgrad = outer_sum(first_norm, query_back)
    qbias_grad = jnp.sum(query_back.astype(f32), axis=0)
    key_wgrad = outer_sum(first_norm, key_back)
    value_wgrad = outer_sum(first_norm, value_back)
    vbias_grad = jnp.sum(value_back.astype(f32), axis=0)
    first_grad = (
        times_transpose(query_back, query_full)
        + times_transpose(key_back, key_full)
        + times_transpose(value_back, value_full)
    )
    attn_pull = jax.vjp(normalize, inputs, gain_attn.astype(f32), shift_attn.astype(f32))[1]
    input_part, again_grad, ashift_grad = attn_pull(first_grad)
    input_grad = (middle_grad + input_part).reshape(batch, tokens, model_width)
    attn_shards = (
        lax.psum_scatter(again_grad, ("narrow", "wide"), scatter_dimension=0, tiled=True),
        lax.psum_scatter(ashift_grad, ("narrow", "wide"), scatter_dimension=0, tiled=True),
        lax.psum_scatter(query_wgrad, ("narrow", "wide"), scatter_dimension=0, tiled=True),
        lax.psum_scatter(qbias_grad, ("narrow", "wide"), scatter_dimension=0, tiled=True),
        lax.psum_scatter(key_wgrad, ("narrow", "wide"), scatter_dimension=0, tiled=True),
        lax.psum_scatter(value_wgrad, ("narrow", "wide"), scatter_dimension=0, tiled=True),
        lax.psum_scatter(vbias_grad, ("narrow", "wide"), scatter_dimension=0, tiled=True),
        lax.psum_scatter(out_grad, ("narrow", "wide"), scatter_dimension=0, tiled=True),
        lax.psum_scatter(obias_grad, ("narrow", "wide"), scatter_dimension=0, tiled=True),
    )
    return (
        block_output,
        input_grad,
        attn_shards[0],
        attn_shards[1],
        attn_shards[2],
        attn_shards[3],
        attn_shards[4],
        attn_shards[5],
        attn_shards[6],
        attn_shards[7],
        attn_shards[8],
        mlp_shards[0],
        mlp_shards[1],
        mlp_shards[2],
        mlp_shards[3],
        mlp_shards[4],
        mlp_shards[5],
    )


def solution(mesh):
    return jax.shard_map(
        on_device,
        mesh=mesh,
        in_specs=(
            P(None, ("narrow", "wide"), None),
            P(None, ("narrow", "wide")),
            P(None, ("narrow", "wide"), None),
            P(("narrow", "wide")),
            P(("narrow", "wide")),
            P(("narrow", "wide"), None),
            P(("narrow", "wide")),
            P(("narrow", "wide"), None),
            P(("narrow", "wide"), None),
            P(("narrow", "wide")),
            P(("narrow", "wide"), None),
            P(("narrow", "wide")),
            P(("narrow", "wide")),
            P(("narrow", "wide")),
            P(("narrow", "wide"), None),
            P(("narrow", "wide")),
            P(("narrow", "wide"), None),
            P(("narrow", "wide")),
        ),
        out_specs=(
            P(None, ("narrow", "wide"), None),
            P(None, ("narrow", "wide"), None),
            P(("narrow", "wide")),
            P(("narrow", "wide")),
            P(("narrow", "wide"), None),
            P(("narrow", "wide")),
            P(("narrow", "wide"), None),
            P(("narrow", "wide"), None),
            P(("narrow", "wide")),
            P(("narrow", "wide"), None),
            P(("narrow", "wide")),
            P(("narrow", "wide")),
            P(("narrow", "wide")),
            P(("narrow", "wide"), None),
            P(("narrow", "wide")),
            P(("narrow", "wide"), None),
            P(("narrow", "wide")),
        ),
        check_vma=False,
    )
```

profile of v0, /device:TPU:0, one launch (start us, length us, event | category | flops | bytes accessed | tf_op | source)
XLA Modules:
  0.0 5611.2 jit_solution(8408947181975963893)
XLA Ops:
  17.9 43.4 all-reduce.18
  67.6 23.9 all-gather.10.cloned.1.call-done
  91.6 5.7 fusion.88
  102.3 69.7 %all-gather.12.cloned.1.call-done = bf16[2048,2048]{1,0:T(8,128)(2,1)} async-done(((bf16[64,2048]{1,0:T(8,128)(2,1)}), bf16[2048,2048]{1,0:T(8,128)(2,1)}) %all-gather.12.cloned.1.call-update) | async-done | bytes 8388624 | tf_op jit(solution)/shard_map/all_gather | solution.py:162
  172.0 5.7 fusion.90
  184.4 14.5 all_gather.56
  203.2 21.4 collective-permute-done
  224.7 36.8 collective-permute-done.3
  261.5 6.4 collective-permute-done.6
  273.5 6.1 fusion.91
  288.1 17.4 collective-permute-done.4
  310.5 17.4 collective-permute-done.5
  329.6 20.8 collective-permute-done.7
  356.9 15.9 collective-permute-done.8
  375.7 19.5 collective-permute-done.10
  432.0 5.6 fusion.196
  442.9 65.2 %all-gather = bf16[32,1,256]{2,1,0:T(2,128)(2,1)S(1)} all-gather(bf16[1,1,256]{2,1,0:T(2,128)(2,1)S(1)} %reshape.831), channel_id=1, replica_groups=mesh['narrow'=4,'wide'=8] {'narrow','wide'}, dimensions={0}, use_global_device_ids=true | all-gather | bytes 16896 | tf_op jit(solution)/shard_map/all_gather | solution.py:226
  510.1 6.2 fusion.197
  516.8 161.5 %all-gather.16.cloned.1.call-done = bf16[2048,8192]{1,0:T(8,128)(2,1)} async-done(((bf16[64,8192]{1,0:T(8,128)(2,1)}), bf16[2048,8192]{1,0:T(8,128)(2,1)}) %all-gather.16.cloned.1.call-update) | async-done | bytes 33554448 | tf_op jit(solution)/shard_map/all_gather | solution.py:225
  678.3 18.0 convolution_add_fusion
  696.3 177.8 %all-gather.18.cloned.1.call-done = bf16[8192,2048]{1,0:T(8,128)(2,1)} async-done(((bf16[256,2048]{1,0:T(8,128)(2,1)}), bf16[8192,2048]{1,0:T(8,128)(2,1)}) %all-gather.18.cloned.1.call-update) | async-done | bytes 33554448 | tf_op jit(solution)/shard_map/all_gather | solution.py:227
  874.1 34.5 convert_reduce_fusion
  908.6 18.6 multiply_reduce_fusion
  932.0 6.2 fusion.89
  944.1 13.5 all-to-all-done.4
  961.2 7.3 fusion.83
  968.5 5.8 multiply_convert_fusion.4
  974.3 5.7 multiply_convert_fusion
  987.4 7.4 multiply_convert_fusion.1
  994.8 6.0 multiply_convert_fusion.2
  1000.8 5.0 fusion.203
  1005.9 5.9 multiply_convert_fusion.3
  1011.8 20.2 collective-permute-done.16
  1032.0 7.5 fusion.64
  1039.5 5.0 collective-permute-start.17
  1052.6 15.8 collective-permute-done.17
  1068.4 5.3 fusion.63
  1073.7 5.2 collective-permute-start.18
  1083.0 7.9 collective-permute-done.13
  1093.4 5.2 collective-permute-start.14
  1098.6 14.7 collective-permute-done.18
  1117.1 5.1 collective-permute-start.19
  1138.3 5.2 collective-permute-start.15
  1143.5 14.7 collective-permute-done.19
  1158.3 7.4 fusion.61
  1171.8 5.0 fusion.205
  1190.6 7.1 fusion.202
  1208.4 6.5 convolution_add_fusion.3
  1215.0 6.9 fusion.189
  1224.8 8.2 fusion.209
  1234.3 8.1 fusion.206
  1243.6 8.3 fusion.208
  1253.1 8.2 fusion.207
  1262.9 25.6 fusion.188
  1288.9 9.3 multiply_convert_fusion.5
  1298.1 25.4 fusion.210
  1324.2 17.3 fusion.60
  1343.9 7.1 all-reduce.21.cloned.1.call-done
  1362.5 350.7 %reduce-scatter.13.cloned.1.call-done = f32[64,2048]{1,0:T(8,128)} async-done(((f32[2048,2048]{1,0:T(8,128)}), f32[64,2048]{1,0:T(8,128)}) %reduce-scatter.13.cloned.1.call-update) | async-done | bytes 524304 | tf_op jit(solution)/shard_map/reduce_scatter | solution.py:352
  1713.2 360.3 %reduce-scatter.7.cloned.1.call-done = f32[64,2048]{1,0:T(8,128)} async-done(((f32[2048,2048]{1,0:T(8,128)}), f32[64,2048]{1,0:T(8,128)}) %reduce-scatter.7.cloned.1.call-update) | async-done | bytes 524304 | tf_op jit(solution)/shard_map/reduce_scatter | solution.py:347
  2073.5 360.2 %reduce-scatter.11.cloned.1.call-done = f32[64,2048]{1,0:T(8,128)} async-done(((f32[2048,2048]{1,0:T(8,128)}), f32[64,2048]{1,0:T(8,128)}) %reduce-scatter.11.cloned.1.call-update) | async-done | bytes 524304 | tf_op jit(solution)/shard_map/reduce_scatter | solution.py:350
  2433.7 360.3 %reduce-scatter.9.cloned.1.call-done = f32[64,2048]{1,0:T(8,128)} async-done(((f32[2048,2048]{1,0:T(8,128)}), f32[64,2048]{1,0:T(8,128)}) %reduce-scatter.9.cloned.1.call-update) | async-done | bytes 524304 | tf_op jit(solution)/shard_map/reduce_scatter | solution.py:349
  2794.0 1404.7 %reduce-scatter.15.cloned.1.call-done = f32[64,8192]{1,0:T(8,128)} async-done(((f32[2048,8192]{1,0:T(8,128)}), f32[64,8192]{1,0:T(8,128)}) %reduce-scatter.15.cloned.1.call-update) | async-done | bytes 2097168 | tf_op jit(solution)/shard_map/reduce_scatter | solution.py:260
  4198.7 1405.6 %reduce-scatter.17.cloned.1.call-done = f32[256,2048]{1,0:T(8,128)} async-done(((f32[8192,2048]{1,0:T(8,128)}), f32[256,2048]{1,0:T(8,128)}) %reduce-scatter.17.cloned.1.call-update) | async-done | bytes 2097168 | tf_op jit(solution)/shard_map/reduce_scatter | solution.py:262
  (406 shorter events, 216.4 us)
Async XLA Ops:
  7.2 84.4 %all-gather.10.cloned.1.call-start = ((), (), s32[]{:S(2)}) async-start(), calls=%async_computation.15 | async-start | bytes 8650752 | tf_op jit(solution)/shard_map/all_gather | solution.py:161
  7.9 164.1 %all-gather.12.cloned.1.call-start = ((), (), s32[]{:S(2)}) async-start(), calls=%async_computation.16 | async-start | bytes 8650752 | tf_op jit(solution)/shard_map/all_gather | solution.py:162
  8.7 264.9 %all-gather.8.cloned.1.call-start = ((), (), s32[]{:S(2)}) async-start(), calls=%async_computation.14 | async-start | bytes 8650752 | tf_op jit(solution)/shard_map/all_gather | solution.py:159
  9.4 500.7 %all-gather.14.cloned.1.call-start = ((), (), s32[]{:S(2)}) async-start(), calls=%async_computation.17 | async-start | bytes 8650752 | tf_op jit(solution)/shard_map/all_gather | solution.py:164
  10.0 668.3 %all-gather.16.cloned.1.call-start = ((), (), s32[]{:S(2)}) async-start(), calls=%async_computation.18 | async-start | bytes 34603008 | tf_op jit(solution)/shard_map/all_gather | solution.py:225
  10.6 863.6 %all-gather.18.cloned.1.call-start = ((), (), s32[]{:S(2)}) async-start(), calls=%async_computation.19 | async-start | bytes 34603008 | tf_op jit(solution)/shard_map/all_gather | solution.py:227
  67.6 104.4 %copy-start.54 = (bf16[256,2048]{1,0:T(8,128)(2,1)}, bf16[256,2048]{1,0:T(8,128)(2,1)S(1)}, u32[]{:S(2)}) copy-start(bf16[256,2048]{1,0:T(8,128)(2,1)S(1)} %add_convert_fusion.3) | copy-start | bytes 3145732
  98.8 80.5 %all-to-all-start.1 = ((bf16[2,128,16,128]{3,1,0,2:T(8,128)(2,1)}), bf16[2,128,16,128]{3,1,0,2:T(8,128)(2,1)S(1)}, u32[]{:S(2)}, u32[]{:S(2)}) async-start(bf16[2,128,16,128]{3,1,0,2:T(8,128)(2,1)} %copy.139), calls=%async_computation.1 | async-start | bytes 2097152 | tf_op jit(solution)/shard_map/all_to_all | solution.py:190
  179.2 21.2 all-to-all-start.2
  182.9 145.1 %copy-start.21 = (bf16[2,128,4,4,128]{4,1,2,3,0:T(8,128)(2,1)}, bf16[2,128,4,4,128]{4,1,2,3,0:T(8,128)(2,1)S(1)}, u32[]{:S(2)}) copy-start(bf16[2,128,4,4,128]{4,1,2,3,0:T(8,128)(2,1)S(1)} %copy.140) | copy-start | bytes 3145732
  182.9 85.0 %collective-permute-start.1 = (bf16[2,512,4,128]{3,1,2,0:T(8,128)(2,1)S(1)}, bf16[2,512,4,128]{3,1,2,0:T(8,128)(2,1)}, u32[]{:S(2)}, u32[]{:S(2)}) collective-permute-start(bf16[2,512,4,128]{3,1,2,0:T(8,128)(2,1)S(1)} %bitcast.362), channel_id=1, source_target_pairs={{0,1},{1,2},{2,3},{3,4},{4,5},{5,6},{6,7},{7,0},{8,9},{9,10},{10,1... | collective-permute-start | bytes 3145736 | tf_op jit(solution)/shard_map/ppermute | solution.py:18
  198.9 25.7 collective-permute-start
  201.6 78.0 %copy-start.55 = (bf16[2,512,4,128]{1,3,2,0:T(8,128)(2,1)}, bf16[2,512,4,128]{1,3,2,0:T(8,128)(2,1)S(1)}, u32[]{:S(2)}) copy-start(bf16[2,512,4,128]{1,3,2,0:T(8,128)(2,1)S(1)} %all_to_all.107) | copy-start | bytes 3145732
  201.6 83.8 %collective-permute-start.2 = (bf16[2,512,4,128]{1,3,2,0:T(8,128)(2,1)S(1)}, bf16[2,512,4,128]{1,3,2,0:T(8,128)(2,1)}, u32[]{:S(2)}, u32[]{:S(2)}) collective-permute-start(bf16[2,512,4,128]{1,3,2,0:T(8,128)(2,1)S(1)} %all_to_all.107), channel_id=1, source_target_pairs={{0,1},{1,2},{2,3},{3,4},{4,5},{5,6},{6,7},{7,0},{8,9},{9,10},{10,1... | collective-permute-start | bytes 3145736 | tf_op jit(solution)/shard_map/ppermute | solution.py:18
  224.6 36.8 collective-permute-start.3
  261.5 6.4 collective-permute-start.6
  267.9 37.6 collective-permute-start.9
  267.9 37.6 collective-permute-start.4
  281.1 27.4 all-to-all-start
  285.4 42.6 collective-permute-start.5
  305.5 44.9 collective-permute-start.7
  308.5 103.1 %copy-start.27 = (pred[2,512,512]{1,2,0:T(8,128)(4,1)}, pred[2,512,512]{1,2,0:T(8,128)(4,1)S(1)}, u32[]{:S(2)}) copy-start(pred[2,512,512]{1,2,0:T(8,128)(4,1)S(1)} %get-tuple-element.59) | copy-start | bytes 1572868
  308.5 107.8 %copy-start.30 = (pred[2,512,512]{1,2,0:T(8,128)(4,1)}, pred[2,512,512]{1,2,0:T(8,128)(4,1)S(1)}, u32[]{:S(2)}) copy-start(pred[2,512,512]{1,2,0:T(8,128)(4,1)S(1)} %get-tuple-element.63) | copy-start | bytes 1572868
  308.5 112.5 %copy-start.33 = (pred[2,512,512]{1,2,0:T(8,128)(4,1)}, pred[2,512,512]{1,2,0:T(8,128)(4,1)S(1)}, u32[]{:S(2)}) copy-start(pred[2,512,512]{1,2,0:T(8,128)(4,1)S(1)} %get-tuple-element.60) | copy-start | bytes 1572868
  308.5 118.5 %copy-start.36 = (pred[2,512,512]{1,2,0:T(8,128)(4,1)}, pred[2,512,512]{1,2,0:T(8,128)(4,1)S(1)}, u32[]{:S(2)}) copy-start(pred[2,512,512]{1,2,0:T(8,128)(4,1)S(1)} %get-tuple-element.61) | copy-start | bytes 1572868
  310.5 84.7 %copy-start = (bf16[2,128,4,4,128]{4,1,2,3,0:T(8,128)(2,1)}, bf16[2,128,4,4,128]{4,1,2,3,0:T(8,128)(2,1)S(1)}, u32[]{:S(2)}) copy-start(bf16[2,128,4,4,128]{4,1,2,3,0:T(8,128)(2,1)S(1)} %copy.138) | copy-start | bytes 3145732
  327.9 44.9 collective-permute-start.8
  329.6 82.0 %copy-start.4 = (f32[2,4,512,512]{2,3,1,0:T(8,128)}, f32[2,4,512,512]{2,3,1,0:T(8,128)S(1)}, u32[]{:S(2)}) copy-start(f32[2,4,512,512]{2,3,1,0:T(8,128)S(1)} %get-tuple-element.80) | copy-start | bytes 25165828
  329.6 97.3 %copy-start.61 = (f32[2,4,512]{2,1,0:T(4,128)}, f32[2,4,512]{2,1,0:T(4,128)S(1)}, u32[]{:S(2)}) copy-start(f32[2,4,512]{2,1,0:T(4,128)S(1)} %get-tuple-element.79) | copy-start | bytes 49156
  350.4 44.8 collective-permute-start.10
  353.2 63.0 %copy-start.5 = (f32[2,4,512,512]{2,3,1,0:T(8,128)}, f32[2,4,512,512]{2,3,1,0:T(8,128)S(1)}, u32[]{:S(2)}) copy-start(f32[2,4,512,512]{2,3,1,0:T(8,128)S(1)} %get-tuple-element.78) | copy-start | bytes 25165828
  353.3 42.0 copy-start.38
  356.9 64.1 %copy-start.6 = (f32[2,4,512,512]{2,3,1,0:T(8,128)}, f32[2,4,512,512]{2,3,1,0:T(8,128)S(1)}, u32[]{:S(2)}) copy-start(f32[2,4,512,512]{2,3,1,0:T(8,128)S(1)} %get-tuple-element.76) | copy-start | bytes 25165828
  372.9 59.0 %collective-permute-start.11 = (bf16[2,512,4,128]{1,3,2,0:T(8,128)(2,1)}, bf16[2,512,4,128]{1,3,2,0:T(8,128)(2,1)}, u32[]{:S(2)}, u32[]{:S(2)}) collective-permute-start(bf16[2,512,4,128]{1,3,2,0:T(8,128)(2,1)} %collective-permute-done.8), channel_id=1, source_target_pairs={{0,1},{1,2},{2,3},{3,4},{4,5},{5,6},{6,7},{7,0},{8,9},{9,10},{10,1... | collective-permute-start | bytes 3145736 | tf_op jit(solution)/shard_map/ppermute | solution.py:18
  375.7 51.3 copy-start.7
  437.6 72.5 %copy-start.2 = (bf16[2,128,2048]{2,1,0:T(8,128)(2,1)S(1)}, bf16[2,128,2048]{2,1,0:T(8,128)(2,1)}, u32[]{:S(2)}) copy-start(bf16[2,128,2048]{2,1,0:T(8,128)(2,1)} %param.18) | copy-start | bytes 3145732
  439.2 68.9 %all-to-all-start.3 = ((bf16[2,512,4,128]{3,2,0,1:T(4,128)(2,1)}), bf16[2,512,4,128]{3,2,0,1:T(4,128)(2,1)S(1)}, u32[]{:S(2)}, u32[]{:S(2)}) async-start(bf16[2,512,4,128]{3,2,0,1:T(4,128)(2,1)} %copy.148), calls=%async_computation.3 | async-start | bytes 2097152 | tf_op jit(solution)/shard_map/all_to_all | solution.py:218
  442.9 484.3 %copy-start.57 = (f32[2048]{0:T(1024)}, f32[2048]{0:T(1024)S(1)}, u32[]{:S(2)}) copy-start(f32[2048]{0:T(1024)S(1)} %convert_element_type.220) | copy-start | bytes 24580
  442.9 235.4 %copy-start.59 = (f32[2048]{0:T(1024)}, f32[2048]{0:T(1024)S(1)}, u32[]{:S(2)}) copy-start(f32[2048]{0:T(1024)S(1)} %convert_element_type.221) | copy-start | bytes 24580
  516.3 410.9 %copy-start.8 = (f32[256,2048]{1,0:T(8,128)}, f32[256,2048]{1,0:T(8,128)S(1)}, u32[]{:S(2)}) copy-start(f32[256,2048]{1,0:T(8,128)S(1)} %get-tuple-element.84) | copy-start | bytes 6291460
  516.4 410.9 %copy-start.81 = (f32[256]{0:T(256)}, f32[256]{0:T(256)S(1)}, u32[]{:S(2)}) copy-start(f32[256]{0:T(256)S(1)} %broadcast_multiply_fusion) | copy-start | bytes 3076
  516.7 410.5 %copy-start.85 = (f32[256]{0:T(256)}, f32[256]{0:T(256)S(1)}, u32[]{:S(2)}) copy-start(f32[256]{0:T(256)S(1)} %fusion.149) | copy-start | bytes 3076
  678.3 195.8 %copy-start.12 = (bf16[2,128,2048]{2,1,0:T(8,128)(2,1)S(1)}, bf16[2,128,2048]{2,1,0:T(8,128)(2,1)}, u32[]{:S(2)}) copy-start(bf16[2,128,2048]{2,1,0:T(8,128)(2,1)} %param.20) | copy-start | bytes 3145732
  939.7 18.0 all-to-all-start.4
  958.8 73.2 %copy-start.45 = (bf16[2,512,4,128]{1,3,2,0:T(8,128)(2,1)}, bf16[2,512,4,128]{1,3,2,0:T(8,128)(2,1)S(1)}, u32[]{:S(2)}) copy-start(bf16[2,512,4,128]{1,3,2,0:T(8,128)(2,1)S(1)} %all_to_all.114) | copy-start | bytes 3145732
  974.2 70.2 %copy-start.15 = (bf16[2,4,512,512]{2,3,1,0:T(8,128)(2,1)}, bf16[2,4,512,512]{2,3,1,0:T(8,128)(2,1)S(1)}, u32[]{:S(2)}) copy-start(bf16[2,4,512,512]{2,3,1,0:T(8,128)(2,1)S(1)} %multiply_convert_fusion.4) | copy-start | bytes 12582916
  984.5 64.3 %collective-permute-start.12 = (bf16[2,512,4,128]{1,3,2,0:T(8,128)(2,1)}, bf16[2,512,4,128]{1,3,2,0:T(8,128)(2,1)}, u32[]{:S(2)}, u32[]{:S(2)}) collective-permute-start(bf16[2,512,4,128]{1,3,2,0:T(8,128)(2,1)} %fusion.86), channel_id=1, source_target_pairs={{0,7},{1,0},{2,1},{3,2},{4,3},{5,4},{6,5},{7,6},{8,15},{9,8},{10,9... | collective-permute-start | bytes 3145736 | tf_op jit(solution)/shard_map/ppermute | solution.py:18
  986.8 45.2 collective-permute-start.16
  1039.5 28.9 collective-permute-start.17
  1052.6 38.2 collective-permute-start.13
  1073.7 39.6 collective-permute-start.18
  1093.4 42.4 collective-permute-start.14
  1117.1 41.1 collective-permute-start.19
  1127.0 41.2 all-to-all-start.5
  1138.3 41.7 collective-permute-start.15
  1168.2 18.1 all-to-all-start.7
  1186.3 18.8 all-to-all-start.6
  1190.5 160.6 %all-reduce.21.cloned.1.call-start = ((), (), s32[]{:S(2)}) async-start(), calls=%async_computation.26 | async-start | bytes 196608
  1224.8 488.4 %reduce-scatter.13.cloned.1.call-start = ((), (), s32[]{:S(2)}) async-start(), calls=%async_computation.23 | async-start | bytes 17301504 | tf_op jit(solution)/shard_map/reduce_scatter | solution.py:352
  1233.0 840.5 %reduce-scatter.7.cloned.1.call-start = ((), (), s32[]{:S(2)}) async-start(), calls=%async_computation.20 | async-start | bytes 17301504 | tf_op jit(solution)/shard_map/reduce_scatter | solution.py:347
  1242.4 1191.3 %reduce-scatter.11.cloned.1.call-start = ((), (), s32[]{:S(2)}) async-start(), calls=%async_computation.22 | async-start | bytes 17301504 | tf_op jit(solution)/shard_map/reduce_scatter | solution.py:350
  1251.9 1542.1 %reduce-scatter.9.cloned.1.call-start = ((), (), s32[]{:S(2)}) async-start(), calls=%async_computation.21 | async-start | bytes 17301504 | tf_op jit(solution)/shard_map/reduce_scatter | solution.py:349
  1261.4 2937.3 %reduce-scatter.15.cloned.1.call-start = ((), (), s32[]{:S(2)}) async-start(), calls=%async_computation.24 | async-start | bytes 69206016 | tf_op jit(solution)/shard_map/reduce_scatter | solution.py:260
  1288.5 4315.7 %reduce-scatter.17.cloned.1.call-start = ((), (), s32[]{:S(2)}) async-start(), calls=%async_computation.25 | async-start | bytes 69206016 | tf_op jit(solution)/shard_map/reduce_scatter | solution.py:262
  (87 other events, 1022.3 us)
Sparse Core Ops, SparseCore 0:
  11.0 80.5 all-gather.9
  94.5 77.4 all-gather.11
  175.0 98.4 all-gather.7
  276.4 205.1 all-gather.13
  484.4 193.8 all-gather.15
  681.1 192.9 all-gather.17
  1224.9 126.1 all-reduce.20
  1354.0 359.1 reduce-scatter.12
  1716.2 357.2 reduce-scatter.6
  2076.3 357.3 reduce-scatter.10
  2436.7 357.3 reduce-scatter.8
  2796.9 1401.7 reduce-scatter.14
  4201.8 1402.4 reduce-scatter.16
where the time goes:
time: 5620 us; the launch traced here: 5610 us
  waiting for transfers between devices  4930 us (88%)
  matrix products  355 us (6%)
  blocking collectives  123 us (2%)
  starting transfers between devices  69.4 us (1%)
  local copies, waits for them, and re-layouts  59.1 us (1%)
    reduce_scatter x1, waiting for transfers between devices, on_device(): lax.psum_scatter(down_grad, ('narrow', 'wide'), scatter_dimension=0, tile...  1410 us
    reduce_scatter x1, waiting for transfers between devices, on_device(): lax.psum_scatter(up_grad, ('narrow', 'wide'), scatter_dimension=0, tiled=...  1400 us
    reduce_scatter x1, waiting for transfers between devices, on_device(): lax.psum_scatter(key_wgrad, ('narrow', 'wide'), scatter_dimension=0, tile...  360 us
    reduce_scatter x1, waiting for transfers between devices, on_device(): lax.psum_scatter(query_wgrad, ('narrow', 'wide'), scatter_dimension=0, ti...  360 us
    reduce_scatter x1, waiting for transfers between devices, on_device(): lax.psum_scatter(value_wgrad, ('narrow', 'wide'), scatter_dimension=0, ti...  360 us
    reduce_scatter x1, waiting for transfers between devices, on_device(): lax.psum_scatter(out_grad, ('narrow', 'wide'), scatter_dimension=0, tiled...  351 us
    ppermute x20, waiting for transfers between devices, shifted(): lax.ppermute(value, axis, [(i, (i + by) % devices) for i in range(devices)])  230 us
    all_gather x1, waiting for transfers between devices, on_device(): lax.all_gather(down_weight, ('narrow', 'wide'), axis=0, tiled=True)  178 us
  transfers between devices with their start and end apart: 41, of which 29 were waited for; matrix products, arithmetic and copies ran while one was open for 6% of the time, Pallas kernels for 0%

commit v1 on v0

--- a/solution.py
+++ b/solution.py
@@ -1,11 +1,16 @@
+import functools
 import math
 
 import jax
 import jax.numpy as jnp
 from jax import lax
+from jax.experimental import pallas as pl
+from jax.experimental.pallas import tpu as pltpu
 from jax.sharding import PartitionSpec as P
 
 HEADS = 16
+NARROW, WIDE = "narrow", "wide"
+BOTH = (NARROW, WIDE)
 REACH = 4
 
 
@@ -123,7 +128,7 @@
     return (query_grad, key_grad, value_grad)
 
 
-def on_device(
+def on_device_ring(
     block_input,
     segment_ids,
     cotangent,
@@ -144,9 +149,9 @@
     down_bias,
 ):
     batch, tokens, model_width = block_input.shape
-    narrow_size = lax.axis_size("narrow")
-    wide_size = lax.axis_size("wide")
-    wide_index = lax.axis_index("wide")
+    narrow_size = lax.axis_size(NARROW)
+    wide_size = lax.axis_size(WIDE)
+    wide_index = lax.axis_index(WIDE)
     group_rows = tokens * narrow_size
     heads_local = HEADS // narrow_size
     head_dim = model_width // HEADS
@@ -154,15 +159,15 @@
     f32 = jnp.float32
     bf16 = jnp.bfloat16
     attn_set = (
-        lax.all_gather(attn_gain, ("narrow", "wide"), axis=0, tiled=True),
-        lax.all_gather(attn_shift, ("narrow", "wide"), axis=0, tiled=True),
-        lax.all_gather(query_weight, ("narrow", "wide"), axis=0, tiled=True),
-        lax.all_gather(query_bias, ("narrow", "wide"), axis=0, tiled=True),
-        lax.all_gather(key_weight, ("narrow", "wide"), axis=0, tiled=True),
-        lax.all_gather(value_weight, ("narrow", "wide"), axis=0, tiled=True),
-        lax.all_gather(value_bias, ("narrow", "wide"), axis=0, tiled=True),
-        lax.all_gather(out_weight, ("narrow", "wide"), axis=0, tiled=True),
-        lax.all_gather(out_bias, ("narrow", "wide"), axis=0, tiled=True),
+        lax.all_gather(attn_gain, BOTH, axis=0, tiled=True),
+        lax.all_gather(attn_shift, BOTH, axis=0, tiled=True),
+        lax.all_gather(query_weight, BOTH, axis=0, tiled=True),
+        lax.all_gather(query_bias, BOTH, axis=0, tiled=True),
+        lax.all_gather(key_weight, BOTH, axis=0, tiled=True),
+        lax.all_gather(value_weight, BOTH, axis=0, tiled=True),
+        lax.all_gather(value_bias, BOTH, axis=0, tiled=True),
+        lax.all_gather(out_weight, BOTH, axis=0, tiled=True),
+        lax.all_gather(out_bias, BOTH, axis=0, tiled=True),
     )
     (
         gain_attn,
@@ -186,11 +191,11 @@
         (matmul(first_norm, value_full) + vbias_full.astype(f32)).astype(bf16).reshape(split_shape)
     )
     query_heads, key_heads, value_heads = (
-        lax.all_to_all(queries, "narrow", split_axis=2, concat_axis=1, tiled=True),
-        lax.all_to_all(key_rows, "narrow", split_axis=2, concat_axis=1, tiled=True),
-        lax.all_to_all(value_rows, "narrow", split_axis=2, concat_axis=1, tiled=True),
-    )
-    query_segs = lax.all_gather(segment_ids, "narrow", axis=1, tiled=True)
+        lax.all_to_all(queries, NARROW, split_axis=2, concat_axis=1, tiled=True),
+        lax.all_to_all(key_rows, NARROW, split_axis=2, concat_axis=1, tiled=True),
+        lax.all_to_all(value_rows, NARROW, split_axis=2, concat_axis=1, tiled=True),
+    )
+    query_segs = lax.all_gather(segment_ids, NARROW, axis=1, tiled=True)
     query_pos = key_positions(wide_index * group_rows, group_rows, tokens, narrow_size, wide_size)
 
     def block_allowed(cycle_step, seg_block):
@@ -207,7 +212,7 @@
     received = []
     for cycle_step in range(REACH + 1):
         if cycle_step > 0:
-            travelling = shifted((travelling[0], travelling[1], travelling[2]), "wide", 1)
+            travelling = shifted((travelling[0], travelling[1], travelling[2]), WIDE, 1)
         received.append(travelling)
         key_block, value_block, seg_block = travelling
         allowed = block_allowed(cycle_step, seg_block)
@@ -216,16 +221,16 @@
     attn_out = weighted / jnp.transpose(row_total, (0, 2, 1))[..., None]
     log_total = row_max + jnp.log(row_total)
     mixed = lax.all_to_all(
-        attn_out.astype(bf16), "narrow", split_axis=1, concat_axis=2, tiled=True
+        attn_out.astype(bf16), NARROW, split_axis=1, concat_axis=2, tiled=True
     ).reshape(-1, model_width)
     middle = inputs + matmul(mixed, out_full) + obias_full.astype(f32)
     mlp_set = (
-        lax.all_gather(mlp_gain, ("narrow", "wide"), axis=0, tiled=True),
-        lax.all_gather(mlp_shift, ("narrow", "wide"), axis=0, tiled=True),
-        lax.all_gather(up_weight, ("narrow", "wide"), axis=0, tiled=True),
-        lax.all_gather(up_bias, ("narrow", "wide"), axis=0, tiled=True),
-        lax.all_gather(down_weight, ("narrow", "wide"), axis=0, tiled=True),
-        lax.all_gather(down_bias, ("narrow", "wide"), axis=0, tiled=True),
+        lax.all_gather(mlp_gain, BOTH, axis=0, tiled=True),
+        lax.all_gather(mlp_shift, BOTH, axis=0, tiled=True),
+        lax.all_gather(up_weight, BOTH, axis=0, tiled=True),
+        lax.all_gather(up_bias, BOTH, axis=0, tiled=True),
+        lax.all_gather(down_weight, BOTH, axis=0, tiled=True),
+        lax.all_gather(down_bias, BOTH, axis=0, tiled=True),
     )
     gain_mlp, shift_mlp, up_full, ubias_full, down_full, dbias_full = mlp_set
     second_norm = normalize(middle, gain_mlp.astype(f32), shift_mlp.astype(f32)).astype(bf16)
@@ -234,12 +239,12 @@
     output = middle + matmul(hidden, down_full) + dbias_full.astype(f32)
     block_output = output.astype(bf16).reshape(batch, tokens, model_width)
     mlp_set = (
-        lax.all_gather(mlp_gain, ("narrow", "wide"), axis=0, tiled=True),
-        lax.all_gather(mlp_shift, ("narrow", "wide"), axis=0, tiled=True),
-        lax.all_gather(up_weight, ("narrow", "wide"), axis=0, tiled=True),
-        lax.all_gather(up_bias, ("narrow", "wide"), axis=0, tiled=True),
-        lax.all_gather(down_weight, ("narrow", "wide"), axis=0, tiled=True),
-        lax.all_gather(down_bias, ("narrow", "wide"), axis=0, tiled=True),
+        lax.all_gather(mlp_gain, BOTH, axis=0, tiled=True),
+        lax.all_gather(mlp_shift, BOTH, axis=0, tiled=True),
+        lax.all_gather(up_weight, BOTH, axis=0, tiled=True),
+        lax.all_gather(up_bias, BOTH, axis=0, tiled=True),
+        lax.all_gather(down_weight, BOTH, axis=0, tiled=True),
+        lax.all_gather(down_bias, BOTH, axis=0, tiled=True),
     )
     gain_mlp, shift_mlp, up_full, ubias_full, down_full, dbias_full = mlp_set
     cotan_rows = cotangent.reshape(-1, model_width)
@@ -255,23 +260,23 @@
     middle_part, mgain_grad, mshift_grad = mlp_pull(second_grad)
     middle_grad = cotan_rows.astype(f32) + middle_part
     mlp_shards = (
-        lax.psum_scatter(mgain_grad, ("narrow", "wide"), scatter_dimension=0, tiled=True),
-        lax.psum_scatter(mshift_grad, ("narrow", "wide"), scatter_dimension=0, tiled=True),
-        lax.psum_scatter(up_grad, ("narrow", "wide"), scatter_dimension=0, tiled=True),
-        lax.psum_scatter(ubias_grad, ("narrow", "wide"), scatter_dimension=0, tiled=True),
-        lax.psum_scatter(down_grad, ("narrow", "wide"), scatter_dimension=0, tiled=True),
-        lax.psum_scatter(dbias_grad, ("narrow", "wide"), scatter_dimension=0, tiled=True),
+        lax.psum_scatter(mgain_grad, BOTH, scatter_dimension=0, tiled=True),
+        lax.psum_scatter(mshift_grad, BOTH, scatter_dimension=0, tiled=True),
+        lax.psum_scatter(up_grad, BOTH, scatter_dimension=0, tiled=True),
+        lax.psum_scatter(ubias_grad, BOTH, scatter_dimension=0, tiled=True),
+        lax.psum_scatter(down_grad, BOTH, scatter_dimension=0, tiled=True),
+        lax.psum_scatter(dbias_grad, BOTH, scatter_dimension=0, tiled=True),
     )
     attn_set = (
-        lax.all_gather(attn_gain, ("narrow", "wide"), axis=0, tiled=True),
-        lax.all_gather(attn_shift, ("narrow", "wide"), axis=0, tiled=True),
-        lax.all_gather(query_weight, ("narrow", "wide"), axis=0, tiled=True),
-        lax.all_gather(query_bias, ("narrow", "wide"), axis=0, tiled=True),
-        lax.all_gather(key_weight, ("narrow", "wide"), axis=0, tiled=True),
-        lax.all_gather(value_weight, ("narrow", "wide"), axis=0, tiled=True),
-        lax.all_gather(value_bias, ("narrow", "wide"), axis=0, tiled=True),
-        lax.all_gather(out_weight, ("narrow", "wide"), axis=0, tiled=True),
-        lax.all_gather(out_bias, ("narrow", "wide"), axis=0, tiled=True),
+        lax.all_gather(attn_gain, BOTH, axis=0, tiled=True),
+        lax.all_gather(attn_shift, BOTH, axis=0, tiled=True),
+        lax.all_gather(query_weight, BOTH, axis=0, tiled=True),
+        lax.all_gather(query_bias, BOTH, axis=0, tiled=True),
+        lax.all_gather(key_weight, BOTH, axis=0, tiled=True),
+        lax.all_gather(value_weight, BOTH, axis=0, tiled=True),
+        lax.all_gather(value_bias, BOTH, axis=0, tiled=True),
+        lax.all_gather(out_weight, BOTH, axis=0, tiled=True),
+        lax.all_gather(out_bias, BOTH, axis=0, tiled=True),
     )
     (
         gain_attn,
@@ -288,13 +293,13 @@
     out_grad = outer_sum(mixed, branch_grad)
     obias_grad = jnp.sum(branch_grad.astype(f32), axis=0)
     mixed_grad = times_transpose(branch_grad, out_full).astype(bf16).reshape(split_shape)
-    dout_heads = lax.all_to_all(mixed_grad, "narrow", split_axis=2, concat_axis=1, tiled=True)
+    dout_heads = lax.all_to_all(mixed_grad, NARROW, split_axis=2, concat_axis=1, tiled=True)
     delta = jnp.transpose(jnp.sum(dout_heads.astype(f32) * attn_out, axis=-1), (0, 2, 1))
     travelling = (key_heads, value_heads, query_segs)
     received = []
     for cycle_step in range(REACH + 1):
         if cycle_step > 0:
-            travelling = shifted((travelling[0], travelling[1], travelling[2]), "wide", 1)
+            travelling = shifted((travelling[0], travelling[1], travelling[2]), WIDE, 1)
         received.append(travelling)
     query_grad = jnp.zeros((batch, group_rows, heads_local, head_dim), f32)
     key_terms = []
@@ -317,13 +322,13 @@
         value_terms.append(value_term)
     carried = (key_terms[REACH], value_terms[REACH])
     for cycle_step in range(REACH - 1, -1, -1):
-        arrived = shifted((as_sent(carried[0]), as_sent(carried[1])), "wide", -1)
+        arrived = shifted((as_sent(carried[0]), as_sent(carried[1])), WIDE, -1)
         carried = (arrived[0] + key_terms[cycle_step], arrived[1] + value_terms[cycle_step])
     key_sum, value_sum = carried
     query_back, key_back, value_back = (
-        lax.all_to_all(query_grad.astype(bf16), "narrow", split_axis=1, concat_axis=2, tiled=True),
-        lax.all_to_all(key_sum.astype(bf16), "narrow", split_axis=1, concat_axis=2, tiled=True),
-        lax.all_to_all(value_sum.astype(bf16), "narrow", split_axis=1, concat_axis=2, tiled=True),
+        lax.all_to_all(query_grad.astype(bf16), NARROW, split_axis=1, concat_axis=2, tiled=True),
+        lax.all_to_all(key_sum.astype(bf16), NARROW, split_axis=1, concat_axis=2, tiled=True),
+        lax.all_to_all(value_sum.astype(bf16), NARROW, split_axis=1, concat_axis=2, tiled=True),
     )
     query_back = query_back.reshape(-1, model_width)
     key_back = key_back.reshape(-1, model_width)
@@ -342,15 +347,15 @@
     input_part, again_grad, ashift_grad = attn_pull(first_grad)
     input_grad = (middle_grad + input_part).reshape(batch, tokens, model_width)
     attn_shards = (
-        lax.psum_scatter(again_grad, ("narrow", "wide"), scatter_dimension=0, tiled=True),
-        lax.psum_scatter(ashift_grad, ("narrow", "wide"), scatter_dimension=0, tiled=True),
-        lax.psum_scatter(query_wgrad, ("narrow", "wide"), scatter_dimension=0, tiled=True),
-        lax.psum_scatter(qbias_grad, ("narrow", "wide"), scatter_dimension=0, tiled=True),
-        lax.psum_scatter(key_wgrad, ("narrow", "wide"), scatter_dimension=0, tiled=True),
-        lax.psum_scatter(value_wgrad, ("narrow", "wide"), scatter_dimension=0, tiled=True),
-        lax.psum_scatter(vbias_grad, ("narrow", "wide"), scatter_dimension=0, tiled=True),
-        lax.psum_scatter(out_grad, ("narrow", "wide"), scatter_dimension=0, tiled=True),
-        lax.psum_scatter(obias_grad, ("narrow", "wide"), scatter_dimension=0, tiled=True),
+        lax.psum_scatter(again_grad, BOTH, scatter_dimension=0, tiled=True),
+        lax.psum_scatter(ashift_grad, BOTH, scatter_dimension=0, tiled=True),
+        lax.psum_scatter(query_wgrad, BOTH, scatter_dimension=0, tiled=True),
+        lax.psum_scatter(qbias_grad, BOTH, scatter_dimension=0, tiled=True),
+        lax.psum_scatter(key_wgrad, BOTH, scatter_dimension=0, tiled=True),
+        lax.psum_scatter(value_wgrad, BOTH, scatter_dimension=0, tiled=True),
+        lax.psum_scatter(vbias_grad, BOTH, scatter_dimension=0, tiled=True),
+        lax.psum_scatter(out_grad, BOTH, scatter_dimension=0, tiled=True),
+        lax.psum_scatter(obias_grad, BOTH, scatter_dimension=0, tiled=True),
     )
     return (
         block_output,
@@ -373,48 +378,349 @@
     )
 
 
+def all_small(parts):
+    packed = jnp.concatenate(parts)[None]
+    return lax.all_gather(packed, BOTH, axis=0, tiled=True)
+
+
+def fwd_kernel(segc_ref, segr_ref, qkv_ref, out_ref, lse_ref, *, blocks, scale2):
+    half = blocks // 4
+    for i in range(blocks):
+        w0, n = 4 * (i % half), i // half
+        q = qkv_ref[w0 : w0 + 4, 0, n].reshape(512, 128)
+        lo = max(i - 1, 0)
+        k = jnp.concatenate(
+            [qkv_ref[4 * (j % half) : 4 * (j % half) + 4, 1, j // half] for j in range(lo, i + 1)]
+        ).reshape(-1, 128)
+        v = jnp.concatenate(
+            [qkv_ref[4 * (j % half) : 4 * (j % half) + 4, 2, j // half] for j in range(lo, i + 1)]
+        ).reshape(-1, 128)
+        allowed = mask_of(segc_ref, segr_ref, i, lo)
+        s = lax.dot_general(q, k, (((1,), (1,)), ((), ())), preferred_element_type=jnp.float32)
+        s = jnp.where(allowed, s * scale2, neg_big)
+        m = jnp.max(s, axis=-1, keepdims=True)
+        p = jnp.exp2(s - m)
+        total = jnp.sum(p, axis=-1, keepdims=True)
+        o = jnp.dot(p.astype(jnp.bfloat16), v, preferred_element_type=jnp.float32)
+        o = o / total
+        out_ref[w0 : w0 + 4, n] = o.astype(jnp.bfloat16).reshape(4, 128, 128)
+        lse_ref[i] = m + jnp.log2(total)
+
+
+def mask_of(segc_ref, segr_ref, i, lo):
+    keys = 512 * (i + 1 - lo)
+    same = segc_ref[i] == segr_ref[:, 512 * lo : 512 * (i + 1)]
+    rows = lax.broadcasted_iota(jnp.int32, (512, keys), 0) + 512 * (i - lo)
+    cols = lax.broadcasted_iota(jnp.int32, (512, keys), 1)
+    return jnp.logical_and(same, cols <= rows)
+
+
+def bwd_kernel(segc_ref, segr_ref, qkv_ref, do_ref, lse_ref, grad_ref, dk_acc, dv_acc, *, blocks, scale, scale2):
+    half = blocks // 4
+    f32 = jnp.float32
+
+    def at(j):
+        return slice(4 * (j % half), 4 * (j % half) + 4), j // half
+
+    for i in range(blocks):
+        wi, n = at(i)
+        q = qkv_ref[wi, 0, n].reshape(512, 128)
+        do = do_ref[wi, n].reshape(512, 128)
+        lo = max(i - 1, 0)
+        k = jnp.concatenate([qkv_ref[at(j)[0], 1, at(j)[1]] for j in range(lo, i + 1)]).reshape(-1, 128)
+        v = jnp.concatenate([qkv_ref[at(j)[0], 2, at(j)[1]] for j in range(lo, i + 1)]).reshape(-1, 128)
+        allowed = mask_of(segc_ref, segr_ref, i, lo)
+        s = lax.dot_general(q, k, (((1,), (1,)), ((), ())), preferred_element_type=f32)
+        p = jnp.exp2(jnp.where(allowed, s * scale2, neg_big) - lse_ref[i])
+        dp = lax.dot_general(do, v, (((1,), (1,)), ((), ())), preferred_element_type=f32)
+        t = p * dp
+        delta = jnp.sum(t, axis=-1, keepdims=True)
+        ds = (t - p * delta).astype(jnp.bfloat16)
+        dq = jnp.dot(ds, k, preferred_element_type=f32) * scale
+        grad_ref[wi, 0, n] = dq.astype(jnp.bfloat16).reshape(4, 128, 128)
+        dk = lax.dot_general(ds, q, (((0,), (0,)), ((), ())), preferred_element_type=f32)
+        dv = lax.dot_general(
+            p.astype(jnp.bfloat16), do, (((0,), (0,)), ((), ())), preferred_element_type=f32
+        )
+        if i > 0:
+            wp, np_ = at(i - 1)
+            grad_ref[wp, 1, np_] = (
+                ((dk_acc[...] + dk[:512]) * scale).astype(jnp.bfloat16).reshape(4, 128, 128)
+            )
+            grad_ref[wp, 2, np_] = (dv_acc[...] + dv[:512]).astype(jnp.bfloat16).reshape(4, 128, 128)
+        if i == blocks - 1:
+            grad_ref[wi, 1, n] = (dk[-512:] * scale).astype(jnp.bfloat16).reshape(4, 128, 128)
+            grad_ref[wi, 2, n] = dv[-512:].astype(jnp.bfloat16).reshape(4, 128, 128)
+        else:
+            dk_acc[...] = dk[-512:]
+            dv_acc[...] = dv[-512:]
+
+
+def whole_vmem(count):
+    return [pl.BlockSpec(memory_space=pltpu.VMEM)] * count
+
+
+def attend_fwd(segc, segr, qkv):
+    blocks = segc.shape[0]
+    wide, _, narrow, rows, width = qkv.shape
+    scale2 = math.log2(math.e) / math.sqrt(width)
+    return pl.pallas_call(
+        functools.partial(fwd_kernel, blocks=blocks, scale2=scale2),
+        out_shape=(
+            jax.ShapeDtypeStruct((wide, narrow, rows, width), jnp.bfloat16),
+            jax.ShapeDtypeStruct((blocks, 512, 1), jnp.float32),
+        ),
+        in_specs=whole_vmem(3),
+        out_specs=tuple(whole_vmem(2)),
+        compiler_params=pltpu.CompilerParams(vmem_limit_bytes=48 << 20),
+        name="attend_fwd",
+    )(segc, segr, qkv)
+
+
+def attend_bwd(segc, segr, qkv, dout, lse):
+    blocks = segc.shape[0]
+    width = qkv.shape[-1]
+    scale = 1.0 / math.sqrt(width)
+    return pl.pallas_call(
+        functools.partial(
+            bwd_kernel, blocks=blocks, scale=scale, scale2=scale * math.log2(math.e)
+        ),
+        out_shape=jax.ShapeDtypeStruct(qkv.shape, jnp.bfloat16),
+        in_specs=whole_vmem(5),
+        out_specs=whole_vmem(1)[0],
+        scratch_shapes=[pltpu.VMEM((512, width), jnp.float32)] * 2,
+        compiler_params=pltpu.CompilerParams(vmem_limit_bytes=48 << 20),
+        name="attend_bwd",
+    )(segc, segr, qkv, dout, lse)
+
+
+def narrow_gather(rows):
+    return lax.all_gather(rows, NARROW, axis=0, tiled=True)
+
+
+def narrow_scatter(partial):
+    return lax.psum_scatter(
+        partial.astype(jnp.bfloat16), NARROW, scatter_dimension=0, tiled=True
+    ).astype(jnp.float32)
+
+
+def wide_swap(parts):
+    return lax.all_to_all(parts, WIDE, split_axis=0, concat_axis=0, tiled=True)
+
+
+def narrow_swap(parts):
+    return lax.all_to_all(parts, NARROW, split_axis=0, concat_axis=0, tiled=True)
+
+
+def wide_gather(shard, axis):
+    return lax.all_gather(shard, WIDE, axis=axis, tiled=True)
+
+
+def wide_scatter(full, axis):
+    return lax.psum_scatter(full.astype(jnp.bfloat16), WIDE, scatter_dimension=axis, tiled=True)
+
+
+def on_device(
+    block_input,
+    segment_ids,
+    cotangent,
+    attn_gain,
+    attn_shift,
+    query_weight,
+    query_bias,
+    key_weight,
+    value_weight,
+    value_bias,
+    out_weight,
+    out_bias,
+    mlp_gain,
+    mlp_shift,
+    up_weight,
+    up_bias,
+    down_weight,
+    down_bias,
+):
+    f32 = jnp.float32
+    bf16 = jnp.bfloat16
+    batch, tokens, width = block_input.shape
+    narrow = lax.axis_size(NARROW)
+    wide = lax.axis_size(WIDE)
+    me_n = lax.axis_index(NARROW)
+    me_w = lax.axis_index(WIDE)
+    rows = batch * tokens
+    heads_local = HEADS // narrow
+    head_dim = width // HEADS
+    cols = heads_local * head_dim
+    shard = width // (narrow * wide)
+
+    qkv_shard = jnp.stack([query_weight, key_weight, value_weight], axis=1)
+    qkv_shard = qkv_shard.reshape(shard, 3, narrow, cols).transpose(2, 0, 1, 3)
+    qkv_shard = narrow_swap(qkv_shard.reshape(narrow, shard, 3 * cols))
+    qkv_w = wide_gather(qkv_shard, 1).reshape(width, 3 * cols)
+    out_w = wide_gather(out_weight, 0)
+    ff_local = up_weight.shape[1] // narrow
+    up_shard = narrow_swap(up_weight.reshape(shard, narrow, ff_local).transpose(1, 0, 2))
+    up_w = wide_gather(up_shard, 1).reshape(width, ff_local)
+    down_w = wide_gather(down_weight, 0)
+
+    smalls = [
+        attn_gain, attn_shift, out_bias, mlp_gain, mlp_shift, down_bias, query_bias, value_bias, up_bias
+    ]
+    small = all_small(smalls)
+
+    def full_vector(k):
+        return small[:, k * shard : (k + 1) * shard].reshape(-1).astype(f32)
+
+    gain_attn, shift_attn, obias, gain_mlp, shift_mlp, dbias = [full_vector(k) for k in range(6)]
+    mine = lax.dynamic_slice_in_dim(small, me_n * wide, wide, 0)
+    qbias = mine[:, 6 * shard : 7 * shard].reshape(-1).astype(f32)
+    vbias = mine[:, 7 * shard : 8 * shard].reshape(-1).astype(f32)
+    ubias = mine[:, 8 * shard :].reshape(-1).astype(f32)
+    qkv_bias = jnp.concatenate([qbias, jnp.zeros_like(qbias), vbias])
+
+    segs = lax.all_gather(segment_ids[None], BOTH, axis=0, tiled=True)
+    unit_segs = lax.dynamic_index_in_dim(segs, me_w // heads_local, 1, keepdims=False).reshape(-1)
+    seq_blocks = unit_segs.shape[0] // 512
+    segc = unit_segs.reshape(seq_blocks, 512, 1)
+    segr = unit_segs.reshape(1, -1)
+
+    inputs = block_input.astype(f32).reshape(rows, width)
+    first_norm = narrow_gather(normalize(inputs, gain_attn, shift_attn).astype(bf16))
+    qkv = (matmul(first_norm, qkv_w) + qkv_bias).astype(bf16)
+    qkv = qkv.reshape(narrow, batch, tokens, 3, heads_local, head_dim).transpose(1, 4, 3, 0, 2, 5)
+    qkv = wide_swap(qkv.reshape(wide, 3, narrow, tokens, head_dim))
+    unit_out, lse = attend_fwd(segc, segr, qkv)
+    mixed = wide_swap(unit_out)
+    mixed = mixed.reshape(batch, heads_local, narrow, tokens, head_dim).transpose(2, 0, 3, 1, 4)
+    mixed = mixed.reshape(narrow * rows, cols)
+    middle = inputs + narrow_scatter(matmul(mixed, out_w)) + obias
+
+    second_norm = narrow_gather(normalize(middle, gain_mlp, shift_mlp).astype(bf16))
+    inner = matmul(second_norm, up_w) + ubias
+    hidden = gelu_exact(inner).astype(bf16)
+    output = middle + narrow_scatter(matmul(hidden, down_w)) + dbias
+    block_output = output.astype(bf16).reshape(batch, tokens, width)
+
+    cotan_own = cotangent.reshape(rows, width)
+    cotan = narrow_gather(cotan_own)
+    down_grad = wide_scatter(outer_sum(hidden, cotan), 0)
+    hidden_grad = times_transpose(cotan, down_w)
+    inner_grad = jax.vjp(gelu_exact, inner)[1](hidden_grad)[0].astype(bf16)
+    up_grad = outer_sum(second_norm, inner_grad).reshape(narrow, wide * shard, ff_local)
+    up_grad = narrow_swap(wide_scatter(up_grad, 1)).transpose(1, 0, 2).reshape(shard, -1)
+    ubias_grad = jnp.sum(inner_grad.astype(f32), axis=0)
+    second_grad = narrow_scatter(times_transpose(inner_grad, up_w))
+    mlp_pull = jax.vjp(normalize, middle, gain_mlp, shift_mlp)[1]
+    middle_part, mgain_grad, mshift_grad = mlp_pull(second_grad)
+    dbias_grad = jnp.sum(cotan_own.astype(f32), axis=0)
+    middle_grad = cotan_own.astype(f32) + middle_part
+
+    branch_own = middle_grad.astype(bf16)
+    obias_grad = jnp.sum(branch_own.astype(f32), axis=0)
+    branch = narrow_gather(branch_own)
+    mixed_grad = times_transpose(branch, out_w).astype(bf16)
+    mixed_grad = mixed_grad.reshape(narrow, batch, tokens, heads_local, head_dim)
+    dout = wide_swap(mixed_grad.transpose(1, 3, 0, 2, 4).reshape(wide, narrow, tokens, head_dim))
+    out_grad = wide_scatter(outer_sum(mixed, branch), 0)
+    unit_grads = attend_bwd(segc, segr, qkv, dout, lse)
+    back = wide_swap(unit_grads)
+    back = back.reshape(batch, heads_local, 3, narrow, tokens, head_dim).transpose(3, 0, 4, 2, 1, 5)
+    back = back.reshape(narrow * rows, 3 * cols)
+    qkv_grad = outer_sum(first_norm, back).reshape(narrow, wide * shard, 3 * cols)
+    qkv_grad = narrow_swap(wide_scatter(qkv_grad, 1)).reshape(narrow, shard, 3, cols)
+    qkv_grad = qkv_grad.transpose(2, 1, 0, 3).reshape(3, shard, width).astype(f32)
+    back_sums = jnp.sum(back.astype(f32), axis=0)
+    first_grad = narrow_scatter(times_transpose(back, qkv_w))
+    attn_pull = jax.vjp(normalize, inputs, gain_attn, shift_attn)[1]
+    input_part, again_grad, ashift_grad = attn_pull(first_grad)
+    input_grad = (middle_grad + input_part).reshape(batch, tokens, width)
+
+    fulls = [again_grad, ashift_grad, obias_grad, mgain_grad, mshift_grad, dbias_grad]
+    fulls = jnp.concatenate([v.reshape(narrow * wide, shard) for v in fulls], axis=1)
+    slices = [back_sums[:cols], back_sums[2 * cols :], ubias_grad]
+    slices = jnp.concatenate([v.reshape(wide, -1) for v in slices], axis=1)
+    placed = jnp.zeros((narrow * wide, slices.shape[1]), f32)
+    placed = lax.dynamic_update_slice_in_dim(placed, slices, me_n * wide, 0)
+    vectors = lax.psum_scatter(
+        jnp.concatenate([fulls, placed], axis=1), BOTH, scatter_dimension=0, tiled=True
+    ).reshape(-1)
+
+    def vector(k):
+        return vectors[k * shard : (k + 1) * shard]
+
+    return (
+        block_output,
+        input_grad,
+        vector(0),
+        vector(1),
+        qkv_grad[0],
+        vector(6),
+        qkv_grad[1],
+        qkv_grad[2],
+        vector(7),
+        out_grad.astype(f32),
+        vector(2),
+        vector(3),
+        vector(4),
+        up_grad.astype(f32),
+        vectors[8 * shard :],
+        down_grad.astype(f32),
+        vector(5),
+    )
+
+
+def body_of(mesh):
+    def body(*args):
+        batch, tokens, width = args[0].shape
+        narrow, wide = mesh.shape[NARROW], mesh.shape[WIDE]
+        one_unit = batch * (HEADS // narrow) == wide and tokens == 128 and narrow == 4
+        return (on_device if one_unit else on_device_ring)(*args)
+
+    return body
+
+
 def solution(mesh):
     return jax.shard_map(
-        on_device,
+        body_of(mesh),
         mesh=mesh,
         in_specs=(
-            P(None, ("narrow", "wide"), None),
-            P(None, ("narrow", "wide")),
-            P(None, ("narrow", "wide"), None),
-            P(("narrow", "wide")),
-            P(("narrow", "wide")),
-            P(("narrow", "wide"), None),
-            P(("narrow", "wide")),
-            P(("narrow", "wide"), None),
-            P(("narrow", "wide"), None),
-            P(("narrow", "wide")),
-            P(("narrow", "wide"), None),
-            P(("narrow", "wide")),
-            P(("narrow", "wide")),
-            P(("narrow", "wide")),
-            P(("narrow", "wide"), None),
-            P(("narrow", "wide")),
-            P(("narrow", "wide"), None),
-            P(("narrow", "wide")),
+            P(None, BOTH, None),
+            P(None, BOTH),
+            P(None, BOTH, None),
+            P(BOTH),
+            P(BOTH),
+            P(BOTH, None),
+            P(BOTH),
+            P(BOTH, None),
+            P(BOTH, None),
+            P(BOTH),
+            P(BOTH, None),
+            P(BOTH),
+            P(BOTH),
+            P(BOTH),
+            P(BOTH, None),
+            P(BOTH),
+            P(BOTH, None),
+            P(BOTH),
         ),
         out_specs=(
-            P(None, ("narrow", "wide"), None),
-            P(None, ("narrow", "wide"), None),
-            P(("narrow", "wide")),
-            P(("narrow", "wide")),
-            P(("narrow", "wide"), None),
-            P(("narrow", "wide")),
-            P(("narrow", "wide"), None),
-            P(("narrow", "wide"), None),
-            P(("narrow", "wide")),
-            P(("narrow", "wide"), None),
-            P(("narrow", "wide")),
-            P(("narrow", "wide")),
-            P(("narrow", "wide")),
-            P(("narrow", "wide"), None),
-            P(("narrow", "wide")),
-            P(("narrow", "wide"), None),
-            P(("narrow", "wide")),
+            P(None, BOTH, None),
+            P(None, BOTH, None),
+            P(BOTH),
+            P(BOTH),
+            P(BOTH, None),
+            P(BOTH),
+            P(BOTH, None),
+            P(BOTH, None),
+            P(BOTH),
+            P(BOTH, None),
+            P(BOTH),
+            P(BOTH),
+            P(BOTH),
+            P(BOTH, None),
+            P(BOTH),
+            P(BOTH, None),
+            P(BOTH),
         ),
         check_vma=False,
     )

time: 5620 us -> 1760 us (0.31)
  waiting for transfers between devices: 4930 us -> 1060 us
  blocking collectives: 123 us -> 349 us
  matrix products: 355 us -> 151 us
    reduce_scatter x6 -> x8, waiting for transfers between devices: 4240 us -> 455 us  [the longest x4 333 us: wide_scatter(): lax.psum_scatter(full.astype(jnp.bfloat16), WIDE, scatter_dimension=axis,...]
    ppermute x20 -> x0, waiting for transfers between devices: 230 us -> none  [shifted(): lax.ppermute(value, axis, [(i, (i + by) % devices) for i in range(devices)])]
    all_gather x2, blocking collectives: 79.7 us -> 220 us  [the longest x1 150 us: on_device(): segs = lax.all_gather(segment_ids[None], BOTH, axis=0, tiled=True)]
    dot_general x30 -> x0, matrix products: 132 us -> none  [the longest x5 31.3 us: backward_block(): jnp.einsum('bhqk,bqhd->bkhd', attn_probs.astype(jnp.bfloat16), dout_heads...]
    all_to_all x0 -> x4, blocking collectives: none -> 129 us  [the longest x2 84.4 us: wide_swap(): return lax.all_to_all(parts, WIDE, split_axis=0, concat_axis=0, tiled=True)]
    unnamed x14 -> x18, waiting for transfers between devices: 10.9 us -> 120 us
    all_to_all x8 -> x4, waiting for transfers between devices: 17 us -> 76.2 us  [the longest x2 76.2 us: wide_swap(): return lax.all_to_all(parts, WIDE, split_axis=0, concat_axis=0, tiled=True)]
    all_gather x6 -> x8, waiting for transfers between devices: 435 us -> 407 us  [the longest x4 345 us: wide_gather(): return lax.all_gather(shard, WIDE, axis=axis, tiled=True)]
  transfers between devices with their start and end apart: 41 -> 21, of which waited for: 29 -> 17; matrix products, arithmetic and copies ran while one was open for 6% -> 10% of each run, Pallas kernels for 0% -> 1%
where the time goes in v1:
time: 1760 us; the launch traced here: 1750 us
  waiting for transfers between devices  1060 us (60%)
  blocking collectives  349 us (20%)
  matrix products  151 us (9%)
  local copies, waits for them, and re-layouts  88.5 us (5%)
  other arithmetic  46.2 us (3%)
  Pallas kernels  25.5 us (1%)
  starting transfers between devices  18.3 us (1%)
    all_gather x4, waiting for transfers between devices, wide_gather(): return lax.all_gather(shard, WIDE, axis=axis, tiled=True)  345 us
    reduce_scatter x4, waiting for transfers between devices, wide_scatter(): lax.psum_scatter(full.astype(jnp.bfloat16), WIDE, scatter_dimension=axis,...  333 us
    all_gather x1, blocking collectives, on_device(): segs = lax.all_gather(segment_ids[None], BOTH, axis=0, tiled=True)  150 us
    reduce_scatter x4, waiting for transfers between devices, narrow_scatter(): lax.psum_scatter(partial.astype(jnp.bfloat16), NARROW, scatter_dimension=...  122 us
    unnamed x18, waiting for transfers between devices  120 us
    all_to_all x2, blocking collectives, wide_swap(): return lax.all_to_all(parts, WIDE, split_axis=0, concat_axis=0, tiled=True)  84.4 us
    all_to_all x2, waiting for transfers between devices, wide_swap(): return lax.all_to_all(parts, WIDE, split_axis=0, concat_axis=0, tiled=True)  76.2 us
    all_gather x1, blocking collectives, all_small(): return lax.all_gather(packed, BOTH, axis=0, tiled=True)  70.2 us
  transfers between devices with their start and end apart: 21, of which 17 were waited for; matrix products, arithmetic and copies ran while one was open for 10% of the time, Pallas kernels for 1%

profile of v1, /device:TPU:0, one launch (start us, length us, event | category | flops | bytes accessed | tf_op | source)
XLA Modules:
  0.0 1751.9 jit_solution(891872655934756459)
XLA Ops:
  7.3 6.1 concatenate.13
  13.4 70.2 %all-gather.3 = bf16[32,1,768]{2,1,0:T(2,128)(2,1)S(1)} all-gather(bf16[1,1,768]{2,1,0:T(2,128)(2,1)S(1)} %reshape.335), channel_id=3, replica_groups=mesh['narrow'=4,'wide'=8] {'narrow','wide'}, dimensions={0}, use_global_device_ids=true | all-gather | bytes 50688 | tf_op jit(solution)/shard_map/all_gather | solution.py:383
  87.6 2.7 fusion.18
  95.1 23.5 %all_to_all.40 = bf16[4,64,1536]{2,1,0:T(8,128)(2,1)} all-to-all(bf16[4,64,1536]{2,1,0:T(8,128)(2,1)S(1)} %reshape.298), channel_id=1, replica_groups=mesh['narrow'=4,'wide'=8] {'narrow'}, dimensions={0} | all-to-all | bytes 1572864 | tf_op jit(solution)/shard_map/all_to_all | solution.py:512
  119.0 10.7 all-gather.13.cloned.1.call-done
  129.6 99.5 %all-gather.15.cloned.1.call-done = bf16[4,512,1536]{2,1,0:T(8,128)(2,1)} async-done(((bf16[4,64,1536]{2,1,0:T(8,128)(2,1)}), bf16[4,512,1536]{2,1,0:T(8,128)(2,1)}) %all-gather.15.cloned.1.call-update) | async-done | bytes 6291472 | tf_op jit(solution)/shard_map/all_gather | solution.py:516
  229.2 11.2 add_convert_fusion.1
  240.4 5.0 reshape.300
  245.4 2.6 copy.73
  247.9 4.6 all-to-all-start.1
  253.4 150.0 %all-gather.2 = s32[32,2,128]{2,1,0:T(2,128)S(1)} all-gather(s32[1,2,128]{2,1,0:T(2,128)S(1)} %bitcast.174), channel_id=2, replica_groups=mesh['narrow'=4,'wide'=8] {'narrow','wide'}, dimensions={0}, use_global_device_ids=true | all-gather | bytes 33792 | tf_op jit(solution)/shard_map/all_gather | solution.py:581
  403.4 1.9 reshape_reshape.8.segc_ref
  405.4 8.2 attend_fwd.1
  414.9 26.9 %all_to_all.41 = bf16[8,4,128,128]{3,2,1,0:T(8,128)(2,1)S(1)} all-to-all(bf16[8,4,128,128]{3,2,1,0:T(8,128)(2,1)S(1)} %get-tuple-element.19), channel_id=1, replica_groups=mesh['narrow'=4,'wide'=8] {'wide'}, dimensions={0} | all-to-all | bytes 2097152 | tf_op jit(solution)/shard_map/all_to_all | solution.py:508
  443.6 5.9 convolution_convert_fusion.6
  452.3 2.2 copy.76
  454.5 20.8 %all_to_all.42 = bf16[4,64,2048]{2,1,0:T(8,128)(2,1)S(1)} all-to-all(bf16[4,64,2048]{2,1,0:T(8,128)(2,1)S(1)} %copy.76), channel_id=1, replica_groups=mesh['narrow'=4,'wide'=8] {'narrow'}, dimensions={0} | all-to-all | bytes 2097152 | tf_op jit(solution)/shard_map/all_to_all | solution.py:512
  477.4 18.3 %reduce-scatter.9.cloned.1.call-done = bf16[256,2048]{1,0:T(8,128)(2,1)} async-done(((bf16[1024,2048]{1,0:T(8,128)(2,1)}), bf16[256,2048]{1,0:T(8,128)(2,1)}) %reduce-scatter.9.cloned.1.call-update) | async-done | bytes 1048592 | tf_op jit(solution)/shard_map/reduce_scatter | solution.py:502
  502.5 118.6 %all-gather.21.cloned.1.call-done = bf16[4,512,2048]{2,0,1:T(4,128)(2,1)} async-done(((bf16[4,64,2048]{2,0,1:T(4,128)(2,1)}), bf16[4,512,2048]{2,0,1:T(4,128)(2,1)}) %all-gather.21.cloned.1.call-update) | async-done | bytes 8388624 | tf_op jit(solution)/shard_map/all_gather | solution.py:516
  621.1 11.5 copy.78
  632.6 23.3 %all-gather.19.cloned.1.call-done = bf16[1024,2048]{1,0:T(8,128)(2,1)} async-done(((bf16[256,2048]{1,0:T(8,128)(2,1)}), bf16[1024,2048]{1,0:T(8,128)(2,1)}) %all-gather.19.cloned.1.call-update) | async-done | bytes 4194320 | tf_op jit(solution)/shard_map/all_gather | solution.py:498
  655.9 14.6 fusion.36
  670.5 21.6 %all-gather.25.cloned.1.call-done = bf16[1024,2048]{1,0:T(8,128)(2,1)} async-done(((bf16[256,2048]{1,0:T(8,128)(2,1)}), bf16[1024,2048]{1,0:T(8,128)(2,1)}) %all-gather.25.cloned.1.call-update) | async-done | bytes 4194320 | tf_op jit(solution)/shard_map/all_gather | solution.py:498
  692.0 127.3 %all-gather.23.cloned.1.call-done = bf16[2048,2048]{1,0:T(8,128)(2,1)} async-done(((bf16[256,2048]{1,0:T(8,128)(2,1)}), bf16[2048,2048]{1,0:T(8,128)(2,1)}) %all-gather.23.cloned.1.call-update) | async-done | bytes 8388624 | tf_op jit(solution)/shard_map/all_gather | solution.py:516
  819.3 33.1 %convert_reduce_fusion = (f32[2048]{0:T(1024)S(1)}, bf16[1024,2048]{1,0:T(8,128)(2,1)S(1)}, f32[1024,2048]{1,0:T(8,128)}) fusion(f32[1024,2048]{1,0:T(8,128)} %fusion.36, f32[2048]{0:T(1024)S(1)} %bitcast.172, bf16[1024,2048]{1,0:T(8,128)(2,1)} %all-gather.25.cloned.1.call-done, bf16[2048,2048]{1,0:T(8,128)(2,1)} %all-gather.23.cloned.1.call-done), kind=kOutput, calls=%fused_computation.2 | convolution fusion | flops 8747218944 | bytes 33570816 | tf_op jit(solution)/shard_map/dot_general | solution.py:56
  852.4 2.0 copy-done.37
  854.4 10.6 convolution_convert_fusion.4
  865.1 9.0 multiply_convert_fusion
  874.2 2.0 copy-done.10
  876.2 12.6 convolution_convert_fusion.5
  889.6 18.3 %reduce-scatter.13.cloned.1.call-done = bf16[256,2048]{1,0:T(8,128)(2,1)} async-done(((bf16[1024,2048]{1,0:T(8,128)(2,1)}), bf16[256,2048]{1,0:T(8,128)(2,1)}) %reduce-scatter.13.cloned.1.call-update) | async-done | bytes 1048592 | tf_op jit(solution)/shard_map/reduce_scatter | solution.py:502
  907.9 2.6 fusion.12
  910.6 44.3 %reduce-scatter.11.cloned.1.call-done = bf16[256,2048]{1,0:T(8,128)(2,1)} async-done(((bf16[1024,2048]{1,0:T(8,128)(2,1)}), bf16[256,2048]{1,0:T(8,128)(2,1)}) %reduce-scatter.11.cloned.1.call-update) | async-done | bytes 1048592 | tf_op jit(solution)/shard_map/reduce_scatter | solution.py:502
  954.8 4.0 fusion.34
  962.1 14.1 convolution_convert_fusion.1
  976.3 14.0 convolution_convert_fusion
  990.3 6.0 all-gather.27.cloned.1.call-done
  996.3 6.2 convolution_convert_fusion.8
  1002.5 2.2 reshape.308
  1006.3 57.6 %all_to_all.43.do_ref = bf16[8,4,128,128]{3,2,1,0:T(8,128)(2,1)S(1)} all-to-all(bf16[8,4,128,128]{3,2,1,0:T(8,128)(2,1)S(1)} %bitcast.156), channel_id=1, replica_groups=mesh['narrow'=4,'wide'=8] {'wide'}, dimensions={0} | all-to-all | bytes 2097152 | tf_op jit(solution)/shard_map/all_to_all | solution.py:508
  1063.8 17.2 attend_bwd.1
  1081.0 4.6 all-to-all-start.5
  1085.7 5.9 convolution_convert_fusion.7
  1091.7 76.2 %all-to-all-done.5 = bf16[8,3,4,128,128]{4,3,2,1,0:T(8,128)(2,1)} async-done(((bf16[8,3,4,128,128]{4,3,2,1,0:T(8,128)(2,1)}), bf16[8,3,4,128,128]{4,3,2,1,0:T(8,128)(2,1)}, u32[]{:S(2)}, u32[]{:S(2)}) %all-to-all-start.5) | async-done | bytes 3145760 | tf_op jit(solution)/shard_map/all_to_all | solution.py:508
  1167.8 6.0 copy.81
  1173.8 6.1 reshape.311
  1179.9 11.7 convolution_convert_fusion.3
  1191.6 6.7 copy.87
  1198.3 6.1 reshape.342
  1204.4 11.4 convolution_convert_fusion.2
  1215.8 2.8 reduce-scatter.21.cloned.1.call-done
  1218.6 3.5 all-to-all-start.7
  1222.7 147.6 %reduce-scatter.23.cloned.1.call-done = bf16[256,2048]{1,0:T(8,128)(2,1)} async-done(((bf16[2048,2048]{1,0:T(8,128)(2,1)}), bf16[256,2048]{1,0:T(8,128)(2,1)}) %reduce-scatter.23.cloned.1.call-update) | async-done | bytes 1048592 | tf_op jit(solution)/shard_map/reduce_scatter | solution.py:520
  1370.3 2.8 convert_element_type.242
  1374.8 66.1 %reduce-scatter.19.cloned.1.call-done = bf16[64,2048]{1,0:T(8,128)(2,1)} async-done(((bf16[512,2048]{1,0:T(8,128)(2,1)}), bf16[64,2048]{1,0:T(8,128)(2,1)}) %reduce-scatter.19.cloned.1.call-update) | async-done | bytes 262160 | tf_op jit(solution)/shard_map/reduce_scatter | solution.py:520
  1442.7 2.6 convert_reduce_fusion.1
  1445.5 41.5 %reduce-scatter.15.cloned.1.call-done = bf16[256,2048]{1,0:T(8,128)(2,1)} async-done(((bf16[1024,2048]{1,0:T(8,128)(2,1)}), bf16[256,2048]{1,0:T(8,128)(2,1)}) %reduce-scatter.15.cloned.1.call-update) | async-done | bytes 1048592 | tf_op jit(solution)/shard_map/reduce_scatter | solution.py:502
  1487.0 1.9 convert_reduce_fusion.2
  1488.9 2.3 fusion.13
  1492.1 116.3 %reduce-scatter.17.cloned.1.call-done = bf16[4,64,1536]{2,1,0:T(8,128)(2,1)} async-done(((bf16[4,512,1536]{2,1,0:T(8,128)(2,1)}), bf16[4,64,1536]{2,1,0:T(8,128)(2,1)}) %reduce-scatter.17.cloned.1.call-update) | async-done | bytes 786448 | tf_op jit(solution)/shard_map/reduce_scatter | solution.py:520
  1608.4 4.5 all-to-all-start.6
  1612.9 3.8 add_add_fusion.2
  1616.7 117.5 %all-reduce.3.cloned.1.call-done = f32[32,768]{1,0:T(8,128)} async-done(((f32[32,768]{1,0:T(8,128)}), f32[32,768]{1,0:T(8,128)}) %all-reduce.3.cloned.1.call-update) | async-done | bytes 98320
  1737.0 2.7 reshape.330
  (183 shorter events, 43.5 us)
Async XLA Ops:
  7.2 83.2 %copy-start.16 = (bf16[64,2048]{1,0:T(8,128)(2,1)S(1)}, bf16[64,2048]{1,0:T(8,128)(2,1)}, u32[]{:S(2)}) copy-start(bf16[64,2048]{1,0:T(8,128)(2,1)} %param.23) | copy-start | bytes 786436
  7.2 83.8 %copy-start.17 = (bf16[64,2048]{1,0:T(8,128)(2,1)S(1)}, bf16[64,2048]{1,0:T(8,128)(2,1)}, u32[]{:S(2)}) copy-start(bf16[64,2048]{1,0:T(8,128)(2,1)} %param.25) | copy-start | bytes 786436
  7.2 84.4 %copy-start.18 = (bf16[64,2048]{1,0:T(8,128)(2,1)S(1)}, bf16[64,2048]{1,0:T(8,128)(2,1)}, u32[]{:S(2)}) copy-start(bf16[64,2048]{1,0:T(8,128)(2,1)} %param.26) | copy-start | bytes 786436
  7.2 122.4 %all-gather.13.cloned.1.call-start = ((), (), s32[]{:S(2)}) async-start(), calls=%async_computation.16 | async-start | bytes 5242880 | tf_op jit(solution)/shard_map/all_gather | solution.py:498
  84.4 5.9 copy-start.19
  85.9 4.4 copy-start.24
  87.6 2.7 copy-start.34
  87.6 2.7 copy-start.28
  90.3 138.8 %all-gather.15.cloned.1.call-start = ((), (), s32[]{:S(2)}) async-start(), calls=%async_computation.17 | async-start | bytes 7077888 | tf_op jit(solution)/shard_map/all_gather | solution.py:516
  247.9 5.4 copy-start.36
  247.9 157.4 %all-to-all-start.1 = ((bf16[8,3,4,128,128]{4,3,2,1,0:T(8,128)(2,1)}), bf16[8,3,4,128,128]{4,3,2,1,0:T(8,128)(2,1)}, u32[]{:S(2)}, u32[]{:S(2)}) async-start(bf16[8,3,4,128,128]{4,3,2,1,0:T(8,128)(2,1)} %bitcast.9), calls=%async_computation.1 | async-start | bytes 6291456 | tf_op jit(solution)/shard_map/all_to_all | solution.py:508
  252.5 190.1 %all-gather.17.cloned.1.call-start = ((), (), s32[]{:S(2)}) async-start(), calls=%async_computation.18 | async-start | bytes 2359296 | tf_op jit(solution)/shard_map/all_gather | solution.py:516
  253.3 242.4 %reduce-scatter.9.cloned.1.call-start = ((), (), s32[]{:S(2)}) async-start(), calls=%async_computation.19 | async-start | bytes 5242880 | tf_op jit(solution)/shard_map/reduce_scatter | solution.py:502
  413.6 1.3 copy-start
  442.6 1.0 copy-start.12
  449.5 1.2 copy-start.11
  449.5 171.6 %all-gather.21.cloned.1.call-start = ((), (), s32[]{:S(2)}) async-start(), calls=%async_computation.21 | async-start | bytes 9437184 | tf_op jit(solution)/shard_map/all_gather | solution.py:516
  452.3 43.4 %copy-start.2 = (bf16[2,128,2048]{2,1,0:T(8,128)(2,1)S(1)}, bf16[2,128,2048]{2,1,0:T(8,128)(2,1)}, u32[]{:S(2)}) copy-start(bf16[2,128,2048]{2,1,0:T(8,128)(2,1)} %param.18) | copy-start | bytes 3145732
  477.1 178.8 %all-gather.19.cloned.1.call-start = ((), (), s32[]{:S(2)}) async-start(), calls=%async_computation.20 | async-start | bytes 5242880 | tf_op jit(solution)/shard_map/all_gather | solution.py:498
  477.2 23.7 %copy-start.14 = (f32[2048]{0:T(1024)}, f32[2048]{0:T(1024)S(1)}, u32[]{:S(2)}) copy-start(f32[2048]{0:T(1024)S(1)} %reshape.324) | copy-start | bytes 24580
  477.3 23.6 %copy-start.21 = (f32[2048]{0:T(1024)}, f32[2048]{0:T(1024)S(1)}, u32[]{:S(2)}) copy-start(f32[2048]{0:T(1024)S(1)} %reshape.325) | copy-start | bytes 24580
  495.6 3.6 copy-start.4
  497.4 5.0 copy-start.26
  499.2 133.4 %copy-start.32 = (f32[256]{0:T(256)}, f32[256]{0:T(256)S(1)}, u32[]{:S(2)}) copy-start(f32[256]{0:T(256)S(1)} %multiply_reduce_fusion) | copy-start | bytes 3076
  499.2 133.4 %copy-start.30 = (f32[256]{0:T(256)}, f32[256]{0:T(256)S(1)}, u32[]{:S(2)}) copy-start(f32[256]{0:T(256)S(1)} %fusion.30) | copy-start | bytes 3076
  500.9 191.1 %all-gather.25.cloned.1.call-start = ((), (), s32[]{:S(2)}) async-start(), calls=%async_computation.24 | async-start | bytes 5242880 | tf_op jit(solution)/shard_map/all_gather | solution.py:498
  501.7 317.7 %all-gather.23.cloned.1.call-start = ((), (), s32[]{:S(2)}) async-start(), calls=%async_computation.22 | async-start | bytes 9437184 | tf_op jit(solution)/shard_map/all_gather | solution.py:516
  502.4 405.5 %reduce-scatter.13.cloned.1.call-start = ((), (), s32[]{:S(2)}) async-start(), calls=%async_computation.25 | async-start | bytes 5242880 | tf_op jit(solution)/shard_map/reduce_scatter | solution.py:502
  819.3 35.1 %copy-start.9 = (bf16[4,512,2048]{2,1,0:T(8,128)(2,1)S(1)}, bf16[4,512,2048]{2,1,0:T(8,128)(2,1)}, u32[]{:S(2)}) copy-start(bf16[4,512,2048]{2,1,0:T(8,128)(2,1)} %copy.78) | copy-start | bytes 25165828
  852.4 2.0 copy-start.37
  865.1 89.7 %reduce-scatter.11.cloned.1.call-start = ((), (), s32[]{:S(2)}) async-start(), calls=%async_computation.23 | async-start | bytes 5242880 | tf_op jit(solution)/shard_map/reduce_scatter | solution.py:502
  874.1 2.0 copy-start.10
  888.8 0.7 copy-start.23
  888.8 19.1 %copy-start.3 = (bf16[2,128,2048]{2,1,0:T(8,128)(2,1)S(1)}, bf16[2,128,2048]{2,1,0:T(8,128)(2,1)}, u32[]{:S(2)}) copy-start(bf16[2,128,2048]{2,1,0:T(8,128)(2,1)} %param.18) | copy-start | bytes 3145732
  888.8 19.1 %copy-start.15 = (f32[2048]{0:T(1024)S(1)}, f32[2048]{0:T(1024)}, u32[]{:S(2)}) copy-start(f32[2048]{0:T(1024)} %copy-done.14) | copy-start | bytes 24580
  888.8 19.1 %copy-start.22 = (f32[2048]{0:T(1024)S(1)}, f32[2048]{0:T(1024)}, u32[]{:S(2)}) copy-start(f32[2048]{0:T(1024)} %copy-done.21) | copy-start | bytes 24580
  888.8 19.1 %copy-start.27 = (f32[256]{0:T(256)S(1)}, f32[256]{0:T(256)}, u32[]{:S(2)}) copy-start(f32[256]{0:T(256)} %copy-done.26) | copy-start | bytes 3076
  888.8 19.1 %copy-start.31 = (f32[256]{0:T(256)S(1)}, f32[256]{0:T(256)}, u32[]{:S(2)}) copy-start(f32[256]{0:T(256)} %copy-done.30) | copy-start | bytes 3076
  888.8 21.7 %copy-start.33 = (f32[256]{0:T(256)S(1)}, f32[256]{0:T(256)}, u32[]{:S(2)}) copy-start(f32[256]{0:T(256)} %copy-done.32) | copy-start | bytes 3076
  888.8 107.4 %all-gather.27.cloned.1.call-start = ((), (), s32[]{:S(2)}) async-start(), calls=%async_computation.26 | async-start | bytes 5242880 | tf_op jit(solution)/shard_map/all_gather | solution.py:498
  954.8 5.3 copy-start.7
  958.8 1.3 copy-start.5
  961.6 257.0 %reduce-scatter.21.cloned.1.call-start = ((), (), s32[]{:S(2)}) async-start(), calls=%async_computation.30 | async-start | bytes 9437184 | tf_op jit(solution)/shard_map/reduce_scatter | solution.py:520
  976.2 394.1 %reduce-scatter.23.cloned.1.call-start = ((), (), s32[]{:S(2)}) async-start(), calls=%async_computation.31 | async-start | bytes 9437184 | tf_op jit(solution)/shard_map/reduce_scatter | solution.py:520
  1004.6 59.2 %copy-start.1 = (f32[8,512,1]{2,1,0:T(8,128)S(1)}, f32[8,512,1]{2,1,0:T(8,128)}, u32[]{:S(2)}) copy-start(f32[8,512,1]{2,1,0:T(8,128)} %copy-done) | copy-start | bytes 49156
  1081.0 4.7 copy-start.13
  1081.0 86.8 %all-to-all-start.5 = ((bf16[8,3,4,128,128]{4,3,2,1,0:T(8,128)(2,1)}), bf16[8,3,4,128,128]{4,3,2,1,0:T(8,128)(2,1)}, u32[]{:S(2)}, u32[]{:S(2)}) async-start(bf16[8,3,4,128,128]{4,3,2,1,0:T(8,128)(2,1)} %attend_bwd.1), calls=%async_computation.8 | async-start | bytes 6291456 | tf_op jit(solution)/shard_map/all_to_all | solution.py:508
  1085.6 355.3 %reduce-scatter.19.cloned.1.call-start = ((), (), s32[]{:S(2)}) async-start(), calls=%async_computation.29 | async-start | bytes 2359296 | tf_op jit(solution)/shard_map/reduce_scatter | solution.py:520
  1091.6 395.4 %reduce-scatter.15.cloned.1.call-start = ((), (), s32[]{:S(2)}) async-start(), calls=%async_computation.27 | async-start | bytes 5242880 | tf_op jit(solution)/shard_map/reduce_scatter | solution.py:502
  1191.6 416.8 %reduce-scatter.17.cloned.1.call-start = ((), (), s32[]{:S(2)}) async-start(), calls=%async_computation.28 | async-start | bytes 7077888 | tf_op jit(solution)/shard_map/reduce_scatter | solution.py:520
  1215.8 6.4 copy-start.8
  1218.6 154.5 %all-to-all-start.7 = ((bf16[4,64,2048]{2,1,0:T(8,128)(2,1)}), bf16[4,64,2048]{2,1,0:T(8,128)(2,1)S(1)}, u32[]{:S(2)}, u32[]{:S(2)}) async-start(bf16[4,64,2048]{2,1,0:T(8,128)(2,1)} %reduce-scatter.21.cloned.1.call-done), calls=%async_computation.14 | async-start | bytes 2097152 | tf_op jit(solution)/shard_map/all_to_all | solution.py:512
  1222.1 512.1 %all-reduce.3.cloned.1.call-start = ((), (), s32[]{:S(2)}) async-start(), calls=%async_computation.32 | async-start | bytes 196608
  1373.3 113.6 %copy-start.20 = (f32[2048]{0:T(1024)S(1)}, f32[2048]{0:T(1024)}, u32[]{:S(2)}) copy-start(f32[2048]{0:T(1024)} %copy-done.19) | copy-start | bytes 24580
  1373.3 113.6 %copy-start.25 = (f32[256]{0:T(256)S(1)}, f32[256]{0:T(256)}, u32[]{:S(2)}) copy-start(f32[256]{0:T(256)} %copy-done.24) | copy-start | bytes 3076
  1373.4 115.5 %copy-start.35 = (f32[2,128]{1,0:T(2,128)S(1)}, f32[2,128]{1,0:T(2,128)}, u32[]{:S(2)}) copy-start(f32[2,128]{1,0:T(2,128)} %copy-done.34) | copy-start | bytes 3076
  1373.4 115.5 %copy-start.29 = (f32[256]{0:T(256)S(1)}, f32[256]{0:T(256)}, u32[]{:S(2)}) copy-start(f32[256]{0:T(256)} %copy-done.28) | copy-start | bytes 3076
  1442.7 170.2 %copy-start.6 = (f32[256,2048]{1,0:T(8,128)S(1)}, f32[256,2048]{1,0:T(8,128)}, u32[]{:S(2)}) copy-start(f32[256,2048]{1,0:T(8,128)} %copy-done.5) | copy-start | bytes 6291460
  1608.4 128.6 %all-to-all-start.6 = ((bf16[4,64,1536]{2,1,0:T(8,128)(2,1)}), bf16[4,64,1536]{2,1,0:T(8,128)(2,1)}, u32[]{:S(2)}, u32[]{:S(2)}) async-start(bf16[4,64,1536]{2,1,0:T(8,128)(2,1)} %reduce-scatter.17.cloned.1.call-done), calls=%async_computation.11 | async-start | bytes 1572864 | tf_op jit(solution)/shard_map/all_to_all | solution.py:512
Sparse Core Ops, SparseCore 0:
  90.4 39.1 all-gather.12
  131.8 97.2 all-gather.14
  255.5 85.9 all-gather.16
  449.6 45.9 reduce-scatter.8
  498.4 122.6 all-gather.20
  623.2 32.6 all-gather.18
  657.5 34.4 all-gather.24
  694.4 124.9 all-gather.22
  865.2 42.6 reduce-scatter.12
  910.3 44.4 reduce-scatter.10
  961.7 34.4 all-gather.26
  1000.2 218.3 reduce-scatter.20
  1222.2 148.0 reduce-scatter.22
  1374.1 66.7 reduce-scatter.18
  1443.5 43.4 reduce-scatter.14
  1490.4 117.9 reduce-scatter.16
  1614.4 119.7 all-reduce.2

commit v2 on v1

--- a/solution.py
+++ b/solution.py
@@ -378,33 +378,252 @@
     )
 
 
-def all_small(parts):
-    packed = jnp.concatenate(parts)[None]
-    return lax.all_gather(packed, BOTH, axis=0, tiled=True)
-
-
-def fwd_kernel(segc_ref, segr_ref, qkv_ref, out_ref, lse_ref, *, blocks, scale2):
-    half = blocks // 4
-    for i in range(blocks):
-        w0, n = 4 * (i % half), i // half
-        q = qkv_ref[w0 : w0 + 4, 0, n].reshape(512, 128)
-        lo = max(i - 1, 0)
-        k = jnp.concatenate(
-            [qkv_ref[4 * (j % half) : 4 * (j % half) + 4, 1, j // half] for j in range(lo, i + 1)]
-        ).reshape(-1, 128)
-        v = jnp.concatenate(
-            [qkv_ref[4 * (j % half) : 4 * (j % half) + 4, 2, j // half] for j in range(lo, i + 1)]
-        ).reshape(-1, 128)
-        allowed = mask_of(segc_ref, segr_ref, i, lo)
-        s = lax.dot_general(q, k, (((1,), (1,)), ((), ())), preferred_element_type=jnp.float32)
-        s = jnp.where(allowed, s * scale2, neg_big)
-        m = jnp.max(s, axis=-1, keepdims=True)
-        p = jnp.exp2(s - m)
-        total = jnp.sum(p, axis=-1, keepdims=True)
-        o = jnp.dot(p.astype(jnp.bfloat16), v, preferred_element_type=jnp.float32)
-        o = o / total
-        out_ref[w0 : w0 + 4, n] = o.astype(jnp.bfloat16).reshape(4, 128, 128)
-        lse_ref[i] = m + jnp.log2(total)
+def flip(value, axis, bits):
+    size = lax.axis_size(axis)
+    return lax.ppermute(value, axis, [(i, i ^ bits) for i in range(size)])
+
+
+def at(value, index, dim=0):
+    return lax.dynamic_index_in_dim(value, index, dim, keepdims=False)
+
+
+def cube(wide):
+    steps = []
+    bits = 1
+    while bits < wide:
+        steps.append((WIDE, bits))
+        bits *= 2
+    return steps + [(NARROW, 1), (NARROW, 2)]
+
+
+def cube_gather(row):
+    for axis, bits in cube(lax.axis_size(WIDE)):
+        other = flip(row, axis, bits)
+        high = (lax.axis_index(axis) & bits) > 0
+        row = jnp.concatenate(
+            [jnp.where(high, other, row), jnp.where(high, row, other)], axis=0
+        )
+    return row
+
+
+def cube_scatter(table):
+    wide = lax.axis_size(WIDE)
+    steps = cube(wide)
+    table = table.reshape((2,) * len(steps) + (table.shape[-1],))
+    order = [len(steps) - 2, len(steps) - 1] + list(range(len(steps) - 2))[::-1]
+    left = list(range(len(steps)))
+    for k in order:
+        axis, bits = steps[k]
+        dim = len(left) - 1 - left.index(k)
+        high = ((lax.axis_index(axis) & bits) > 0).astype(jnp.int32)
+        table = at(table, high, dim) + flip(at(table, 1 - high, dim), axis, bits)
+        left.remove(k)
+    return table
+
+
+def narrow_gather(own):
+    across = flip(own, NARROW, 2)
+    beside = flip(own, NARROW, 1)
+    return jnp.concatenate([own, beside, across, flip(across, NARROW, 1)], axis=0)
+
+
+def narrow_scatter(partial):
+    f32 = jnp.float32
+    parts = partial.reshape(4, -1, partial.shape[-1])
+    far = flip(parts[3], NARROW, 1)
+    near = flip(parts[1], NARROW, 1)
+    passed = (parts[2].astype(f32) + far.astype(f32)).astype(jnp.bfloat16)
+    across = flip(passed, NARROW, 2)
+    return parts[0].astype(f32) + near.astype(f32) + across.astype(f32)
+
+
+def narrow_swap(blocks):
+    me = lax.axis_index(NARROW)
+    result = jnp.zeros_like(blocks)
+    for j in (3, 2, 1, 0):
+        block = at(blocks, me ^ j)
+        block = flip(block, NARROW, j) if j else block
+        result = lax.dynamic_update_slice_in_dim(result, block[None], me ^ j, 0)
+    return result
+
+
+def ring_order(wide):
+    return list(range(0, wide, 2)) + list(range(wide - 1, 0, -2))
+
+
+def ring_at(position, wide):
+    position = position % wide
+    return jnp.where(position < wide // 2, 2 * position, 2 * (wide - 1 - position) + 1)
+
+
+def ring_position(wide):
+    me = lax.axis_index(WIDE)
+    return jnp.where(me % 2 == 0, me // 2, wide - 1 - me // 2)
+
+
+def ring_step(value, by):
+    order = ring_order(lax.axis_size(WIDE))
+    size = len(order)
+    return lax.ppermute(
+        value, WIDE, [(order[i], order[(i + by) % size]) for i in range(size)]
+    )
+
+
+def ring_gather(shard, axis):
+    wide = lax.axis_size(WIDE)
+    here = ring_position(wide)
+    shape = list(shard.shape)
+    shape.insert(axis, wide)
+    full = jnp.zeros(shape, shard.dtype)
+
+    def put(full, piece, position):
+        return lax.dynamic_update_slice_in_dim(
+            full, jnp.expand_dims(piece, axis), ring_at(position, wide), axis
+        )
+
+    full = put(full, shard, here)
+    ahead = behind = shard
+    for k in range(1, wide // 2 + 1):
+        ahead = ring_step(ahead, 1)
+        full = put(full, ahead, here - k + wide)
+        if k < wide - wide // 2:
+            behind = ring_step(behind, -1)
+            full = put(full, behind, here + k)
+    return full
+
+
+def ring_scatter(full, axis):
+    wide = lax.axis_size(WIDE)
+    here = ring_position(wide)
+    bf16, f32 = jnp.bfloat16, jnp.float32
+
+    def local(position):
+        return at(full, ring_at(position + wide, wide), axis).astype(f32)
+
+    half = wide // 2
+    ahead = behind = None
+    for k in range(half, 0, -1):
+        term = local(here + k)
+        term = term if ahead is None else term + ahead
+        ahead = ring_step(term.astype(bf16), 1).astype(f32)
+        if k < wide - half:
+            term = local(here - k)
+            term = term if behind is None else term + behind
+            behind = ring_step(term.astype(bf16), -1).astype(f32)
+    return local(here) + ahead + behind
+
+
+def wide_swap(parts):
+    return [parts[0]] + [flip(parts[d], WIDE, d) for d in range(1, parts.shape[0])]
+
+
+def wide_gather(shard, axis):
+    return lax.all_gather(shard, WIDE, axis=axis, tiled=True)
+
+
+def wide_scatter(full, axis):
+    return lax.psum_scatter(full.astype(jnp.bfloat16), WIDE, scatter_dimension=axis, tiled=True)
+
+
+def vmem_specs(count):
+    return [pl.BlockSpec(memory_space=pltpu.VMEM)] * count
+
+
+SMEM_SPEC = pl.BlockSpec(memory_space=pltpu.SMEM)
+BIG = pltpu.CompilerParams(vmem_limit_bytes=48 << 20)
+CONTRACT_LAST = (((1,), (1,)), ((), ()))
+CONTRACT_FIRST = (((0,), (0,)), ((), ()))
+
+
+def project_kernel(me_ref, rows_ref, weight_ref, bias_ref, out_ref, *, heads, by_last):
+    me = me_ref[1]
+    if by_last:
+        acc = lax.dot_general(
+            rows_ref[...], weight_ref[...], CONTRACT_LAST, preferred_element_type=jnp.float32
+        )
+    else:
+        acc = jnp.dot(rows_ref[...], weight_ref[...], preferred_element_type=jnp.float32)
+    acc = (acc + bias_ref[...]).astype(jnp.bfloat16)
+    units, parts, _, tokens, head_dim = out_ref.shape
+    for unit in range(units):
+        b, h = divmod(unit, heads)
+        for part in range(parts):
+            c = (part * heads + h) * head_dim
+            out_ref[unit ^ me, part, 0] = acc[b * tokens : (b + 1) * tokens, c : c + head_dim]
+
+
+def project(me, rows, weight, bias, units, parts, heads, tokens, by_last):
+    blocks, width = 4, rows.shape[1]
+    head_dim = bias.shape[0] // (parts * heads)
+    step = rows.shape[0] // blocks
+    return pl.pallas_call(
+        functools.partial(project_kernel, heads=heads, by_last=by_last),
+        grid=(blocks,),
+        out_shape=jax.ShapeDtypeStruct((units, parts, blocks, tokens, head_dim), jnp.bfloat16),
+        in_specs=[
+            SMEM_SPEC,
+            pl.BlockSpec((step, width), lambda i: (i, 0)),
+            pl.BlockSpec(weight.shape, lambda i: (0, 0), pipeline_mode=pl.Buffered(1)),
+            pl.BlockSpec((1, bias.shape[0]), lambda i: (0, 0)),
+        ],
+        out_specs=pl.BlockSpec(
+            (units, parts, 1, tokens, head_dim), lambda i: (0, 0, i, 0, 0)
+        ),
+        compiler_params=BIG,
+        name="project",
+    )(me, rows, weight, bias.reshape(1, -1))
+
+
+def unproject_kernel(me_ref, *refs, heads, by_last):
+    units = len(refs) - 4
+    pieces, weight_ref, out_ref, rows_ref, held = refs[:units], *refs[units:]
+    me = me_ref[1]
+    for d in range(units):
+        held[d ^ me] = pieces[d][:, 0]
+    parts = held.shape[1]
+    rows = jnp.concatenate(
+        [
+            jnp.concatenate(
+                [held[b * heads + h, part] for part in range(parts) for h in range(heads)], axis=1
+            )
+            for b in range(units // heads)
+        ],
+        axis=0,
+    )
+    rows_ref[...] = rows
+    if by_last:
+        acc = lax.dot_general(
+            rows, weight_ref[...], CONTRACT_LAST, preferred_element_type=jnp.float32
+        )
+    else:
+        acc = jnp.dot(rows, weight_ref[...], preferred_element_type=jnp.float32)
+    out_ref[...] = acc.astype(jnp.bfloat16)
+
+
+def unproject(me, pieces, weight, heads, by_last):
+    units = len(pieces)
+    parts, blocks, tokens, head_dim = pieces[0].shape
+    step = tokens * units // heads
+    inner = parts * heads * head_dim
+    width = weight.shape[0] if by_last else weight.shape[1]
+    return pl.pallas_call(
+        functools.partial(unproject_kernel, heads=heads, by_last=by_last),
+        grid=(blocks,),
+        out_shape=(
+            jax.ShapeDtypeStruct((blocks * step, width), jnp.bfloat16),
+            jax.ShapeDtypeStruct((blocks * step, inner), jnp.bfloat16),
+        ),
+        in_specs=[SMEM_SPEC]
+        + [pl.BlockSpec((parts, 1, tokens, head_dim), lambda i: (0, i, 0, 0))] * units
+        + [pl.BlockSpec(weight.shape, lambda i: (0, 0), pipeline_mode=pl.Buffered(1))],
+        out_specs=(
+            pl.BlockSpec((step, width), lambda i: (i, 0)),
+            pl.BlockSpec((step, inner), lambda i: (i, 0)),
+        ),
+        scratch_shapes=[pltpu.VMEM((units, parts, tokens, head_dim), jnp.bfloat16)],
+        compiler_params=BIG,
+        name="unproject",
+    )(me, *pieces, weight)
 
 
 def mask_of(segc_ref, segr_ref, i, lo):
@@ -415,109 +634,163 @@
     return jnp.logical_and(same, cols <= rows)
 
 
-def bwd_kernel(segc_ref, segr_ref, qkv_ref, do_ref, lse_ref, grad_ref, dk_acc, dv_acc, *, blocks, scale, scale2):
+def collect(me_ref, pieces, held):
+    for d, piece in enumerate(pieces):
+        for j in range(4):
+            held[d ^ me_ref[1], :, j ^ me_ref[0]] = piece[:, j]
+
+
+def take(held, part, first, last, half):
+    blocks = [
+        held[4 * (i % half) : 4 * (i % half) + 4, part, i // half].reshape(512, -1)
+        for i in range(first, last + 1)
+    ]
+    return blocks[0] if len(blocks) == 1 else jnp.concatenate(blocks, axis=0)
+
+
+def give(me_ref, out_ref, part, i, half, rows):
+    rows = rows.astype(out_ref.dtype).reshape(4, 128, -1)
+    for c in range(4):
+        out_ref[(4 * (i % half) + c) ^ me_ref[1], part, (i // half) ^ me_ref[0]] = rows[c]
+
+
+def fwd_kernel(me_ref, segc_ref, segr_ref, *refs, blocks, scale2):
+    pieces, (out_ref, lse_ref, held) = refs[:-3], refs[-3:]
+    half = blocks // 4
+    collect(me_ref, pieces, held)
+    for i in range(blocks):
+        lo = max(i - 1, 0)
+        q = take(held, 0, i, i, half)
+        k = take(held, 1, lo, i, half)
+        v = take(held, 2, lo, i, half)
+        s = lax.dot_general(q, k, CONTRACT_LAST, preferred_element_type=jnp.float32)
+        s = jnp.where(mask_of(segc_ref, segr_ref, i, lo), s * scale2, neg_big)
+        m = jnp.max(s, axis=-1, keepdims=True)
+        p = jnp.exp2(s - m)
+        total = jnp.sum(p, axis=-1, keepdims=True)
+        o = jnp.dot(p.astype(jnp.bfloat16), v, preferred_element_type=jnp.float32)
+        give(me_ref, out_ref, 0, i, half, o / total)
+        lse_ref[i] = m + jnp.log2(total)
+
+
+def bwd_kernel(me_ref, segc_ref, segr_ref, lse_ref, *refs, blocks, scale, scale2):
+    grad_ref, held, held_do, dk_acc, dv_acc = refs[-5:]
+    pieces, douts = refs[: (len(refs) - 5) // 2], refs[(len(refs) - 5) // 2 : -5]
     half = blocks // 4
     f32 = jnp.float32
-
-    def at(j):
-        return slice(4 * (j % half), 4 * (j % half) + 4), j // half
-
+    collect(me_ref, pieces, held)
+    collect(me_ref, douts, held_do)
     for i in range(blocks):
-        wi, n = at(i)
-        q = qkv_ref[wi, 0, n].reshape(512, 128)
-        do = do_ref[wi, n].reshape(512, 128)
         lo = max(i - 1, 0)
-        k = jnp.concatenate([qkv_ref[at(j)[0], 1, at(j)[1]] for j in range(lo, i + 1)]).reshape(-1, 128)
-        v = jnp.concatenate([qkv_ref[at(j)[0], 2, at(j)[1]] for j in range(lo, i + 1)]).reshape(-1, 128)
-        allowed = mask_of(segc_ref, segr_ref, i, lo)
-        s = lax.dot_general(q, k, (((1,), (1,)), ((), ())), preferred_element_type=f32)
-        p = jnp.exp2(jnp.where(allowed, s * scale2, neg_big) - lse_ref[i])
-        dp = lax.dot_general(do, v, (((1,), (1,)), ((), ())), preferred_element_type=f32)
+        q = take(held, 0, i, i, half)
+        k = take(held, 1, lo, i, half)
+        v = take(held, 2, lo, i, half)
+        do = take(held_do, 0, i, i, half)
+        s = lax.dot_general(q, k, CONTRACT_LAST, preferred_element_type=f32)
+        s = jnp.where(mask_of(segc_ref, segr_ref, i, lo), s * scale2, neg_big)
+        p = jnp.exp2(s - lse_ref[i])
+        dp = lax.dot_general(do, v, CONTRACT_LAST, preferred_element_type=f32)
         t = p * dp
         delta = jnp.sum(t, axis=-1, keepdims=True)
         ds = (t - p * delta).astype(jnp.bfloat16)
-        dq = jnp.dot(ds, k, preferred_element_type=f32) * scale
-        grad_ref[wi, 0, n] = dq.astype(jnp.bfloat16).reshape(4, 128, 128)
-        dk = lax.dot_general(ds, q, (((0,), (0,)), ((), ())), preferred_element_type=f32)
+        give(me_ref, grad_ref, 0, i, half, jnp.dot(ds, k, preferred_element_type=f32) * scale)
+        dk = lax.dot_general(ds, q, CONTRACT_FIRST, preferred_element_type=f32)
         dv = lax.dot_general(
-            p.astype(jnp.bfloat16), do, (((0,), (0,)), ((), ())), preferred_element_type=f32
+            p.astype(jnp.bfloat16), do, CONTRACT_FIRST, preferred_element_type=f32
         )
         if i > 0:
-            wp, np_ = at(i - 1)
-            grad_ref[wp, 1, np_] = (
-                ((dk_acc[...] + dk[:512]) * scale).astype(jnp.bfloat16).reshape(4, 128, 128)
-            )
-            grad_ref[wp, 2, np_] = (dv_acc[...] + dv[:512]).astype(jnp.bfloat16).reshape(4, 128, 128)
+            give(me_ref, grad_ref, 1, i - 1, half, (dk_acc[...] + dk[:512]) * scale)
+            give(me_ref, grad_ref, 2, i - 1, half, dv_acc[...] + dv[:512])
         if i == blocks - 1:
-            grad_ref[wi, 1, n] = (dk[-512:] * scale).astype(jnp.bfloat16).reshape(4, 128, 128)
-            grad_ref[wi, 2, n] = dv[-512:].astype(jnp.bfloat16).reshape(4, 128, 128)
+            give(me_ref, grad_ref, 1, i, half, dk[-512:] * scale)
+            give(me_ref, grad_ref, 2, i, half, dv[-512:])
         else:
             dk_acc[...] = dk[-512:]
             dv_acc[...] = dv[-512:]
 
 
-def whole_vmem(count):
-    return [pl.BlockSpec(memory_space=pltpu.VMEM)] * count
-
-
-def attend_fwd(segc, segr, qkv):
-    blocks = segc.shape[0]
-    wide, _, narrow, rows, width = qkv.shape
+def attend_fwd(me, segc, segr, pieces):
+    blocks, units = segc.shape[0], len(pieces)
+    parts, narrow, rows, width = pieces[0].shape
     scale2 = math.log2(math.e) / math.sqrt(width)
     return pl.pallas_call(
         functools.partial(fwd_kernel, blocks=blocks, scale2=scale2),
         out_shape=(
-            jax.ShapeDtypeStruct((wide, narrow, rows, width), jnp.bfloat16),
+            jax.ShapeDtypeStruct((units, 1, narrow, rows, width), jnp.bfloat16),
             jax.ShapeDtypeStruct((blocks, 512, 1), jnp.float32),
         ),
-        in_specs=whole_vmem(3),
-        out_specs=tuple(whole_vmem(2)),
-        compiler_params=pltpu.CompilerParams(vmem_limit_bytes=48 << 20),
+        in_specs=[SMEM_SPEC] + vmem_specs(2 + units),
+        out_specs=tuple(vmem_specs(2)),
+        scratch_shapes=[pltpu.VMEM((units, parts, narrow, rows, width), jnp.bfloat16)],
+        compiler_params=BIG,
         name="attend_fwd",
-    )(segc, segr, qkv)
-
-
-def attend_bwd(segc, segr, qkv, dout, lse):
-    blocks = segc.shape[0]
-    width = qkv.shape[-1]
+    )(me, segc, segr, *pieces)
+
+
+def attend_bwd(me, segc, segr, lse, pieces, douts):
+    blocks, units = segc.shape[0], len(pieces)
+    parts, narrow, rows, width = pieces[0].shape
     scale = 1.0 / math.sqrt(width)
+    shape = (units, parts, narrow, rows, width)
     return pl.pallas_call(
         functools.partial(
             bwd_kernel, blocks=blocks, scale=scale, scale2=scale * math.log2(math.e)
         ),
-        out_shape=jax.ShapeDtypeStruct(qkv.shape, jnp.bfloat16),
-        in_specs=whole_vmem(5),
-        out_specs=whole_vmem(1)[0],
-        scratch_shapes=[pltpu.VMEM((512, width), jnp.float32)] * 2,
-        compiler_params=pltpu.CompilerParams(vmem_limit_bytes=48 << 20),
+        out_shape=jax.ShapeDtypeStruct(shape, jnp.bfloat16),
+        in_specs=[SMEM_SPEC] + vmem_specs(3 + 2 * units),
+        out_specs=vmem_specs(1)[0],
+        scratch_shapes=[
+            pltpu.VMEM(shape, jnp.bfloat16),
+            pltpu.VMEM((units, 1, narrow, rows, width), jnp.bfloat16),
+            pltpu.VMEM((512, width), jnp.float32),
+            pltpu.VMEM((512, width), jnp.float32),
+        ],
+        compiler_params=BIG,
         name="attend_bwd",
-    )(segc, segr, qkv, dout, lse)
-
-
-def narrow_gather(rows):
-    return lax.all_gather(rows, NARROW, axis=0, tiled=True)
-
-
-def narrow_scatter(partial):
-    return lax.psum_scatter(
-        partial.astype(jnp.bfloat16), NARROW, scatter_dimension=0, tiled=True
-    ).astype(jnp.float32)
-
-
-def wide_swap(parts):
-    return lax.all_to_all(parts, WIDE, split_axis=0, concat_axis=0, tiled=True)
-
-
-def narrow_swap(parts):
-    return lax.all_to_all(parts, NARROW, split_axis=0, concat_axis=0, tiled=True)
-
-
-def wide_gather(shard, axis):
-    return lax.all_gather(shard, WIDE, axis=axis, tiled=True)
-
-
-def wide_scatter(full, axis):
-    return lax.psum_scatter(full.astype(jnp.bfloat16), WIDE, scatter_dimension=axis, tiled=True)
+    )(me, segc, segr, lse, *pieces, *douts)
+
+
+def ff_kernel(rows_ref, weight_ref, bias_ref, pull_ref, hidden_ref, grad_ref, sum_ref):
+    step = 256
+    total = jnp.zeros((1, weight_ref.shape[1]), jnp.float32)
+    for r in range(0, rows_ref.shape[0], step):
+        x = jnp.dot(rows_ref[r : r + step], weight_ref[...], preferred_element_type=jnp.float32)
+        x = x + bias_ref[...]
+        below = 0.5 * (1.0 + lax.erf(x * math.sqrt(0.5)))
+        hidden_ref[r : r + step] = (x * below).astype(jnp.bfloat16)
+        slope = below + x * (jnp.exp(-0.5 * x * x) * (1.0 / math.sqrt(2.0 * math.pi)))
+        grad = (pull_ref[r : r + step] * slope).astype(jnp.bfloat16)
+        grad_ref[r : r + step] = grad
+        total = total + jnp.sum(grad.astype(jnp.float32), axis=0, keepdims=True)
+    sum_ref[...] = total
+
+
+def feed_forward(rows, weight, bias, pull):
+    count, width = rows.shape
+    inner = weight.shape[1]
+    step = 256
+    return pl.pallas_call(
+        ff_kernel,
+        grid=(inner // step,),
+        out_shape=(
+            jax.ShapeDtypeStruct((count, inner), jnp.bfloat16),
+            jax.ShapeDtypeStruct((count, inner), jnp.bfloat16),
+            jax.ShapeDtypeStruct((1, inner), jnp.float32),
+        ),
+        in_specs=[
+            pl.BlockSpec((count, width), lambda i: (0, 0), pipeline_mode=pl.Buffered(1)),
+            pl.BlockSpec((width, step), lambda i: (0, i)),
+            pl.BlockSpec((1, step), lambda i: (0, i)),
+            pl.BlockSpec((count, step), lambda i: (0, i)),
+        ],
+        out_specs=(
+            pl.BlockSpec((count, step), lambda i: (0, i)),
+            pl.BlockSpec((count, step), lambda i: (0, i)),
+            pl.BlockSpec((1, step), lambda i: (0, i)),
+        ),
+        compiler_params=BIG,
+        name="feed_forward",
+    )(rows, weight, bias.reshape(1, -1), pull)
 
 
 def on_device(
@@ -547,26 +820,23 @@
     wide = lax.axis_size(WIDE)
     me_n = lax.axis_index(NARROW)
     me_w = lax.axis_index(WIDE)
+    me = jnp.stack([me_n, me_w]).astype(jnp.int32)
     rows = batch * tokens
-    heads_local = HEADS // narrow
+    heads = HEADS // narrow
     head_dim = width // HEADS
-    cols = heads_local * head_dim
+    cols = heads * head_dim
     shard = width // (narrow * wide)
-
-    qkv_shard = jnp.stack([query_weight, key_weight, value_weight], axis=1)
-    qkv_shard = qkv_shard.reshape(shard, 3, narrow, cols).transpose(2, 0, 1, 3)
-    qkv_shard = narrow_swap(qkv_shard.reshape(narrow, shard, 3 * cols))
-    qkv_w = wide_gather(qkv_shard, 1).reshape(width, 3 * cols)
-    out_w = wide_gather(out_weight, 0)
     ff_local = up_weight.shape[1] // narrow
-    up_shard = narrow_swap(up_weight.reshape(shard, narrow, ff_local).transpose(1, 0, 2))
-    up_w = wide_gather(up_shard, 1).reshape(width, ff_local)
-    down_w = wide_gather(down_weight, 0)
 
     smalls = [
         attn_gain, attn_shift, out_bias, mlp_gain, mlp_shift, down_bias, query_bias, value_bias, up_bias
     ]
-    small = all_small(smalls)
+    ids = segment_ids.astype(bf16).reshape(-1)
+    small = cube_gather(jnp.concatenate(smalls + [ids])[None])
+    ids = small[:, -batch * tokens :].reshape(narrow * wide, batch, tokens)
+    unit_ids = at(ids, me_w // heads, 1).reshape(-1).astype(jnp.int32)
+    segc = unit_ids.reshape(-1, 512, 1)
+    segr = unit_ids.reshape(1, -1)
 
     def full_vector(k):
         return small[:, k * shard : (k + 1) * shard].reshape(-1).astype(f32)
@@ -575,41 +845,37 @@
     mine = lax.dynamic_slice_in_dim(small, me_n * wide, wide, 0)
     qbias = mine[:, 6 * shard : 7 * shard].reshape(-1).astype(f32)
     vbias = mine[:, 7 * shard : 8 * shard].reshape(-1).astype(f32)
-    ubias = mine[:, 8 * shard :].reshape(-1).astype(f32)
+    ubias = mine[:, 8 * shard : 8 * shard + ff_local // wide].reshape(-1).astype(f32)
     qkv_bias = jnp.concatenate([qbias, jnp.zeros_like(qbias), vbias])
 
-    segs = lax.all_gather(segment_ids[None], BOTH, axis=0, tiled=True)
-    unit_segs = lax.dynamic_index_in_dim(segs, me_w // heads_local, 1, keepdims=False).reshape(-1)
-    seq_blocks = unit_segs.shape[0] // 512
-    segc = unit_segs.reshape(seq_blocks, 512, 1)
-    segr = unit_segs.reshape(1, -1)
+    qkv_shard = jnp.stack([query_weight, key_weight, value_weight], axis=1)
+    qkv_shard = qkv_shard.reshape(shard, 3, narrow, cols).transpose(2, 0, 1, 3)
+    qkv_shard = narrow_swap(qkv_shard.reshape(narrow, shard, 3 * cols))
+    qkv_w = ring_gather(qkv_shard, 1).reshape(width, 3 * cols)
+    down_w = wide_gather(down_weight, 0)
+    up_shard = narrow_swap(up_weight.reshape(shard, narrow, ff_local).transpose(1, 0, 2))
+    up_w = wide_gather(up_shard, 1).reshape(width, ff_local)
+    out_w = wide_gather(out_weight, 0)
 
     inputs = block_input.astype(f32).reshape(rows, width)
     first_norm = narrow_gather(normalize(inputs, gain_attn, shift_attn).astype(bf16))
-    qkv = (matmul(first_norm, qkv_w) + qkv_bias).astype(bf16)
-    qkv = qkv.reshape(narrow, batch, tokens, 3, heads_local, head_dim).transpose(1, 4, 3, 0, 2, 5)
-    qkv = wide_swap(qkv.reshape(wide, 3, narrow, tokens, head_dim))
-    unit_out, lse = attend_fwd(segc, segr, qkv)
-    mixed = wide_swap(unit_out)
-    mixed = mixed.reshape(batch, heads_local, narrow, tokens, head_dim).transpose(2, 0, 3, 1, 4)
-    mixed = mixed.reshape(narrow * rows, cols)
-    middle = inputs + narrow_scatter(matmul(mixed, out_w)) + obias
-
-    second_norm = narrow_gather(normalize(middle, gain_mlp, shift_mlp).astype(bf16))
-    inner = matmul(second_norm, up_w) + ubias
-    hidden = gelu_exact(inner).astype(bf16)
-    output = middle + narrow_scatter(matmul(hidden, down_w)) + dbias
-    block_output = output.astype(bf16).reshape(batch, tokens, width)
+    sent = project(me, first_norm, qkv_w, qkv_bias, wide, 3, heads, tokens, False)
+    qkv = wide_swap(sent)
+    unit_out, lse = attend_fwd(me, segc, segr, qkv)
+    partial, mixed = unproject(me, wide_swap(unit_out), out_w, heads, False)
+    middle = inputs + narrow_scatter(partial) + obias
 
     cotan_own = cotangent.reshape(rows, width)
     cotan = narrow_gather(cotan_own)
+    hidden_grad = times_transpose(cotan, down_w)
+    second_norm = narrow_gather(normalize(middle, gain_mlp, shift_mlp).astype(bf16))
+    hidden, inner_grad, ubias_grad = feed_forward(second_norm, up_w, ubias, hidden_grad)
+    second_grad = narrow_scatter(times_transpose(inner_grad, up_w).astype(bf16))
+    output = middle + narrow_scatter(matmul(hidden, down_w).astype(bf16)) + dbias
+    block_output = output.astype(bf16).reshape(batch, tokens, width)
     down_grad = wide_scatter(outer_sum(hidden, cotan), 0)
-    hidden_grad = times_transpose(cotan, down_w)
-    inner_grad = jax.vjp(gelu_exact, inner)[1](hidden_grad)[0].astype(bf16)
     up_grad = outer_sum(second_norm, inner_grad).reshape(narrow, wide * shard, ff_local)
     up_grad = narrow_swap(wide_scatter(up_grad, 1)).transpose(1, 0, 2).reshape(shard, -1)
-    ubias_grad = jnp.sum(inner_grad.astype(f32), axis=0)
-    second_grad = narrow_scatter(times_transpose(inner_grad, up_w))
     mlp_pull = jax.vjp(normalize, middle, gain_mlp, shift_mlp)[1]
     middle_part, mgain_grad, mshift_grad = mlp_pull(second_grad)
     dbias_grad = jnp.sum(cotan_own.astype(f32), axis=0)
@@ -618,19 +884,17 @@
     branch_own = middle_grad.astype(bf16)
     obias_grad = jnp.sum(branch_own.astype(f32), axis=0)
     branch = narrow_gather(branch_own)
-    mixed_grad = times_transpose(branch, out_w).astype(bf16)
-    mixed_grad = mixed_grad.reshape(narrow, batch, tokens, heads_local, head_dim)
-    dout = wide_swap(mixed_grad.transpose(1, 3, 0, 2, 4).reshape(wide, narrow, tokens, head_dim))
+    no_bias = jnp.zeros((cols,), f32)
+    sent = project(me, branch, out_w, no_bias, wide, 1, heads, tokens, True)
+    unit_grads = attend_bwd(me, segc, segr, lse, qkv, wide_swap(sent))
     out_grad = wide_scatter(outer_sum(mixed, branch), 0)
-    unit_grads = attend_bwd(segc, segr, qkv, dout, lse)
-    back = wide_swap(unit_grads)
-    back = back.reshape(batch, heads_local, 3, narrow, tokens, head_dim).transpose(3, 0, 4, 2, 1, 5)
-    back = back.reshape(narrow * rows, 3 * cols)
-    qkv_grad = outer_sum(first_norm, back).reshape(narrow, wide * shard, 3 * cols)
-    qkv_grad = narrow_swap(wide_scatter(qkv_grad, 1)).reshape(narrow, shard, 3, cols)
+    partial, back = unproject(me, wide_swap(unit_grads), qkv_w, heads, True)
+    first_grad = narrow_scatter(partial)
+    qkv_grad = outer_sum(first_norm, back).astype(bf16).reshape(narrow, wide, shard, 3 * cols)
+    qkv_grad = narrow_swap(ring_scatter(qkv_grad, 1).astype(bf16))
+    qkv_grad = qkv_grad.reshape(narrow, shard, 3, cols)
     qkv_grad = qkv_grad.transpose(2, 1, 0, 3).reshape(3, shard, width).astype(f32)
     back_sums = jnp.sum(back.astype(f32), axis=0)
-    first_grad = narrow_scatter(times_transpose(back, qkv_w))
     attn_pull = jax.vjp(normalize, inputs, gain_attn, shift_attn)[1]
     input_part, again_grad, ashift_grad = attn_pull(first_grad)
     input_grad = (middle_grad + input_part).reshape(batch, tokens, width)
@@ -641,9 +905,7 @@
     slices = jnp.concatenate([v.reshape(wide, -1) for v in slices], axis=1)
     placed = jnp.zeros((narrow * wide, slices.shape[1]), f32)
     placed = lax.dynamic_update_slice_in_dim(placed, slices, me_n * wide, 0)
-    vectors = lax.psum_scatter(
-        jnp.concatenate([fulls, placed], axis=1), BOTH, scatter_dimension=0, tiled=True
-    ).reshape(-1)
+    vectors = cube_scatter(jnp.concatenate([fulls, placed], axis=1))
 
     def vector(k):
         return vectors[k * shard : (k + 1) * shard]

time: 1760 us -> 1090 us (0.62)
  waiting for transfers between devices: 1060 us -> 517 us
  blocking collectives: 349 us -> 0 us
  starting transfers between devices: 18.3 us -> 253 us
  matrix products: 151 us -> 80.8 us
  Pallas kernels: 25.5 us -> 79.1 us
    ppermute x0 -> x88, waiting for transfers between devices: none -> 515 us  [the longest x74 394 us: flip(): return lax.ppermute(value, axis, [(i, i ^ bits) for i in range(size)])]
    all_gather x4 -> x3, waiting for transfers between devices: 345 us -> 0.01 us  [wide_gather(): return lax.all_gather(shard, WIDE, axis=axis, tiled=True)]
    reduce_scatter x4 -> x3, waiting for transfers between devices: 333 us -> 0.02 us  [wide_scatter(): lax.psum_scatter(full.astype(jnp.bfloat16), WIDE, scatter_dimension=axis,...]
    ppermute x0 -> x88, starting transfers between devices: none -> 253 us  [the longest x74 168 us: flip(): return lax.ppermute(value, axis, [(i, i ^ bits) for i in range(size)])]
    all_gather x2 -> x0, blocking collectives: 220 us -> none  [the longest x1 150 us: on_device(): segs = lax.all_gather(segment_ids[None], BOTH, axis=0, tiled=True)]
    all_to_all x4 -> x0, blocking collectives: 129 us -> none  [the longest x2 84.4 us: wide_swap(): return lax.all_to_all(parts, WIDE, split_axis=0, concat_axis=0, tiled=True)]
    reduce_scatter x4 -> x0, waiting for transfers between devices: 122 us -> none  [narrow_scatter(): lax.psum_scatter(partial.astype(jnp.bfloat16), NARROW, scatter_dimension=...]
    unnamed x18 -> x6, waiting for transfers between devices: 120 us -> 1.44 us
  transfers between devices with their start and end apart: 21 -> 94, of which waited for: 17 -> 46; matrix products, arithmetic and copies ran while one was open for 10% -> 18% of each run, Pallas kernels for 1% -> 6%
where the time goes in v2:
time: 1090 us; the launch traced here: 1080 us
  waiting for transfers between devices  517 us (47%)
  starting transfers between devices  253 us (23%)
  matrix products  80.8 us (7%)
  local copies, waits for them, and re-layouts  79.1 us (7%)
  Pallas kernels  79.1 us (7%)
  other arithmetic  59.6 us (5%)
  between operations  15.8 us (1%)
    ppermute x74, waiting for transfers between devices, flip(): return lax.ppermute(value, axis, [(i, i ^ bits) for i in range(size)])  394 us
    ppermute x74, starting transfers between devices, flip(): return lax.ppermute(value, axis, [(i, i ^ bits) for i in range(size)])  168 us
    ppermute x14, waiting for transfers between devices, ring_step(): lax.ppermute(value, WIDE, [(order[i], order[(i + by) % size]) for i in ra...  121 us
    ppermute x14, starting transfers between devices, ring_step(): lax.ppermute(value, WIDE, [(order[i], order[(i + by) % size]) for i in ra...  85 us
    dot_general x4, matrix products, outer_sum(): lax.dot_general(left, right, (((0,), (0,)), ((), ())), preferred_element_...  42.1 us
    dot_general x2, matrix products, times_transpose(): lax.dot_general(left, right, (((1,), (1,)), ((), ())), preferred_element_...  27.4 us
  transfers between devices with their start and end apart: 94, of which 46 were waited for; matrix products, arithmetic and copies ran while one was open for 18% of the time, Pallas kernels for 6%

profile of v2, /device:TPU:0, one launch (start us, length us, event | category | flops | bytes accessed | tf_op | source)
XLA Modules:
  0.0 1084.1 jit_solution(5021244785135460339)
XLA Ops:
  53.0 3.3 broadcast_in_dim.105
  64.3 18.6 %collective-permute-done.11 = bf16[4,64,1536]{2,1,0:T(8,128)(2,1)} collective-permute-done((bf16[4,64,1536]{2,1,0:T(8,128)(2,1)}, bf16[4,64,1536]{2,1,0:T(8,128)(2,1)}, u32[]{:S(2)}, u32[]{:S(2)}) %collective-permute-start.11) | collective-permute-done | bytes 786464 | tf_op jit(solution)/shard_map/ppermute | solution.py:467
  82.9 5.1 collective-permute-start.13
  88.0 8.4 collective-permute-done.12
  100.6 21.1 %collective-permute-done.13 = bf16[4,64,1536]{2,1,0:T(8,128)(2,1)S(1)} collective-permute-done((bf16[4,64,1536]{2,1,0:T(8,128)(2,1)}, bf16[4,64,1536]{2,1,0:T(8,128)(2,1)S(1)}, u32[]{:S(2)}, u32[]{:S(2)}) %collective-permute-start.13) | collective-permute-done | bytes 786464 | tf_op jit(solution)/shard_map/ppermute | solution.py:467
  121.7 7.9 collective-permute-start.15
  133.7 4.0 pad_maximum_fusion.rows_ref
  137.7 18.3 %collective-permute-done.15 = bf16[4,64,1536]{2,1,0:T(8,128)(2,1)S(1)} collective-permute-done((bf16[4,64,1536]{2,1,0:T(8,128)(2,1)S(1)}, bf16[4,64,1536]{2,1,0:T(8,128)(2,1)S(1)}, u32[]{:S(2)}, u32[]{:S(2)}) %collective-permute-start.15) | collective-permute-done | bytes 786464 | tf_op jit(solution)/shard_map/ppermute | solution.py:467
  156.0 18.0 %collective-permute-start.17 = (bf16[4,64,1536]{2,1,0:T(8,128)(2,1)S(1)}, bf16[4,64,1536]{2,1,0:T(8,128)(2,1)S(1)}, u32[]{:S(2)}, u32[]{:S(2)}) collective-permute-start(bf16[4,64,1536]{2,1,0:T(8,128)(2,1)S(1)} %collective-permute-done.15), channel_id=1, source_target_pairs={{0,2},{2,4},{4,6},{6,7},{7,5},{5,3},{3,1},{1,0},{8,10},{10,12},{12... | collective-permute-start | bytes 2359304 | tf_op jit(solution)/shard_map/ppermute | solution.py:467
  177.5 27.4 %collective-permute-done.17 = bf16[4,64,1536]{2,1,0:T(8,128)(2,1)S(1)} collective-permute-done((bf16[4,64,1536]{2,1,0:T(8,128)(2,1)S(1)}, bf16[4,64,1536]{2,1,0:T(8,128)(2,1)S(1)}, u32[]{:S(2)}, u32[]{:S(2)}) %collective-permute-start.17) | collective-permute-done | bytes 786464 | tf_op jit(solution)/shard_map/ppermute | solution.py:467
  205.8 10.7 project.2
  217.8 21.5 %collective-permute-start.18 = (bf16[3,4,128,128]{3,2,1,0:T(8,128)(2,1)S(1)}, bf16[3,4,128,128]{3,2,1,0:T(8,128)(2,1)S(1)}, u32[]{:S(2)}, u32[]{:S(2)}) collective-permute-start(bf16[3,4,128,128]{3,2,1,0:T(8,128)(2,1)S(1)} %get-tuple-element.79), channel_id=1, source_target_pairs={{0,1},{1,0},{2,3},{3,2},{4,5},{5,4},{6,7},{7,6},{8,9},{9,8},{10,11... | collective-permute-start | bytes 1179656 | tf_op jit(solution)/shard_map/ppermute | solution.py:383
  239.9 3.3 reshape.410.segc_ref
  244.7 4.6 collective-permute-start.21
  249.3 3.8 collective-permute-start.23
  253.1 9.7 collective-permute-done.19.refs_2_
  262.8 3.3 collective-permute-start.24
  266.8 15.5 %collective-permute-done.20.refs_3_ = bf16[3,4,128,128]{3,2,1,0:T(8,128)(2,1)S(1)} collective-permute-done((bf16[3,4,128,128]{3,2,1,0:T(8,128)(2,1)}, bf16[3,4,128,128]{3,2,1,0:T(8,128)(2,1)S(1)}, u32[]{:S(2)}, u32[]{:S(2)}) %collective-permute-start.20) | collective-permute-done | bytes 393248 | tf_op jit(solution)/shard_map/ppermute | solution.py:383
  282.3 13.5 %collective-permute-done.21.refs_4_ = bf16[3,4,128,128]{3,2,1,0:T(8,128)(2,1)S(1)} collective-permute-done((bf16[3,4,128,128]{3,2,1,0:T(8,128)(2,1)}, bf16[3,4,128,128]{3,2,1,0:T(8,128)(2,1)S(1)}, u32[]{:S(2)}, u32[]{:S(2)}) %collective-permute-start.21) | collective-permute-done | bytes 393248 | tf_op jit(solution)/shard_map/ppermute | solution.py:383
  295.8 35.7 %collective-permute-done.22.refs_5_ = bf16[3,4,128,128]{3,2,1,0:T(8,128)(2,1)S(1)} collective-permute-done((bf16[3,4,128,128]{3,2,1,0:T(8,128)(2,1)}, bf16[3,4,128,128]{3,2,1,0:T(8,128)(2,1)S(1)}, u32[]{:S(2)}, u32[]{:S(2)}) %collective-permute-start.22) | collective-permute-done | bytes 393248 | tf_op jit(solution)/shard_map/ppermute | solution.py:383
  331.5 9.4 attend_fwd.1
  344.2 42.1 %collective-permute-start.26 = (bf16[1,4,128,128]{3,2,1,0:T(8,128)(2,1)S(1)}, bf16[1,4,128,128]{3,2,1,0:T(8,128)(2,1)S(1)}, u32[]{:S(2)}, u32[]{:S(2)}) collective-permute-start(bf16[1,4,128,128]{3,2,1,0:T(8,128)(2,1)S(1)} %get-tuple-element.105), channel_id=1, source_target_pairs={{0,2},{1,3},{2,0},{3,1},{4,6},{5,7},{6,4},{7,5},{8,10},{9,11},{10,... | collective-permute-start | bytes 393224 | tf_op jit(solution)/shard_map/ppermute | solution.py:383
  387.8 4.1 collective-permute-start.28
  400.1 15.7 %collective-permute-done.29.refs_5_ = bf16[1,4,128,128]{3,2,1,0:T(8,128)(2,1)} collective-permute-done((bf16[1,4,128,128]{3,2,1,0:T(8,128)(2,1)}, bf16[1,4,128,128]{3,2,1,0:T(8,128)(2,1)}, u32[]{:S(2)}, u32[]{:S(2)}) %collective-permute-start.29) | collective-permute-done | bytes 131104 | tf_op jit(solution)/shard_map/ppermute | solution.py:383
  420.5 5.4 unproject.2
  430.1 3.6 collective-permute-done.33
  436.5 25.3 %collective-permute-done.34 = bf16[256,2048]{1,0:T(8,128)(2,1)} collective-permute-done((bf16[256,2048]{1,0:T(8,128)(2,1)}, bf16[256,2048]{1,0:T(8,128)(2,1)}, u32[]{:S(2)}, u32[]{:S(2)}) %collective-permute-start.34) | collective-permute-done | bytes 1048608 | tf_op jit(solution)/shard_map/ppermute | solution.py:383
  467.6 24.1 %collective-permute-done.36 = bf16[256,2048]{1,0:T(8,128)(2,1)S(1)} collective-permute-done((bf16[256,2048]{1,0:T(8,128)(2,1)S(1)}, bf16[256,2048]{1,0:T(8,128)(2,1)S(1)}, u32[]{:S(2)}, u32[]{:S(2)}) %collective-permute-start.36) | collective-permute-done | bytes 1048608 | tf_op jit(solution)/shard_map/ppermute | solution.py:383
  492.2 20.2 %collective-permute-done.42 = bf16[256,2048]{1,0:T(8,128)(2,1)S(1)} collective-permute-done((bf16[256,2048]{1,0:T(8,128)(2,1)S(1)}, bf16[256,2048]{1,0:T(8,128)(2,1)S(1)}, u32[]{:S(2)}, u32[]{:S(2)}) %collective-permute-start.42) | collective-permute-done | bytes 1048608 | tf_op jit(solution)/shard_map/ppermute | solution.py:383
  516.8 14.4 %fusion.20.pull_ref = f32[1024,2048]{1,0:T(8,128)} fusion(bf16[2048,2048]{1,0:T(8,128)(2,1)} %all-gather.8.cloned.1.call-done, bf16[256,2048]{1,0:T(8,128)(2,1)} %collective-permute-done.43, bf16[256,2048]{1,0:T(8,128)(2,1)} %copy-done.65, bf16[256,2048]{1,0:T(8,128)(2,1)} %copy-done.66, bf16[256,2048]{1,0:T(8,128)(2,1)} %bitcast.285), kind=kOutput, calls=%fused_computation.70 | convolution fusion | flops 8606711808 | bytes 20971520 | tf_op jit(solution)/shard_map/dot_general | solution.py:56
  531.2 18.8 %feed_forward.1 = (bf16[1024,2048]{1,0:T(8,128)(2,1)S(1)}, bf16[1024,2048]{1,0:T(8,128)(2,1)}, f32[1,2048]{1,0:T(1,128)S(1)}) custom-call(bf16[1024,2048]{1,0:T(8,128)(2,1)} %pad_maximum_fusion.1.rows_ref, bf16[2048,2048]{1,0:T(8,128)(2,1)} %bitcast.289, f32[1,2048]{1,0:T(1,128)S(1)} %bitcast.284, f32[1024,2048]{1,0:T(8,128)} %fusion.20.pull_ref), custom_call_target="tpu_custom_call" | custom-call | tf_op jit(solution)/shard_map/feed_forward/pallas_call | solution.py:772
  550.1 14.8 %convolution_convert_fusion.1 = bf16[2048,2048]{1,0:T(8,128)(2,1)} fusion(bf16[1024,2048]{1,0:T(8,128)(2,1)} %get-tuple-element.29, bf16[256,2048]{1,0:T(8,128)(2,1)S(1)} %copy-done.38, bf16[256,2048]{1,0:T(8,128)(2,1)S(1)} %copy-done.34, bf16[256,2048]{1,0:T(8,128)(2,1)S(1)} %copy-done.36, bf16[256,2048]{1,0:T(8,128)(2,1)S(1)} %copy-done.27), kind=kOutput, calls=%fused_computation.1 | convolution fusion | flops 8610906112 | bytes 16777216 | tf_op jit(solution)/shard_map/dot_general | solution.py:50
  565.0 13.0 %convolution_convert_fusion.3 = bf16[1024,2048]{1,0:T(8,128)(2,1)S(1)} fusion(bf16[1024,2048]{1,0:T(8,128)(2,1)} %get-tuple-element.29, bf16[2048,2048]{1,0:T(8,128)(2,1)} %bitcast.290), kind=kOutput, calls=%fused_computation.8 | convolution fusion | flops 8592031744 | bytes 16777216 | tf_op jit(solution)/shard_map/dot_general | solution.py:56
  582.1 11.2 %convolution_convert_fusion.4 = bf16[1024,2048]{1,0:T(8,128)(2,1)S(1)} fusion(bf16[1024,2048]{1,0:T(8,128)(2,1)S(1)} %copy-done.6, bf16[2048,2048]{1,0:T(8,128)(2,1)} %all-gather.8.cloned.1.call-done), kind=kOutput, calls=%fused_computation.9 | convolution fusion | flops 8592031744 | bytes 16777216 | tf_op jit(solution)/shard_map/dot_general | solution.py:46
  600.8 22.0 %collective-permute-done.49 = bf16[256,2048]{1,0:T(8,128)(2,1)} collective-permute-done((bf16[256,2048]{1,0:T(8,128)(2,1)}, bf16[256,2048]{1,0:T(8,128)(2,1)}, u32[]{:S(2)}, u32[]{:S(2)}) %collective-permute-start.49) | collective-permute-done | bytes 1048608 | tf_op jit(solution)/shard_map/ppermute | solution.py:383
  622.7 3.5 multiply_reduce_fusion
  626.3 18.5 %collective-permute-done.46 = bf16[256,2048]{1,0:T(8,128)(2,1)} collective-permute-done((bf16[256,2048]{1,0:T(8,128)(2,1)}, bf16[256,2048]{1,0:T(8,128)(2,1)}, u32[]{:S(2)}, u32[]{:S(2)}) %collective-permute-start.46) | collective-permute-done | bytes 1048608 | tf_op jit(solution)/shard_map/ppermute | solution.py:383
  644.8 5.3 fusion.50
  652.7 24.1 %collective-permute-done.51 = bf16[256,2048]{1,0:T(8,128)(2,1)S(1)} collective-permute-done((bf16[256,2048]{1,0:T(8,128)(2,1)S(1)}, bf16[256,2048]{1,0:T(8,128)(2,1)S(1)}, u32[]{:S(2)}, u32[]{:S(2)}) %collective-permute-start.51) | collective-permute-done | bytes 1048608 | tf_op jit(solution)/shard_map/ppermute | solution.py:383
  680.4 3.8 convolution_convert_fusion.5
  684.3 14.2 %convolution_convert_fusion = bf16[2048,2048]{1,0:T(8,128)(2,1)} fusion(bf16[1024,2048]{1,0:T(8,128)(2,1)} %copy-done.5, bf16[256,2048]{1,0:T(8,128)(2,1)} %collective-permute-done.43, bf16[256,2048]{1,0:T(8,128)(2,1)} %copy-done.65, bf16[256,2048]{1,0:T(8,128)(2,1)} %copy-done.66, bf16[256,2048]{1,0:T(8,128)(2,1)} %bitcast.286), kind=kOutput, calls=%fused_computation | convolution fusion | flops 8610906112 | bytes 16777216 | tf_op jit(solution)/shard_map/dot_general | solution.py:50
  698.5 4.0 pad_maximum_fusion.3.rows_ref
  702.5 4.9 project.3
  709.2 8.6 collective-permute-start.54
  725.1 4.0 collective-permute-start.59
  730.6 7.1 collective-permute-done.56.refs_12_
  737.8 6.5 collective-permute-done.57.refs_13_
  744.3 18.1 %attend_bwd.1 = bf16[8,3,4,128,128]{4,3,2,1,0:T(8,128)(2,1)} custom-call(s32[2]{0:T(128)S(1)} %copy-done.4, s32[8,512,1]{2,1,0:T(8,128)} %reshape.410.segc_ref, s32[1,4096]{1,0:T(1,128)S(1)} %convert_bitcast_fusion.1.segr_ref, f32[8,512,1]{2,1,0:T(8,128)} %get-tuple-element.30.lse_ref, bf16[3,4,128,128]{3,2,1,0:T(8,128)(2,1)S(1)} %get-tuple-element.80.refs_0_, ...), custom_call_target="tpu_custom_call" | custom-call | tf_op jit(solution)/shard_map/attend_bwd/pallas_call | solution.py:735
  762.4 3.2 slice_bitcast_fusion
  765.6 3.9 collective-permute-start.60
  769.5 14.9 %collective-permute-start.61 = (bf16[3,4,128,128]{3,2,1,0:T(8,128)(2,1)S(1)}, bf16[3,4,128,128]{3,2,1,0:T(8,128)(2,1)S(1)}, u32[]{:S(2)}, u32[]{:S(2)}) collective-permute-start(bf16[3,4,128,128]{3,2,1,0:T(8,128)(2,1)S(1)} %get-tuple-element.70), channel_id=1, source_target_pairs={{0,2},{1,3},{2,0},{3,1},{4,6},{5,7},{6,4},{7,5},{8,10},{9,11},{10,... | collective-permute-start | bytes 1179656 | tf_op jit(solution)/shard_map/ppermute | solution.py:383
  789.7 23.5 %collective-permute-done.61.refs_2_ = bf16[3,4,128,128]{3,2,1,0:T(8,128)(2,1)S(1)} collective-permute-done((bf16[3,4,128,128]{3,2,1,0:T(8,128)(2,1)S(1)}, bf16[3,4,128,128]{3,2,1,0:T(8,128)(2,1)S(1)}, u32[]{:S(2)}, u32[]{:S(2)}) %collective-permute-start.61) | collective-permute-done | bytes 393248 | tf_op jit(solution)/shard_map/ppermute | solution.py:383
  818.1 47.7 %collective-permute-done.64.refs_5_ = bf16[3,4,128,128]{3,2,1,0:T(8,128)(2,1)S(1)} collective-permute-done((bf16[3,4,128,128]{3,2,1,0:T(8,128)(2,1)}, bf16[3,4,128,128]{3,2,1,0:T(8,128)(2,1)S(1)}, u32[]{:S(2)}, u32[]{:S(2)}) %collective-permute-start.64) | collective-permute-done | bytes 393248 | tf_op jit(solution)/shard_map/ppermute | solution.py:383
  865.9 11.7 %unproject.3 = (bf16[1024,2048]{1,0:T(8,128)(2,1)}, bf16[1024,1536]{1,0:T(8,128)(2,1)}) custom-call(s32[2]{0:T(128)S(1)} %copy-done.4, bf16[3,4,128,128]{3,2,1,0:T(8,128)(2,1)S(1)} %get-tuple-element.72.refs_0_, bf16[3,4,128,128]{3,2,1,0:T(8,128)(2,1)S(1)} %collective-permute-done.60.refs_1_, bf16[3,4,128,128]{3,2,1,0:T(8,128)(2,1)S(1)} %collective-permute-done.61.refs_2_, ...), custom_call_target="tpu_custom_call" | custom-call | tf_op jit(solution)/shard_map/unproject/pallas_call | solution.py:609
  877.6 9.4 convolution_convert_fusion.2
  888.3 44.7 %collective-permute-start.75 = (bf16[4,64,1536]{2,1,0:T(8,128)(2,1)}, bf16[4,64,1536]{2,1,0:T(8,128)(2,1)}, u32[]{:S(2)}, u32[]{:S(2)}) collective-permute-start(bf16[4,64,1536]{2,1,0:T(8,128)(2,1)} %get-tuple-element.55), channel_id=1, source_target_pairs={{0,2},{2,4},{4,6},{6,7},{7,5},{5,3},{3,1},{1,0},{8,10},{10,12},{12... | collective-permute-start | bytes 2359304 | tf_op jit(solution)/shard_map/ppermute | solution.py:467
  936.9 6.9 collective-permute-done.75
  954.9 10.7 collective-permute-done.79
  967.6 3.4 fusion.15
  981.6 38.6 %collective-permute-done.72 = f32[2,2,768]{2,1,0:T(2,128)S(1)} collective-permute-done((f32[2,2,768]{2,1,0:T(2,128)S(1)}, f32[2,2,768]{2,1,0:T(2,128)S(1)}, u32[]{:S(2)}, u32[]{:S(2)}) %collective-permute-start.72) | collective-permute-done | bytes 12320 | tf_op jit(solution)/shard_map/ppermute | solution.py:383
  1020.3 3.8 collective-permute-done.80
  1031.3 10.6 collective-permute-done.74
  1049.2 6.6 collective-permute-done.83
  1070.3 4.1 collective-permute-done.86
  (442 shorter events, 204.2 us)
Async XLA Ops:
  7.2 390.0 %all-gather.4.cloned.1.call-start = ((), (), s32[]{:S(2)}) async-start(), calls=%async_computation.3 | async-start | bytes 2359296 | tf_op jit(solution)/shard_map/all_gather | solution.py:521
  7.9 508.8 %all-gather.8.cloned.1.call-start = ((), (), s32[]{:S(2)}) async-start(), calls=%async_computation.5 | async-start | bytes 9437184 | tf_op jit(solution)/shard_map/all_gather | solution.py:521
  8.7 522.5 %all-gather.6.cloned.1.call-start = ((), (), s32[]{:S(2)}) async-start(), calls=%async_computation.4 | async-start | bytes 9437184 | tf_op jit(solution)/shard_map/all_gather | solution.py:521
  17.3 28.0 %collective-permute-start.8 = (bf16[64,1536]{1,0:T(8,128)(2,1)}, bf16[64,1536]{1,0:T(8,128)(2,1)}, u32[]{:S(2)}, u32[]{:S(2)}) collective-permute-start(bf16[64,1536]{1,0:T(8,128)(2,1)} %get-tuple-element.113), channel_id=1, source_target_pairs={{0,24},{8,16},{16,8},{24,0},{1,25},{9,17},{17,9},{25,1},{2,26},{10... | collective-permute-start | bytes 589832 | tf_op jit(solution)/shard_map/ppermute | solution.py:383
  19.7 28.3 %collective-permute-start.9 = (bf16[64,1536]{1,0:T(8,128)(2,1)}, bf16[64,1536]{1,0:T(8,128)(2,1)}, u32[]{:S(2)}, u32[]{:S(2)}) collective-permute-start(bf16[64,1536]{1,0:T(8,128)(2,1)} %get-tuple-element.112), channel_id=1, source_target_pairs={{0,16},{8,24},{16,0},{24,8},{1,17},{9,25},{17,1},{25,9},{2,18},{10... | collective-permute-start | bytes 589832 | tf_op jit(solution)/shard_map/ppermute | solution.py:383
  20.3 30.2 %collective-permute-start.10 = (bf16[64,1536]{1,0:T(8,128)(2,1)}, bf16[64,1536]{1,0:T(8,128)(2,1)}, u32[]{:S(2)}, u32[]{:S(2)}) collective-permute-start(bf16[64,1536]{1,0:T(8,128)(2,1)} %get-tuple-element.111), channel_id=1, source_target_pairs={{0,8},{8,0},{16,24},{24,16},{1,9},{9,1},{17,25},{25,17},{2,10},{10... | collective-permute-start | bytes 589832 | tf_op jit(solution)/shard_map/ppermute | solution.py:383
  27.6 30.8 %collective-permute-start.38 = (bf16[64,2048]{1,0:T(8,128)(2,1)S(1)}, bf16[64,2048]{1,0:T(8,128)(2,1)}, u32[]{:S(2)}, u32[]{:S(2)}) collective-permute-start(bf16[64,2048]{1,0:T(8,128)(2,1)S(1)} %bitcast.307), channel_id=1, source_target_pairs={{0,24},{8,16},{16,8},{24,0},{1,25},{9,17},{17,9},{25,1},{2,26},{10... | collective-permute-start | bytes 786440 | tf_op jit(solution)/shard_map/ppermute | solution.py:383
  42.5 18.5 %collective-permute-start.39 = (bf16[64,2048]{1,0:T(8,128)(2,1)}, bf16[64,2048]{1,0:T(8,128)(2,1)}, u32[]{:S(2)}, u32[]{:S(2)}) collective-permute-start(bf16[64,2048]{1,0:T(8,128)(2,1)} %bitcast.282), channel_id=1, source_target_pairs={{0,16},{8,24},{16,0},{24,8},{1,17},{9,25},{17,1},{25,9},{2,18},{10... | collective-permute-start | bytes 786440 | tf_op jit(solution)/shard_map/ppermute | solution.py:383
  45.4 17.7 %collective-permute-start.40 = (bf16[64,2048]{1,0:T(8,128)(2,1)}, bf16[64,2048]{1,0:T(8,128)(2,1)S(1)}, u32[]{:S(2)}, u32[]{:S(2)}) collective-permute-start(bf16[64,2048]{1,0:T(8,128)(2,1)} %bitcast.308), channel_id=1, source_target_pairs={{0,8},{8,0},{16,24},{24,16},{1,9},{9,1},{17,25},{25,17},{2,10},{10... | collective-permute-start | bytes 786440 | tf_op jit(solution)/shard_map/ppermute | solution.py:383
  48.0 50.5 %collective-permute-start.6 = (bf16[256,2048]{1,0:T(8,128)(2,1)S(1)}, bf16[256,2048]{1,0:T(8,128)(2,1)}, u32[]{:S(2)}, u32[]{:S(2)}) collective-permute-start(bf16[256,2048]{1,0:T(8,128)(2,1)S(1)} %fusion.6), channel_id=1, source_target_pairs={{0,16},{8,24},{16,0},{24,8},{1,17},{9,25},{17,1},{25,9},{2,18},{10... | collective-permute-start | bytes 3145736 | tf_op jit(solution)/shard_map/ppermute | solution.py:383
  50.5 83.2 %collective-permute-start.5 = (bf16[256,2048]{1,0:T(8,128)(2,1)S(1)}, bf16[256,2048]{1,0:T(8,128)(2,1)}, u32[]{:S(2)}, u32[]{:S(2)}) collective-permute-start(bf16[256,2048]{1,0:T(8,128)(2,1)S(1)} %fusion.6), channel_id=1, source_target_pairs={{0,8},{8,0},{16,24},{24,16},{1,9},{9,1},{17,25},{25,17},{2,10},{10... | collective-permute-start | bytes 3145736 | tf_op jit(solution)/shard_map/ppermute | solution.py:383
  58.4 24.5 %collective-permute-start.11 = (bf16[4,64,1536]{2,1,0:T(8,128)(2,1)}, bf16[4,64,1536]{2,1,0:T(8,128)(2,1)}, u32[]{:S(2)}, u32[]{:S(2)}) collective-permute-start(bf16[4,64,1536]{2,1,0:T(8,128)(2,1)} %dynamic-slice_dynamic-update-slice_fusion.2), channel_id=1, source_target_pairs={{0,2},{2,4},{4,6},{6,7},{7,5},{5,3},{3,1},{1,0},{8,10},{10,12},{12... | collective-permute-start | bytes 2359304 | tf_op jit(solution)/shard_map/ppermute | solution.py:467
  61.0 35.4 %collective-permute-start.12 = (bf16[4,64,1536]{2,1,0:T(8,128)(2,1)}, bf16[4,64,1536]{2,1,0:T(8,128)(2,1)}, u32[]{:S(2)}, u32[]{:S(2)}) collective-permute-start(bf16[4,64,1536]{2,1,0:T(8,128)(2,1)} %dynamic-slice_dynamic-update-slice_fusion.2), channel_id=1, source_target_pairs={{0,1},{2,0},{4,2},{6,4},{7,6},{5,7},{3,5},{1,3},{8,9},{10,8},{12,1... | collective-permute-start | bytes 2359304 | tf_op jit(solution)/shard_map/ppermute | solution.py:467
  64.3 993.0 %reduce-scatter.6.cloned.1.call-start = ((), (), s32[]{:S(2)}) async-start(), calls=%async_computation.7 | async-start | bytes 9437184 | tf_op jit(solution)/shard_map/reduce_scatter | solution.py:525
  82.9 38.8 %collective-permute-start.13 = (bf16[4,64,1536]{2,1,0:T(8,128)(2,1)}, bf16[4,64,1536]{2,1,0:T(8,128)(2,1)S(1)}, u32[]{:S(2)}, u32[]{:S(2)}) collective-permute-start(bf16[4,64,1536]{2,1,0:T(8,128)(2,1)} %collective-permute-done.11), channel_id=1, source_target_pairs={{0,2},{2,4},{4,6},{6,7},{7,5},{5,3},{3,1},{1,0},{8,10},{10,12},{12... | collective-permute-start | bytes 2359304 | tf_op jit(solution)/shard_map/ppermute | solution.py:467
  96.4 35.4 %collective-permute-start.14 = (bf16[4,64,1536]{2,1,0:T(8,128)(2,1)}, bf16[4,64,1536]{2,1,0:T(8,128)(2,1)S(1)}, u32[]{:S(2)}, u32[]{:S(2)}) collective-permute-start(bf16[4,64,1536]{2,1,0:T(8,128)(2,1)} %collective-permute-done.12), channel_id=1, source_target_pairs={{0,1},{2,0},{4,2},{6,4},{7,6},{5,7},{3,5},{1,3},{8,9},{10,8},{12,1... | collective-permute-start | bytes 2359304 | tf_op jit(solution)/shard_map/ppermute | solution.py:467
  98.5 35.2 %collective-permute-start.7 = (bf16[256,2048]{1,0:T(8,128)(2,1)}, bf16[256,2048]{1,0:T(8,128)(2,1)S(1)}, u32[]{:S(2)}, u32[]{:S(2)}) collective-permute-start(bf16[256,2048]{1,0:T(8,128)(2,1)} %collective-permute-done.6), channel_id=1, source_target_pairs={{0,8},{8,0},{16,24},{24,16},{1,9},{9,1},{17,25},{25,17},{2,10},{10... | collective-permute-start | bytes 3145736 | tf_op jit(solution)/shard_map/ppermute | solution.py:383
  121.7 34.3 %collective-permute-start.15 = (bf16[4,64,1536]{2,1,0:T(8,128)(2,1)S(1)}, bf16[4,64,1536]{2,1,0:T(8,128)(2,1)S(1)}, u32[]{:S(2)}, u32[]{:S(2)}) collective-permute-start(bf16[4,64,1536]{2,1,0:T(8,128)(2,1)S(1)} %collective-permute-done.13), channel_id=1, source_target_pairs={{0,2},{2,4},{4,6},{6,7},{7,5},{5,3},{3,1},{1,0},{8,10},{10,12},{12... | collective-permute-start | bytes 2359304 | tf_op jit(solution)/shard_map/ppermute | solution.py:467
  131.8 44.7 %collective-permute-start.16 = (bf16[4,64,1536]{2,1,0:T(8,128)(2,1)S(1)}, bf16[4,64,1536]{2,1,0:T(8,128)(2,1)S(1)}, u32[]{:S(2)}, u32[]{:S(2)}) collective-permute-start(bf16[4,64,1536]{2,1,0:T(8,128)(2,1)S(1)} %collective-permute-done.14), channel_id=1, source_target_pairs={{0,1},{2,0},{4,2},{6,4},{7,6},{5,7},{3,5},{1,3},{8,9},{10,8},{12,1... | collective-permute-start | bytes 2359304 | tf_op jit(solution)/shard_map/ppermute | solution.py:467
  156.0 48.8 %collective-permute-start.17 = (bf16[4,64,1536]{2,1,0:T(8,128)(2,1)S(1)}, bf16[4,64,1536]{2,1,0:T(8,128)(2,1)S(1)}, u32[]{:S(2)}, u32[]{:S(2)}) collective-permute-start(bf16[4,64,1536]{2,1,0:T(8,128)(2,1)S(1)} %collective-permute-done.15), channel_id=1, source_target_pairs={{0,2},{2,4},{4,6},{6,7},{7,5},{5,3},{3,1},{1,0},{8,10},{10,12},{12... | collective-permute-start | bytes 2359304 | tf_op jit(solution)/shard_map/ppermute | solution.py:467
  217.8 31.5 %collective-permute-start.18 = (bf16[3,4,128,128]{3,2,1,0:T(8,128)(2,1)S(1)}, bf16[3,4,128,128]{3,2,1,0:T(8,128)(2,1)S(1)}, u32[]{:S(2)}, u32[]{:S(2)}) collective-permute-start(bf16[3,4,128,128]{3,2,1,0:T(8,128)(2,1)S(1)} %get-tuple-element.79), channel_id=1, source_target_pairs={{0,1},{1,0},{2,3},{3,2},{4,5},{5,4},{6,7},{7,6},{8,9},{9,8},{10,11... | collective-permute-start | bytes 1179656 | tf_op jit(solution)/shard_map/ppermute | solution.py:383
  239.3 23.4 %collective-permute-start.19 = (bf16[3,4,128,128]{3,2,1,0:T(8,128)(2,1)S(1)}, bf16[3,4,128,128]{3,2,1,0:T(8,128)(2,1)S(1)}, u32[]{:S(2)}, u32[]{:S(2)}) collective-permute-start(bf16[3,4,128,128]{3,2,1,0:T(8,128)(2,1)S(1)} %get-tuple-element.78), channel_id=1, source_target_pairs={{0,2},{1,3},{2,0},{3,1},{4,6},{5,7},{6,4},{7,5},{8,10},{9,11},{10,... | collective-permute-start | bytes 1179656 | tf_op jit(solution)/shard_map/ppermute | solution.py:383
  243.2 39.1 %collective-permute-start.20 = (bf16[3,4,128,128]{3,2,1,0:T(8,128)(2,1)}, bf16[3,4,128,128]{3,2,1,0:T(8,128)(2,1)S(1)}, u32[]{:S(2)}, u32[]{:S(2)}) collective-permute-start(bf16[3,4,128,128]{3,2,1,0:T(8,128)(2,1)} %get-tuple-element.77), channel_id=1, source_target_pairs={{0,3},{1,2},{2,1},{3,0},{4,7},{5,6},{6,5},{7,4},{8,11},{9,10},{10,... | collective-permute-start | bytes 1179656 | tf_op jit(solution)/shard_map/ppermute | solution.py:383
  244.7 51.1 %collective-permute-start.21 = (bf16[3,4,128,128]{3,2,1,0:T(8,128)(2,1)}, bf16[3,4,128,128]{3,2,1,0:T(8,128)(2,1)S(1)}, u32[]{:S(2)}, u32[]{:S(2)}) collective-permute-start(bf16[3,4,128,128]{3,2,1,0:T(8,128)(2,1)} %get-tuple-element.76), channel_id=1, source_target_pairs={{0,4},{1,5},{2,6},{3,7},{4,0},{5,1},{6,2},{7,3},{8,12},{9,13},{10,... | collective-permute-start | bytes 1179656 | tf_op jit(solution)/shard_map/ppermute | solution.py:383
  249.3 82.2 %collective-permute-start.22 = (bf16[3,4,128,128]{3,2,1,0:T(8,128)(2,1)}, bf16[3,4,128,128]{3,2,1,0:T(8,128)(2,1)S(1)}, u32[]{:S(2)}, u32[]{:S(2)}) collective-permute-start(bf16[3,4,128,128]{3,2,1,0:T(8,128)(2,1)} %get-tuple-element.75), channel_id=1, source_target_pairs={{0,5},{1,4},{2,7},{3,6},{4,1},{5,0},{6,3},{7,2},{8,13},{9,12},{10,... | collective-permute-start | bytes 1179656 | tf_op jit(solution)/shard_map/ppermute | solution.py:383
  249.3 82.2 %collective-permute-start.23 = (bf16[3,4,128,128]{3,2,1,0:T(8,128)(2,1)}, bf16[3,4,128,128]{3,2,1,0:T(8,128)(2,1)S(1)}, u32[]{:S(2)}, u32[]{:S(2)}) collective-permute-start(bf16[3,4,128,128]{3,2,1,0:T(8,128)(2,1)} %get-tuple-element.74), channel_id=1, source_target_pairs={{0,6},{1,7},{2,4},{3,5},{4,2},{5,3},{6,0},{7,1},{8,14},{9,15},{10,... | collective-permute-start | bytes 1179656 | tf_op jit(solution)/shard_map/ppermute | solution.py:383
  262.8 68.8 %collective-permute-start.24 = (bf16[3,4,128,128]{3,2,1,0:T(8,128)(2,1)}, bf16[3,4,128,128]{3,2,1,0:T(8,128)(2,1)S(1)}, u32[]{:S(2)}, u32[]{:S(2)}) collective-permute-start(bf16[3,4,128,128]{3,2,1,0:T(8,128)(2,1)} %get-tuple-element.73), channel_id=1, source_target_pairs={{0,7},{1,6},{2,5},{3,4},{4,3},{5,2},{6,1},{7,0},{8,15},{9,14},{10,... | collective-permute-start | bytes 1179656 | tf_op jit(solution)/shard_map/ppermute | solution.py:383
  341.8 51.6 %collective-permute-start.25 = (bf16[1,4,128,128]{3,2,1,0:T(8,128)(2,1)S(1)}, bf16[1,4,128,128]{3,2,1,0:T(8,128)(2,1)S(1)}, u32[]{:S(2)}, u32[]{:S(2)}) collective-permute-start(bf16[1,4,128,128]{3,2,1,0:T(8,128)(2,1)S(1)} %get-tuple-element.106), channel_id=1, source_target_pairs={{0,1},{1,0},{2,3},{3,2},{4,5},{5,4},{6,7},{7,6},{8,9},{9,8},{10,11... | collective-permute-start | bytes 393224 | tf_op jit(solution)/shard_map/ppermute | solution.py:383
  344.2 51.5 %collective-permute-start.26 = (bf16[1,4,128,128]{3,2,1,0:T(8,128)(2,1)S(1)}, bf16[1,4,128,128]{3,2,1,0:T(8,128)(2,1)S(1)}, u32[]{:S(2)}, u32[]{:S(2)}) collective-permute-start(bf16[1,4,128,128]{3,2,1,0:T(8,128)(2,1)S(1)} %get-tuple-element.105), channel_id=1, source_target_pairs={{0,2},{1,3},{2,0},{3,1},{4,6},{5,7},{6,4},{7,5},{8,10},{9,11},{10,... | collective-permute-start | bytes 393224 | tf_op jit(solution)/shard_map/ppermute | solution.py:383
  391.9 23.9 %collective-permute-start.29 = (bf16[1,4,128,128]{3,2,1,0:T(8,128)(2,1)}, bf16[1,4,128,128]{3,2,1,0:T(8,128)(2,1)}, u32[]{:S(2)}, u32[]{:S(2)}) collective-permute-start(bf16[1,4,128,128]{3,2,1,0:T(8,128)(2,1)} %get-tuple-element.102), channel_id=1, source_target_pairs={{0,5},{1,4},{2,7},{3,6},{4,1},{5,0},{6,3},{7,2},{8,13},{9,12},{10,... | collective-permute-start | bytes 393224 | tf_op jit(solution)/shard_map/ppermute | solution.py:383
  393.4 22.5 %collective-permute-start.30 = (bf16[1,4,128,128]{3,2,1,0:T(8,128)(2,1)}, bf16[1,4,128,128]{3,2,1,0:T(8,128)(2,1)}, u32[]{:S(2)}, u32[]{:S(2)}) collective-permute-start(bf16[1,4,128,128]{3,2,1,0:T(8,128)(2,1)} %get-tuple-element.101), channel_id=1, source_target_pairs={{0,6},{1,7},{2,4},{3,5},{4,2},{5,3},{6,0},{7,1},{8,14},{9,15},{10,... | collective-permute-start | bytes 393224 | tf_op jit(solution)/shard_map/ppermute | solution.py:383
  395.7 22.5 %collective-permute-start.31 = (bf16[1,4,128,128]{3,2,1,0:T(8,128)(2,1)}, bf16[1,4,128,128]{3,2,1,0:T(8,128)(2,1)}, u32[]{:S(2)}, u32[]{:S(2)}) collective-permute-start(bf16[1,4,128,128]{3,2,1,0:T(8,128)(2,1)} %get-tuple-element.100), channel_id=1, source_target_pairs={{0,7},{1,6},{2,5},{3,4},{4,3},{5,2},{6,1},{7,0},{8,15},{9,14},{10,... | collective-permute-start | bytes 393224 | tf_op jit(solution)/shard_map/ppermute | solution.py:383
  436.3 25.5 %collective-permute-start.34 = (bf16[256,2048]{1,0:T(8,128)(2,1)}, bf16[256,2048]{1,0:T(8,128)(2,1)}, u32[]{:S(2)}, u32[]{:S(2)}) collective-permute-start(bf16[256,2048]{1,0:T(8,128)(2,1)} %add_convert_fusion.5), channel_id=1, source_target_pairs={{0,16},{8,24},{16,0},{24,8},{1,17},{9,25},{17,1},{25,9},{2,18},{10... | collective-permute-start | bytes 3145736 | tf_op jit(solution)/shard_map/ppermute | solution.py:383
  465.5 26.2 %collective-permute-start.36 = (bf16[256,2048]{1,0:T(8,128)(2,1)S(1)}, bf16[256,2048]{1,0:T(8,128)(2,1)S(1)}, u32[]{:S(2)}, u32[]{:S(2)}) collective-permute-start(bf16[256,2048]{1,0:T(8,128)(2,1)S(1)} %add_convert_fusion.4), channel_id=1, source_target_pairs={{0,16},{8,24},{16,0},{24,8},{1,17},{9,25},{17,1},{25,9},{2,18},{10... | collective-permute-start | bytes 3145736 | tf_op jit(solution)/shard_map/ppermute | solution.py:383
  466.7 45.8 %collective-permute-start.42 = (bf16[256,2048]{1,0:T(8,128)(2,1)S(1)}, bf16[256,2048]{1,0:T(8,128)(2,1)S(1)}, u32[]{:S(2)}, u32[]{:S(2)}) collective-permute-start(bf16[256,2048]{1,0:T(8,128)(2,1)S(1)} %bitcast.287), channel_id=1, source_target_pairs={{0,16},{8,24},{16,0},{24,8},{1,17},{9,25},{17,1},{25,9},{2,18},{10... | collective-permute-start | bytes 3145736 | tf_op jit(solution)/shard_map/ppermute | solution.py:383
  467.6 45.5 %collective-permute-start.35 = (bf16[256,2048]{1,0:T(8,128)(2,1)S(1)}, bf16[256,2048]{1,0:T(8,128)(2,1)S(1)}, u32[]{:S(2)}, u32[]{:S(2)}) collective-permute-start(bf16[256,2048]{1,0:T(8,128)(2,1)S(1)} %add_convert_fusion.4), channel_id=1, source_target_pairs={{0,8},{8,0},{16,24},{24,16},{1,9},{9,1},{17,25},{25,17},{2,10},{10... | collective-permute-start | bytes 3145736 | tf_op jit(solution)/shard_map/ppermute | solution.py:383
  491.7 21.4 %collective-permute-start.37 = (bf16[256,2048]{1,0:T(8,128)(2,1)S(1)}, bf16[256,2048]{1,0:T(8,128)(2,1)S(1)}, u32[]{:S(2)}, u32[]{:S(2)}) collective-permute-start(bf16[256,2048]{1,0:T(8,128)(2,1)S(1)} %collective-permute-done.36), channel_id=1, source_target_pairs={{0,8},{8,0},{16,24},{24,16},{1,9},{9,1},{17,25},{25,17},{2,10},{10... | collective-permute-start | bytes 3145736 | tf_op jit(solution)/shard_map/ppermute | solution.py:383
  491.7 24.0 %collective-permute-start.41 = (bf16[256,2048]{1,0:T(8,128)(2,1)S(1)}, bf16[256,2048]{1,0:T(8,128)(2,1)S(1)}, u32[]{:S(2)}, u32[]{:S(2)}) collective-permute-start(bf16[256,2048]{1,0:T(8,128)(2,1)S(1)} %bitcast.288), channel_id=1, source_target_pairs={{0,8},{8,0},{16,24},{24,16},{1,9},{9,1},{17,25},{25,17},{2,10},{10... | collective-permute-start | bytes 3145736 | tf_op jit(solution)/shard_map/ppermute | solution.py:383
  564.9 499.6 %reduce-scatter.4.cloned.1.call-start = ((), (), s32[]{:S(2)}) async-start(), calls=%async_computation.6 | async-start | bytes 2359296 | tf_op jit(solution)/shard_map/reduce_scatter | solution.py:525
  596.5 26.3 %collective-permute-start.49 = (bf16[256,2048]{1,0:T(8,128)(2,1)}, bf16[256,2048]{1,0:T(8,128)(2,1)}, u32[]{:S(2)}, u32[]{:S(2)}) collective-permute-start(bf16[256,2048]{1,0:T(8,128)(2,1)} %add_convert_fusion.1), channel_id=1, source_target_pairs={{0,16},{8,24},{16,0},{24,8},{1,17},{9,25},{17,1},{25,9},{2,18},{10... | collective-permute-start | bytes 3145736 | tf_op jit(solution)/shard_map/ppermute | solution.py:383
  597.1 29.2 %collective-permute-start.44 = (bf16[256,2048]{1,0:T(8,128)(2,1)}, bf16[256,2048]{1,0:T(8,128)(2,1)}, u32[]{:S(2)}, u32[]{:S(2)}) collective-permute-start(bf16[256,2048]{1,0:T(8,128)(2,1)} %get-tuple-element.61), channel_id=1, source_target_pairs={{0,8},{8,0},{16,24},{24,16},{1,9},{9,1},{17,25},{25,17},{2,10},{10... | collective-permute-start | bytes 3145736 | tf_op jit(solution)/shard_map/ppermute | solution.py:383
  599.9 44.9 %collective-permute-start.46 = (bf16[256,2048]{1,0:T(8,128)(2,1)}, bf16[256,2048]{1,0:T(8,128)(2,1)}, u32[]{:S(2)}, u32[]{:S(2)}) collective-permute-start(bf16[256,2048]{1,0:T(8,128)(2,1)} %add_convert_fusion.3), channel_id=1, source_target_pairs={{0,16},{8,24},{16,0},{24,8},{1,17},{9,25},{17,1},{25,9},{2,18},{10... | collective-permute-start | bytes 3145736 | tf_op jit(solution)/shard_map/ppermute | solution.py:383
  651.9 24.8 %collective-permute-start.51 = (bf16[256,2048]{1,0:T(8,128)(2,1)S(1)}, bf16[256,2048]{1,0:T(8,128)(2,1)S(1)}, u32[]{:S(2)}, u32[]{:S(2)}) collective-permute-start(bf16[256,2048]{1,0:T(8,128)(2,1)S(1)} %get-tuple-element.44), channel_id=1, source_target_pairs={{0,16},{8,24},{16,0},{24,8},{1,17},{9,25},{17,1},{25,9},{2,18},{10... | collective-permute-start | bytes 3145736 | tf_op jit(solution)/shard_map/ppermute | solution.py:383
  652.7 24.1 %collective-permute-start.50 = (bf16[256,2048]{1,0:T(8,128)(2,1)S(1)}, bf16[256,2048]{1,0:T(8,128)(2,1)S(1)}, u32[]{:S(2)}, u32[]{:S(2)}) collective-permute-start(bf16[256,2048]{1,0:T(8,128)(2,1)S(1)} %get-tuple-element.44), channel_id=1, source_target_pairs={{0,8},{8,0},{16,24},{24,16},{1,9},{9,1},{17,25},{25,17},{2,10},{10... | collective-permute-start | bytes 3145736 | tf_op jit(solution)/shard_map/ppermute | solution.py:383
  684.2 383.1 %reduce-scatter.8.cloned.1.call-start = ((), (), s32[]{:S(2)}) async-start(), calls=%async_computation.8 | async-start | bytes 9437184 | tf_op jit(solution)/shard_map/reduce_scatter | solution.py:525
  719.2 18.5 %collective-permute-start.56 = (bf16[1,4,128,128]{3,2,1,0:T(8,128)(2,1)S(1)}, bf16[1,4,128,128]{3,2,1,0:T(8,128)(2,1)S(1)}, u32[]{:S(2)}, u32[]{:S(2)}) collective-permute-start(bf16[1,4,128,128]{3,2,1,0:T(8,128)(2,1)S(1)} %get-tuple-element.91), channel_id=1, source_target_pairs={{0,4},{1,5},{2,6},{3,7},{4,0},{5,1},{6,2},{7,3},{8,12},{9,13},{10,... | collective-permute-start | bytes 393224 | tf_op jit(solution)/shard_map/ppermute | solution.py:383
  721.1 23.2 %collective-permute-start.57 = (bf16[1,4,128,128]{3,2,1,0:T(8,128)(2,1)S(1)}, bf16[1,4,128,128]{3,2,1,0:T(8,128)(2,1)S(1)}, u32[]{:S(2)}, u32[]{:S(2)}) collective-permute-start(bf16[1,4,128,128]{3,2,1,0:T(8,128)(2,1)S(1)} %get-tuple-element.90), channel_id=1, source_target_pairs={{0,5},{1,4},{2,7},{3,6},{4,1},{5,0},{6,3},{7,2},{8,13},{9,12},{10,... | collective-permute-start | bytes 393224 | tf_op jit(solution)/shard_map/ppermute | solution.py:383
  722.1 22.2 %collective-permute-start.58 = (bf16[1,4,128,128]{3,2,1,0:T(8,128)(2,1)S(1)}, bf16[1,4,128,128]{3,2,1,0:T(8,128)(2,1)S(1)}, u32[]{:S(2)}, u32[]{:S(2)}) collective-permute-start(bf16[1,4,128,128]{3,2,1,0:T(8,128)(2,1)S(1)} %get-tuple-element.89), channel_id=1, source_target_pairs={{0,6},{1,7},{2,4},{3,5},{4,2},{5,3},{6,0},{7,1},{8,14},{9,15},{10,... | collective-permute-start | bytes 393224 | tf_op jit(solution)/shard_map/ppermute | solution.py:383
  725.1 19.2 %collective-permute-start.59 = (bf16[1,4,128,128]{3,2,1,0:T(8,128)(2,1)S(1)}, bf16[1,4,128,128]{3,2,1,0:T(8,128)(2,1)S(1)}, u32[]{:S(2)}, u32[]{:S(2)}) collective-permute-start(bf16[1,4,128,128]{3,2,1,0:T(8,128)(2,1)S(1)} %get-tuple-element.88), channel_id=1, source_target_pairs={{0,7},{1,6},{2,5},{3,4},{4,3},{5,2},{6,1},{7,0},{8,15},{9,14},{10,... | collective-permute-start | bytes 393224 | tf_op jit(solution)/shard_map/ppermute | solution.py:383
  765.6 22.6 %collective-permute-start.60 = (bf16[3,4,128,128]{3,2,1,0:T(8,128)(2,1)S(1)}, bf16[3,4,128,128]{3,2,1,0:T(8,128)(2,1)S(1)}, u32[]{:S(2)}, u32[]{:S(2)}) collective-permute-start(bf16[3,4,128,128]{3,2,1,0:T(8,128)(2,1)S(1)} %get-tuple-element.71), channel_id=1, source_target_pairs={{0,1},{1,0},{2,3},{3,2},{4,5},{5,4},{6,7},{7,6},{8,9},{9,8},{10,11... | collective-permute-start | bytes 1179656 | tf_op jit(solution)/shard_map/ppermute | solution.py:383
  769.5 43.7 %collective-permute-start.61 = (bf16[3,4,128,128]{3,2,1,0:T(8,128)(2,1)S(1)}, bf16[3,4,128,128]{3,2,1,0:T(8,128)(2,1)S(1)}, u32[]{:S(2)}, u32[]{:S(2)}) collective-permute-start(bf16[3,4,128,128]{3,2,1,0:T(8,128)(2,1)S(1)} %get-tuple-element.70), channel_id=1, source_target_pairs={{0,2},{1,3},{2,0},{3,1},{4,6},{5,7},{6,4},{7,5},{8,10},{9,11},{10,... | collective-permute-start | bytes 1179656 | tf_op jit(solution)/shard_map/ppermute | solution.py:383
  784.4 33.6 %collective-permute-start.62 = (bf16[3,4,128,128]{3,2,1,0:T(8,128)(2,1)}, bf16[3,4,128,128]{3,2,1,0:T(8,128)(2,1)S(1)}, u32[]{:S(2)}, u32[]{:S(2)}) collective-permute-start(bf16[3,4,128,128]{3,2,1,0:T(8,128)(2,1)} %get-tuple-element.69), channel_id=1, source_target_pairs={{0,3},{1,2},{2,1},{3,0},{4,7},{5,6},{6,5},{7,4},{8,11},{9,10},{10,... | collective-permute-start | bytes 1179656 | tf_op jit(solution)/shard_map/ppermute | solution.py:383
  784.4 33.7 %collective-permute-start.63 = (bf16[3,4,128,128]{3,2,1,0:T(8,128)(2,1)}, bf16[3,4,128,128]{3,2,1,0:T(8,128)(2,1)S(1)}, u32[]{:S(2)}, u32[]{:S(2)}) collective-permute-start(bf16[3,4,128,128]{3,2,1,0:T(8,128)(2,1)} %get-tuple-element.68), channel_id=1, source_target_pairs={{0,4},{1,5},{2,6},{3,7},{4,0},{5,1},{6,2},{7,3},{8,12},{9,13},{10,... | collective-permute-start | bytes 1179656 | tf_op jit(solution)/shard_map/ppermute | solution.py:383
  785.2 80.7 %collective-permute-start.64 = (bf16[3,4,128,128]{3,2,1,0:T(8,128)(2,1)}, bf16[3,4,128,128]{3,2,1,0:T(8,128)(2,1)S(1)}, u32[]{:S(2)}, u32[]{:S(2)}) collective-permute-start(bf16[3,4,128,128]{3,2,1,0:T(8,128)(2,1)} %get-tuple-element.67), channel_id=1, source_target_pairs={{0,5},{1,4},{2,7},{3,6},{4,1},{5,0},{6,3},{7,2},{8,13},{9,12},{10,... | collective-permute-start | bytes 1179656 | tf_op jit(solution)/shard_map/ppermute | solution.py:383
  788.2 77.6 %collective-permute-start.65 = (bf16[3,4,128,128]{3,2,1,0:T(8,128)(2,1)}, bf16[3,4,128,128]{3,2,1,0:T(8,128)(2,1)S(1)}, u32[]{:S(2)}, u32[]{:S(2)}) collective-permute-start(bf16[3,4,128,128]{3,2,1,0:T(8,128)(2,1)} %get-tuple-element.66), channel_id=1, source_target_pairs={{0,6},{1,7},{2,4},{3,5},{4,2},{5,3},{6,0},{7,1},{8,14},{9,15},{10,... | collective-permute-start | bytes 1179656 | tf_op jit(solution)/shard_map/ppermute | solution.py:383
  813.2 52.7 %collective-permute-start.66 = (bf16[3,4,128,128]{3,2,1,0:T(8,128)(2,1)}, bf16[3,4,128,128]{3,2,1,0:T(8,128)(2,1)S(1)}, u32[]{:S(2)}, u32[]{:S(2)}) collective-permute-start(bf16[3,4,128,128]{3,2,1,0:T(8,128)(2,1)} %get-tuple-element.65), channel_id=1, source_target_pairs={{0,7},{1,6},{2,5},{3,4},{4,3},{5,2},{6,1},{7,0},{8,15},{9,14},{10,... | collective-permute-start | bytes 1179656 | tf_op jit(solution)/shard_map/ppermute | solution.py:383
  888.3 55.5 %collective-permute-start.75 = (bf16[4,64,1536]{2,1,0:T(8,128)(2,1)}, bf16[4,64,1536]{2,1,0:T(8,128)(2,1)}, u32[]{:S(2)}, u32[]{:S(2)}) collective-permute-start(bf16[4,64,1536]{2,1,0:T(8,128)(2,1)} %get-tuple-element.55), channel_id=1, source_target_pairs={{0,2},{2,4},{4,6},{6,7},{7,5},{5,3},{3,1},{1,0},{8,10},{10,12},{12... | collective-permute-start | bytes 2359304 | tf_op jit(solution)/shard_map/ppermute | solution.py:467
  936.2 29.4 %collective-permute-start.79 = (bf16[4,64,1536]{2,1,0:T(8,128)(2,1)}, bf16[4,64,1536]{2,1,0:T(8,128)(2,1)}, u32[]{:S(2)}, u32[]{:S(2)}) collective-permute-start(bf16[4,64,1536]{2,1,0:T(8,128)(2,1)} %get-tuple-element.56), channel_id=1, source_target_pairs={{0,1},{2,0},{4,2},{6,4},{7,6},{5,7},{3,5},{1,3},{8,9},{10,8},{12,1... | collective-permute-start | bytes 2359304 | tf_op jit(solution)/shard_map/ppermute | solution.py:467
  936.3 36.9 %collective-permute-start.67 = (bf16[256,2048]{1,0:T(8,128)(2,1)}, bf16[256,2048]{1,0:T(8,128)(2,1)S(1)}, u32[]{:S(2)}, u32[]{:S(2)}) collective-permute-start(bf16[256,2048]{1,0:T(8,128)(2,1)} %get-tuple-element.57), channel_id=1, source_target_pairs={{0,8},{8,0},{16,24},{24,16},{1,9},{9,1},{17,25},{25,17},{2,10},{10... | collective-permute-start | bytes 3145736 | tf_op jit(solution)/shard_map/ppermute | solution.py:383
  946.2 21.4 %collective-permute-start.76 = (bf16[4,64,1536]{2,1,0:T(8,128)(2,1)}, bf16[4,64,1536]{2,1,0:T(8,128)(2,1)}, u32[]{:S(2)}, u32[]{:S(2)}) collective-permute-start(bf16[4,64,1536]{2,1,0:T(8,128)(2,1)} %fusion.14), channel_id=1, source_target_pairs={{0,2},{2,4},{4,6},{6,7},{7,5},{5,3},{3,1},{1,0},{8,10},{10,12},{12... | collective-permute-start | bytes 2359304 | tf_op jit(solution)/shard_map/ppermute | solution.py:467
  951.3 21.9 %collective-permute-start.69 = (bf16[256,2048]{1,0:T(8,128)(2,1)}, bf16[256,2048]{1,0:T(8,128)(2,1)}, u32[]{:S(2)}, u32[]{:S(2)}) collective-permute-start(bf16[256,2048]{1,0:T(8,128)(2,1)} %add_convert_fusion), channel_id=1, source_target_pairs={{0,16},{8,24},{16,0},{24,8},{1,17},{9,25},{17,1},{25,9},{2,18},{10... | collective-permute-start | bytes 3145736 | tf_op jit(solution)/shard_map/ppermute | solution.py:383
  971.0 49.3 %collective-permute-start.77 = (bf16[4,64,1536]{2,1,0:T(8,128)(2,1)}, bf16[4,64,1536]{2,1,0:T(8,128)(2,1)}, u32[]{:S(2)}, u32[]{:S(2)}) collective-permute-start(bf16[4,64,1536]{2,1,0:T(8,128)(2,1)} %get-tuple-element.53), channel_id=1, source_target_pairs={{0,2},{2,4},{4,6},{6,7},{7,5},{5,3},{3,1},{1,0},{8,10},{10,12},{12... | collective-permute-start | bytes 2359304 | tf_op jit(solution)/shard_map/ppermute | solution.py:467
  971.0 53.1 %collective-permute-start.80 = (bf16[4,64,1536]{2,1,0:T(8,128)(2,1)}, bf16[4,64,1536]{2,1,0:T(8,128)(2,1)}, u32[]{:S(2)}, u32[]{:S(2)}) collective-permute-start(bf16[4,64,1536]{2,1,0:T(8,128)(2,1)} %get-tuple-element.54), channel_id=1, source_target_pairs={{0,1},{2,0},{4,2},{6,4},{7,6},{5,7},{3,5},{1,3},{8,9},{10,8},{12,1... | collective-permute-start | bytes 2359304 | tf_op jit(solution)/shard_map/ppermute | solution.py:467
  981.5 38.7 %collective-permute-start.72 = (f32[2,2,768]{2,1,0:T(2,128)S(1)}, f32[2,2,768]{2,1,0:T(2,128)S(1)}, u32[]{:S(2)}, u32[]{:S(2)}) collective-permute-start(f32[2,2,768]{2,1,0:T(2,128)S(1)} %fusion.25), channel_id=1, source_target_pairs={{0,4},{1,5},{2,6},{3,7},{4,0},{5,1},{6,2},{7,3},{8,12},{9,13},{10,... | collective-permute-start | bytes 36872 | tf_op jit(solution)/shard_map/ppermute | solution.py:383
  (98 other events, 1697.5 us)
Sparse Core Ops, SparseCore 0:
  10.1 52.3 all-gather.3
  64.7 169.0 all-gather.7
  236.0 195.6 all-gather.5
  565.1 155.8 reduce-scatter.5
  724.8 84.4 reduce-scatter.3
  813.1 211.9 reduce-scatter.7

commit v3 on v2

--- a/solution.py
+++ b/solution.py
@@ -437,14 +437,77 @@
     return parts[0].astype(f32) + near.astype(f32) + across.astype(f32)
 
 
-def narrow_swap(blocks):
+def hold(value, *events):
+    return lax.optimization_barrier((value,) + events)[0]
+
+
+def bit_of(axis, bits):
+    return (lax.axis_index(axis) & bits) > 0
+
+
+def in_order(relative):
+    swap = bit_of(NARROW, 1)
+    r = [
+        jnp.where(swap, relative[k ^ 1], relative[k]) for k in range(4)
+    ]
+    swap = bit_of(NARROW, 2)
+    return jnp.stack([jnp.where(swap, r[k ^ 2], r[k]) for k in range(4)])
+
+
+def narrow_swap(block_of):
     me = lax.axis_index(NARROW)
-    result = jnp.zeros_like(blocks)
-    for j in (3, 2, 1, 0):
-        block = at(blocks, me ^ j)
-        block = flip(block, NARROW, j) if j else block
-        result = lax.dynamic_update_slice_in_dim(result, block[None], me ^ j, 0)
-    return result
+    return in_order([
+        flip(block_of(me ^ j), NARROW, j) if j else block_of(me) for j in range(4)
+    ])
+
+
+def pair_swap(block_of):
+    me = lax.axis_index(WIDE) & 1
+    own, other = block_of(me), flip(block_of(1 - me), WIDE, 1)
+    high = me > 0
+    return jnp.stack([jnp.where(high, other, own), jnp.where(high, own, other)])
+
+
+def spread(own):
+    half = own.shape[1] // 2
+    over_y = flip(own, WIDE, 1)
+    over_x = flip(own, NARROW, 2)
+    both = jnp.concatenate(
+        [flip(over_y[:, :half], NARROW, 2), flip(over_x[:, half:], WIDE, 1)], axis=1
+    )
+    near = [own, over_x, over_y, both]
+    return jnp.concatenate(near + [flip(part, NARROW, 1) for part in near], axis=0)
+
+
+def fold(partial):
+    f32, bf16 = jnp.float32, jnp.bfloat16
+    parts = partial.reshape(8, -1, partial.shape[-1])
+    half = partial.shape[-1] // 2
+    both, over_y, over_x, own = [
+        parts[k].astype(f32) + flip(parts[4 + k], NARROW, 1).astype(f32) for k in (3, 2, 1, 0)
+    ]
+    both = both.astype(bf16)
+    first = flip(both[:, :half], WIDE, 1).astype(f32)
+    last = flip(both[:, half:], NARROW, 2).astype(f32)
+    over_x = jnp.concatenate([over_x[:, :half] + first, over_x[:, half:]], axis=1).astype(bf16)
+    over_y = jnp.concatenate([over_y[:, :half], over_y[:, half:] + last], axis=1).astype(bf16)
+    return own + flip(over_x, NARROW, 2).astype(f32) + flip(over_y, WIDE, 1).astype(f32)
+
+
+def columns(wide):
+    return [list(range(y, wide, 2)) for y in range(2)]
+
+
+def z_gather(shard, axis):
+    groups = columns(lax.axis_size(WIDE))
+    return lax.all_gather(shard, WIDE, axis=axis, tiled=True, axis_index_groups=groups)
+
+
+def z_scatter(full, axis):
+    groups = columns(lax.axis_size(WIDE))
+    return lax.psum_scatter(
+        full.astype(jnp.bfloat16), WIDE, scatter_dimension=axis, tiled=True, axis_index_groups=groups
+    )
 
 
 def ring_order(wide):
@@ -826,7 +889,10 @@
     head_dim = width // HEADS
     cols = heads * head_dim
     shard = width // (narrow * wide)
-    ff_local = up_weight.shape[1] // narrow
+    deep = wide // 2
+    ff_shard = up_bias.shape[0]
+    ff_local = ff_shard * deep
+    me_y = me_w & 1
 
     smalls = [
         attn_gain, attn_shift, out_bias, mlp_gain, mlp_shift, down_bias, query_bias, value_bias, up_bias
@@ -845,37 +911,50 @@
     mine = lax.dynamic_slice_in_dim(small, me_n * wide, wide, 0)
     qbias = mine[:, 6 * shard : 7 * shard].reshape(-1).astype(f32)
     vbias = mine[:, 7 * shard : 8 * shard].reshape(-1).astype(f32)
-    ubias = mine[:, 8 * shard : 8 * shard + ff_local // wide].reshape(-1).astype(f32)
+    ubias = mine[:, 8 * shard : 8 * shard + ff_shard].reshape(deep, 2, ff_shard)
+    ubias = at(ubias, me_y, 1).reshape(-1).astype(f32)
     qkv_bias = jnp.concatenate([qbias, jnp.zeros_like(qbias), vbias])
 
-    qkv_shard = jnp.stack([query_weight, key_weight, value_weight], axis=1)
-    qkv_shard = qkv_shard.reshape(shard, 3, narrow, cols).transpose(2, 0, 1, 3)
-    qkv_shard = narrow_swap(qkv_shard.reshape(narrow, shard, 3 * cols))
-    qkv_w = ring_gather(qkv_shard, 1).reshape(width, 3 * cols)
-    down_w = wide_gather(down_weight, 0)
-    up_shard = narrow_swap(up_weight.reshape(shard, narrow, ff_local).transpose(1, 0, 2))
-    up_w = wide_gather(up_shard, 1).reshape(width, ff_local)
+    def qkv_block(n):
+        return jnp.concatenate(
+            [
+                lax.dynamic_slice_in_dim(weight, n * cols, cols, 1)
+                for weight in (query_weight, key_weight, value_weight)
+            ],
+            axis=1,
+        )
+
+    qkv_w = ring_gather(narrow_swap(qkv_block), 1).reshape(width, 3 * cols)
     out_w = wide_gather(out_weight, 0)
 
     inputs = block_input.astype(f32).reshape(rows, width)
     first_norm = narrow_gather(normalize(inputs, gain_attn, shift_attn).astype(bf16))
+    cotan_own = cotangent.reshape(rows, width)
+    cotan = spread(hold(cotan_own, first_norm))
+
+    down_w = z_gather(hold(down_weight, qkv_w), 0)
+    up_cols = hold(up_weight, first_norm).reshape(shard, narrow, deep, 2, ff_shard)
+    up_shard = pair_swap(lambda y: at(up_cols, y, 3).reshape(shard, narrow, ff_local))
+    up_pair = up_shard
+    up_shard = narrow_swap(lambda n: at(up_pair, n, 2))
+    up_shard = up_shard.reshape(narrow, 2 * shard, ff_local)
+    up_w = z_gather(hold(up_shard, qkv_w), 1).reshape(width, ff_local)
+
     sent = project(me, first_norm, qkv_w, qkv_bias, wide, 3, heads, tokens, False)
     qkv = wide_swap(sent)
     unit_out, lse = attend_fwd(me, segc, segr, qkv)
     partial, mixed = unproject(me, wide_swap(unit_out), out_w, heads, False)
     middle = inputs + narrow_scatter(partial) + obias
 
-    cotan_own = cotangent.reshape(rows, width)
-    cotan = narrow_gather(cotan_own)
     hidden_grad = times_transpose(cotan, down_w)
-    second_norm = narrow_gather(normalize(middle, gain_mlp, shift_mlp).astype(bf16))
+    second_norm = spread(normalize(middle, gain_mlp, shift_mlp).astype(bf16))
     hidden, inner_grad, ubias_grad = feed_forward(second_norm, up_w, ubias, hidden_grad)
-    second_grad = narrow_scatter(times_transpose(inner_grad, up_w).astype(bf16))
-    output = middle + narrow_scatter(matmul(hidden, down_w).astype(bf16)) + dbias
-    block_output = output.astype(bf16).reshape(batch, tokens, width)
-    down_grad = wide_scatter(outer_sum(hidden, cotan), 0)
-    up_grad = outer_sum(second_norm, inner_grad).reshape(narrow, wide * shard, ff_local)
-    up_grad = narrow_swap(wide_scatter(up_grad, 1)).transpose(1, 0, 2).reshape(shard, -1)
+    second_part = times_transpose(inner_grad, up_w).astype(bf16)
+    second_grad = fold(second_part)
+    hidden_late = hold(hidden, second_part)
+    down_grad = z_scatter(outer_sum(hidden_late, cotan), 0)
+    up_grad = outer_sum(second_norm, hold(inner_grad, second_part))
+    up_grad = z_scatter(up_grad.reshape(narrow, 2 * deep * shard, ff_local), 1)
     mlp_pull = jax.vjp(normalize, middle, gain_mlp, shift_mlp)[1]
     middle_part, mgain_grad, mshift_grad = mlp_pull(second_grad)
     dbias_grad = jnp.sum(cotan_own.astype(f32), axis=0)
@@ -887,12 +966,21 @@
     no_bias = jnp.zeros((cols,), f32)
     sent = project(me, branch, out_w, no_bias, wide, 1, heads, tokens, True)
     unit_grads = attend_bwd(me, segc, segr, lse, qkv, wide_swap(sent))
-    out_grad = wide_scatter(outer_sum(mixed, branch), 0)
+    out_grad = wide_scatter(outer_sum(mixed, hold(branch, sent)), 0)
+    output = middle + fold(matmul(hold(hidden, unit_grads), down_w).astype(bf16)) + dbias
+    block_output = output.astype(bf16).reshape(batch, tokens, width)
+    up_grad = up_grad.reshape(narrow, 2, shard, ff_local)
+    up_rows = up_grad
+    up_swapped = narrow_swap(lambda n: at(up_rows, n))
+    up_back = pair_swap(lambda y: at(up_swapped, y, 1))
+    up_back = up_back.reshape(2, narrow, shard, deep, ff_shard).transpose(2, 1, 3, 0, 4)
+    up_back = up_back.reshape(shard, -1)
     partial, back = unproject(me, wide_swap(unit_grads), qkv_w, heads, True)
     first_grad = narrow_scatter(partial)
     qkv_grad = outer_sum(first_norm, back).astype(bf16).reshape(narrow, wide, shard, 3 * cols)
-    qkv_grad = narrow_swap(ring_scatter(qkv_grad, 1).astype(bf16))
-    qkv_grad = qkv_grad.reshape(narrow, shard, 3, cols)
+    qkv_grad = ring_scatter(qkv_grad, 1).astype(bf16)
+    qkv_rows = qkv_grad
+    qkv_grad = narrow_swap(lambda n: at(qkv_rows, n)).reshape(narrow, shard, 3, cols)
     qkv_grad = qkv_grad.transpose(2, 1, 0, 3).reshape(3, shard, width).astype(f32)
     back_sums = jnp.sum(back.astype(f32), axis=0)
     attn_pull = jax.vjp(normalize, inputs, gain_attn, shift_attn)[1]
@@ -901,7 +989,11 @@
 
     fulls = [again_grad, ashift_grad, obias_grad, mgain_grad, mshift_grad, dbias_grad]
     fulls = jnp.concatenate([v.reshape(narrow * wide, shard) for v in fulls], axis=1)
-    slices = [back_sums[:cols], back_sums[2 * cols :], ubias_grad]
+    ubias_rows = jnp.zeros((deep, 2, ff_shard), f32)
+    ubias_rows = lax.dynamic_update_slice_in_dim(
+        ubias_rows, ubias_grad.reshape(deep, 1, ff_shard), me_y, 1
+    )
+    slices = [back_sums[:cols], back_sums[2 * cols :], ubias_rows]
     slices = jnp.concatenate([v.reshape(wide, -1) for v in slices], axis=1)
     placed = jnp.zeros((narrow * wide, slices.shape[1]), f32)
     placed = lax.dynamic_update_slice_in_dim(placed, slices, me_n * wide, 0)
@@ -924,7 +1016,7 @@
         vector(2),
         vector(3),
         vector(4),
-        up_grad.astype(f32),
+        up_back.astype(f32),
         vectors[8 * shard :],
         down_grad.astype(f32),
         vector(5),

time: 1090 us -> 985 us (0.904)
  waiting for transfers between devices: 517 us -> 404 us
  starting transfers between devices: 253 us -> 200 us
  local copies, waits for them, and re-layouts: 79.1 us -> 117 us
  other arithmetic: 59.6 us -> 78 us
    ppermute x74 -> x96, waiting for transfers between devices: 394 us -> 312 us  [flip(): return lax.ppermute(value, axis, [(i, i ^ bits) for i in range(size)])]
    ppermute x14, starting transfers between devices: 85 us -> 13.9 us  [ring_step(): lax.ppermute(value, WIDE, [(order[i], order[(i + by) % size]) for i in ra...]
    ppermute x14, waiting for transfers between devices: 121 us -> 91.8 us  [ring_step(): lax.ppermute(value, WIDE, [(order[i], order[(i + by) % size]) for i in ra...]
    ppermute x74 -> x96, starting transfers between devices: 168 us -> 186 us  [flip(): return lax.ppermute(value, axis, [(i, i ^ bits) for i in range(size)])]
    unnamed x143 -> x120, local copies, waits for them, and re-layouts: 17 us -> 28.9 us
  transfers between devices with their start and end apart: 94 -> 116, of which waited for: 46 -> 48; matrix products, arithmetic and copies ran while one was open for 18% -> 24% of each run, Pallas kernels for 6% -> 6%
where the time goes in v3:
time: 985 us; the launch traced here: 979 us
  waiting for transfers between devices  404 us (41%)
  starting transfers between devices  200 us (20%)
  local copies, waits for them, and re-layouts  117 us (12%)
  matrix products  82.9 us (8%)
  Pallas kernels  80.9 us (8%)
  other arithmetic  78 us (8%)
  between operations  15.6 us (2%)
    ppermute x96, waiting for transfers between devices, flip(): return lax.ppermute(value, axis, [(i, i ^ bits) for i in range(size)])  312 us
    ppermute x96, starting transfers between devices, flip(): return lax.ppermute(value, axis, [(i, i ^ bits) for i in range(size)])  186 us
    ppermute x14, waiting for transfers between devices, ring_step(): lax.ppermute(value, WIDE, [(order[i], order[(i + by) % size]) for i in ra...  91.8 us
    dot_general x4, matrix products, outer_sum(): lax.dot_general(left, right, (((0,), (0,)), ((), ())), preferred_element_...  43.9 us
    dot_general x2, matrix products, times_transpose(): lax.dot_general(left, right, (((1,), (1,)), ((), ())), preferred_element_...  29.6 us
    unnamed x120, local copies, waits for them, and re-layouts  28.9 us
    pallas_call x1, Pallas kernels, feed_forward(): pl.pallas_call(ff_kernel, grid=(inner // step,), out_shape=(jax.ShapeDtyp...  19.9 us
  transfers between devices with their start and end apart: 116, of which 48 were waited for; matrix products, arithmetic and copies ran while one was open for 24% of the time, Pallas kernels for 6%

profile of v3, /device:TPU:0, one launch (start us, length us, event | category | flops | bytes accessed | tf_op | source)
XLA Modules:
  0.0 979.2 jit_solution(17619435950448373165)
XLA Ops:
  8.7 6.1 concatenate.91
  46.4 21.6 %collective-permute-done.11 = bf16[4,64,1536]{2,1,0:T(8,128)(2,1)} collective-permute-done((bf16[4,64,1536]{2,1,0:T(8,128)(2,1)}, bf16[4,64,1536]{2,1,0:T(8,128)(2,1)}, u32[]{:S(2)}, u32[]{:S(2)}) %collective-permute-start.11) | collective-permute-done | bytes 786464 | tf_op jit(solution)/shard_map/ppermute | solution.py:530
  67.9 5.6 collective-permute-start.13
  78.5 12.1 %collective-permute-done.13 = bf16[4,64,1536]{2,1,0:T(8,128)(2,1)S(1)} collective-permute-done((bf16[4,64,1536]{2,1,0:T(8,128)(2,1)}, bf16[4,64,1536]{2,1,0:T(8,128)(2,1)S(1)}, u32[]{:S(2)}, u32[]{:S(2)}) %collective-permute-start.13) | collective-permute-done | bytes 786464 | tf_op jit(solution)/shard_map/ppermute | solution.py:530
  94.5 13.8 %collective-permute-done.15 = bf16[4,64,1536]{2,1,0:T(8,128)(2,1)S(1)} collective-permute-done((bf16[4,64,1536]{2,1,0:T(8,128)(2,1)S(1)}, bf16[4,64,1536]{2,1,0:T(8,128)(2,1)S(1)}, u32[]{:S(2)}, u32[]{:S(2)}) %collective-permute-start.15) | collective-permute-done | bytes 786464 | tf_op jit(solution)/shard_map/ppermute | solution.py:530
  110.6 14.0 %collective-permute-done.17 = bf16[4,64,1536]{2,1,0:T(8,128)(2,1)S(1)} collective-permute-done((bf16[4,64,1536]{2,1,0:T(8,128)(2,1)S(1)}, bf16[4,64,1536]{2,1,0:T(8,128)(2,1)S(1)}, u32[]{:S(2)}, u32[]{:S(2)}) %collective-permute-start.17) | collective-permute-done | bytes 786464 | tf_op jit(solution)/shard_map/ppermute | solution.py:530
  126.2 3.7 pad_maximum_fusion.rows_ref
  129.9 10.9 %project.2 = bf16[8,3,4,128,128]{4,3,2,1,0:T(8,128)(2,1)S(1)} custom-call(s32[2]{0:T(128)S(1)} %pad_add_fusion.me_ref, bf16[1024,2048]{1,0:T(8,128)(2,1)} %pad_maximum_fusion.rows_ref, bf16[2048,1536]{1,0:T(8,128)(2,1)} %bitcast.27.weight_ref.refs_8_, f32[1,1536]{1,0:T(1,128)S(1)} %reshape.416.bias_ref), custom_call_target="tpu_custom_call" | custom-call | tf_op jit(solution)/shard_map/project/pallas_call | solution.py:622
  142.2 3.9 collective-permute-start.24
  155.0 10.2 %collective-permute-done.24.refs_7_ = bf16[3,4,128,128]{3,2,1,0:T(8,128)(2,1)S(1)} collective-permute-done((bf16[3,4,128,128]{3,2,1,0:T(8,128)(2,1)S(1)}, bf16[3,4,128,128]{3,2,1,0:T(8,128)(2,1)S(1)}, u32[]{:S(2)}, u32[]{:S(2)}) %collective-permute-start.24) | collective-permute-done | bytes 393248 | tf_op jit(solution)/shard_map/ppermute | solution.py:383
  165.2 46.9 %collective-permute-start.19 = (bf16[3,4,128,128]{3,2,1,0:T(8,128)(2,1)}, bf16[3,4,128,128]{3,2,1,0:T(8,128)(2,1)S(1)}, u32[]{:S(2)}, u32[]{:S(2)}) collective-permute-start(bf16[3,4,128,128]{3,2,1,0:T(8,128)(2,1)} %get-tuple-element.109), channel_id=1, source_target_pairs={{0,2},{1,3},{2,0},{3,1},{4,6},{5,7},{6,4},{7,5},{8,10},{9,11},{10,... | collective-permute-start | bytes 1179656 | tf_op jit(solution)/shard_map/ppermute | solution.py:383
  212.7 47.7 %collective-permute-done.22.refs_5_ = bf16[3,4,128,128]{3,2,1,0:T(8,128)(2,1)S(1)} collective-permute-done((bf16[3,4,128,128]{3,2,1,0:T(8,128)(2,1)}, bf16[3,4,128,128]{3,2,1,0:T(8,128)(2,1)S(1)}, u32[]{:S(2)}, u32[]{:S(2)}) %collective-permute-start.22) | collective-permute-done | bytes 393248 | tf_op jit(solution)/shard_map/ppermute | solution.py:383
  260.4 13.0 %collective-permute-done.21.refs_4_ = bf16[3,4,128,128]{3,2,1,0:T(8,128)(2,1)S(1)} collective-permute-done((bf16[3,4,128,128]{3,2,1,0:T(8,128)(2,1)}, bf16[3,4,128,128]{3,2,1,0:T(8,128)(2,1)S(1)}, u32[]{:S(2)}, u32[]{:S(2)}) %collective-permute-start.21) | collective-permute-done | bytes 393248 | tf_op jit(solution)/shard_map/ppermute | solution.py:383
  273.4 9.4 attend_fwd.1
  292.9 7.0 collective-permute-start.26
  310.1 5.7 unproject.2
  315.8 3.5 fusion.65
  319.4 7.3 dynamic-slice_reduce_fusion
  336.6 9.2 collective-permute-done.43
  352.5 11.4 %collective-permute-done.44 = bf16[2,64,1024]{2,1,0:T(8,128)(2,1)S(1)} collective-permute-done((bf16[2,64,1024]{2,1,0:T(8,128)(2,1)S(1)}, bf16[2,64,1024]{2,1,0:T(8,128)(2,1)S(1)}, u32[]{:S(2)}, u32[]{:S(2)}) %collective-permute-start.44) | collective-permute-done | bytes 262176 | tf_op jit(solution)/shard_map/ppermute | solution.py:383
  366.8 3.7 collective-permute-done.45
  380.3 12.9 %collective-permute-done.34 = bf16[256,2048]{1,0:T(8,128)(2,1)} collective-permute-done((bf16[256,2048]{1,0:T(8,128)(2,1)}, bf16[256,2048]{1,0:T(8,128)(2,1)}, u32[]{:S(2)}, u32[]{:S(2)}) %collective-permute-start.34) | collective-permute-done | bytes 1048608 | tf_op jit(solution)/shard_map/ppermute | solution.py:383
  397.9 5.4 collective-permute-done.49
  416.5 10.9 %collective-permute-done.36 = bf16[256,2048]{1,0:T(8,128)(2,1)S(1)} collective-permute-done((bf16[256,2048]{1,0:T(8,128)(2,1)S(1)}, bf16[256,2048]{1,0:T(8,128)(2,1)S(1)}, u32[]{:S(2)}, u32[]{:S(2)}) %collective-permute-start.36) | collective-permute-done | bytes 1048608 | tf_op jit(solution)/shard_map/ppermute | solution.py:383
  433.7 6.0 collective-permute-done.37
  448.5 14.7 %fusion.71.pull_ref = f32[2048,1024]{1,0:T(8,128)} fusion(bf16[2048,2048]{1,0:T(8,128)(2,1)} %constant_dynamic-update-slice_fusion.8, bf16[1024,2048]{1,0:T(8,128)(2,1)} %all-gather.8.cloned.1.call-done), kind=kOutput, calls=%fused_computation.315 | convolution fusion | flops 8589934592 | bytes 20971520 | tf_op jit(solution)/shard_map/dot_general | solution.py:56
  463.2 19.9 %feed_forward.1 = (bf16[2048,1024]{1,0:T(8,128)(2,1)S(1)}, bf16[2048,1024]{1,0:T(8,128)(2,1)}, f32[1,1024]{1,0:T(1,128)S(1)}) custom-call(bf16[2048,2048]{1,0:T(8,128)(2,1)} %constant_dynamic-update-slice_fusion.rows_ref, bf16[2048,1024]{1,0:T(8,128)(2,1)} %bitcast.316, f32[1,1024]{1,0:T(1,128)S(1)} %convert.56.bias_ref, f32[2048,1024]{1,0:T(8,128)} %fusion.71.pull_ref), custom_call_target="tpu_custom_call" | custom-call | tf_op jit(solution)/shard_map/feed_forward/pallas_call | solution.py:835
  483.1 15.0 %convolution_convert_fusion.2 = bf16[2048,2048]{1,0:T(8,128)(2,1)} fusion(bf16[2048,1024]{1,0:T(8,128)(2,1)} %get-tuple-element.49, bf16[2048,1024]{1,0:T(8,128)(2,1)S(1)} %bitcast.317), kind=kOutput, calls=%fused_computation.2 | convolution fusion | flops 8594128896 | bytes 16777216 | tf_op jit(solution)/shard_map/dot_general | solution.py:56
  498.1 13.3 %convolution_convert_fusion.4 = bf16[2048,1024]{1,0:T(8,128)(2,1)} fusion(bf16[2048,2048]{1,0:T(8,128)(2,1)} %constant_dynamic-update-slice_fusion.rows_ref, bf16[2048,1024]{1,0:T(8,128)(2,1)S(1)} %copy-done.50), kind=kOutput, calls=%fused_computation.7 | convolution fusion | flops 8592031744 | bytes 16777216 | tf_op jit(solution)/shard_map/dot_general | solution.py:50
  511.4 4.5 fusion.63
  517.0 13.3 %convolution_convert_fusion.3 = bf16[1024,2048]{1,0:T(8,128)(2,1)} fusion(bf16[2048,1024]{1,0:T(8,128)(2,1)S(1)} %copy-done.8, bf16[2048,2048]{1,0:T(8,128)(2,1)} %constant_dynamic-update-slice_fusion.8), kind=kOutput, calls=%fused_computation.6 | convolution fusion | flops 8592031744 | bytes 16777216 | tf_op jit(solution)/shard_map/dot_general | solution.py:50
  530.4 4.2 convert_add_fusion.5
  537.3 11.4 %collective-permute-done.61 = bf16[256,1024]{1,0:T(8,128)(2,1)S(1)} collective-permute-done((bf16[256,1024]{1,0:T(8,128)(2,1)S(1)}, bf16[256,1024]{1,0:T(8,128)(2,1)S(1)}, u32[]{:S(2)}, u32[]{:S(2)}) %collective-permute-start.61) | collective-permute-done | bytes 524320 | tf_op jit(solution)/shard_map/ppermute | solution.py:383
  551.8 21.8 %collective-permute-done.62 = bf16[256,2048]{1,0:T(8,128)(2,1)S(1)} collective-permute-done((bf16[256,2048]{1,0:T(8,128)(2,1)S(1)}, bf16[256,2048]{1,0:T(8,128)(2,1)S(1)}, u32[]{:S(2)}, u32[]{:S(2)}) %collective-permute-start.62) | collective-permute-done | bytes 1048608 | tf_op jit(solution)/shard_map/ppermute | solution.py:383
  579.1 3.9 convert_reduce_fusion.3
  584.3 23.0 %collective-permute-done.64 = bf16[256,2048]{1,0:T(8,128)(2,1)} collective-permute-done((bf16[256,2048]{1,0:T(8,128)(2,1)}, bf16[256,2048]{1,0:T(8,128)(2,1)}, u32[]{:S(2)}, u32[]{:S(2)}) %collective-permute-start.64) | collective-permute-done | bytes 1048608 | tf_op jit(solution)/shard_map/ppermute | solution.py:383
  610.3 3.8 pad_maximum_fusion.1.rows_ref
  614.1 5.1 project.3
  620.1 3.9 collective-permute-start.72
  641.4 4.9 collective-permute-start.67
  646.5 6.2 convolution_convert_fusion.5
  652.7 13.5 %collective-permute-done.70.refs_13_ = bf16[1,4,128,128]{3,2,1,0:T(8,128)(2,1)} collective-permute-done((bf16[1,4,128,128]{3,2,1,0:T(8,128)(2,1)}, bf16[1,4,128,128]{3,2,1,0:T(8,128)(2,1)}, u32[]{:S(2)}, u32[]{:S(2)}) %collective-permute-start.70) | collective-permute-done | bytes 131104 | tf_op jit(solution)/shard_map/ppermute | solution.py:383
  666.2 10.3 %collective-permute-done.69.refs_12_ = bf16[1,4,128,128]{3,2,1,0:T(8,128)(2,1)} collective-permute-done((bf16[1,4,128,128]{3,2,1,0:T(8,128)(2,1)}, bf16[1,4,128,128]{3,2,1,0:T(8,128)(2,1)}, u32[]{:S(2)}, u32[]{:S(2)}) %collective-permute-start.69) | collective-permute-done | bytes 131104 | tf_op jit(solution)/shard_map/ppermute | solution.py:383
  677.2 18.4 %attend_bwd.1 = bf16[8,3,4,128,128]{4,3,2,1,0:T(8,128)(2,1)} custom-call(s32[2]{0:T(128)S(1)} %copy-done.5, s32[8,512,1]{2,1,0:T(8,128)} %reshape.450.segc_ref, s32[1,4096]{1,0:T(1,128)S(1)} %convert_bitcast_fusion.2.segr_ref, f32[8,512,1]{2,1,0:T(8,128)} %get-tuple-element.41.lse_ref, bf16[3,4,128,128]{3,2,1,0:T(8,128)(2,1)S(1)} %get-tuple-element.111.refs_0_, ...), custom_call_target="tpu_custom_call" | custom-call | tf_op jit(solution)/shard_map/attend_bwd/pallas_call | solution.py:798
  698.0 4.2 collective-permute-start.87
  707.5 9.3 convolution_convert_fusion.1
  716.9 32.7 %collective-permute-start.82 = (bf16[3,4,128,128]{3,2,1,0:T(8,128)(2,1)S(1)}, bf16[3,4,128,128]{3,2,1,0:T(8,128)(2,1)S(1)}, u32[]{:S(2)}, u32[]{:S(2)}) collective-permute-start(bf16[3,4,128,128]{3,2,1,0:T(8,128)(2,1)S(1)} %get-tuple-element.101), channel_id=1, source_target_pairs={{0,2},{1,3},{2,0},{3,1},{4,6},{5,7},{6,4},{7,5},{8,10},{9,11},{10,... | collective-permute-start | bytes 1179656 | tf_op jit(solution)/shard_map/ppermute | solution.py:383
  749.6 3.4 collective-permute-start.81
  754.7 20.6 %collective-permute-done.85.refs_5_ = bf16[3,4,128,128]{3,2,1,0:T(8,128)(2,1)S(1)} collective-permute-done((bf16[3,4,128,128]{3,2,1,0:T(8,128)(2,1)S(1)}, bf16[3,4,128,128]{3,2,1,0:T(8,128)(2,1)S(1)}, u32[]{:S(2)}, u32[]{:S(2)}) %collective-permute-start.85) | collective-permute-done | bytes 393248 | tf_op jit(solution)/shard_map/ppermute | solution.py:383
  775.3 7.6 collective-permute-done.84.refs_4_
  783.5 11.5 %unproject.3 = (bf16[1024,2048]{1,0:T(8,128)(2,1)}, bf16[1024,1536]{1,0:T(8,128)(2,1)}) custom-call(s32[2]{0:T(128)S(1)} %copy-done.5, bf16[3,4,128,128]{3,2,1,0:T(8,128)(2,1)S(1)} %get-tuple-element.103.refs_0_, bf16[3,4,128,128]{3,2,1,0:T(8,128)(2,1)S(1)} %collective-permute-done.81.refs_1_, bf16[3,4,128,128]{3,2,1,0:T(8,128)(2,1)S(1)} %collective-permute-done.82.refs_2_, ...), custom_call_target="tpu_custom_call" | custom-call | tf_op jit(solution)/shard_map/unproject/pallas_call | solution.py:672
  797.8 11.1 %convolution_convert_fusion = bf16[2048,1536]{1,0:T(8,128)(2,1)} fusion(bf16[1024,1536]{1,0:T(8,128)(2,1)} %get-tuple-element.45, bf16[256,2048]{1,0:T(8,128)(2,1)S(1)} %copy-done.27, bf16[256,2048]{1,0:T(8,128)(2,1)S(1)} %copy-done.25, bf16[256,2048]{1,0:T(8,128)(2,1)} %collective-permute-done.5, bf16[256,2048]{1,0:T(8,128)(2,1)S(1)} %copy-done.23), kind=kOutput, calls=%fused_computation | convolution fusion | flops 6462373888 | bytes 13631488 | tf_op jit(solution)/shard_map/dot_general | solution.py:50
  815.8 3.7 convert_add_fusion.2
  819.8 11.7 %collective-permute-done.96 = bf16[4,64,1536]{2,1,0:T(8,128)(2,1)S(1)} collective-permute-done((bf16[4,64,1536]{2,1,0:T(8,128)(2,1)S(1)}, bf16[4,64,1536]{2,1,0:T(8,128)(2,1)S(1)}, u32[]{:S(2)}, u32[]{:S(2)}) %collective-permute-start.96) | collective-permute-done | bytes 786464 | tf_op jit(solution)/shard_map/ppermute | solution.py:530
  836.3 8.8 collective-permute-done.76
  853.4 16.9 %collective-permute-done.90 = bf16[256,2048]{1,0:T(8,128)(2,1)S(1)} collective-permute-done((bf16[256,2048]{1,0:T(8,128)(2,1)S(1)}, bf16[256,2048]{1,0:T(8,128)(2,1)S(1)}, u32[]{:S(2)}, u32[]{:S(2)}) %collective-permute-start.90) | collective-permute-done | bytes 1048608 | tf_op jit(solution)/shard_map/ppermute | solution.py:383
  881.5 10.1 %collective-permute-done.93 = f32[2,2,768]{2,1,0:T(2,128)S(1)} collective-permute-done((f32[2,2,768]{2,1,0:T(2,128)S(1)}, f32[2,2,768]{2,1,0:T(2,128)S(1)}, u32[]{:S(2)}, u32[]{:S(2)}) %collective-permute-start.93) | collective-permute-done | bytes 12320 | tf_op jit(solution)/shard_map/ppermute | solution.py:383
  896.8 4.0 collective-permute-start.95
  900.8 4.8 collective-permute-done.98
  917.0 8.1 collective-permute-done.101
  929.9 3.6 add_convert_fusion.1
  937.0 4.8 collective-permute-done.106
  945.4 4.3 collective-permute-done.102
  954.3 4.3 collective-permute-done.109
  (488 shorter events, 264.9 us)
Async XLA Ops:
  7.2 295.9 %all-gather.4.cloned.1.call-start = ((), (), s32[]{:S(2)}) async-start(), calls=%async_computation.3 | async-start | bytes 2359296 | tf_op jit(solution)/shard_map/all_gather | solution.py:584
  7.9 440.6 %all-gather.8.cloned.1.call-start = ((), (), s32[]{:S(2)}) async-start(), calls=%async_computation.5 | async-start | bytes 5242880 | tf_op jit(solution)/shard_map/all_gather | solution.py:503
  37.2 30.7 %collective-permute-start.11 = (bf16[4,64,1536]{2,1,0:T(8,128)(2,1)}, bf16[4,64,1536]{2,1,0:T(8,128)(2,1)}, u32[]{:S(2)}, u32[]{:S(2)}) collective-permute-start(bf16[4,64,1536]{2,1,0:T(8,128)(2,1)} %pad_maximum_fusion.10), channel_id=1, source_target_pairs={{0,2},{2,4},{4,6},{6,7},{7,5},{5,3},{3,1},{1,0},{8,10},{10,12},{12... | collective-permute-start | bytes 2359304 | tf_op jit(solution)/shard_map/ppermute | solution.py:530
  38.7 35.4 %collective-permute-start.12 = (bf16[4,64,1536]{2,1,0:T(8,128)(2,1)}, bf16[4,64,1536]{2,1,0:T(8,128)(2,1)}, u32[]{:S(2)}, u32[]{:S(2)}) collective-permute-start(bf16[4,64,1536]{2,1,0:T(8,128)(2,1)} %pad_maximum_fusion.10), channel_id=1, source_target_pairs={{0,1},{2,0},{4,2},{6,4},{7,6},{5,7},{3,5},{1,3},{8,9},{10,8},{12,1... | collective-permute-start | bytes 2359304 | tf_op jit(solution)/shard_map/ppermute | solution.py:530
  40.6 37.9 %collective-permute-start.6 = (bf16[256,2048]{1,0:T(8,128)(2,1)S(1)}, bf16[256,2048]{1,0:T(8,128)(2,1)S(1)}, u32[]{:S(2)}, u32[]{:S(2)}) collective-permute-start(bf16[256,2048]{1,0:T(8,128)(2,1)S(1)} %fusion.6), channel_id=1, source_target_pairs={{0,16},{8,24},{16,0},{24,8},{1,17},{9,25},{17,1},{25,9},{2,18},{10... | collective-permute-start | bytes 3145736 | tf_op jit(solution)/shard_map/ppermute | solution.py:383
  42.1 84.1 %collective-permute-start.5 = (bf16[256,2048]{1,0:T(8,128)(2,1)S(1)}, bf16[256,2048]{1,0:T(8,128)(2,1)}, u32[]{:S(2)}, u32[]{:S(2)}) collective-permute-start(bf16[256,2048]{1,0:T(8,128)(2,1)S(1)} %fusion.6), channel_id=1, source_target_pairs={{0,8},{8,0},{16,24},{24,16},{1,9},{9,1},{17,25},{25,17},{2,10},{10... | collective-permute-start | bytes 3145736 | tf_op jit(solution)/shard_map/ppermute | solution.py:383
  67.9 22.6 %collective-permute-start.13 = (bf16[4,64,1536]{2,1,0:T(8,128)(2,1)}, bf16[4,64,1536]{2,1,0:T(8,128)(2,1)S(1)}, u32[]{:S(2)}, u32[]{:S(2)}) collective-permute-start(bf16[4,64,1536]{2,1,0:T(8,128)(2,1)} %collective-permute-done.11), channel_id=1, source_target_pairs={{0,2},{2,4},{4,6},{6,7},{7,5},{5,3},{3,1},{1,0},{8,10},{10,12},{12... | collective-permute-start | bytes 2359304 | tf_op jit(solution)/shard_map/ppermute | solution.py:530
  78.5 47.7 %collective-permute-start.7 = (bf16[256,2048]{1,0:T(8,128)(2,1)S(1)}, bf16[256,2048]{1,0:T(8,128)(2,1)S(1)}, u32[]{:S(2)}, u32[]{:S(2)}) collective-permute-start(bf16[256,2048]{1,0:T(8,128)(2,1)S(1)} %collective-permute-done.6), channel_id=1, source_target_pairs={{0,8},{8,0},{16,24},{24,16},{1,9},{9,1},{17,25},{25,17},{2,10},{10... | collective-permute-start | bytes 3145736 | tf_op jit(solution)/shard_map/ppermute | solution.py:383
  125.6 337.6 %all-gather.6.cloned.1.call-start = ((), (), s32[]{:S(2)}) async-start(), calls=%async_computation.4 | async-start | bytes 5242880 | tf_op jit(solution)/shard_map/all_gather | solution.py:503
  142.2 23.1 %collective-permute-start.24 = (bf16[3,4,128,128]{3,2,1,0:T(8,128)(2,1)S(1)}, bf16[3,4,128,128]{3,2,1,0:T(8,128)(2,1)S(1)}, u32[]{:S(2)}, u32[]{:S(2)}) collective-permute-start(bf16[3,4,128,128]{3,2,1,0:T(8,128)(2,1)S(1)} %get-tuple-element.104), channel_id=1, source_target_pairs={{0,7},{1,6},{2,5},{3,4},{4,3},{5,2},{6,1},{7,0},{8,15},{9,14},{10,... | collective-permute-start | bytes 1179656 | tf_op jit(solution)/shard_map/ppermute | solution.py:383
  146.1 66.1 %collective-permute-start.23 = (bf16[3,4,128,128]{3,2,1,0:T(8,128)(2,1)S(1)}, bf16[3,4,128,128]{3,2,1,0:T(8,128)(2,1)S(1)}, u32[]{:S(2)}, u32[]{:S(2)}) collective-permute-start(bf16[3,4,128,128]{3,2,1,0:T(8,128)(2,1)S(1)} %get-tuple-element.105), channel_id=1, source_target_pairs={{0,6},{1,7},{2,4},{3,5},{4,2},{5,3},{6,0},{7,1},{8,14},{9,15},{10,... | collective-permute-start | bytes 1179656 | tf_op jit(solution)/shard_map/ppermute | solution.py:383
  150.1 110.3 %collective-permute-start.22 = (bf16[3,4,128,128]{3,2,1,0:T(8,128)(2,1)}, bf16[3,4,128,128]{3,2,1,0:T(8,128)(2,1)S(1)}, u32[]{:S(2)}, u32[]{:S(2)}) collective-permute-start(bf16[3,4,128,128]{3,2,1,0:T(8,128)(2,1)} %get-tuple-element.106), channel_id=1, source_target_pairs={{0,5},{1,4},{2,7},{3,6},{4,1},{5,0},{6,3},{7,2},{8,13},{9,12},{10,... | collective-permute-start | bytes 1179656 | tf_op jit(solution)/shard_map/ppermute | solution.py:383
  150.5 122.8 %collective-permute-start.21 = (bf16[3,4,128,128]{3,2,1,0:T(8,128)(2,1)}, bf16[3,4,128,128]{3,2,1,0:T(8,128)(2,1)S(1)}, u32[]{:S(2)}, u32[]{:S(2)}) collective-permute-start(bf16[3,4,128,128]{3,2,1,0:T(8,128)(2,1)} %get-tuple-element.107), channel_id=1, source_target_pairs={{0,4},{1,5},{2,6},{3,7},{4,0},{5,1},{6,2},{7,3},{8,12},{9,13},{10,... | collective-permute-start | bytes 1179656 | tf_op jit(solution)/shard_map/ppermute | solution.py:383
  153.5 119.8 %collective-permute-start.20 = (bf16[3,4,128,128]{3,2,1,0:T(8,128)(2,1)}, bf16[3,4,128,128]{3,2,1,0:T(8,128)(2,1)S(1)}, u32[]{:S(2)}, u32[]{:S(2)}) collective-permute-start(bf16[3,4,128,128]{3,2,1,0:T(8,128)(2,1)} %get-tuple-element.108), channel_id=1, source_target_pairs={{0,3},{1,2},{2,1},{3,0},{4,7},{5,6},{6,5},{7,4},{8,11},{9,10},{10,... | collective-permute-start | bytes 1179656 | tf_op jit(solution)/shard_map/ppermute | solution.py:383
  165.2 108.1 %collective-permute-start.19 = (bf16[3,4,128,128]{3,2,1,0:T(8,128)(2,1)}, bf16[3,4,128,128]{3,2,1,0:T(8,128)(2,1)S(1)}, u32[]{:S(2)}, u32[]{:S(2)}) collective-permute-start(bf16[3,4,128,128]{3,2,1,0:T(8,128)(2,1)} %get-tuple-element.109), channel_id=1, source_target_pairs={{0,2},{1,3},{2,0},{3,1},{4,6},{5,7},{6,4},{7,5},{8,10},{9,11},{10,... | collective-permute-start | bytes 1179656 | tf_op jit(solution)/shard_map/ppermute | solution.py:383
  212.1 61.2 %collective-permute-start.18 = (bf16[3,4,128,128]{3,2,1,0:T(8,128)(2,1)}, bf16[3,4,128,128]{3,2,1,0:T(8,128)(2,1)S(1)}, u32[]{:S(2)}, u32[]{:S(2)}) collective-permute-start(bf16[3,4,128,128]{3,2,1,0:T(8,128)(2,1)} %get-tuple-element.110), channel_id=1, source_target_pairs={{0,1},{1,0},{2,3},{3,2},{4,5},{5,4},{6,7},{7,6},{8,9},{9,8},{10,11... | collective-permute-start | bytes 1179656 | tf_op jit(solution)/shard_map/ppermute | solution.py:383
  319.3 29.8 %collective-permute-start.33 = (bf16[256,2048]{1,0:T(8,128)(2,1)}, bf16[256,2048]{1,0:T(8,128)(2,1)}, u32[]{:S(2)}, u32[]{:S(2)}) collective-permute-start(bf16[256,2048]{1,0:T(8,128)(2,1)} %get-tuple-element.95), channel_id=1, source_target_pairs={{0,8},{8,0},{16,24},{24,16},{1,9},{9,1},{17,25},{25,17},{2,10},{10... | collective-permute-start | bytes 3145736 | tf_op jit(solution)/shard_map/ppermute | solution.py:383
  331.6 40.2 %collective-permute-start.48 = (bf16[256,2048]{1,0:T(8,128)(2,1)}, bf16[256,2048]{1,0:T(8,128)(2,1)}, u32[]{:S(2)}, u32[]{:S(2)}) collective-permute-start(bf16[256,2048]{1,0:T(8,128)(2,1)} %bitcast.56), channel_id=1, source_target_pairs={{0,1},{1,0},{2,3},{3,2},{4,5},{5,4},{6,7},{7,6},{8,9},{9,8},{10,11... | collective-permute-start | bytes 3145736 | tf_op jit(solution)/shard_map/ppermute | solution.py:383
  333.1 42.2 %collective-permute-start.47 = (bf16[256,2048]{1,0:T(8,128)(2,1)}, bf16[256,2048]{1,0:T(8,128)(2,1)}, u32[]{:S(2)}, u32[]{:S(2)}) collective-permute-start(bf16[256,2048]{1,0:T(8,128)(2,1)} %bitcast.56), channel_id=1, source_target_pairs={{0,16},{8,24},{16,0},{24,8},{1,17},{9,25},{17,1},{25,9},{2,18},{10... | collective-permute-start | bytes 3145736 | tf_op jit(solution)/shard_map/ppermute | solution.py:383
  349.1 21.4 %collective-permute-start.45 = (bf16[2,64,1024]{2,1,0:T(8,128)(2,1)S(1)}, bf16[2,64,1024]{2,1,0:T(8,128)(2,1)S(1)}, u32[]{:S(2)}, u32[]{:S(2)}) collective-permute-start(bf16[2,64,1024]{2,1,0:T(8,128)(2,1)S(1)} %get-tuple-element.145), channel_id=1, source_target_pairs={{0,16},{8,24},{16,0},{24,8},{1,17},{9,25},{17,1},{25,9},{2,18},{10... | collective-permute-start | bytes 786440 | tf_op jit(solution)/shard_map/ppermute | solution.py:383
  352.5 27.6 %collective-permute-start.32 = (bf16[256,2048]{1,0:T(8,128)(2,1)}, bf16[256,2048]{1,0:T(8,128)(2,1)}, u32[]{:S(2)}, u32[]{:S(2)}) collective-permute-start(bf16[256,2048]{1,0:T(8,128)(2,1)} %get-tuple-element.94), channel_id=1, source_target_pairs={{0,8},{8,0},{16,24},{24,16},{1,9},{9,1},{17,25},{25,17},{2,10},{10... | collective-permute-start | bytes 3145736 | tf_op jit(solution)/shard_map/ppermute | solution.py:383
  364.0 29.2 %collective-permute-start.34 = (bf16[256,2048]{1,0:T(8,128)(2,1)}, bf16[256,2048]{1,0:T(8,128)(2,1)}, u32[]{:S(2)}, u32[]{:S(2)}) collective-permute-start(bf16[256,2048]{1,0:T(8,128)(2,1)} %add_convert_fusion.5), channel_id=1, source_target_pairs={{0,16},{8,24},{16,0},{24,8},{1,17},{9,25},{17,1},{25,9},{2,18},{10... | collective-permute-start | bytes 3145736 | tf_op jit(solution)/shard_map/ppermute | solution.py:383
  370.6 36.3 %collective-permute-start.51 = (bf16[256,2048]{1,0:T(8,128)(2,1)}, bf16[256,2048]{1,0:T(8,128)(2,1)}, u32[]{:S(2)}, u32[]{:S(2)}) collective-permute-start(bf16[256,2048]{1,0:T(8,128)(2,1)} %bitcast.56), channel_id=1, source_target_pairs={{0,8},{8,0},{16,24},{24,16},{1,9},{9,1},{17,25},{25,17},{2,10},{10... | collective-permute-start | bytes 3145736 | tf_op jit(solution)/shard_map/ppermute | solution.py:383
  373.7 29.6 %collective-permute-start.49 = (bf16[256,1024]{1,0:T(8,128)(2,1)}, bf16[256,1024]{1,0:T(8,128)(2,1)}, u32[]{:S(2)}, u32[]{:S(2)}) collective-permute-start(bf16[256,1024]{1,0:T(8,128)(2,1)} %slice.456), channel_id=1, source_target_pairs={{0,16},{8,24},{16,0},{24,8},{1,17},{9,25},{17,1},{25,9},{2,18},{10... | collective-permute-start | bytes 1572872 | tf_op jit(solution)/shard_map/ppermute | solution.py:383
  377.1 26.8 %collective-permute-start.50 = (bf16[256,1024]{1,0:T(8,128)(2,1)}, bf16[256,1024]{1,0:T(8,128)(2,1)}, u32[]{:S(2)}, u32[]{:S(2)}) collective-permute-start(bf16[256,1024]{1,0:T(8,128)(2,1)} %slice.457), channel_id=1, source_target_pairs={{0,1},{1,0},{2,3},{3,2},{4,5},{5,4},{6,7},{7,6},{8,9},{9,8},{10,11... | collective-permute-start | bytes 1572872 | tf_op jit(solution)/shard_map/ppermute | solution.py:383
  380.1 534.9 %reduce-scatter.6.cloned.1.call-start = ((), (), s32[]{:S(2)}) async-start(), calls=%async_computation.7 | async-start | bytes 5242880 | tf_op jit(solution)/shard_map/reduce_scatter | solution.py:508
  380.2 49.7 %collective-permute-start.53 = (bf16[256,2048]{1,0:T(8,128)(2,1)}, bf16[256,2048]{1,0:T(8,128)(2,1)S(1)}, u32[]{:S(2)}, u32[]{:S(2)}) collective-permute-start(bf16[256,2048]{1,0:T(8,128)(2,1)} %collective-permute-done.48), channel_id=1, source_target_pairs={{0,8},{8,0},{16,24},{24,16},{1,9},{9,1},{17,25},{25,17},{2,10},{10... | collective-permute-start | bytes 3145736 | tf_op jit(solution)/shard_map/ppermute | solution.py:383
  393.1 22.2 %collective-permute-start.52 = (bf16[256,2048]{1,0:T(8,128)(2,1)}, bf16[256,2048]{1,0:T(8,128)(2,1)S(1)}, u32[]{:S(2)}, u32[]{:S(2)}) collective-permute-start(bf16[256,2048]{1,0:T(8,128)(2,1)} %collective-permute-done.47), channel_id=1, source_target_pairs={{0,8},{8,0},{16,24},{24,16},{1,9},{9,1},{17,25},{25,17},{2,10},{10... | collective-permute-start | bytes 3145736 | tf_op jit(solution)/shard_map/ppermute | solution.py:383
  403.3 24.1 %collective-permute-start.36 = (bf16[256,2048]{1,0:T(8,128)(2,1)S(1)}, bf16[256,2048]{1,0:T(8,128)(2,1)S(1)}, u32[]{:S(2)}, u32[]{:S(2)}) collective-permute-start(bf16[256,2048]{1,0:T(8,128)(2,1)S(1)} %get-tuple-element.71), channel_id=1, source_target_pairs={{0,1},{1,0},{2,3},{3,2},{4,5},{5,4},{6,7},{7,6},{8,9},{9,8},{10,11... | collective-permute-start | bytes 3145736 | tf_op jit(solution)/shard_map/ppermute | solution.py:383
  403.9 25.2 %collective-permute-start.35 = (bf16[256,2048]{1,0:T(8,128)(2,1)S(1)}, bf16[256,2048]{1,0:T(8,128)(2,1)S(1)}, u32[]{:S(2)}, u32[]{:S(2)}) collective-permute-start(bf16[256,2048]{1,0:T(8,128)(2,1)S(1)} %get-tuple-element.71), channel_id=1, source_target_pairs={{0,16},{8,24},{16,0},{24,8},{1,17},{9,25},{17,1},{25,9},{2,18},{10... | collective-permute-start | bytes 3145736 | tf_op jit(solution)/shard_map/ppermute | solution.py:383
  406.8 24.1 %collective-permute-start.54 = (bf16[256,2048]{1,0:T(8,128)(2,1)S(1)}, bf16[256,2048]{1,0:T(8,128)(2,1)S(1)}, u32[]{:S(2)}, u32[]{:S(2)}) collective-permute-start(bf16[256,2048]{1,0:T(8,128)(2,1)S(1)} %pad_maximum_fusion.4), channel_id=1, source_target_pairs={{0,8},{8,0},{16,24},{24,16},{1,9},{9,1},{17,25},{25,17},{2,10},{10... | collective-permute-start | bytes 3145736 | tf_op jit(solution)/shard_map/ppermute | solution.py:383
  511.4 422.2 %reduce-scatter.8.cloned.1.call-start = ((), (), s32[]{:S(2)}) async-start(), calls=%async_computation.8 | async-start | bytes 5242880 | tf_op jit(solution)/shard_map/reduce_scatter | solution.py:508
  530.3 413.3 %reduce-scatter.4.cloned.1.call-start = ((), (), s32[]{:S(2)}) async-start(), calls=%async_computation.6 | async-start | bytes 2359296 | tf_op jit(solution)/shard_map/reduce_scatter | solution.py:588
  549.0 24.6 %collective-permute-start.62 = (bf16[256,2048]{1,0:T(8,128)(2,1)S(1)}, bf16[256,2048]{1,0:T(8,128)(2,1)S(1)}, u32[]{:S(2)}, u32[]{:S(2)}) collective-permute-start(bf16[256,2048]{1,0:T(8,128)(2,1)S(1)} %pad_maximum_fusion.6), channel_id=1, source_target_pairs={{0,1},{1,0},{2,3},{3,2},{4,5},{5,4},{6,7},{7,6},{8,9},{9,8},{10,11... | collective-permute-start | bytes 3145736 | tf_op jit(solution)/shard_map/ppermute | solution.py:383
  550.6 24.8 %collective-permute-start.59 = (bf16[256,2048]{1,0:T(8,128)(2,1)S(1)}, bf16[256,2048]{1,0:T(8,128)(2,1)S(1)}, u32[]{:S(2)}, u32[]{:S(2)}) collective-permute-start(bf16[256,2048]{1,0:T(8,128)(2,1)S(1)} %pad_maximum_fusion.5), channel_id=1, source_target_pairs={{0,16},{8,24},{16,0},{24,8},{1,17},{9,25},{17,1},{25,9},{2,18},{10... | collective-permute-start | bytes 3145736 | tf_op jit(solution)/shard_map/ppermute | solution.py:383
  583.1 24.2 %collective-permute-start.64 = (bf16[256,2048]{1,0:T(8,128)(2,1)}, bf16[256,2048]{1,0:T(8,128)(2,1)}, u32[]{:S(2)}, u32[]{:S(2)}) collective-permute-start(bf16[256,2048]{1,0:T(8,128)(2,1)} %get-tuple-element.62), channel_id=1, source_target_pairs={{0,16},{8,24},{16,0},{24,8},{1,17},{9,25},{17,1},{25,9},{2,18},{10... | collective-permute-start | bytes 3145736 | tf_op jit(solution)/shard_map/ppermute | solution.py:383
  584.3 23.0 %collective-permute-start.63 = (bf16[256,2048]{1,0:T(8,128)(2,1)}, bf16[256,2048]{1,0:T(8,128)(2,1)}, u32[]{:S(2)}, u32[]{:S(2)}) collective-permute-start(bf16[256,2048]{1,0:T(8,128)(2,1)} %get-tuple-element.62), channel_id=1, source_target_pairs={{0,8},{8,0},{16,24},{24,16},{1,9},{9,1},{17,25},{25,17},{2,10},{10... | collective-permute-start | bytes 3145736 | tf_op jit(solution)/shard_map/ppermute | solution.py:383
  620.1 21.3 %collective-permute-start.72 = (bf16[1,4,128,128]{3,2,1,0:T(8,128)(2,1)}, bf16[1,4,128,128]{3,2,1,0:T(8,128)(2,1)S(1)}, u32[]{:S(2)}, u32[]{:S(2)}) collective-permute-start(bf16[1,4,128,128]{3,2,1,0:T(8,128)(2,1)} %get-tuple-element.130), channel_id=1, source_target_pairs={{0,7},{1,6},{2,5},{3,4},{4,3},{5,2},{6,1},{7,0},{8,15},{9,14},{10,... | collective-permute-start | bytes 393224 | tf_op jit(solution)/shard_map/ppermute | solution.py:383
  624.0 22.3 %collective-permute-start.71 = (bf16[1,4,128,128]{3,2,1,0:T(8,128)(2,1)}, bf16[1,4,128,128]{3,2,1,0:T(8,128)(2,1)S(1)}, u32[]{:S(2)}, u32[]{:S(2)}) collective-permute-start(bf16[1,4,128,128]{3,2,1,0:T(8,128)(2,1)} %get-tuple-element.131), channel_id=1, source_target_pairs={{0,6},{1,7},{2,4},{3,5},{4,2},{5,3},{6,0},{7,1},{8,14},{9,15},{10,... | collective-permute-start | bytes 393224 | tf_op jit(solution)/shard_map/ppermute | solution.py:383
  637.0 29.2 %collective-permute-start.70 = (bf16[1,4,128,128]{3,2,1,0:T(8,128)(2,1)}, bf16[1,4,128,128]{3,2,1,0:T(8,128)(2,1)}, u32[]{:S(2)}, u32[]{:S(2)}) collective-permute-start(bf16[1,4,128,128]{3,2,1,0:T(8,128)(2,1)} %get-tuple-element.132), channel_id=1, source_target_pairs={{0,5},{1,4},{2,7},{3,6},{4,1},{5,0},{6,3},{7,2},{8,13},{9,12},{10,... | collective-permute-start | bytes 393224 | tf_op jit(solution)/shard_map/ppermute | solution.py:383
  637.8 38.7 %collective-permute-start.69 = (bf16[1,4,128,128]{3,2,1,0:T(8,128)(2,1)}, bf16[1,4,128,128]{3,2,1,0:T(8,128)(2,1)}, u32[]{:S(2)}, u32[]{:S(2)}) collective-permute-start(bf16[1,4,128,128]{3,2,1,0:T(8,128)(2,1)} %get-tuple-element.133), channel_id=1, source_target_pairs={{0,4},{1,5},{2,6},{3,7},{4,0},{5,1},{6,2},{7,3},{8,12},{9,13},{10,... | collective-permute-start | bytes 393224 | tf_op jit(solution)/shard_map/ppermute | solution.py:383
  639.9 36.7 %collective-permute-start.68 = (bf16[1,4,128,128]{3,2,1,0:T(8,128)(2,1)}, bf16[1,4,128,128]{3,2,1,0:T(8,128)(2,1)}, u32[]{:S(2)}, u32[]{:S(2)}) collective-permute-start(bf16[1,4,128,128]{3,2,1,0:T(8,128)(2,1)} %get-tuple-element.134), channel_id=1, source_target_pairs={{0,3},{1,2},{2,1},{3,0},{4,7},{5,6},{6,5},{7,4},{8,11},{9,10},{10,... | collective-permute-start | bytes 393224 | tf_op jit(solution)/shard_map/ppermute | solution.py:383
  641.4 35.1 %collective-permute-start.67 = (bf16[1,4,128,128]{3,2,1,0:T(8,128)(2,1)}, bf16[1,4,128,128]{3,2,1,0:T(8,128)(2,1)}, u32[]{:S(2)}, u32[]{:S(2)}) collective-permute-start(bf16[1,4,128,128]{3,2,1,0:T(8,128)(2,1)} %get-tuple-element.135), channel_id=1, source_target_pairs={{0,2},{1,3},{2,0},{3,1},{4,6},{5,7},{6,4},{7,5},{8,10},{9,11},{10,... | collective-permute-start | bytes 393224 | tf_op jit(solution)/shard_map/ppermute | solution.py:383
  646.4 30.2 %collective-permute-start.66 = (bf16[1,4,128,128]{3,2,1,0:T(8,128)(2,1)}, bf16[1,4,128,128]{3,2,1,0:T(8,128)(2,1)}, u32[]{:S(2)}, u32[]{:S(2)}) collective-permute-start(bf16[1,4,128,128]{3,2,1,0:T(8,128)(2,1)} %get-tuple-element.136), channel_id=1, source_target_pairs={{0,1},{1,0},{2,3},{3,2},{4,5},{5,4},{6,7},{7,6},{8,9},{9,8},{10,11... | collective-permute-start | bytes 393224 | tf_op jit(solution)/shard_map/ppermute | solution.py:383
  702.2 47.4 %collective-permute-start.86 = (bf16[3,4,128,128]{3,2,1,0:T(8,128)(2,1)S(1)}, bf16[3,4,128,128]{3,2,1,0:T(8,128)(2,1)S(1)}, u32[]{:S(2)}, u32[]{:S(2)}) collective-permute-start(bf16[3,4,128,128]{3,2,1,0:T(8,128)(2,1)S(1)} %get-tuple-element.97), channel_id=1, source_target_pairs={{0,6},{1,7},{2,4},{3,5},{4,2},{5,3},{6,0},{7,1},{8,14},{9,15},{10,... | collective-permute-start | bytes 1179656 | tf_op jit(solution)/shard_map/ppermute | solution.py:383
  702.8 72.5 %collective-permute-start.85 = (bf16[3,4,128,128]{3,2,1,0:T(8,128)(2,1)S(1)}, bf16[3,4,128,128]{3,2,1,0:T(8,128)(2,1)S(1)}, u32[]{:S(2)}, u32[]{:S(2)}) collective-permute-start(bf16[3,4,128,128]{3,2,1,0:T(8,128)(2,1)S(1)} %get-tuple-element.98), channel_id=1, source_target_pairs={{0,5},{1,4},{2,7},{3,6},{4,1},{5,0},{6,3},{7,2},{8,13},{9,12},{10,... | collective-permute-start | bytes 1179656 | tf_op jit(solution)/shard_map/ppermute | solution.py:383
  702.8 80.2 %collective-permute-start.84 = (bf16[3,4,128,128]{3,2,1,0:T(8,128)(2,1)S(1)}, bf16[3,4,128,128]{3,2,1,0:T(8,128)(2,1)S(1)}, u32[]{:S(2)}, u32[]{:S(2)}) collective-permute-start(bf16[3,4,128,128]{3,2,1,0:T(8,128)(2,1)S(1)} %get-tuple-element.99), channel_id=1, source_target_pairs={{0,4},{1,5},{2,6},{3,7},{4,0},{5,1},{6,2},{7,3},{8,12},{9,13},{10,... | collective-permute-start | bytes 1179656 | tf_op jit(solution)/shard_map/ppermute | solution.py:383
  705.7 77.3 %collective-permute-start.83 = (bf16[3,4,128,128]{3,2,1,0:T(8,128)(2,1)S(1)}, bf16[3,4,128,128]{3,2,1,0:T(8,128)(2,1)S(1)}, u32[]{:S(2)}, u32[]{:S(2)}) collective-permute-start(bf16[3,4,128,128]{3,2,1,0:T(8,128)(2,1)S(1)} %get-tuple-element.100), channel_id=1, source_target_pairs={{0,3},{1,2},{2,1},{3,0},{4,7},{5,6},{6,5},{7,4},{8,11},{9,10},{10,... | collective-permute-start | bytes 1179656 | tf_op jit(solution)/shard_map/ppermute | solution.py:383
  716.9 66.6 %collective-permute-start.82 = (bf16[3,4,128,128]{3,2,1,0:T(8,128)(2,1)S(1)}, bf16[3,4,128,128]{3,2,1,0:T(8,128)(2,1)S(1)}, u32[]{:S(2)}, u32[]{:S(2)}) collective-permute-start(bf16[3,4,128,128]{3,2,1,0:T(8,128)(2,1)S(1)} %get-tuple-element.101), channel_id=1, source_target_pairs={{0,2},{1,3},{2,0},{3,1},{4,6},{5,7},{6,4},{7,5},{8,10},{9,11},{10,... | collective-permute-start | bytes 1179656 | tf_op jit(solution)/shard_map/ppermute | solution.py:383
  749.6 34.0 %collective-permute-start.81 = (bf16[3,4,128,128]{3,2,1,0:T(8,128)(2,1)S(1)}, bf16[3,4,128,128]{3,2,1,0:T(8,128)(2,1)S(1)}, u32[]{:S(2)}, u32[]{:S(2)}) collective-permute-start(bf16[3,4,128,128]{3,2,1,0:T(8,128)(2,1)S(1)} %get-tuple-element.102), channel_id=1, source_target_pairs={{0,1},{1,0},{2,3},{3,2},{4,5},{5,4},{6,7},{7,6},{8,9},{9,8},{10,11... | collective-permute-start | bytes 1179656 | tf_op jit(solution)/shard_map/ppermute | solution.py:383
  775.3 152.3 %collective-permute-start.73 = (bf16[256,2048]{1,0:T(8,128)(2,1)}, bf16[256,2048]{1,0:T(8,128)(2,1)}, u32[]{:S(2)}, u32[]{:S(2)}) collective-permute-start(bf16[256,2048]{1,0:T(8,128)(2,1)} %get-tuple-element.74), channel_id=1, source_target_pairs={{0,8},{8,0},{16,24},{24,16},{1,9},{9,1},{17,25},{25,17},{2,10},{10... | collective-permute-start | bytes 3145736 | tf_op jit(solution)/shard_map/ppermute | solution.py:383
  782.9 30.3 %collective-permute-start.78 = (bf16[256,2048]{1,0:T(8,128)(2,1)}, bf16[256,2048]{1,0:T(8,128)(2,1)S(1)}, u32[]{:S(2)}, u32[]{:S(2)}) collective-permute-start(bf16[256,2048]{1,0:T(8,128)(2,1)} %get-tuple-element.75), channel_id=1, source_target_pairs={{0,8},{8,0},{16,24},{24,16},{1,9},{9,1},{17,25},{25,17},{2,10},{10... | collective-permute-start | bytes 3145736 | tf_op jit(solution)/shard_map/ppermute | solution.py:383
  783.0 32.4 %collective-permute-start.75 = (bf16[256,2048]{1,0:T(8,128)(2,1)S(1)}, bf16[256,2048]{1,0:T(8,128)(2,1)}, u32[]{:S(2)}, u32[]{:S(2)}) collective-permute-start(bf16[256,2048]{1,0:T(8,128)(2,1)S(1)} %get-tuple-element.76), channel_id=1, source_target_pairs={{0,8},{8,0},{16,24},{24,16},{1,9},{9,1},{17,25},{25,17},{2,10},{10... | collective-permute-start | bytes 3145736 | tf_op jit(solution)/shard_map/ppermute | solution.py:383
  783.5 31.9 %collective-permute-start.74 = (bf16[256,2048]{1,0:T(8,128)(2,1)S(1)}, bf16[256,2048]{1,0:T(8,128)(2,1)}, u32[]{:S(2)}, u32[]{:S(2)}) collective-permute-start(bf16[256,2048]{1,0:T(8,128)(2,1)S(1)} %get-tuple-element.77), channel_id=1, source_target_pairs={{0,8},{8,0},{16,24},{24,16},{1,9},{9,1},{17,25},{25,17},{2,10},{10... | collective-permute-start | bytes 3145736 | tf_op jit(solution)/shard_map/ppermute | solution.py:383
  811.5 19.9 %collective-permute-start.96 = (bf16[4,64,1536]{2,1,0:T(8,128)(2,1)S(1)}, bf16[4,64,1536]{2,1,0:T(8,128)(2,1)S(1)}, u32[]{:S(2)}, u32[]{:S(2)}) collective-permute-start(bf16[4,64,1536]{2,1,0:T(8,128)(2,1)S(1)} %get-tuple-element.90), channel_id=1, source_target_pairs={{0,2},{2,4},{4,6},{6,7},{7,5},{5,3},{3,1},{1,0},{8,10},{10,12},{12... | collective-permute-start | bytes 2359304 | tf_op jit(solution)/shard_map/ppermute | solution.py:530
  813.2 83.6 %collective-permute-start.100 = (bf16[4,64,1536]{2,1,0:T(8,128)(2,1)}, bf16[4,64,1536]{2,1,0:T(8,128)(2,1)}, u32[]{:S(2)}, u32[]{:S(2)}) collective-permute-start(bf16[4,64,1536]{2,1,0:T(8,128)(2,1)} %get-tuple-element.91), channel_id=1, source_target_pairs={{0,1},{2,0},{4,2},{6,4},{7,6},{5,7},{3,5},{1,3},{8,9},{10,8},{12,1... | collective-permute-start | bytes 2359304 | tf_op jit(solution)/shard_map/ppermute | solution.py:530
  815.3 36.0 %collective-permute-start.88 = (bf16[256,2048]{1,0:T(8,128)(2,1)S(1)}, bf16[256,2048]{1,0:T(8,128)(2,1)S(1)}, u32[]{:S(2)}, u32[]{:S(2)}) collective-permute-start(bf16[256,2048]{1,0:T(8,128)(2,1)S(1)} %get-tuple-element.92), channel_id=1, source_target_pairs={{0,8},{8,0},{16,24},{24,16},{1,9},{9,1},{17,25},{25,17},{2,10},{10... | collective-permute-start | bytes 3145736 | tf_op jit(solution)/shard_map/ppermute | solution.py:383
  845.1 25.2 %collective-permute-start.90 = (bf16[256,2048]{1,0:T(8,128)(2,1)S(1)}, bf16[256,2048]{1,0:T(8,128)(2,1)S(1)}, u32[]{:S(2)}, u32[]{:S(2)}) collective-permute-start(bf16[256,2048]{1,0:T(8,128)(2,1)S(1)} %add_convert_fusion), channel_id=1, source_target_pairs={{0,16},{8,24},{16,0},{24,8},{1,17},{9,25},{17,1},{25,9},{2,18},{10... | collective-permute-start | bytes 3145736 | tf_op jit(solution)/shard_map/ppermute | solution.py:383
  849.0 22.9 %collective-permute-start.97 = (bf16[4,64,1536]{2,1,0:T(8,128)(2,1)}, bf16[4,64,1536]{2,1,0:T(8,128)(2,1)}, u32[]{:S(2)}, u32[]{:S(2)}) collective-permute-start(bf16[4,64,1536]{2,1,0:T(8,128)(2,1)} %fusion.14), channel_id=1, source_target_pairs={{0,2},{2,4},{4,6},{6,7},{7,5},{5,3},{3,1},{1,0},{8,10},{10,12},{12... | collective-permute-start | bytes 2359304 | tf_op jit(solution)/shard_map/ppermute | solution.py:530
  851.4 78.0 %collective-permute-start.80 = (bf16[256,2048]{1,0:T(8,128)(2,1)}, bf16[256,2048]{1,0:T(8,128)(2,1)}, u32[]{:S(2)}, u32[]{:S(2)}) collective-permute-start(bf16[256,2048]{1,0:T(8,128)(2,1)} %pad_maximum_fusion.8), channel_id=1, source_target_pairs={{0,1},{1,0},{2,3},{3,2},{4,5},{5,4},{6,7},{7,6},{8,9},{9,8},{10,11... | collective-permute-start | bytes 3145736 | tf_op jit(solution)/shard_map/ppermute | solution.py:383
  873.5 32.1 %collective-permute-start.98 = (bf16[4,64,1536]{2,1,0:T(8,128)(2,1)S(1)}, bf16[4,64,1536]{2,1,0:T(8,128)(2,1)S(1)}, u32[]{:S(2)}, u32[]{:S(2)}) collective-permute-start(bf16[4,64,1536]{2,1,0:T(8,128)(2,1)S(1)} %fusion.15), channel_id=1, source_target_pairs={{0,2},{2,4},{4,6},{6,7},{7,5},{5,3},{3,1},{1,0},{8,10},{10,12},{12... | collective-permute-start | bytes 2359304 | tf_op jit(solution)/shard_map/ppermute | solution.py:530
  895.3 34.2 %collective-permute-start.77 = (bf16[256,2048]{1,0:T(8,128)(2,1)}, bf16[256,2048]{1,0:T(8,128)(2,1)S(1)}, u32[]{:S(2)}, u32[]{:S(2)}) collective-permute-start(bf16[256,2048]{1,0:T(8,128)(2,1)} %pad_maximum_fusion.7), channel_id=1, source_target_pairs={{0,16},{8,24},{16,0},{24,8},{1,17},{9,25},{17,1},{25,9},{2,18},{10... | collective-permute-start | bytes 3145736 | tf_op jit(solution)/shard_map/ppermute | solution.py:383
  913.0 32.4 %collective-permute-start.99 = (bf16[4,64,1536]{2,1,0:T(8,128)(2,1)}, bf16[4,64,1536]{2,1,0:T(8,128)(2,1)}, u32[]{:S(2)}, u32[]{:S(2)}) collective-permute-start(bf16[4,64,1536]{2,1,0:T(8,128)(2,1)} %get-tuple-element.88), channel_id=1, source_target_pairs={{0,2},{2,4},{4,6},{6,7},{7,5},{5,3},{3,1},{1,0},{8,10},{10,12},{12... | collective-permute-start | bytes 2359304 | tf_op jit(solution)/shard_map/ppermute | solution.py:530
  929.5 20.2 %collective-permute-start.102 = (bf16[4,64,1536]{2,1,0:T(8,128)(2,1)}, bf16[4,64,1536]{2,1,0:T(8,128)(2,1)}, u32[]{:S(2)}, u32[]{:S(2)}) collective-permute-start(bf16[4,64,1536]{2,1,0:T(8,128)(2,1)} %fusion.13), channel_id=1, source_target_pairs={{0,1},{2,0},{4,2},{6,4},{7,6},{5,7},{3,5},{1,3},{8,9},{10,8},{12,1... | collective-permute-start | bytes 2359304 | tf_op jit(solution)/shard_map/ppermute | solution.py:530
  (104 other events, 1499.3 us)
Sparse Core Ops, SparseCore 0:
  10.2 62.2 all-gather.3
  125.7 146.6 all-gather.7
  380.2 80.2 all-gather.5
  511.5 76.0 reduce-scatter.5
  589.8 94.1 reduce-scatter.7
  687.4 119.7 reduce-scatter.3

commit v4 on v3

--- a/solution.py
+++ b/solution.py
@@ -1,19 +1,15 @@
 import functools
 import math
-
 import jax
 import jax.numpy as jnp
 from jax import lax
 from jax.experimental import pallas as pl
 from jax.experimental.pallas import tpu as pltpu
 from jax.sharding import PartitionSpec as P
-
 HEADS = 16
 NARROW, WIDE = "narrow", "wide"
 BOTH = (NARROW, WIDE)
 REACH = 4
-
-
 eps = 1e-05
 neg_big = -1e30
 
@@ -421,15 +417,15 @@
     return table
 
 
-def narrow_gather(own):
+def narrow_gather(own, *made):
     across = flip(own, NARROW, 2)
     beside = flip(own, NARROW, 1)
-    return jnp.concatenate([own, beside, across, flip(across, NARROW, 1)], axis=0)
-
-
-def narrow_scatter(partial):
+    across = hold(across, *made) if made else across
+    return [own, beside, across, flip(across, NARROW, 1)]
+
+
+def narrow_scatter(parts):
     f32 = jnp.float32
-    parts = partial.reshape(4, -1, partial.shape[-1])
     far = flip(parts[3], NARROW, 1)
     near = flip(parts[1], NARROW, 1)
     passed = (parts[2].astype(f32) + far.astype(f32)).astype(jnp.bfloat16)
@@ -454,11 +450,13 @@
     return jnp.stack([jnp.where(swap, r[k ^ 2], r[k]) for k in range(4)])
 
 
+def narrow_blocks(block_of):
+    me = lax.axis_index(NARROW)
+    return [flip(block_of(me ^ j), NARROW, j) if j else block_of(me) for j in range(4)]
+
+
 def narrow_swap(block_of):
-    me = lax.axis_index(NARROW)
-    return in_order([
-        flip(block_of(me ^ j), NARROW, j) if j else block_of(me) for j in range(4)
-    ])
+    return in_order(narrow_blocks(block_of))
 
 
 def pair_swap(block_of):
@@ -468,30 +466,37 @@
     return jnp.stack([jnp.where(high, other, own), jnp.where(high, own, other)])
 
 
-def spread(own):
+def spread_near(own):
     half = own.shape[1] // 2
     over_y = flip(own, WIDE, 1)
     over_x = flip(own, NARROW, 2)
     both = jnp.concatenate(
         [flip(over_y[:, :half], NARROW, 2), flip(over_x[:, half:], WIDE, 1)], axis=1
     )
-    near = [own, over_x, over_y, both]
-    return jnp.concatenate(near + [flip(part, NARROW, 1) for part in near], axis=0)
-
-
-def fold(partial):
+    return [own, over_x, over_y, both]
+
+
+def spread(own):
+    near = spread_near(own)
+    return near + [flip(part, NARROW, 1) for part in near]
+
+
+def fold(far, near, made=None):
     f32, bf16 = jnp.float32, jnp.bfloat16
-    parts = partial.reshape(8, -1, partial.shape[-1])
-    half = partial.shape[-1] // 2
-    both, over_y, over_x, own = [
-        parts[k].astype(f32) + flip(parts[4 + k], NARROW, 1).astype(f32) for k in (3, 2, 1, 0)
-    ]
-    both = both.astype(bf16)
+    width = far.shape[-1]
+    half = width // 2
+    far, near = far.reshape(4, -1, width), near.reshape(4, -1, width)
+    far = flip(far, NARROW, 1)
+    both = (near[3].astype(f32) + far[3].astype(f32)).astype(bf16)
+    own, over_x, over_y = [near[k].astype(f32) + far[k].astype(f32) for k in range(3)]
     first = flip(both[:, :half], WIDE, 1).astype(f32)
     last = flip(both[:, half:], NARROW, 2).astype(f32)
     over_x = jnp.concatenate([over_x[:, :half] + first, over_x[:, half:]], axis=1).astype(bf16)
     over_y = jnp.concatenate([over_y[:, :half], over_y[:, half:] + last], axis=1).astype(bf16)
-    return own + flip(over_x, NARROW, 2).astype(f32) + flip(over_y, WIDE, 1).astype(f32)
+    last = flip(over_x, NARROW, 2)
+    if made is not None:
+        last = hold(last, made(over_x))
+    return own + last.astype(f32) + flip(over_y, WIDE, 1).astype(f32)
 
 
 def columns(wide):
@@ -532,52 +537,64 @@
     )
 
 
-def ring_gather(shard, axis):
+def ring_gather(shard):
     wide = lax.axis_size(WIDE)
     here = ring_position(wide)
-    shape = list(shard.shape)
-    shape.insert(axis, wide)
-    full = jnp.zeros(shape, shard.dtype)
+    middle = shard.shape[-1] // 2
+    full = jnp.zeros((wide,) + shard.shape, shard.dtype)
 
     def put(full, piece, position):
         return lax.dynamic_update_slice_in_dim(
-            full, jnp.expand_dims(piece, axis), ring_at(position, wide), axis
+            full, piece[None], ring_at(position + wide, wide), 0
         )
 
     full = put(full, shard, here)
     ahead = behind = shard
-    for k in range(1, wide // 2 + 1):
-        ahead = ring_step(ahead, 1)
-        full = put(full, ahead, here - k + wide)
-        if k < wide - wide // 2:
-            behind = ring_step(behind, -1)
-            full = put(full, behind, here + k)
-    return full
-
-
-def ring_scatter(full, axis):
+    for k in range(1, wide // 2):
+        ahead, behind = ring_step(ahead, 1), ring_step(behind, -1)
+        full = put(put(full, ahead, here - k), behind, here + k)
+    ahead = ring_step(ahead[..., :middle], 1)
+    behind = ring_step(behind[..., middle:], -1)
+    return put(full, jnp.concatenate([ahead, behind], axis=-1), here + wide // 2)
+
+
+def ring_scatter(full, beside):
     wide = lax.axis_size(WIDE)
     here = ring_position(wide)
     bf16, f32 = jnp.bfloat16, jnp.float32
+    middle = full.shape[-1] // 2
 
     def local(position):
-        return at(full, ring_at(position + wide, wide), axis).astype(f32)
-
-    half = wide // 2
-    ahead = behind = None
-    for k in range(half, 0, -1):
-        term = local(here + k)
-        term = term if ahead is None else term + ahead
-        ahead = ring_step(term.astype(bf16), 1).astype(f32)
-        if k < wide - half:
-            term = local(here - k)
-            term = term if behind is None else term + behind
-            behind = ring_step(term.astype(bf16), -1).astype(f32)
-    return local(here) + ahead + behind
+        return at(full, ring_at(position + wide, wide))
+
+    far = local(here + wide // 2)
+    ahead, behind = lax.optimization_barrier((far[..., :middle], far[..., middle:]))
+    event = ahead
+    stage = 0
+    for k in range(wide // 2 - 1, -1, -1):
+        ahead, behind = ring_step(ahead, 1).astype(f32), ring_step(behind, -1).astype(f32)
+        values = beside(stage, event)
+        stage += 1
+        if k == 0:
+            break
+        to_ahead, to_behind = local(here + k).astype(f32), local(here - k).astype(f32)
+        if k == wide // 2 - 1:
+            to_ahead = jnp.concatenate(
+                [to_ahead[..., :middle] + ahead, to_ahead[..., middle:]], axis=-1
+            )
+            to_behind = jnp.concatenate(
+                [to_behind[..., :middle], to_behind[..., middle:] + behind], axis=-1
+            )
+        else:
+            to_ahead, to_behind = to_ahead + ahead, to_behind + behind
+        ahead, behind = lax.optimization_barrier(
+            (to_ahead.astype(bf16), to_behind.astype(bf16)) + values
+        )[:2]
+    return local(here).astype(f32) + ahead + behind
 
 
 def wide_swap(parts):
-    return [parts[0]] + [flip(parts[d], WIDE, d) for d in range(1, parts.shape[0])]
+    return lax.all_to_all(parts, WIDE, split_axis=0, concat_axis=0, tiled=True)
 
 
 def wide_gather(shard, axis):
@@ -598,95 +615,230 @@
 CONTRACT_FIRST = (((0,), (0,)), ((), ()))
 
 
-def project_kernel(me_ref, rows_ref, weight_ref, bias_ref, out_ref, *, heads, by_last):
-    me = me_ref[1]
-    if by_last:
-        acc = lax.dot_general(
-            rows_ref[...], weight_ref[...], CONTRACT_LAST, preferred_element_type=jnp.float32
-        )
-    else:
-        acc = jnp.dot(rows_ref[...], weight_ref[...], preferred_element_type=jnp.float32)
-    acc = (acc + bias_ref[...]).astype(jnp.bfloat16)
+def project_kernel(*refs, heads, by_last):
+    rows, (weight_ref, bias_ref, out_ref) = refs[:-3], refs[-3:]
     units, parts, _, tokens, head_dim = out_ref.shape
-    for unit in range(units):
-        b, h = divmod(unit, heads)
-        for part in range(parts):
-            c = (part * heads + h) * head_dim
-            out_ref[unit ^ me, part, 0] = acc[b * tokens : (b + 1) * tokens, c : c + head_dim]
-
-
-def project(me, rows, weight, bias, units, parts, heads, tokens, by_last):
-    blocks, width = 4, rows.shape[1]
+    for j, rows_ref in enumerate(rows):
+
+        @pl.when(pl.program_id(0) == j)
+        def _():
+            if by_last:
+                acc = lax.dot_general(
+                    rows_ref[...], weight_ref[...], CONTRACT_LAST, preferred_element_type=jnp.float32
+                )
+            else:
+                acc = jnp.dot(rows_ref[...], weight_ref[...], preferred_element_type=jnp.float32)
+            acc = (acc + bias_ref[...]).astype(jnp.bfloat16)
+            for unit in range(units):
+                b, h = divmod(unit, heads)
+                for part in range(parts):
+                    c = (part * heads + h) * head_dim
+                    out_ref[unit, part, 0] = acc[
+                        b * tokens : (b + 1) * tokens, c : c + head_dim
+                    ]
+
+
+def resident(shape):
+    return pl.BlockSpec(shape, lambda i: (0,) * len(shape), pipeline_mode=pl.Buffered(1))
+
+
+def project(rows, weight, bias, units, parts, heads, tokens, by_last):
+    blocks = len(rows)
     head_dim = bias.shape[0] // (parts * heads)
-    step = rows.shape[0] // blocks
     return pl.pallas_call(
         functools.partial(project_kernel, heads=heads, by_last=by_last),
         grid=(blocks,),
         out_shape=jax.ShapeDtypeStruct((units, parts, blocks, tokens, head_dim), jnp.bfloat16),
-        in_specs=[
-            SMEM_SPEC,
-            pl.BlockSpec((step, width), lambda i: (i, 0)),
-            pl.BlockSpec(weight.shape, lambda i: (0, 0), pipeline_mode=pl.Buffered(1)),
-            pl.BlockSpec((1, bias.shape[0]), lambda i: (0, 0)),
-        ],
+        in_specs=[resident(block.shape) for block in rows]
+        + [resident(weight.shape), resident((1, bias.shape[0]))],
         out_specs=pl.BlockSpec(
             (units, parts, 1, tokens, head_dim), lambda i: (0, 0, i, 0, 0)
         ),
         compiler_params=BIG,
         name="project",
-    )(me, rows, weight, bias.reshape(1, -1))
-
-
-def unproject_kernel(me_ref, *refs, heads, by_last):
-    units = len(refs) - 4
-    pieces, weight_ref, out_ref, rows_ref, held = refs[:units], *refs[units:]
-    me = me_ref[1]
-    for d in range(units):
-        held[d ^ me] = pieces[d][:, 0]
-    parts = held.shape[1]
-    rows = jnp.concatenate(
+    )(*rows, weight, bias.reshape(1, -1))
+
+
+def project_parts_kernel(*refs, heads, blocks):
+    rows, weights, (bias_ref, out_ref) = refs[:blocks], refs[blocks:-2], refs[-2:]
+    units, parts, _, tokens, head_dim = out_ref.shape
+    depth = rows[0].shape[1] // len(weights)
+    for j, rows_ref in enumerate(rows):
+
+        @pl.when(pl.program_id(0) == j)
+        def _():
+            acc = bias_ref[...]
+            for k, weight_ref in enumerate(weights):
+                acc = acc + jnp.dot(
+                    rows_ref[:, k * depth : (k + 1) * depth],
+                    weight_ref[...].reshape(depth, -1),
+                    preferred_element_type=jnp.float32,
+                )
+            acc = acc.astype(jnp.bfloat16)
+            for unit in range(units):
+                b, h = divmod(unit, heads)
+                for part in range(parts):
+                    c = (part * heads + h) * head_dim
+                    out_ref[unit, part, 0] = acc[b * tokens : (b + 1) * tokens, c : c + head_dim]
+
+
+def project_parts(rows, weight, bias, units, parts, heads, tokens):
+    blocks, head_dim = len(rows), bias.shape[0] // (parts * heads)
+    wide, narrow, shard, _ = weight.shape
+    width = bias.shape[0]
+    return pl.pallas_call(
+        functools.partial(project_parts_kernel, heads=heads, blocks=blocks),
+        grid=(blocks,),
+        out_shape=jax.ShapeDtypeStruct((units, parts, blocks, tokens, head_dim), jnp.bfloat16),
+        in_specs=[resident(block.shape) for block in rows]
+        + [
+            pl.BlockSpec(
+                (wide, 1, shard, width), lambda i, k=k: (0, k, 0, 0), pipeline_mode=pl.Buffered(1)
+            )
+            for k in range(narrow)
+        ]
+        + [resident((1, bias.shape[0]))],
+        out_specs=pl.BlockSpec((units, parts, 1, tokens, head_dim), lambda i: (0, 0, i, 0, 0)),
+        compiler_params=BIG,
+        name="project_parts",
+    )(*rows, *[weight] * narrow, bias.reshape(1, -1))
+
+
+def times_parts_kernel(rows_ref, weight_ref, out_ref):
+    inner = rows_ref.shape[1]
+    weight = weight_ref[...].reshape(out_ref.shape[1], -1)[:, :inner]
+    acc = lax.dot_general(
+        rows_ref[...], weight, CONTRACT_LAST, preferred_element_type=jnp.float32
+    )
+    out_ref[...] = acc.astype(jnp.bfloat16)
+
+
+def times_parts(rows, block, count, weight):
+    gathered, narrow, shard, _ = weight.shape
+    inner = rows.shape[1]
+    step = gathered * shard
+    return pl.pallas_call(
+        times_parts_kernel,
+        grid=(narrow,),
+        out_shape=jax.ShapeDtypeStruct((count, narrow * step), jnp.bfloat16),
+        in_specs=[
+            pl.BlockSpec((count, inner), lambda i: (block, 0), pipeline_mode=pl.Buffered(1)),
+            pl.BlockSpec((gathered, 1, shard, inner), lambda i: (0, i, 0, 0)),
+        ],
+        out_specs=pl.BlockSpec((count, step), lambda i: (0, i)),
+        compiler_params=BIG,
+        name="times_parts",
+    )(rows, weight)
+
+
+def wide_outer_kernel(*refs):
+    lefts, (right_ref, extra_ref, out_ref) = refs[:-3], refs[-3:]
+    pair, narrow, shard, total = out_ref.shape
+    width = right_ref.shape[1]
+    more = total - width
+    for n in range(narrow):
+        left = jnp.concatenate([ref[...] for ref in lefts[n::narrow]], axis=0)
+        acc = lax.dot_general(
+            left, right_ref[...], CONTRACT_FIRST, preferred_element_type=jnp.float32
+        )
+        for y in range(pair):
+            out_ref[y, n, :, :width] = acc[y * shard : (y + 1) * shard].astype(jnp.bfloat16)
+        for y in range(pair):
+            out_ref[y, n, :, width:] = extra_ref[
+                y * shard : (y + 1) * shard, n * more : (n + 1) * more
+            ]
+
+
+def wide_outer(lefts, right, extra, wide):
+    shard, narrow, width = extra.shape[0] // wide, 4, right.shape[1]
+    more = extra.shape[1] // narrow
+    block = lefts[0].shape[0]
+    deep = wide // 2
+    return pl.pallas_call(
+        wide_outer_kernel,
+        grid=(deep,),
+        out_shape=jax.ShapeDtypeStruct((wide, narrow, shard, width + more), jnp.bfloat16),
+        in_specs=[
+            pl.BlockSpec((block, 2 * shard), lambda i, n=n: (0, n * deep + i))
+            for _ in lefts
+            for n in range(narrow)
+        ]
+        + [
+            resident(right.shape),
+            pl.BlockSpec((2 * shard, extra.shape[1]), lambda i: (i, 0)),
+        ],
+        out_specs=pl.BlockSpec((2, narrow, shard, width + more), lambda i: (i, 0, 0, 0)),
+        compiler_params=BIG,
+        name="wide_outer",
+    )(*[left for left in lefts for _ in range(narrow)], right, extra)
+
+
+def row_block(parts_ref, j, b, heads):
+    return jnp.concatenate(
         [
-            jnp.concatenate(
-                [held[b * heads + h, part] for part in range(parts) for h in range(heads)], axis=1
+            parts_ref[b * heads + h, part, j]
+            for part in range(parts_ref.shape[1])
+            for h in range(heads)
+        ],
+        axis=1,
+    )
+
+
+def unproject_kernel(parts_ref, weight_ref, *refs, heads, order):
+    outs, rows_ref = refs[:-1], refs[-1]
+    for step, j in enumerate(order):
+
+        @pl.when(pl.program_id(0) == step)
+        def _():
+            rows = jnp.concatenate(
+                [row_block(parts_ref, j, b, heads) for b in range(parts_ref.shape[0] // heads)],
+                axis=0,
             )
-            for b in range(units // heads)
-        ],
-        axis=0,
-    )
-    rows_ref[...] = rows
-    if by_last:
-        acc = lax.dot_general(
-            rows, weight_ref[...], CONTRACT_LAST, preferred_element_type=jnp.float32
-        )
-    else:
-        acc = jnp.dot(rows, weight_ref[...], preferred_element_type=jnp.float32)
-    out_ref[...] = acc.astype(jnp.bfloat16)
-
-
-def unproject(me, pieces, weight, heads, by_last):
-    units = len(pieces)
-    parts, blocks, tokens, head_dim = pieces[0].shape
+            rows_ref[j] = rows
+            acc = jnp.dot(rows, weight_ref[...], preferred_element_type=jnp.float32)
+            outs[j][...] = acc.astype(jnp.bfloat16)
+
+
+def unproject(parts, weight, heads):
+    units, count, blocks, tokens, head_dim = parts.shape
     step = tokens * units // heads
-    inner = parts * heads * head_dim
-    width = weight.shape[0] if by_last else weight.shape[1]
-    return pl.pallas_call(
-        functools.partial(unproject_kernel, heads=heads, by_last=by_last),
+    inner = count * heads * head_dim
+    width = weight.shape[1]
+    results = pl.pallas_call(
+        functools.partial(unproject_kernel, heads=heads, order=(3, 1, 2, 0)),
         grid=(blocks,),
-        out_shape=(
-            jax.ShapeDtypeStruct((blocks * step, width), jnp.bfloat16),
-            jax.ShapeDtypeStruct((blocks * step, inner), jnp.bfloat16),
-        ),
-        in_specs=[SMEM_SPEC]
-        + [pl.BlockSpec((parts, 1, tokens, head_dim), lambda i: (0, i, 0, 0))] * units
-        + [pl.BlockSpec(weight.shape, lambda i: (0, 0), pipeline_mode=pl.Buffered(1))],
-        out_specs=(
-            pl.BlockSpec((step, width), lambda i: (i, 0)),
-            pl.BlockSpec((step, inner), lambda i: (i, 0)),
-        ),
-        scratch_shapes=[pltpu.VMEM((units, parts, tokens, head_dim), jnp.bfloat16)],
+        out_shape=[jax.ShapeDtypeStruct((step, width), jnp.bfloat16)] * blocks
+        + [jax.ShapeDtypeStruct((blocks, step, inner), jnp.bfloat16)],
+        in_specs=[resident(parts.shape), resident(weight.shape)],
+        out_specs=[pl.BlockSpec((step, width), lambda i: (0, 0))] * blocks
+        + [pl.BlockSpec((blocks, step, inner), lambda i: (0, 0, 0))],
         compiler_params=BIG,
         name="unproject",
-    )(me, *pieces, weight)
+    )(parts, weight)
+    return results[:blocks], results[blocks].reshape(blocks * step, inner)
+
+
+def join_kernel(parts_ref, rows_ref, *, heads, order):
+    units, tokens = parts_ref.shape[0], parts_ref.shape[3]
+    row = 0
+    for j in order:
+        for b in range(units // heads):
+            rows_ref[row : row + tokens] = row_block(parts_ref, j, b, heads)
+            row += tokens
+
+
+def join(parts, heads, order):
+    units, count, blocks, tokens, head_dim = parts.shape
+    return pl.pallas_call(
+        functools.partial(join_kernel, heads=heads, order=order),
+        out_shape=jax.ShapeDtypeStruct(
+            (blocks * tokens * units // heads, count * heads * head_dim), jnp.bfloat16
+        ),
+        in_specs=vmem_specs(1),
+        out_specs=vmem_specs(1)[0],
+        compiler_params=BIG,
+        name="join",
+    )(parts)
 
 
 def mask_of(segc_ref, segr_ref, i, lo):
@@ -697,15 +849,9 @@
     return jnp.logical_and(same, cols <= rows)
 
 
-def collect(me_ref, pieces, held):
-    for d, piece in enumerate(pieces):
-        for j in range(4):
-            held[d ^ me_ref[1], :, j ^ me_ref[0]] = piece[:, j]
-
-
-def take(held, part, first, last, half):
+def take(me_ref, parts_ref, part, first, last, half):
     blocks = [
-        held[4 * (i % half) : 4 * (i % half) + 4, part, i // half].reshape(512, -1)
+        parts_ref[4 * (i % half) : 4 * (i % half) + 4, part, (i // half) ^ me_ref[0]].reshape(512, -1)
         for i in range(first, last + 1)
     ]
     return blocks[0] if len(blocks) == 1 else jnp.concatenate(blocks, axis=0)
@@ -713,19 +859,16 @@
 
 def give(me_ref, out_ref, part, i, half, rows):
     rows = rows.astype(out_ref.dtype).reshape(4, 128, -1)
-    for c in range(4):
-        out_ref[(4 * (i % half) + c) ^ me_ref[1], part, (i // half) ^ me_ref[0]] = rows[c]
-
-
-def fwd_kernel(me_ref, segc_ref, segr_ref, *refs, blocks, scale2):
-    pieces, (out_ref, lse_ref, held) = refs[:-3], refs[-3:]
+    out_ref[4 * (i % half) : 4 * (i % half) + 4, part, (i // half) ^ me_ref[0]] = rows
+
+
+def fwd_kernel(me_ref, segc_ref, segr_ref, parts_ref, out_ref, lse_ref, *, blocks, scale2):
     half = blocks // 4
-    collect(me_ref, pieces, held)
     for i in range(blocks):
         lo = max(i - 1, 0)
-        q = take(held, 0, i, i, half)
-        k = take(held, 1, lo, i, half)
-        v = take(held, 2, lo, i, half)
+        q = take(me_ref, parts_ref, 0, i, i, half)
+        k = take(me_ref, parts_ref, 1, lo, i, half)
+        v = take(me_ref, parts_ref, 2, lo, i, half)
         s = lax.dot_general(q, k, CONTRACT_LAST, preferred_element_type=jnp.float32)
         s = jnp.where(mask_of(segc_ref, segr_ref, i, lo), s * scale2, neg_big)
         m = jnp.max(s, axis=-1, keepdims=True)
@@ -736,19 +879,17 @@
         lse_ref[i] = m + jnp.log2(total)
 
 
-def bwd_kernel(me_ref, segc_ref, segr_ref, lse_ref, *refs, blocks, scale, scale2):
-    grad_ref, held, held_do, dk_acc, dv_acc = refs[-5:]
-    pieces, douts = refs[: (len(refs) - 5) // 2], refs[(len(refs) - 5) // 2 : -5]
+def bwd_kernel(
+    me_ref, segc_ref, segr_ref, lse_ref, parts_ref, do_ref, grad_ref, dk_acc, dv_acc, *, blocks, scale, scale2
+):
     half = blocks // 4
     f32 = jnp.float32
-    collect(me_ref, pieces, held)
-    collect(me_ref, douts, held_do)
     for i in range(blocks):
         lo = max(i - 1, 0)
-        q = take(held, 0, i, i, half)
-        k = take(held, 1, lo, i, half)
-        v = take(held, 2, lo, i, half)
-        do = take(held_do, 0, i, i, half)
+        q = take(me_ref, parts_ref, 0, i, i, half)
+        k = take(me_ref, parts_ref, 1, lo, i, half)
+        v = take(me_ref, parts_ref, 2, lo, i, half)
+        do = take(me_ref, do_ref, 0, i, i, half)
         s = lax.dot_general(q, k, CONTRACT_LAST, preferred_element_type=f32)
         s = jnp.where(mask_of(segc_ref, segr_ref, i, lo), s * scale2, neg_big)
         p = jnp.exp2(s - lse_ref[i])
@@ -772,9 +913,9 @@
             dv_acc[...] = dv[-512:]
 
 
-def attend_fwd(me, segc, segr, pieces):
-    blocks, units = segc.shape[0], len(pieces)
-    parts, narrow, rows, width = pieces[0].shape
+def attend_fwd(me, segc, segr, parts):
+    blocks = segc.shape[0]
+    units, _, narrow, rows, width = parts.shape
     scale2 = math.log2(math.e) / math.sqrt(width)
     return pl.pallas_call(
         functools.partial(fwd_kernel, blocks=blocks, scale2=scale2),
@@ -782,78 +923,140 @@
             jax.ShapeDtypeStruct((units, 1, narrow, rows, width), jnp.bfloat16),
             jax.ShapeDtypeStruct((blocks, 512, 1), jnp.float32),
         ),
-        in_specs=[SMEM_SPEC] + vmem_specs(2 + units),
+        in_specs=[SMEM_SPEC] + vmem_specs(3),
         out_specs=tuple(vmem_specs(2)),
-        scratch_shapes=[pltpu.VMEM((units, parts, narrow, rows, width), jnp.bfloat16)],
         compiler_params=BIG,
         name="attend_fwd",
-    )(me, segc, segr, *pieces)
-
-
-def attend_bwd(me, segc, segr, lse, pieces, douts):
-    blocks, units = segc.shape[0], len(pieces)
-    parts, narrow, rows, width = pieces[0].shape
+    )(me, segc, segr, parts)
+
+
+def attend_bwd(me, segc, segr, lse, parts, dout):
+    blocks = segc.shape[0]
+    width = parts.shape[-1]
     scale = 1.0 / math.sqrt(width)
-    shape = (units, parts, narrow, rows, width)
     return pl.pallas_call(
         functools.partial(
             bwd_kernel, blocks=blocks, scale=scale, scale2=scale * math.log2(math.e)
         ),
-        out_shape=jax.ShapeDtypeStruct(shape, jnp.bfloat16),
-        in_specs=[SMEM_SPEC] + vmem_specs(3 + 2 * units),
+        out_shape=jax.ShapeDtypeStruct(parts.shape, jnp.bfloat16),
+        in_specs=[SMEM_SPEC] + vmem_specs(5),
         out_specs=vmem_specs(1)[0],
-        scratch_shapes=[
-            pltpu.VMEM(shape, jnp.bfloat16),
-            pltpu.VMEM((units, 1, narrow, rows, width), jnp.bfloat16),
-            pltpu.VMEM((512, width), jnp.float32),
-            pltpu.VMEM((512, width), jnp.float32),
-        ],
+        scratch_shapes=[pltpu.VMEM((512, width), jnp.float32)] * 2,
         compiler_params=BIG,
         name="attend_bwd",
-    )(me, segc, segr, lse, *pieces, *douts)
-
-
-def ff_kernel(rows_ref, weight_ref, bias_ref, pull_ref, hidden_ref, grad_ref, sum_ref):
-    step = 256
-    total = jnp.zeros((1, weight_ref.shape[1]), jnp.float32)
-    for r in range(0, rows_ref.shape[0], step):
-        x = jnp.dot(rows_ref[r : r + step], weight_ref[...], preferred_element_type=jnp.float32)
-        x = x + bias_ref[...]
+    )(me, segc, segr, lse, parts, dout)
+
+
+def ff_kernel(*refs, count):
+    rows, weights, (bias_ref, hidden_ref, slope_ref) = refs[:count], refs[count:-3], refs[-3:]
+    step = rows[0].shape[0]
+    depth = rows[0].shape[1] // len(weights)
+    for k, rows_ref in enumerate(rows):
+        r = k * step
+        x = bias_ref[...]
+        for n, weight_ref in enumerate(weights):
+            x = x + jnp.dot(
+                rows_ref[:, n * depth : (n + 1) * depth],
+                weight_ref[...].reshape(depth, -1),
+                preferred_element_type=jnp.float32,
+            )
         below = 0.5 * (1.0 + lax.erf(x * math.sqrt(0.5)))
         hidden_ref[r : r + step] = (x * below).astype(jnp.bfloat16)
-        slope = below + x * (jnp.exp(-0.5 * x * x) * (1.0 / math.sqrt(2.0 * math.pi)))
-        grad = (pull_ref[r : r + step] * slope).astype(jnp.bfloat16)
+        slope_ref[r : r + step] = below + x * (
+            jnp.exp(-0.5 * x * x) * (1.0 / math.sqrt(2.0 * math.pi))
+        )
+
+
+def feed_forward(rows, weight, bias):
+    count = len(rows) * rows[0].shape[0]
+    deep, narrow, shard, inner = weight.shape
+    step = 256
+    return pl.pallas_call(
+        functools.partial(ff_kernel, count=len(rows)),
+        grid=(inner // step,),
+        out_shape=(
+            jax.ShapeDtypeStruct((count, inner), jnp.bfloat16),
+            jax.ShapeDtypeStruct((count, inner), jnp.float32),
+        ),
+        in_specs=[resident(block.shape) for block in rows]
+        + [
+            pl.BlockSpec((deep, 1, shard, step), lambda i, n=n: (0, n, 0, i)) for n in range(narrow)
+        ]
+        + [pl.BlockSpec((1, step), lambda i: (0, i))],
+        out_specs=(
+            pl.BlockSpec((count, step), lambda i: (0, i)),
+            pl.BlockSpec((count, step), lambda i: (0, i)),
+        ),
+        compiler_params=BIG,
+        name="feed_forward",
+    )(*rows, *[weight] * narrow, bias.reshape(1, -1))
+
+
+def pull_kernel(rows_ref, weight_ref, slope_ref, grad_ref, sum_ref):
+    step = 256
+    total = jnp.zeros((1, weight_ref.shape[0]), jnp.float32)
+    for r in range(0, rows_ref.shape[0], step):
+        pull = lax.dot_general(
+            rows_ref[r : r + step],
+            weight_ref[...],
+            CONTRACT_LAST,
+            preferred_element_type=jnp.float32,
+        )
+        grad = (pull * slope_ref[r : r + step]).astype(jnp.bfloat16)
         grad_ref[r : r + step] = grad
         total = total + jnp.sum(grad.astype(jnp.float32), axis=0, keepdims=True)
     sum_ref[...] = total
 
 
-def feed_forward(rows, weight, bias, pull):
-    count, width = rows.shape
-    inner = weight.shape[1]
+def pull_back(rows, weight, slope):
+    count, inner = slope.shape
+    width = weight.shape[1]
     step = 256
     return pl.pallas_call(
-        ff_kernel,
+        pull_kernel,
         grid=(inner // step,),
         out_shape=(
-            jax.ShapeDtypeStruct((count, inner), jnp.bfloat16),
             jax.ShapeDtypeStruct((count, inner), jnp.bfloat16),
             jax.ShapeDtypeStruct((1, inner), jnp.float32),
         ),
         in_specs=[
-            pl.BlockSpec((count, width), lambda i: (0, 0), pipeline_mode=pl.Buffered(1)),
-            pl.BlockSpec((width, step), lambda i: (0, i)),
-            pl.BlockSpec((1, step), lambda i: (0, i)),
+            resident(rows.shape),
+            pl.BlockSpec((step, width), lambda i: (i, 0)),
             pl.BlockSpec((count, step), lambda i: (0, i)),
         ],
         out_specs=(
             pl.BlockSpec((count, step), lambda i: (0, i)),
-            pl.BlockSpec((count, step), lambda i: (0, i)),
             pl.BlockSpec((1, step), lambda i: (0, i)),
         ),
         compiler_params=BIG,
-        name="feed_forward",
-    )(rows, weight, bias.reshape(1, -1), pull)
+        name="pull_back",
+    )(rows, weight, slope)
+
+
+def pick_kernel(me_ref, weight_ref, out_ref):
+    _, narrow, shard, inner = out_ref.shape
+    high = (me_ref[1] & 1) > 0
+    step = 256
+    for n in range(narrow):
+        for z in range(inner // step):
+            c = (n * (inner // step) + z) * 2 * step
+            low_part = weight_ref[:, c : c + step]
+            high_part = weight_ref[:, c + step : c + 2 * step]
+            cols = slice(z * step, (z + 1) * step)
+            out_ref[0, n, :, cols] = jnp.where(high, high_part, low_part)
+            out_ref[1, n, :, cols] = jnp.where(high, low_part, high_part)
+
+
+def pick(me, weight, narrow):
+    shard, total = weight.shape
+    return pl.pallas_call(
+        pick_kernel,
+        out_shape=jax.ShapeDtypeStruct((2, narrow, shard, total // (2 * narrow)), weight.dtype),
+        in_specs=[SMEM_SPEC] + vmem_specs(1),
+        out_specs=vmem_specs(1)[0],
+        compiler_params=BIG,
+        name="pick",
+    )(me, weight)
 
 
 def on_device(
@@ -894,27 +1097,6 @@
     ff_local = ff_shard * deep
     me_y = me_w & 1
 
-    smalls = [
-        attn_gain, attn_shift, out_bias, mlp_gain, mlp_shift, down_bias, query_bias, value_bias, up_bias
-    ]
-    ids = segment_ids.astype(bf16).reshape(-1)
-    small = cube_gather(jnp.concatenate(smalls + [ids])[None])
-    ids = small[:, -batch * tokens :].reshape(narrow * wide, batch, tokens)
-    unit_ids = at(ids, me_w // heads, 1).reshape(-1).astype(jnp.int32)
-    segc = unit_ids.reshape(-1, 512, 1)
-    segr = unit_ids.reshape(1, -1)
-
-    def full_vector(k):
-        return small[:, k * shard : (k + 1) * shard].reshape(-1).astype(f32)
-
-    gain_attn, shift_attn, obias, gain_mlp, shift_mlp, dbias = [full_vector(k) for k in range(6)]
-    mine = lax.dynamic_slice_in_dim(small, me_n * wide, wide, 0)
-    qbias = mine[:, 6 * shard : 7 * shard].reshape(-1).astype(f32)
-    vbias = mine[:, 7 * shard : 8 * shard].reshape(-1).astype(f32)
-    ubias = mine[:, 8 * shard : 8 * shard + ff_shard].reshape(deep, 2, ff_shard)
-    ubias = at(ubias, me_y, 1).reshape(-1).astype(f32)
-    qkv_bias = jnp.concatenate([qbias, jnp.zeros_like(qbias), vbias])
-
     def qkv_block(n):
         return jnp.concatenate(
             [
@@ -924,80 +1106,148 @@
             axis=1,
         )
 
-    qkv_w = ring_gather(narrow_swap(qkv_block), 1).reshape(width, 3 * cols)
     out_w = wide_gather(out_weight, 0)
+    qkv_shard = narrow_swap(qkv_block)
+    attn_parts = ring_gather(qkv_shard)
+
+    smalls = [
+        attn_gain, attn_shift, out_bias, mlp_gain, mlp_shift, down_bias, query_bias, value_bias, up_bias
+    ]
+    ids = segment_ids.astype(bf16).reshape(-1)
+    small = cube_gather(hold(jnp.concatenate(smalls + [ids])[None], qkv_shard))
+
+    def full_vector(k):
+        return small[:, k * shard : (k + 1) * shard].reshape(-1).astype(f32)
+
+    gain_attn, shift_attn, obias, gain_mlp, shift_mlp, dbias = [full_vector(k) for k in range(6)]
+    mine = lax.dynamic_slice_in_dim(small, me_n * wide, wide, 0)
+    qbias = mine[:, 6 * shard : 7 * shard].reshape(-1).astype(f32)
+    vbias = mine[:, 7 * shard : 8 * shard].reshape(-1).astype(f32)
+    ubias = mine[:, 8 * shard : 8 * shard + ff_shard].reshape(deep, 2, ff_shard)
+    ubias = at(ubias, me_y, 1).reshape(-1).astype(f32)
+    qkv_bias = jnp.concatenate([qbias, jnp.zeros_like(qbias), vbias])
 
     inputs = block_input.astype(f32).reshape(rows, width)
     first_norm = narrow_gather(normalize(inputs, gain_attn, shift_attn).astype(bf16))
     cotan_own = cotangent.reshape(rows, width)
-    cotan = spread(hold(cotan_own, first_norm))
-
-    down_w = z_gather(hold(down_weight, qkv_w), 0)
-    up_cols = hold(up_weight, first_norm).reshape(shard, narrow, deep, 2, ff_shard)
-    up_shard = pair_swap(lambda y: at(up_cols, y, 3).reshape(shard, narrow, ff_local))
-    up_pair = up_shard
-    up_shard = narrow_swap(lambda n: at(up_pair, n, 2))
-    up_shard = up_shard.reshape(narrow, 2 * shard, ff_local)
-    up_w = z_gather(hold(up_shard, qkv_w), 1).reshape(width, ff_local)
-
-    sent = project(me, first_norm, qkv_w, qkv_bias, wide, 3, heads, tokens, False)
+    attn_parts = hold(attn_parts, out_w)
+    sent = project_parts(first_norm, attn_parts, qkv_bias, wide, 3, heads, tokens)
     qkv = wide_swap(sent)
+
+    picked = pick(me, hold(up_weight, first_norm[3]), narrow)
+    high = me_y > 0
+    here, there = picked[0], flip(hold(picked[1], sent), WIDE, 1)
+    up_pair = jnp.stack([jnp.where(high, there, here), jnp.where(high, here, there)], axis=1)
+    up_shard = narrow_swap(lambda n: at(up_pair, n)).reshape(narrow, 2 * shard, ff_local)
+    ids = hold(small, sent)[:, -batch * tokens :].reshape(narrow * wide, batch, tokens)
+    unit_ids = at(ids, me_w // heads, 1).reshape(-1).astype(jnp.int32)
+    segc = unit_ids.reshape(-1, 512, 1)
+    segr = unit_ids.reshape(1, -1)
+    qkv = hold(qkv, up_shard)
     unit_out, lse = attend_fwd(me, segc, segr, qkv)
-    partial, mixed = unproject(me, wide_swap(unit_out), out_w, heads, False)
+    up_parts = z_gather(hold(up_shard, unit_out)[None], 0)
+    unit_back = wide_swap(unit_out)
+    near = spread_near(hold(cotan_own, unit_out))
+    unit_back = hold(unit_back, *near)
+    cotan = jnp.concatenate(near + [flip(hold(part, unit_back), NARROW, 1) for part in near], axis=0)
+    partial, mixed = unproject(unit_back, out_w, heads)
     middle = inputs + narrow_scatter(partial) + obias
-
-    hidden_grad = times_transpose(cotan, down_w)
+    down_late, middle = lax.optimization_barrier((down_weight, middle, up_parts, cotan))[:2]
+    down_w = z_gather(down_late, 0)
+
     second_norm = spread(normalize(middle, gain_mlp, shift_mlp).astype(bf16))
-    hidden, inner_grad, ubias_grad = feed_forward(second_norm, up_w, ubias, hidden_grad)
-    second_part = times_transpose(inner_grad, up_w).astype(bf16)
-    second_grad = fold(second_part)
-    hidden_late = hold(hidden, second_part)
-    down_grad = z_scatter(outer_sum(hidden_late, cotan), 0)
-    up_grad = outer_sum(second_norm, hold(inner_grad, second_part))
-    up_grad = z_scatter(up_grad.reshape(narrow, 2 * deep * shard, ff_local), 1)
+    hidden, slope = feed_forward(second_norm, up_parts, ubias)
+    down_grad = outer_sum(hidden, cotan).astype(bf16)
+    slope = hold(slope, down_grad)
+    down_grad = z_scatter(down_grad, 0)
+    inner_grad, ubias_grad = pull_back(cotan, down_w, slope)
+    split = inner_grad.shape[0] // 2
+    far = times_parts(inner_grad, 1, split, up_parts)
+    near = times_parts(hold(inner_grad, far), 0, split, up_parts)
+    norm_rows = jnp.concatenate(second_norm, axis=0)
+    up_made = []
+
+    def make_up_grad(event):
+        up_made.append(outer_sum(norm_rows, hold(inner_grad, event)).astype(bf16))
+        return up_made[0]
+
+    second_grad = fold(far, near, make_up_grad)
     mlp_pull = jax.vjp(normalize, middle, gain_mlp, shift_mlp)[1]
     middle_part, mgain_grad, mshift_grad = mlp_pull(second_grad)
+    middle_grad = cotan_own.astype(f32) + middle_part
+    branch_own = middle_grad.astype(bf16)
     dbias_grad = jnp.sum(cotan_own.astype(f32), axis=0)
-    middle_grad = cotan_own.astype(f32) + middle_part
-
-    branch_own = middle_grad.astype(bf16)
+
     obias_grad = jnp.sum(branch_own.astype(f32), axis=0)
-    branch = narrow_gather(branch_own)
+    hidden_late = hold(hidden, branch_own)
+    out_far = matmul(hidden_late[split:], down_w).astype(bf16)
+    out_near = matmul(hidden_late[:split], down_w).astype(bf16)
+    branch = narrow_gather(branch_own, out_far, out_near)
+    up_grad = hold(up_made[0], branch[2], down_grad)
+    up_grad = z_scatter(up_grad.reshape(narrow, 2 * deep * shard, ff_local), 1)
     no_bias = jnp.zeros((cols,), f32)
-    sent = project(me, branch, out_w, no_bias, wide, 1, heads, tokens, True)
-    unit_grads = attend_bwd(me, segc, segr, lse, qkv, wide_swap(sent))
-    out_grad = wide_scatter(outer_sum(mixed, hold(branch, sent)), 0)
-    output = middle + fold(matmul(hold(hidden, unit_grads), down_w).astype(bf16)) + dbias
+    sent = project(branch, out_w, no_bias, wide, 1, heads, tokens, True)
+    out_grad = outer_sum(hold(mixed, sent), jnp.concatenate(branch, axis=0)).astype(bf16)
+    output = middle + fold(out_far, out_near) + dbias
     block_output = output.astype(bf16).reshape(batch, tokens, width)
-    up_grad = up_grad.reshape(narrow, 2, shard, ff_local)
-    up_rows = up_grad
+    dout = hold(wide_swap(sent), out_grad, block_output)
+    unit_grads = attend_bwd(me, segc, segr, lse, qkv, dout)
+    grads = wide_swap(unit_grads)
+    up_rows = hold(up_grad, unit_grads).reshape(narrow, 2, shard, ff_local)
     up_swapped = narrow_swap(lambda n: at(up_rows, n))
     up_back = pair_swap(lambda y: at(up_swapped, y, 1))
     up_back = up_back.reshape(2, narrow, shard, deep, ff_shard).transpose(2, 1, 3, 0, 4)
-    up_back = up_back.reshape(shard, -1)
-    partial, back = unproject(me, wide_swap(unit_grads), qkv_w, heads, True)
-    first_grad = narrow_scatter(partial)
-    qkv_grad = outer_sum(first_norm, back).astype(bf16).reshape(narrow, wide, shard, 3 * cols)
-    qkv_grad = ring_scatter(qkv_grad, 1).astype(bf16)
-    qkv_rows = qkv_grad
-    qkv_grad = narrow_swap(lambda n: at(qkv_rows, n)).reshape(narrow, shard, 3, cols)
+    up_back = up_back.reshape(shard, -1).astype(f32)
+    down_grad = down_grad.astype(f32)
+    grads = hold(grads, up_back)
+    order = (1, 3, 0, 2)
+    back = join(grads, heads, order)
+    sums = wide_outer([first_norm[j] for j in order], back, out_grad, wide)
+    made = {}
+
+    def beside(stage, event):
+        if stage == 0:
+            late = hold(back, event)
+            far = times_parts(late, 0, 2 * rows, attn_parts)
+            near = times_parts(hold(late, far), 1, 2 * rows, attn_parts)
+            made["far"] = far.reshape(2, rows, width)
+            made["near"] = near.reshape(2, rows, width)
+            return far, near
+        if stage == 1:
+            near, far = made["near"], made["far"]
+            made["first"] = narrow_scatter([near[0], far[0], near[1], far[1]])
+            return (made["first"],)
+        if stage == 2:
+            attn_pull = jax.vjp(normalize, inputs, gain_attn, shift_attn)[1]
+            input_part, again_grad, ashift_grad = attn_pull(made["first"])
+            made["pulled"] = middle_grad + input_part, again_grad, ashift_grad
+            return made["pulled"] + (down_grad,)
+        return ()
+
+    qkv_rows = ring_scatter(sums, beside).astype(bf16)
+    out_grad = qkv_rows[..., 3 * cols :].transpose(1, 0, 2).reshape(shard, width)
+    qkv_rows = qkv_rows[..., : 3 * cols]
+    swapped = narrow_blocks(lambda n: at(qkv_rows, n))
+    qkv_grad = in_order(swapped).reshape(narrow, shard, 3, cols)
     qkv_grad = qkv_grad.transpose(2, 1, 0, 3).reshape(3, shard, width).astype(f32)
     back_sums = jnp.sum(back.astype(f32), axis=0)
-    attn_pull = jax.vjp(normalize, inputs, gain_attn, shift_attn)[1]
-    input_part, again_grad, ashift_grad = attn_pull(first_grad)
-    input_grad = (middle_grad + input_part).reshape(batch, tokens, width)
+    input_grad, again_grad, ashift_grad = made["pulled"]
+    input_grad = input_grad.reshape(batch, tokens, width)
 
     fulls = [again_grad, ashift_grad, obias_grad, mgain_grad, mshift_grad, dbias_grad]
     fulls = jnp.concatenate([v.reshape(narrow * wide, shard) for v in fulls], axis=1)
     ubias_rows = jnp.zeros((deep, 2, ff_shard), f32)
     ubias_rows = lax.dynamic_update_slice_in_dim(
-        ubias_rows, ubias_grad.reshape(deep, 1, ff_shard), me_y, 1
+        ubias_rows,
+        ubias_grad.reshape(deep, 1, ff_shard),
+        me_y,
+        1,
     )
     slices = [back_sums[:cols], back_sums[2 * cols :], ubias_rows]
     slices = jnp.concatenate([v.reshape(wide, -1) for v in slices], axis=1)
     placed = jnp.zeros((narrow * wide, slices.shape[1]), f32)
     placed = lax.dynamic_update_slice_in_dim(placed, slices, me_n * wide, 0)
-    vectors = cube_scatter(jnp.concatenate([fulls, placed], axis=1))
+    vectors = cube_scatter(hold(jnp.concatenate([fulls, placed], axis=1), swapped[1]))
 
     def vector(k):
         return vectors[k * shard : (k + 1) * shard]
@@ -1016,9 +1266,9 @@
         vector(2),
         vector(3),
         vector(4),
-        up_back.astype(f32),
+        up_back,
         vectors[8 * shard :],
-        down_grad.astype(f32),
+        down_grad,
         vector(5),
     )
 

time: 985 us -> 873 us (0.89)
  starting transfers between devices: 200 us -> 89.9 us
  Pallas kernels: 80.9 us -> 123 us
  matrix products: 82.9 us -> 45.9 us
  other arithmetic: 78 us -> 63.8 us
    ppermute x96 -> x62, starting transfers between devices: 186 us -> 50.9 us  [flip(): return lax.ppermute(value, axis, [(i, i ^ bits) for i in range(size)])]
    pallas_call x3 -> x11, Pallas kernels: 37.1 us -> 92.1 us  [the longest x4 27 us: times_parts(): pl.pallas_call(times_parts_kernel, grid=(narrow,), out_shape=jax.ShapeDty...]
    ppermute x96 -> x62, waiting for transfers between devices: 312 us -> 262 us  [flip(): return lax.ppermute(value, axis, [(i, i ^ bits) for i in range(size)])]
    all_to_all x0 -> x4, waiting for transfers between devices: none -> 29.9 us  [wide_swap(): return lax.all_to_all(parts, WIDE, split_axis=0, concat_axis=0, tiled=True)]
    dot_general x2 -> x0, matrix products: 29.6 us -> none  [times_transpose(): lax.dot_general(left, right, (((1,), (1,)), ((), ())), preferred_element_...]
    ppermute x14 -> x16, waiting for transfers between devices: 91.8 us -> 119 us  [ring_step(): lax.ppermute(value, WIDE, [(order[i], order[(i + by) % size]) for i in ra...]
    unnamed x120 -> x142, local copies, waits for them, and re-layouts: 28.9 us -> 54.6 us
    all_to_all x0 -> x4, starting transfers between devices: none -> 18.9 us  [wide_swap(): return lax.all_to_all(parts, WIDE, split_axis=0, concat_axis=0, tiled=True)]
  transfers between devices with their start and end apart: 116 -> 87, of which waited for: 48 -> 52; matrix products, arithmetic and copies ran while one was open for 24% -> 22% of each run, Pallas kernels for 6% -> 8%
where the time goes in v4:
time: 873 us; the launch traced here: 864 us
  waiting for transfers between devices  412 us (47%)
  Pallas kernels  123 us (14%)
  local copies, waits for them, and re-layouts  114 us (13%)
  starting transfers between devices  89.9 us (10%)
  other arithmetic  63.8 us (7%)
  matrix products  45.9 us (5%)
  between operations  15.6 us (2%)
    ppermute x62, waiting for transfers between devices, flip(): return lax.ppermute(value, axis, [(i, i ^ bits) for i in range(size)])  262 us
    ppermute x16, waiting for transfers between devices, ring_step(): lax.ppermute(value, WIDE, [(order[i], order[(i + by) % size]) for i in ra...  119 us
    unnamed x142, local copies, waits for them, and re-layouts  54.6 us
    ppermute x62, starting transfers between devices, flip(): return lax.ppermute(value, axis, [(i, i ^ bits) for i in range(size)])  50.9 us
    dot_general x3, matrix products, outer_sum(): lax.dot_general(left, right, (((0,), (0,)), ((), ())), preferred_element_...  33.7 us
    all_to_all x4, waiting for transfers between devices, wide_swap(): return lax.all_to_all(parts, WIDE, split_axis=0, concat_axis=0, tiled=True)  29.9 us
    pallas_call x4, Pallas kernels, times_parts(): pl.pallas_call(times_parts_kernel, grid=(narrow,), out_shape=jax.ShapeDty...  27 us
    ppermute x16, starting transfers between devices, ring_step(): lax.ppermute(value, WIDE, [(order[i], order[(i + by) % size]) for i in ra...  19 us
  transfers between devices with their start and end apart: 87, of which 52 were waited for; matrix products, arithmetic and copies ran while one was open for 22% of the time, Pallas kernels for 8%

profile of v4, /device:TPU:0, one launch (start us, length us, event | category | flops | bytes accessed | tf_op | source)
XLA Modules:
  0.0 863.7 jit_solution(2688589291181785212)
XLA Ops:
  13.7 4.9 collective-permute-done
  18.6 4.4 collective-permute-done.1
  40.4 3.3 broadcast_in_dim.71
  46.2 23.2 %collective-permute-done.11 = bf16[4,64,1536]{2,1,0:T(8,128)(2,1)} collective-permute-done((bf16[4,64,1536]{2,1,0:T(8,128)(2,1)}, bf16[4,64,1536]{2,1,0:T(8,128)(2,1)}, u32[]{:S(2)}, u32[]{:S(2)}) %collective-permute-start.11) | collective-permute-done | bytes 786464 | tf_op jit(solution)/shard_map/ppermute | solution.py:535
  69.4 4.9 collective-permute-start.13
  79.3 13.1 %collective-permute-done.13 = bf16[4,64,1536]{2,1,0:T(8,128)(2,1)S(1)} collective-permute-done((bf16[4,64,1536]{2,1,0:T(8,128)(2,1)}, bf16[4,64,1536]{2,1,0:T(8,128)(2,1)S(1)}, u32[]{:S(2)}, u32[]{:S(2)}) %collective-permute-start.13) | collective-permute-done | bytes 786464 | tf_op jit(solution)/shard_map/ppermute | solution.py:535
  96.4 14.3 %collective-permute-done.15 = bf16[4,64,1536]{2,1,0:T(8,128)(2,1)S(1)} collective-permute-done((bf16[4,64,1536]{2,1,0:T(8,128)(2,1)S(1)}, bf16[4,64,1536]{2,1,0:T(8,128)(2,1)S(1)}, u32[]{:S(2)}, u32[]{:S(2)}) %collective-permute-start.15) | collective-permute-done | bytes 786464 | tf_op jit(solution)/shard_map/ppermute | solution.py:535
  114.7 4.9 collective-permute-done.17
  121.7 11.5 %project_parts.1 = bf16[8,3,4,128,128]{4,3,2,1,0:T(8,128)(2,1)} custom-call(bf16[256,2048]{1,0:T(8,128)(2,1)S(1)} %fusion.32.refs_0_.refs_8_.refs_9_.refs_10_.refs_11_, bf16[256,2048]{1,0:T(8,128)(2,1)S(1)} %collective-permute-done.8.refs_1_.refs_0_.refs_2_.refs_3_, bf16[256,2048]{1,0:T(8,128)(2,1)S(1)} %collective-permute-done.9.refs_2_.refs_12_.refs_13_.refs_14_.refs_15_, ...), custom_call_target="tpu_custom_call" | custom-call | tf_op jit(solution)/shard_map/project_parts/pallas_call | solution.py:689
  133.2 5.8 all-to-all-start
  145.1 3.3 reshape.454.segc_ref
  148.4 31.0 %collective-permute-done.19 = bf16[4,64,1024]{2,1,0:T(8,128)(2,1)} collective-permute-done((bf16[4,64,1024]{2,1,0:T(8,128)(2,1)}, bf16[4,64,1024]{2,1,0:T(8,128)(2,1)}, u32[]{:S(2)}, u32[]{:S(2)}) %collective-permute-start.19) | collective-permute-done | bytes 524320 | tf_op jit(solution)/shard_map/ppermute | solution.py:379
  183.0 6.1 collective-permute-done.20
  189.1 6.0 collective-permute-done.21
  196.4 10.6 %all-to-all-done.parts_ref = bf16[8,3,4,128,128]{4,3,2,1,0:T(8,128)(2,1)} async-done(((bf16[8,3,4,128,128]{4,3,2,1,0:T(8,128)(2,1)}), bf16[8,3,4,128,128]{4,3,2,1,0:T(8,128)(2,1)}, u32[]{:S(2)}, u32[]{:S(2)}) %all-to-all-start) | async-done | bytes 3145760 | tf_op jit(solution)/shard_map/all_to_all | solution.py:597
  208.6 8.2 attend_fwd.1
  220.6 4.2 all-to-all-start.1
  227.0 24.7 %collective-permute-done.24 = bf16[256,2048]{1,0:T(8,128)(2,1)} collective-permute-done((bf16[256,2048]{1,0:T(8,128)(2,1)}, bf16[256,2048]{1,0:T(8,128)(2,1)}, u32[]{:S(2)}, u32[]{:S(2)}) %collective-permute-start.24) | collective-permute-done | bytes 1048608 | tf_op jit(solution)/shard_map/ppermute | solution.py:379
  265.4 3.1 collective-permute-done.26
  269.6 8.2 all-to-all-done.1.parts_ref
  277.8 5.9 unproject.1
  300.7 14.3 %collective-permute-done.29 = bf16[256,2048]{1,0:T(8,128)(2,1)} collective-permute-done((bf16[256,2048]{1,0:T(8,128)(2,1)}, bf16[256,2048]{1,0:T(8,128)(2,1)}, u32[]{:S(2)}, u32[]{:S(2)}) %collective-permute-start.29) | collective-permute-done | bytes 1048608 | tf_op jit(solution)/shard_map/ppermute | solution.py:379
  315.0 3.5 fusion.37
  326.7 22.7 %collective-permute-done.35.refs_2_ = bf16[256,2048]{1,0:T(8,128)(2,1)} collective-permute-done((bf16[256,2048]{1,0:T(8,128)(2,1)}, bf16[256,2048]{1,0:T(8,128)(2,1)}, u32[]{:S(2)}, u32[]{:S(2)}) %collective-permute-start.35) | collective-permute-done | bytes 1048608 | tf_op jit(solution)/shard_map/ppermute | solution.py:379
  359.5 3.3 collective-permute-done.36
  363.9 3.6 collective-permute-done.37
  368.7 2.9 collective-permute-done.41.refs_7_
  371.6 18.3 %feed_forward.1 = (bf16[2048,1024]{1,0:T(8,128)(2,1)}, f32[2048,1024]{1,0:T(8,128)}) custom-call(bf16[256,2048]{1,0:T(8,128)(2,1)} %get-tuple-element.129.refs_0_, bf16[256,2048]{1,0:T(8,128)(2,1)} %collective-permute-done.34.refs_1_, bf16[256,2048]{1,0:T(8,128)(2,1)} %collective-permute-done.35.refs_2_, bf16[256,2048]{1,0:T(8,128)(2,1)} %get-tuple-element.185.refs_3_, ...), custom_call_target="tpu_custom_call" | custom-call | tf_op jit(solution)/shard_map/feed_forward/pallas_call | solution.py:974
  389.9 14.1 %convolution_convert_fusion = bf16[1024,2048]{1,0:T(8,128)(2,1)} fusion(bf16[2048,1024]{1,0:T(8,128)(2,1)} %get-tuple-element.92, bf16[2048,2048]{1,0:T(8,128)(2,1)} %constant_dynamic-update-slice_fusion.2.rows_ref), kind=kOutput, calls=%fused_computation.9 | convolution fusion | flops 8592031744 | bytes 16777216 | tf_op jit(solution)/shard_map/dot_general | solution.py:46
  403.9 14.6 %pull_back.1 = (bf16[2048,1024]{1,0:T(8,128)(2,1)S(1)}, f32[1,1024]{1,0:T(1,128)S(1)}) custom-call(bf16[2048,2048]{1,0:T(8,128)(2,1)} %constant_dynamic-update-slice_fusion.2.rows_ref, bf16[1024,2048]{1,0:T(8,128)(2,1)} %all-gather.7.cloned.1.call-done.weight_ref, f32[2048,1024]{1,0:T(8,128)} %get-tuple-element.87.slope_ref), custom_call_target="tpu_custom_call" | custom-call | tf_op jit(solution)/shard_map/pull_back/pallas_call | solution.py:1015
  420.7 7.4 times_parts.4
  430.5 7.4 times_parts.5
  437.9 3.8 convert_add_fusion.11
  454.1 4.0 collective-permute-done.43
  460.0 8.8 %collective-permute-done.45 = bf16[256,1024]{1,0:T(8,128)(2,1)S(1)} collective-permute-done((bf16[256,1024]{1,0:T(8,128)(2,1)}, bf16[256,1024]{1,0:T(8,128)(2,1)S(1)}, u32[]{:S(2)}, u32[]{:S(2)}) %collective-permute-start.45) | collective-permute-done | bytes 524320 | tf_op jit(solution)/shard_map/ppermute | solution.py:379
  469.6 13.3 %convolution_convert_fusion.3 = bf16[2048,1024]{1,0:T(8,128)(2,1)} fusion(bf16[2048,2048]{1,0:T(8,128)(2,1)} %constant_dynamic-update-slice_fusion.12, bf16[2048,1024]{1,0:T(8,128)(2,1)S(1)} %copy-done.5), kind=kOutput, calls=%fused_computation.12 | convolution fusion | flops 8592031744 | bytes 16777216 | tf_op jit(solution)/shard_map/dot_general | solution.py:46
  482.9 7.3 collective-permute-done.44
  492.5 2.8 multiply_reduce_fusion
  500.3 6.1 convolution_convert_fusion.1
  506.8 6.1 convolution_convert_fusion.2
  512.8 19.3 %collective-permute-done.53.refs_2_ = bf16[256,2048]{1,0:T(8,128)(2,1)} collective-permute-done((bf16[256,2048]{1,0:T(8,128)(2,1)S(1)}, bf16[256,2048]{1,0:T(8,128)(2,1)}, u32[]{:S(2)}, u32[]{:S(2)}) %collective-permute-start.53) | collective-permute-done | bytes 1048608 | tf_op jit(solution)/shard_map/ppermute | solution.py:379
  532.8 6.2 convert_add_fusion.7
  540.6 5.1 project.1
  548.7 4.4 all-to-all-start.2
  560.4 14.8 %collective-permute-done.48 = bf16[256,1024]{1,0:T(8,128)(2,1)S(1)} collective-permute-done((bf16[256,1024]{1,0:T(8,128)(2,1)}, bf16[256,1024]{1,0:T(8,128)(2,1)S(1)}, u32[]{:S(2)}, u32[]{:S(2)}) %collective-permute-start.48) | collective-permute-done | bytes 524320 | tf_op jit(solution)/shard_map/ppermute | solution.py:379
  578.0 6.3 fusion.8.refs_17_
  584.3 16.7 %collective-permute-done.51 = bf16[256,2048]{1,0:T(8,128)(2,1)} collective-permute-done((bf16[256,2048]{1,0:T(8,128)(2,1)}, bf16[256,2048]{1,0:T(8,128)(2,1)}, u32[]{:S(2)}, u32[]{:S(2)}) %collective-permute-start.51) | collective-permute-done | bytes 1048608 | tf_op jit(solution)/shard_map/ppermute | solution.py:379
  601.0 4.1 fusion.22
  610.5 17.5 %attend_bwd.1 = bf16[8,3,4,128,128]{4,3,2,1,0:T(8,128)(2,1)} custom-call(s32[2]{0:T(128)S(1)} %pad_add_fusion.me_ref, s32[8,512,1]{2,1,0:T(8,128)S(1)} %copy-done.3, s32[1,4096]{1,0:T(1,128)S(1)} %convert_bitcast_fusion.3.segr_ref, f32[8,512,1]{2,1,0:T(8,128)S(1)} %copy-done.12, bf16[8,3,4,128,128]{4,3,2,1,0:T(8,128)(2,1)} %all-to-all-done.parts_ref, ...), custom_call_target="tpu_custom_call" | custom-call | tf_op jit(solution)/shard_map/attend_bwd/pallas_call | solution.py:937
  628.1 4.5 all-to-all-start.3
  636.4 7.6 collective-permute-done.56
  644.0 4.8 collective-permute-done.55
  652.2 28.3 %collective-permute-done.58 = bf16[4,64,1024]{2,1,0:T(8,128)(2,1)S(1)} collective-permute-done((bf16[4,64,1024]{2,1,0:T(8,128)(2,1)S(1)}, bf16[4,64,1024]{2,1,0:T(8,128)(2,1)S(1)}, u32[]{:S(2)}, u32[]{:S(2)}) %collective-permute-start.58) | collective-permute-done | bytes 524320 | tf_op jit(solution)/shard_map/ppermute | solution.py:379
  687.9 2.9 copy.54
  690.8 3.9 reshape.446
  694.7 8.8 %all-to-all-done.3.parts_ref = bf16[8,3,4,128,128]{4,3,2,1,0:T(8,128)(2,1)} async-done(((bf16[8,3,4,128,128]{4,3,2,1,0:T(8,128)(2,1)}), bf16[8,3,4,128,128]{4,3,2,1,0:T(8,128)(2,1)}, u32[]{:S(2)}, u32[]{:S(2)}) %all-to-all-start.3) | async-done | bytes 3145760 | tf_op jit(solution)/shard_map/all_to_all | solution.py:597
  707.6 11.8 %wide_outer.1 = bf16[8,4,64,2048]{3,2,1,0:T(8,128)(2,1)} custom-call(bf16[256,2048]{1,0:T(8,128)(2,1)S(1)} %collective-permute-done.8.refs_1_.refs_0_.refs_2_.refs_3_, bf16[256,2048]{1,0:T(8,128)(2,1)S(1)} %collective-permute-done.8.refs_1_.refs_0_.refs_2_.refs_3_, bf16[256,2048]{1,0:T(8,128)(2,1)S(1)} %collective-permute-done.8.refs_1_.refs_0_.refs_2_.refs_3_, ...), custom_call_target="tpu_custom_call" | custom-call | tf_op jit(solution)/shard_map/wide_outer/pallas_call | solution.py:757
  724.8 6.0 times_parts.6
  734.1 6.2 times_parts.7
  750.2 19.7 %collective-permute-done.64 = bf16[4,64,2048]{2,1,0:T(8,128)(2,1)S(1)} collective-permute-done((bf16[4,64,2048]{2,1,0:T(8,128)(2,1)S(1)}, bf16[4,64,2048]{2,1,0:T(8,128)(2,1)S(1)}, u32[]{:S(2)}, u32[]{:S(2)}) %collective-permute-start.64) | collective-permute-done | bytes 1048608 | tf_op jit(solution)/shard_map/ppermute | solution.py:535
  779.3 19.6 %collective-permute-done.66 = bf16[4,64,2048]{2,1,0:T(8,128)(2,1)S(1)} collective-permute-done((bf16[4,64,2048]{2,1,0:T(8,128)(2,1)S(1)}, bf16[4,64,2048]{2,1,0:T(8,128)(2,1)S(1)}, u32[]{:S(2)}, u32[]{:S(2)}) %collective-permute-start.66) | collective-permute-done | bytes 1048608 | tf_op jit(solution)/shard_map/ppermute | solution.py:535
  805.6 19.7 %collective-permute-done.68 = bf16[4,64,2048]{2,1,0:T(8,128)(2,1)} collective-permute-done((bf16[4,64,2048]{2,1,0:T(8,128)(2,1)}, bf16[4,64,2048]{2,1,0:T(8,128)(2,1)}, u32[]{:S(2)}, u32[]{:S(2)}) %collective-permute-start.68) | collective-permute-done | bytes 1048608 | tf_op jit(solution)/shard_map/ppermute | solution.py:535
  837.4 3.8 collective-permute-done.76
  841.2 4.3 collective-permute-done.77
  (452 shorter events, 235.9 us)
Async XLA Ops:
  7.3 114.4 %all-gather.5.cloned.1.call-start = ((), (), s32[]{:S(2)}) async-start(), calls=%async_computation.6 | async-start | bytes 2359296 | tf_op jit(solution)/shard_map/all_gather | solution.py:601
  13.4 9.7 %collective-permute-start.1 = (bf16[64,1536]{1,0:T(8,128)(2,1)S(1)}, bf16[64,1536]{1,0:T(8,128)(2,1)S(1)}, u32[]{:S(2)}, u32[]{:S(2)}) collective-permute-start(bf16[64,1536]{1,0:T(8,128)(2,1)S(1)} %pad_maximum_fusion.10), channel_id=1, source_target_pairs={{0,16},{8,24},{16,0},{24,8},{1,17},{9,25},{17,1},{25,9},{2,18},{10... | collective-permute-start | bytes 589832 | tf_op jit(solution)/shard_map/ppermute | solution.py:379
  36.6 32.7 %collective-permute-start.11 = (bf16[4,64,1536]{2,1,0:T(8,128)(2,1)}, bf16[4,64,1536]{2,1,0:T(8,128)(2,1)}, u32[]{:S(2)}, u32[]{:S(2)}) collective-permute-start(bf16[4,64,1536]{2,1,0:T(8,128)(2,1)} %pad_maximum_fusion.8), channel_id=1, source_target_pairs={{0,2},{2,4},{4,6},{6,7},{7,5},{5,3},{3,1},{1,0},{8,10},{10,12},{12... | collective-permute-start | bytes 2359304 | tf_op jit(solution)/shard_map/ppermute | solution.py:535
  38.4 36.5 %collective-permute-start.12 = (bf16[4,64,1536]{2,1,0:T(8,128)(2,1)}, bf16[4,64,1536]{2,1,0:T(8,128)(2,1)}, u32[]{:S(2)}, u32[]{:S(2)}) collective-permute-start(bf16[4,64,1536]{2,1,0:T(8,128)(2,1)} %pad_maximum_fusion.8), channel_id=1, source_target_pairs={{0,1},{2,0},{4,2},{6,4},{7,6},{5,7},{3,5},{1,3},{8,9},{10,8},{12,1... | collective-permute-start | bytes 2359304 | tf_op jit(solution)/shard_map/ppermute | solution.py:535
  45.5 33.9 %collective-permute-start.9 = (bf16[256,2048]{1,0:T(8,128)(2,1)S(1)}, bf16[256,2048]{1,0:T(8,128)(2,1)S(1)}, u32[]{:S(2)}, u32[]{:S(2)}) collective-permute-start(bf16[256,2048]{1,0:T(8,128)(2,1)S(1)} %fusion.32.refs_0_.refs_8_.refs_9_.refs_10_.refs_11_), channel_id=1, source_target_pairs={{0,16},{8,24},{16,0},{24,8},{1,17},{9,25},{17,1},{25,9},{2,18},{10... | collective-permute-start | bytes 3145736 | tf_op jit(solution)/shard_map/ppermute | solution.py:379
  45.9 75.7 %collective-permute-start.8 = (bf16[256,2048]{1,0:T(8,128)(2,1)S(1)}, bf16[256,2048]{1,0:T(8,128)(2,1)S(1)}, u32[]{:S(2)}, u32[]{:S(2)}) collective-permute-start(bf16[256,2048]{1,0:T(8,128)(2,1)S(1)} %fusion.32.refs_0_.refs_8_.refs_9_.refs_10_.refs_11_), channel_id=1, source_target_pairs={{0,8},{8,0},{16,24},{24,16},{1,9},{9,1},{17,25},{25,17},{2,10},{10... | collective-permute-start | bytes 3145736 | tf_op jit(solution)/shard_map/ppermute | solution.py:379
  69.4 23.1 %collective-permute-start.13 = (bf16[4,64,1536]{2,1,0:T(8,128)(2,1)}, bf16[4,64,1536]{2,1,0:T(8,128)(2,1)S(1)}, u32[]{:S(2)}, u32[]{:S(2)}) collective-permute-start(bf16[4,64,1536]{2,1,0:T(8,128)(2,1)} %collective-permute-done.11), channel_id=1, source_target_pairs={{0,2},{2,4},{4,6},{6,7},{7,5},{5,3},{3,1},{1,0},{8,10},{10,12},{12... | collective-permute-start | bytes 2359304 | tf_op jit(solution)/shard_map/ppermute | solution.py:535
  74.9 19.1 %collective-permute-start.14 = (bf16[4,64,1536]{2,1,0:T(8,128)(2,1)}, bf16[4,64,1536]{2,1,0:T(8,128)(2,1)S(1)}, u32[]{:S(2)}, u32[]{:S(2)}) collective-permute-start(bf16[4,64,1536]{2,1,0:T(8,128)(2,1)} %collective-permute-done.12), channel_id=1, source_target_pairs={{0,1},{2,0},{4,2},{6,4},{7,6},{5,7},{3,5},{1,3},{8,9},{10,8},{12,1... | collective-permute-start | bytes 2359304 | tf_op jit(solution)/shard_map/ppermute | solution.py:535
  79.3 42.3 %collective-permute-start.10 = (bf16[256,2048]{1,0:T(8,128)(2,1)S(1)}, bf16[256,2048]{1,0:T(8,128)(2,1)}, u32[]{:S(2)}, u32[]{:S(2)}) collective-permute-start(bf16[256,2048]{1,0:T(8,128)(2,1)S(1)} %collective-permute-done.9.refs_2_.refs_12_.refs_13_.refs_14_.refs_15_), channel_id=1, source_target_pairs={{0,8},{8,0},{16,24},{24,16},{1,9},{9,1},{17,25},{25,17},{2,10},{10... | collective-permute-start | bytes 3145736 | tf_op jit(solution)/shard_map/ppermute | solution.py:379
  92.4 18.2 %collective-permute-start.15 = (bf16[4,64,1536]{2,1,0:T(8,128)(2,1)S(1)}, bf16[4,64,1536]{2,1,0:T(8,128)(2,1)S(1)}, u32[]{:S(2)}, u32[]{:S(2)}) collective-permute-start(bf16[4,64,1536]{2,1,0:T(8,128)(2,1)S(1)} %collective-permute-done.13), channel_id=1, source_target_pairs={{0,2},{2,4},{4,6},{6,7},{7,5},{5,3},{3,1},{1,0},{8,10},{10,12},{12... | collective-permute-start | bytes 2359304 | tf_op jit(solution)/shard_map/ppermute | solution.py:535
  94.0 18.0 %collective-permute-start.16 = (bf16[4,64,1536]{2,1,0:T(8,128)(2,1)S(1)}, bf16[4,64,1536]{2,1,0:T(8,128)(2,1)S(1)}, u32[]{:S(2)}, u32[]{:S(2)}) collective-permute-start(bf16[4,64,1536]{2,1,0:T(8,128)(2,1)S(1)} %collective-permute-done.14), channel_id=1, source_target_pairs={{0,1},{2,0},{4,2},{6,4},{7,6},{5,7},{3,5},{1,3},{8,9},{10,8},{12,1... | collective-permute-start | bytes 2359304 | tf_op jit(solution)/shard_map/ppermute | solution.py:535
  110.7 8.9 %collective-permute-start.17 = (bf16[4,64,768]{2,1,0:T(8,128)(2,1)S(1)}, bf16[4,64,768]{2,1,0:T(8,128)(2,1)S(1)}, u32[]{:S(2)}, u32[]{:S(2)}) collective-permute-start(bf16[4,64,768]{2,1,0:T(8,128)(2,1)S(1)} %slice.345), channel_id=1, source_target_pairs={{0,2},{2,4},{4,6},{6,7},{7,5},{5,3},{3,1},{1,0},{8,10},{10,12},{12... | collective-permute-start | bytes 1179656 | tf_op jit(solution)/shard_map/ppermute | solution.py:535
  133.2 73.8 %all-to-all-start = ((bf16[8,3,4,128,128]{4,3,2,1,0:T(8,128)(2,1)}), bf16[8,3,4,128,128]{4,3,2,1,0:T(8,128)(2,1)}, u32[]{:S(2)}, u32[]{:S(2)}) async-start(bf16[8,3,4,128,128]{4,3,2,1,0:T(8,128)(2,1)} %project_parts.1), calls=%async_computation | async-start | bytes 6291456 | tf_op jit(solution)/shard_map/all_to_all | solution.py:597
  139.0 179.5 %all-gather.9.cloned.1.call-start = ((), (), s32[]{:S(2)}) async-start(), calls=%async_computation.10 | async-start | bytes 5242880 | tf_op jit(solution)/shard_map/all_gather | solution.py:508
  143.1 36.3 %collective-permute-start.19 = (bf16[4,64,1024]{2,1,0:T(8,128)(2,1)}, bf16[4,64,1024]{2,1,0:T(8,128)(2,1)}, u32[]{:S(2)}, u32[]{:S(2)}) collective-permute-start(bf16[4,64,1024]{2,1,0:T(8,128)(2,1)} %slice_bitcast_fusion.9), channel_id=1, source_target_pairs={{0,1},{1,0},{2,3},{3,2},{4,5},{5,4},{6,7},{7,6},{8,9},{9,8},{10,11... | collective-permute-start | bytes 1572872 | tf_op jit(solution)/shard_map/ppermute | solution.py:379
  182.5 12.6 %collective-permute-start.21 = (bf16[2,64,1024]{2,1,0:T(8,128)(2,1)S(1)}, bf16[2,64,1024]{2,1,0:T(8,128)(2,1)S(1)}, u32[]{:S(2)}, u32[]{:S(2)}) collective-permute-start(bf16[2,64,1024]{2,1,0:T(8,128)(2,1)S(1)} %get-tuple-element.176), channel_id=1, source_target_pairs={{0,16},{8,24},{16,0},{24,8},{1,17},{9,25},{17,1},{25,9},{2,18},{10... | collective-permute-start | bytes 786440 | tf_op jit(solution)/shard_map/ppermute | solution.py:379
  219.0 32.6 %collective-permute-start.24 = (bf16[256,2048]{1,0:T(8,128)(2,1)}, bf16[256,2048]{1,0:T(8,128)(2,1)}, u32[]{:S(2)}, u32[]{:S(2)}) collective-permute-start(bf16[256,2048]{1,0:T(8,128)(2,1)} %bitcast.274), channel_id=1, source_target_pairs={{0,1},{1,0},{2,3},{3,2},{4,5},{5,4},{6,7},{7,6},{8,9},{9,8},{10,11... | collective-permute-start | bytes 3145736 | tf_op jit(solution)/shard_map/ppermute | solution.py:379
  220.6 57.3 %all-to-all-start.1 = ((bf16[8,1,4,128,128]{4,3,2,1,0:T(8,128)(2,1)}), bf16[8,1,4,128,128]{4,3,2,1,0:T(8,128)(2,1)}, u32[]{:S(2)}, u32[]{:S(2)}) async-start(bf16[8,1,4,128,128]{4,3,2,1,0:T(8,128)(2,1)} %copy-done.14), calls=%async_computation.1 | async-start | bytes 2097152 | tf_op jit(solution)/shard_map/all_to_all | solution.py:597
  224.8 179.1 %all-gather.7.cloned.1.call-start = ((), (), s32[]{:S(2)}) async-start(), calls=%async_computation.7 | async-start | bytes 5242880 | tf_op jit(solution)/shard_map/all_gather | solution.py:508
  225.4 31.3 %collective-permute-start.23 = (bf16[256,2048]{1,0:T(8,128)(2,1)}, bf16[256,2048]{1,0:T(8,128)(2,1)}, u32[]{:S(2)}, u32[]{:S(2)}) collective-permute-start(bf16[256,2048]{1,0:T(8,128)(2,1)} %bitcast.275), channel_id=1, source_target_pairs={{0,16},{8,24},{16,0},{24,8},{1,17},{9,25},{17,1},{25,9},{2,18},{10... | collective-permute-start | bytes 3145736 | tf_op jit(solution)/shard_map/ppermute | solution.py:379
  252.8 11.5 %collective-permute-start.25 = (bf16[256,1024]{1,0:T(8,128)(2,1)S(1)}, bf16[256,1024]{1,0:T(8,128)(2,1)S(1)}, u32[]{:S(2)}, u32[]{:S(2)}) collective-permute-start(bf16[256,1024]{1,0:T(8,128)(2,1)S(1)} %slice.351), channel_id=1, source_target_pairs={{0,16},{8,24},{16,0},{24,8},{1,17},{9,25},{17,1},{25,9},{2,18},{10... | collective-permute-start | bytes 1572872 | tf_op jit(solution)/shard_map/ppermute | solution.py:379
  257.8 10.8 %collective-permute-start.26 = (bf16[256,1024]{1,0:T(8,128)(2,1)S(1)}, bf16[256,1024]{1,0:T(8,128)(2,1)S(1)}, u32[]{:S(2)}, u32[]{:S(2)}) collective-permute-start(bf16[256,1024]{1,0:T(8,128)(2,1)S(1)} %slice.352), channel_id=1, source_target_pairs={{0,1},{1,0},{2,3},{3,2},{4,5},{5,4},{6,7},{7,6},{8,9},{9,8},{10,11... | collective-permute-start | bytes 1572872 | tf_op jit(solution)/shard_map/ppermute | solution.py:379
  284.3 9.1 %collective-permute-start.31 = (bf16[256,2048]{1,0:T(8,128)(2,1)}, bf16[256,2048]{1,0:T(8,128)(2,1)}, u32[]{:S(2)}, u32[]{:S(2)}) collective-permute-start(bf16[256,2048]{1,0:T(8,128)(2,1)} %collective-permute-done.23), channel_id=1, source_target_pairs={{0,8},{8,0},{16,24},{24,16},{1,9},{9,1},{17,25},{25,17},{2,10},{10... | collective-permute-start | bytes 3145736 | tf_op jit(solution)/shard_map/ppermute | solution.py:379
  284.4 11.4 %collective-permute-start.32 = (bf16[256,2048]{1,0:T(8,128)(2,1)}, bf16[256,2048]{1,0:T(8,128)(2,1)}, u32[]{:S(2)}, u32[]{:S(2)}) collective-permute-start(bf16[256,2048]{1,0:T(8,128)(2,1)} %collective-permute-done.24), channel_id=1, source_target_pairs={{0,8},{8,0},{16,24},{24,16},{1,9},{9,1},{17,25},{25,17},{2,10},{10... | collective-permute-start | bytes 3145736 | tf_op jit(solution)/shard_map/ppermute | solution.py:379
  284.8 13.5 %collective-permute-start.33 = (bf16[256,2048]{1,0:T(8,128)(2,1)}, bf16[256,2048]{1,0:T(8,128)(2,1)}, u32[]{:S(2)}, u32[]{:S(2)}) collective-permute-start(bf16[256,2048]{1,0:T(8,128)(2,1)} %get-tuple-element.82), channel_id=1, source_target_pairs={{0,8},{8,0},{16,24},{24,16},{1,9},{9,1},{17,25},{25,17},{2,10},{10... | collective-permute-start | bytes 3145736 | tf_op jit(solution)/shard_map/ppermute | solution.py:379
  286.4 14.2 %collective-permute-start.27 = (bf16[256,2048]{1,0:T(8,128)(2,1)}, bf16[256,2048]{1,0:T(8,128)(2,1)}, u32[]{:S(2)}, u32[]{:S(2)}) collective-permute-start(bf16[256,2048]{1,0:T(8,128)(2,1)} %get-tuple-element.75), channel_id=1, source_target_pairs={{0,8},{8,0},{16,24},{24,16},{1,9},{9,1},{17,25},{25,17},{2,10},{10... | collective-permute-start | bytes 3145736 | tf_op jit(solution)/shard_map/ppermute | solution.py:379
  289.4 25.5 %collective-permute-start.29 = (bf16[256,2048]{1,0:T(8,128)(2,1)}, bf16[256,2048]{1,0:T(8,128)(2,1)}, u32[]{:S(2)}, u32[]{:S(2)}) collective-permute-start(bf16[256,2048]{1,0:T(8,128)(2,1)} %add_convert_fusion.2), channel_id=1, source_target_pairs={{0,16},{8,24},{16,0},{24,8},{1,17},{9,25},{17,1},{25,9},{2,18},{10... | collective-permute-start | bytes 3145736 | tf_op jit(solution)/shard_map/ppermute | solution.py:379
  318.5 213.6 %reduce-scatter.3.cloned.1.call-start = ((), (), s32[]{:S(2)}) async-start(), calls=%async_computation.8 | async-start | bytes 5242880 | tf_op jit(solution)/shard_map/reduce_scatter | solution.py:513
  324.5 24.8 %collective-permute-start.35 = (bf16[256,2048]{1,0:T(8,128)(2,1)}, bf16[256,2048]{1,0:T(8,128)(2,1)}, u32[]{:S(2)}, u32[]{:S(2)}) collective-permute-start(bf16[256,2048]{1,0:T(8,128)(2,1)} %get-tuple-element.129.refs_0_), channel_id=1, source_target_pairs={{0,1},{1,0},{2,3},{3,2},{4,5},{5,4},{6,7},{7,6},{8,9},{9,8},{10,11... | collective-permute-start | bytes 3145736 | tf_op jit(solution)/shard_map/ppermute | solution.py:379
  325.1 26.9 %collective-permute-start.34 = (bf16[256,2048]{1,0:T(8,128)(2,1)}, bf16[256,2048]{1,0:T(8,128)(2,1)}, u32[]{:S(2)}, u32[]{:S(2)}) collective-permute-start(bf16[256,2048]{1,0:T(8,128)(2,1)} %get-tuple-element.129.refs_0_), channel_id=1, source_target_pairs={{0,16},{8,24},{16,0},{24,8},{1,17},{9,25},{17,1},{25,9},{2,18},{10... | collective-permute-start | bytes 3145736 | tf_op jit(solution)/shard_map/ppermute | solution.py:379
  350.4 12.4 %collective-permute-start.36 = (bf16[256,1024]{1,0:T(8,128)(2,1)S(1)}, bf16[256,1024]{1,0:T(8,128)(2,1)S(1)}, u32[]{:S(2)}, u32[]{:S(2)}) collective-permute-start(bf16[256,1024]{1,0:T(8,128)(2,1)S(1)} %slice.359), channel_id=1, source_target_pairs={{0,16},{8,24},{16,0},{24,8},{1,17},{9,25},{17,1},{25,9},{2,18},{10... | collective-permute-start | bytes 1572872 | tf_op jit(solution)/shard_map/ppermute | solution.py:379
  352.0 16.6 %collective-permute-start.38 = (bf16[256,2048]{1,0:T(8,128)(2,1)}, bf16[256,2048]{1,0:T(8,128)(2,1)}, u32[]{:S(2)}, u32[]{:S(2)}) collective-permute-start(bf16[256,2048]{1,0:T(8,128)(2,1)} %get-tuple-element.129.refs_0_), channel_id=1, source_target_pairs={{0,8},{8,0},{16,24},{24,16},{1,9},{9,1},{17,25},{25,17},{2,10},{10... | collective-permute-start | bytes 3145736 | tf_op jit(solution)/shard_map/ppermute | solution.py:379
  353.1 14.4 %collective-permute-start.37 = (bf16[256,1024]{1,0:T(8,128)(2,1)S(1)}, bf16[256,1024]{1,0:T(8,128)(2,1)S(1)}, u32[]{:S(2)}, u32[]{:S(2)}) collective-permute-start(bf16[256,1024]{1,0:T(8,128)(2,1)S(1)} %slice.360), channel_id=1, source_target_pairs={{0,1},{1,0},{2,3},{3,2},{4,5},{5,4},{6,7},{7,6},{8,9},{9,8},{10,11... | collective-permute-start | bytes 1572872 | tf_op jit(solution)/shard_map/ppermute | solution.py:379
  354.4 14.3 %collective-permute-start.40 = (bf16[256,2048]{1,0:T(8,128)(2,1)}, bf16[256,2048]{1,0:T(8,128)(2,1)}, u32[]{:S(2)}, u32[]{:S(2)}) collective-permute-start(bf16[256,2048]{1,0:T(8,128)(2,1)} %collective-permute-done.35.refs_2_), channel_id=1, source_target_pairs={{0,8},{8,0},{16,24},{24,16},{1,9},{9,1},{17,25},{25,17},{2,10},{10... | collective-permute-start | bytes 3145736 | tf_op jit(solution)/shard_map/ppermute | solution.py:379
  354.6 14.1 %collective-permute-start.39 = (bf16[256,2048]{1,0:T(8,128)(2,1)}, bf16[256,2048]{1,0:T(8,128)(2,1)}, u32[]{:S(2)}, u32[]{:S(2)}) collective-permute-start(bf16[256,2048]{1,0:T(8,128)(2,1)} %collective-permute-done.34.refs_1_), channel_id=1, source_target_pairs={{0,8},{8,0},{16,24},{24,16},{1,9},{9,1},{17,25},{25,17},{2,10},{10... | collective-permute-start | bytes 3145736 | tf_op jit(solution)/shard_map/ppermute | solution.py:379
  428.1 9.9 %collective-permute-start.42 = (bf16[4,256,2048]{2,1,0:T(8,128)(2,1)S(1)}, bf16[4,256,2048]{2,1,0:T(8,128)(2,1)S(1)}, u32[]{:S(2)}, u32[]{:S(2)}) collective-permute-start(bf16[4,256,2048]{2,1,0:T(8,128)(2,1)S(1)} %bitcast.263), channel_id=1, source_target_pairs={{0,8},{8,0},{16,24},{24,16},{1,9},{9,1},{17,25},{25,17},{2,10},{10... | collective-permute-start | bytes 12582920 | tf_op jit(solution)/shard_map/ppermute | solution.py:379
  443.5 14.6 %collective-permute-start.43 = (bf16[256,1024]{1,0:T(8,128)(2,1)}, bf16[256,1024]{1,0:T(8,128)(2,1)}, u32[]{:S(2)}, u32[]{:S(2)}) collective-permute-start(bf16[256,1024]{1,0:T(8,128)(2,1)} %get-tuple-element.169), channel_id=1, source_target_pairs={{0,1},{1,0},{2,3},{3,2},{4,5},{5,4},{6,7},{7,6},{8,9},{9,8},{10,11... | collective-permute-start | bytes 1572872 | tf_op jit(solution)/shard_map/ppermute | solution.py:379
  449.5 183.0 %reduce-scatter.5.cloned.1.call-start = ((), (), s32[]{:S(2)}) async-start(), calls=%async_computation.9 | async-start | bytes 5242880 | tf_op jit(solution)/shard_map/reduce_scatter | solution.py:513
  453.7 15.1 %collective-permute-start.45 = (bf16[256,1024]{1,0:T(8,128)(2,1)}, bf16[256,1024]{1,0:T(8,128)(2,1)S(1)}, u32[]{:S(2)}, u32[]{:S(2)}) collective-permute-start(bf16[256,1024]{1,0:T(8,128)(2,1)} %get-tuple-element.170), channel_id=1, source_target_pairs={{0,16},{8,24},{16,0},{24,8},{1,17},{9,25},{17,1},{25,9},{2,18},{10... | collective-permute-start | bytes 1572872 | tf_op jit(solution)/shard_map/ppermute | solution.py:379
  459.4 30.9 %collective-permute-start.44 = (bf16[256,2048]{1,0:T(8,128)(2,1)S(1)}, bf16[256,2048]{1,0:T(8,128)(2,1)S(1)}, u32[]{:S(2)}, u32[]{:S(2)}) collective-permute-start(bf16[256,2048]{1,0:T(8,128)(2,1)S(1)} %pad_maximum_fusion.1), channel_id=1, source_target_pairs={{0,16},{8,24},{16,0},{24,8},{1,17},{9,25},{17,1},{25,9},{2,18},{10... | collective-permute-start | bytes 3145736 | tf_op jit(solution)/shard_map/ppermute | solution.py:379
  469.0 23.5 %collective-permute-start.46 = (bf16[256,2048]{1,0:T(8,128)(2,1)S(1)}, bf16[256,2048]{1,0:T(8,128)(2,1)S(1)}, u32[]{:S(2)}, u32[]{:S(2)}) collective-permute-start(bf16[256,2048]{1,0:T(8,128)(2,1)S(1)} %pad_maximum_fusion.2), channel_id=1, source_target_pairs={{0,1},{1,0},{2,3},{3,2},{4,5},{5,4},{6,7},{7,6},{8,9},{9,8},{10,11... | collective-permute-start | bytes 3145736 | tf_op jit(solution)/shard_map/ppermute | solution.py:379
  506.5 26.3 %collective-permute-start.47 = (bf16[4,256,2048]{2,1,0:T(8,128)(2,1)}, bf16[4,256,2048]{2,1,0:T(8,128)(2,1)}, u32[]{:S(2)}, u32[]{:S(2)}) collective-permute-start(bf16[4,256,2048]{2,1,0:T(8,128)(2,1)} %bitcast.39), channel_id=1, source_target_pairs={{0,8},{8,0},{16,24},{24,16},{1,9},{9,1},{17,25},{25,17},{2,10},{10... | collective-permute-start | bytes 12582920 | tf_op jit(solution)/shard_map/ppermute | solution.py:379
  506.5 25.7 %collective-permute-start.53 = (bf16[256,2048]{1,0:T(8,128)(2,1)S(1)}, bf16[256,2048]{1,0:T(8,128)(2,1)}, u32[]{:S(2)}, u32[]{:S(2)}) collective-permute-start(bf16[256,2048]{1,0:T(8,128)(2,1)S(1)} %get-tuple-element.123.refs_0_), channel_id=1, source_target_pairs={{0,16},{8,24},{16,0},{24,8},{1,17},{9,25},{17,1},{25,9},{2,18},{10... | collective-permute-start | bytes 3145736 | tf_op jit(solution)/shard_map/ppermute | solution.py:379
  540.0 17.8 %collective-permute-start.50 = (bf16[256,1024]{1,0:T(8,128)(2,1)}, bf16[256,1024]{1,0:T(8,128)(2,1)}, u32[]{:S(2)}, u32[]{:S(2)}) collective-permute-start(bf16[256,1024]{1,0:T(8,128)(2,1)} %get-tuple-element.168), channel_id=1, source_target_pairs={{0,16},{8,24},{16,0},{24,8},{1,17},{9,25},{17,1},{25,9},{2,18},{10... | collective-permute-start | bytes 1572872 | tf_op jit(solution)/shard_map/ppermute | solution.py:379
  548.7 58.7 %all-to-all-start.2 = ((bf16[8,1,4,128,128]{4,3,2,1,0:T(8,128)(2,1)}), bf16[8,1,4,128,128]{4,3,2,1,0:T(8,128)(2,1)}, u32[]{:S(2)}, u32[]{:S(2)}) async-start(bf16[8,1,4,128,128]{4,3,2,1,0:T(8,128)(2,1)} %copy-done.10), calls=%async_computation.2 | async-start | bytes 2097152 | tf_op jit(solution)/shard_map/all_to_all | solution.py:597
  555.9 19.3 %collective-permute-start.48 = (bf16[256,1024]{1,0:T(8,128)(2,1)}, bf16[256,1024]{1,0:T(8,128)(2,1)S(1)}, u32[]{:S(2)}, u32[]{:S(2)}) collective-permute-start(bf16[256,1024]{1,0:T(8,128)(2,1)} %get-tuple-element.167), channel_id=1, source_target_pairs={{0,1},{1,0},{2,3},{3,2},{4,5},{5,4},{6,7},{7,6},{8,9},{9,8},{10,11... | collective-permute-start | bytes 1572872 | tf_op jit(solution)/shard_map/ppermute | solution.py:379
  560.1 40.9 %collective-permute-start.51 = (bf16[256,2048]{1,0:T(8,128)(2,1)}, bf16[256,2048]{1,0:T(8,128)(2,1)}, u32[]{:S(2)}, u32[]{:S(2)}) collective-permute-start(bf16[256,2048]{1,0:T(8,128)(2,1)} %pad_maximum_fusion.4), channel_id=1, source_target_pairs={{0,1},{1,0},{2,3},{3,2},{4,5},{5,4},{6,7},{7,6},{8,9},{9,8},{10,11... | collective-permute-start | bytes 3145736 | tf_op jit(solution)/shard_map/ppermute | solution.py:379
  576.5 24.5 %collective-permute-start.49 = (bf16[256,2048]{1,0:T(8,128)(2,1)}, bf16[256,2048]{1,0:T(8,128)(2,1)}, u32[]{:S(2)}, u32[]{:S(2)}) collective-permute-start(bf16[256,2048]{1,0:T(8,128)(2,1)} %pad_maximum_fusion.3), channel_id=1, source_target_pairs={{0,16},{8,24},{16,0},{24,8},{1,17},{9,25},{17,1},{25,9},{2,18},{10... | collective-permute-start | bytes 3145736 | tf_op jit(solution)/shard_map/ppermute | solution.py:379
  628.1 75.4 %all-to-all-start.3 = ((bf16[8,3,4,128,128]{4,3,2,1,0:T(8,128)(2,1)}), bf16[8,3,4,128,128]{4,3,2,1,0:T(8,128)(2,1)}, u32[]{:S(2)}, u32[]{:S(2)}) async-start(bf16[8,3,4,128,128]{4,3,2,1,0:T(8,128)(2,1)} %attend_bwd.1), calls=%async_computation.3 | async-start | bytes 6291456 | tf_op jit(solution)/shard_map/all_to_all | solution.py:597
  634.6 9.4 %collective-permute-start.56 = (bf16[2,64,1024]{2,1,0:T(8,128)(2,1)}, bf16[2,64,1024]{2,1,0:T(8,128)(2,1)}, u32[]{:S(2)}, u32[]{:S(2)}) collective-permute-start(bf16[2,64,1024]{2,1,0:T(8,128)(2,1)} %get-tuple-element.165), channel_id=1, source_target_pairs={{0,16},{8,24},{16,0},{24,8},{1,17},{9,25},{17,1},{25,9},{2,18},{10... | collective-permute-start | bytes 786440 | tf_op jit(solution)/shard_map/ppermute | solution.py:379
  636.0 12.9 %collective-permute-start.55 = (bf16[2,64,1024]{2,1,0:T(8,128)(2,1)}, bf16[2,64,1024]{2,1,0:T(8,128)(2,1)}, u32[]{:S(2)}, u32[]{:S(2)}) collective-permute-start(bf16[2,64,1024]{2,1,0:T(8,128)(2,1)} %get-tuple-element.166), channel_id=1, source_target_pairs={{0,24},{8,16},{16,8},{24,0},{1,25},{9,17},{17,9},{25,1},{2,26},{10... | collective-permute-start | bytes 786440 | tf_op jit(solution)/shard_map/ppermute | solution.py:379
  650.2 30.3 %collective-permute-start.58 = (bf16[4,64,1024]{2,1,0:T(8,128)(2,1)S(1)}, bf16[4,64,1024]{2,1,0:T(8,128)(2,1)S(1)}, u32[]{:S(2)}, u32[]{:S(2)}) collective-permute-start(bf16[4,64,1024]{2,1,0:T(8,128)(2,1)S(1)} %dynamic-slice_bitcast_fusion.3), channel_id=1, source_target_pairs={{0,1},{1,0},{2,3},{3,2},{4,5},{5,4},{6,7},{7,6},{8,9},{9,8},{10,11... | collective-permute-start | bytes 1572872 | tf_op jit(solution)/shard_map/ppermute | solution.py:379
  722.7 20.2 %collective-permute-start.62 = (bf16[4,64,1024]{2,1,0:T(8,128)(2,1)}, bf16[4,64,1024]{2,1,0:T(8,128)(2,1)}, u32[]{:S(2)}, u32[]{:S(2)}) collective-permute-start(bf16[4,64,1024]{2,1,0:T(8,128)(2,1)} %get-tuple-element.101), channel_id=1, source_target_pairs={{0,2},{2,4},{4,6},{6,7},{7,5},{5,3},{3,1},{1,0},{8,10},{10,12},{12... | collective-permute-start | bytes 1572872 | tf_op jit(solution)/shard_map/ppermute | solution.py:535
  722.8 17.6 %collective-permute-start.63 = (bf16[4,64,1024]{2,1,0:T(8,128)(2,1)S(1)}, bf16[4,64,1024]{2,1,0:T(8,128)(2,1)}, u32[]{:S(2)}, u32[]{:S(2)}) collective-permute-start(bf16[4,64,1024]{2,1,0:T(8,128)(2,1)S(1)} %get-tuple-element.105), channel_id=1, source_target_pairs={{0,1},{2,0},{4,2},{6,4},{7,6},{5,7},{3,5},{1,3},{8,9},{10,8},{12,1... | collective-permute-start | bytes 1572872 | tf_op jit(solution)/shard_map/ppermute | solution.py:535
  744.4 25.5 %collective-permute-start.64 = (bf16[4,64,2048]{2,1,0:T(8,128)(2,1)S(1)}, bf16[4,64,2048]{2,1,0:T(8,128)(2,1)S(1)}, u32[]{:S(2)}, u32[]{:S(2)}) collective-permute-start(bf16[4,64,2048]{2,1,0:T(8,128)(2,1)S(1)} %pad_maximum_fusion.6), channel_id=1, source_target_pairs={{0,2},{2,4},{4,6},{6,7},{7,5},{5,3},{3,1},{1,0},{8,10},{10,12},{12... | collective-permute-start | bytes 3145736 | tf_op jit(solution)/shard_map/ppermute | solution.py:535
  744.5 25.9 %collective-permute-start.65 = (bf16[4,64,2048]{2,1,0:T(8,128)(2,1)S(1)}, bf16[4,64,2048]{2,1,0:T(8,128)(2,1)S(1)}, u32[]{:S(2)}, u32[]{:S(2)}) collective-permute-start(bf16[4,64,2048]{2,1,0:T(8,128)(2,1)S(1)} %pad_maximum_fusion.7), channel_id=1, source_target_pairs={{0,1},{2,0},{4,2},{6,4},{7,6},{5,7},{3,5},{1,3},{8,9},{10,8},{12,1... | collective-permute-start | bytes 3145736 | tf_op jit(solution)/shard_map/ppermute | solution.py:535
  746.9 24.3 %collective-permute-start.59 = (bf16[256,2048]{1,0:T(8,128)(2,1)S(1)}, bf16[256,2048]{1,0:T(8,128)(2,1)S(1)}, u32[]{:S(2)}, u32[]{:S(2)}) collective-permute-start(bf16[256,2048]{1,0:T(8,128)(2,1)S(1)} %copy-done.40), channel_id=1, source_target_pairs={{0,8},{8,0},{16,24},{24,16},{1,9},{9,1},{17,25},{25,17},{2,10},{10... | collective-permute-start | bytes 3145736 | tf_op jit(solution)/shard_map/ppermute | solution.py:379
  747.3 25.6 %collective-permute-start.61 = (bf16[256,2048]{1,0:T(8,128)(2,1)S(1)}, bf16[256,2048]{1,0:T(8,128)(2,1)S(1)}, u32[]{:S(2)}, u32[]{:S(2)}) collective-permute-start(bf16[256,2048]{1,0:T(8,128)(2,1)S(1)} %add_convert_fusion), channel_id=1, source_target_pairs={{0,16},{8,24},{16,0},{24,8},{1,17},{9,25},{17,1},{25,9},{2,18},{10... | collective-permute-start | bytes 3145736 | tf_op jit(solution)/shard_map/ppermute | solution.py:379
  774.0 24.8 %collective-permute-start.66 = (bf16[4,64,2048]{2,1,0:T(8,128)(2,1)S(1)}, bf16[4,64,2048]{2,1,0:T(8,128)(2,1)S(1)}, u32[]{:S(2)}, u32[]{:S(2)}) collective-permute-start(bf16[4,64,2048]{2,1,0:T(8,128)(2,1)S(1)} %get-tuple-element.108), channel_id=1, source_target_pairs={{0,2},{2,4},{4,6},{6,7},{7,5},{5,3},{3,1},{1,0},{8,10},{10,12},{12... | collective-permute-start | bytes 3145736 | tf_op jit(solution)/shard_map/ppermute | solution.py:535
  774.2 24.8 %collective-permute-start.67 = (bf16[4,64,2048]{2,1,0:T(8,128)(2,1)S(1)}, bf16[4,64,2048]{2,1,0:T(8,128)(2,1)S(1)}, u32[]{:S(2)}, u32[]{:S(2)}) collective-permute-start(bf16[4,64,2048]{2,1,0:T(8,128)(2,1)S(1)} %get-tuple-element.109), channel_id=1, source_target_pairs={{0,1},{2,0},{4,2},{6,4},{7,6},{5,7},{3,5},{1,3},{8,9},{10,8},{12,1... | collective-permute-start | bytes 3145736 | tf_op jit(solution)/shard_map/ppermute | solution.py:535
  801.2 24.2 %collective-permute-start.68 = (bf16[4,64,2048]{2,1,0:T(8,128)(2,1)}, bf16[4,64,2048]{2,1,0:T(8,128)(2,1)}, u32[]{:S(2)}, u32[]{:S(2)}) collective-permute-start(bf16[4,64,2048]{2,1,0:T(8,128)(2,1)} %get-tuple-element.110), channel_id=1, source_target_pairs={{0,2},{2,4},{4,6},{6,7},{7,5},{5,3},{3,1},{1,0},{8,10},{10,12},{12... | collective-permute-start | bytes 3145736 | tf_op jit(solution)/shard_map/ppermute | solution.py:535
  802.5 23.8 %collective-permute-start.69 = (bf16[4,64,2048]{2,1,0:T(8,128)(2,1)}, bf16[4,64,2048]{2,1,0:T(8,128)(2,1)}, u32[]{:S(2)}, u32[]{:S(2)}) collective-permute-start(bf16[4,64,2048]{2,1,0:T(8,128)(2,1)} %get-tuple-element.111), channel_id=1, source_target_pairs={{0,1},{2,0},{4,2},{6,4},{7,6},{5,7},{3,5},{1,3},{8,9},{10,8},{12,1... | collective-permute-start | bytes 3145736 | tf_op jit(solution)/shard_map/ppermute | solution.py:535
  834.2 11.2 %collective-permute-start.77 = (bf16[64,1536]{1,0:T(8,128)(2,1)S(1)}, bf16[64,1536]{1,0:T(8,128)(2,1)S(1)}, u32[]{:S(2)}, u32[]{:S(2)}) collective-permute-start(bf16[64,1536]{1,0:T(8,128)(2,1)S(1)} %get-tuple-element.178), channel_id=1, source_target_pairs={{0,16},{8,24},{16,0},{24,8},{1,17},{9,25},{17,1},{25,9},{2,18},{10... | collective-permute-start | bytes 589832 | tf_op jit(solution)/shard_map/ppermute | solution.py:379
  835.7 10.4 %collective-permute-start.73 = (f32[2,2,768]{2,1,0:T(2,128)S(1)}, f32[2,2,768]{2,1,0:T(2,128)S(1)}, u32[]{:S(2)}, u32[]{:S(2)}) collective-permute-start(f32[2,2,768]{2,1,0:T(2,128)S(1)} %fusion.57), channel_id=1, source_target_pairs={{0,4},{1,5},{2,6},{3,7},{4,0},{5,1},{6,2},{7,3},{8,12},{9,13},{10,... | collective-permute-start | bytes 36872 | tf_op jit(solution)/shard_map/ppermute | solution.py:379
  (85 other events, 578.7 us)
Sparse Core Ops, SparseCore 0:
  10.3 62.4 all-gather.4
  219.2 98.6 all-gather.8
  319.5 79.5 all-gather.6
  449.6 74.2 reduce-scatter.2
  532.3 91.0 reduce-scatter.4

commit v5 on v4

--- a/solution.py
+++ b/solution.py
@@ -402,7 +402,7 @@
     return row
 
 
-def cube_scatter(table):
+def cube_scatter(table, event):
     wide = lax.axis_size(WIDE)
     steps = cube(wide)
     table = table.reshape((2,) * len(steps) + (table.shape[-1],))
@@ -414,13 +414,16 @@
         high = ((lax.axis_index(axis) & bits) > 0).astype(jnp.int32)
         table = at(table, high, dim) + flip(at(table, 1 - high, dim), axis, bits)
         left.remove(k)
+        if len(left) == len(steps) - 2:
+            table = hold(table, event)
     return table
 
 
-def narrow_gather(own, *made):
+def narrow_gather(own, made=None):
     across = flip(own, NARROW, 2)
     beside = flip(own, NARROW, 1)
-    across = hold(across, *made) if made else across
+    if made is not None:
+        across = hold(across, *made(beside))
     return [own, beside, across, flip(across, NARROW, 1)]
 
 
@@ -435,6 +438,10 @@
 
 def hold(value, *events):
     return lax.optimization_barrier((value,) + events)[0]
+
+
+def hold_all(values, *events):
+    return lax.optimization_barrier(tuple(values) + events)[: len(values)]
 
 
 def bit_of(axis, bits):
@@ -590,6 +597,7 @@
         ahead, behind = lax.optimization_barrier(
             (to_ahead.astype(bf16), to_behind.astype(bf16)) + values
         )[:2]
+        event = ahead
     return local(here).astype(f32) + ahead + behind
 
 
@@ -947,16 +955,15 @@
     )(me, segc, segr, lse, parts, dout)
 
 
-def ff_kernel(*refs, count):
-    rows, weights, (bias_ref, hidden_ref, slope_ref) = refs[:count], refs[count:-3], refs[-3:]
-    step = rows[0].shape[0]
-    depth = rows[0].shape[1] // len(weights)
-    for k, rows_ref in enumerate(rows):
-        r = k * step
+def ff_kernel(rows_ref, *refs):
+    weights, (bias_ref, hidden_ref, slope_ref) = refs[:-3], refs[-3:]
+    step = 256
+    depth = rows_ref.shape[1] // len(weights)
+    for r in range(0, rows_ref.shape[0], step):
         x = bias_ref[...]
         for n, weight_ref in enumerate(weights):
             x = x + jnp.dot(
-                rows_ref[:, n * depth : (n + 1) * depth],
+                rows_ref[r : r + step, n * depth : (n + 1) * depth],
                 weight_ref[...].reshape(depth, -1),
                 preferred_element_type=jnp.float32,
             )
@@ -968,17 +975,17 @@
 
 
 def feed_forward(rows, weight, bias):
-    count = len(rows) * rows[0].shape[0]
+    count = rows.shape[0]
     deep, narrow, shard, inner = weight.shape
     step = 256
     return pl.pallas_call(
-        functools.partial(ff_kernel, count=len(rows)),
+        ff_kernel,
         grid=(inner // step,),
         out_shape=(
             jax.ShapeDtypeStruct((count, inner), jnp.bfloat16),
             jax.ShapeDtypeStruct((count, inner), jnp.float32),
         ),
-        in_specs=[resident(block.shape) for block in rows]
+        in_specs=[resident(rows.shape)]
         + [
             pl.BlockSpec((deep, 1, shard, step), lambda i, n=n: (0, n, 0, i)) for n in range(narrow)
         ]
@@ -989,7 +996,7 @@
         ),
         compiler_params=BIG,
         name="feed_forward",
-    )(*rows, *[weight] * narrow, bias.reshape(1, -1))
+    )(rows, *[weight] * narrow, bias.reshape(1, -1))
 
 
 def pull_kernel(rows_ref, weight_ref, slope_ref, grad_ref, sum_ref):
@@ -1031,6 +1038,56 @@
         compiler_params=BIG,
         name="pull_back",
     )(rows, weight, slope)
+
+
+def place_qkv_kernel(me_ref, *refs):
+    pieces, outs = refs[:4], refs[4:]
+    cols = pieces[0].shape[1] // len(outs)
+    for part, out_ref in enumerate(outs):
+        blocks = [piece[:, part * cols : (part + 1) * cols].astype(jnp.float32) for piece in pieces]
+        for n in range(4):
+            value = blocks[n]
+            for me in range(1, 4):
+                value = jnp.where(me_ref[0] == me, blocks[n ^ me], value)
+            out_ref[:, n * cols : (n + 1) * cols] = value
+
+
+def place_qkv(me, pieces):
+    rows, width = pieces[0].shape
+    shape = jax.ShapeDtypeStruct((rows, width // 3 * 4), jnp.float32)
+    return pl.pallas_call(
+        place_qkv_kernel,
+        out_shape=(shape,) * 3,
+        in_specs=[SMEM_SPEC] + vmem_specs(4),
+        out_specs=tuple(vmem_specs(3)),
+        compiler_params=BIG,
+        name="place_qkv",
+    )(me, *pieces)
+
+
+def place_up_kernel(me_ref, own_ref, other_ref, out_ref, *, step):
+    narrow, _, inner = own_ref.shape
+    high = (me_ref[1] & 1) > 0
+    for n in range(narrow):
+        own, other = own_ref[n ^ me_ref[0]], other_ref[n ^ me_ref[0]]
+        for z in range(inner // step):
+            c = (n * (inner // step) + z) * 2 * step
+            a = own[:, z * step : (z + 1) * step].astype(jnp.float32)
+            b = other[:, z * step : (z + 1) * step].astype(jnp.float32)
+            out_ref[:, c : c + step] = jnp.where(high, b, a)
+            out_ref[:, c + step : c + 2 * step] = jnp.where(high, a, b)
+
+
+def place_up(me, own, other, step):
+    narrow, shard, inner = own.shape
+    return pl.pallas_call(
+        functools.partial(place_up_kernel, step=step),
+        out_shape=jax.ShapeDtypeStruct((shard, 2 * narrow * inner), jnp.float32),
+        in_specs=[SMEM_SPEC] + vmem_specs(2),
+        out_specs=vmem_specs(1)[0],
+        compiler_params=BIG,
+        name="place_up",
+    )(me, own, other)
 
 
 def pick_kernel(me_ref, weight_ref, out_ref):
@@ -1114,7 +1171,7 @@
         attn_gain, attn_shift, out_bias, mlp_gain, mlp_shift, down_bias, query_bias, value_bias, up_bias
     ]
     ids = segment_ids.astype(bf16).reshape(-1)
-    small = cube_gather(hold(jnp.concatenate(smalls + [ids])[None], qkv_shard))
+    small = cube_gather(jnp.concatenate(smalls + [ids])[None])
 
     def full_vector(k):
         return small[:, k * shard : (k + 1) * shard].reshape(-1).astype(f32)
@@ -1156,6 +1213,7 @@
     down_w = z_gather(down_late, 0)
 
     second_norm = spread(normalize(middle, gain_mlp, shift_mlp).astype(bf16))
+    second_norm = jnp.concatenate(second_norm, axis=0)
     hidden, slope = feed_forward(second_norm, up_parts, ubias)
     down_grad = outer_sum(hidden, cotan).astype(bf16)
     slope = hold(slope, down_grad)
@@ -1164,11 +1222,10 @@
     split = inner_grad.shape[0] // 2
     far = times_parts(inner_grad, 1, split, up_parts)
     near = times_parts(hold(inner_grad, far), 0, split, up_parts)
-    norm_rows = jnp.concatenate(second_norm, axis=0)
     up_made = []
 
     def make_up_grad(event):
-        up_made.append(outer_sum(norm_rows, hold(inner_grad, event)).astype(bf16))
+        up_made.append(outer_sum(second_norm, hold(inner_grad, event)).astype(bf16))
         return up_made[0]
 
     second_grad = fold(far, near, make_up_grad)
@@ -1179,25 +1236,31 @@
     dbias_grad = jnp.sum(cotan_own.astype(f32), axis=0)
 
     obias_grad = jnp.sum(branch_own.astype(f32), axis=0)
-    hidden_late = hold(hidden, branch_own)
-    out_far = matmul(hidden_late[split:], down_w).astype(bf16)
-    out_near = matmul(hidden_late[:split], down_w).astype(bf16)
-    branch = narrow_gather(branch_own, out_far, out_near)
-    up_grad = hold(up_made[0], branch[2], down_grad)
+    out_made = []
+
+    def make_outputs(beside):
+        late = hold(hidden, beside)
+        out_made.append(matmul(late[split:], down_w).astype(bf16))
+        out_made.append(matmul(late[:split], down_w).astype(bf16))
+        return out_made
+
+    branch = narrow_gather(branch_own, make_outputs)
+    up_grad = hold(up_made[0], out_made[1], down_grad)
     up_grad = z_scatter(up_grad.reshape(narrow, 2 * deep * shard, ff_local), 1)
     no_bias = jnp.zeros((cols,), f32)
     sent = project(branch, out_w, no_bias, wide, 1, heads, tokens, True)
     out_grad = outer_sum(hold(mixed, sent), jnp.concatenate(branch, axis=0)).astype(bf16)
-    output = middle + fold(out_far, out_near) + dbias
+    output = middle + fold(*hold_all(out_made, sent)) + dbias
     block_output = output.astype(bf16).reshape(batch, tokens, width)
     dout = hold(wide_swap(sent), out_grad, block_output)
     unit_grads = attend_bwd(me, segc, segr, lse, qkv, dout)
     grads = wide_swap(unit_grads)
     up_rows = hold(up_grad, unit_grads).reshape(narrow, 2, shard, ff_local)
-    up_swapped = narrow_swap(lambda n: at(up_rows, n))
-    up_back = pair_swap(lambda y: at(up_swapped, y, 1))
-    up_back = up_back.reshape(2, narrow, shard, deep, ff_shard).transpose(2, 1, 3, 0, 4)
-    up_back = up_back.reshape(shard, -1).astype(f32)
+    up_sent = up_rows
+    up_rows = narrow_blocks(lambda n: at(up_sent, n))
+    up_own = jnp.stack([at(block, me_y) for block in up_rows])
+    up_other = flip(jnp.stack([at(block, 1 - me_y) for block in up_rows]), WIDE, 1)
+    up_back = place_up(me, up_own, up_other, ff_shard)
     down_grad = down_grad.astype(f32)
     grads = hold(grads, up_back)
     order = (1, 3, 0, 2)
@@ -1207,16 +1270,15 @@
 
     def beside(stage, event):
         if stage == 0:
-            late = hold(back, event)
-            far = times_parts(late, 0, 2 * rows, attn_parts)
-            near = times_parts(hold(late, far), 1, 2 * rows, attn_parts)
+            far = times_parts(hold(back, event), 0, 2 * rows, attn_parts)
             made["far"] = far.reshape(2, rows, width)
-            made["near"] = near.reshape(2, rows, width)
-            return far, near
+            return (far,)
         if stage == 1:
-            near, far = made["near"], made["far"]
+            far = made["far"]
+            near = times_parts(hold(back, event), 1, 2 * rows, attn_parts)
+            near = near.reshape(2, rows, width)
             made["first"] = narrow_scatter([near[0], far[0], near[1], far[1]])
-            return (made["first"],)
+            return (near,)
         if stage == 2:
             attn_pull = jax.vjp(normalize, inputs, gain_attn, shift_attn)[1]
             input_part, again_grad, ashift_grad = attn_pull(made["first"])
@@ -1228,8 +1290,7 @@
     out_grad = qkv_rows[..., 3 * cols :].transpose(1, 0, 2).reshape(shard, width)
     qkv_rows = qkv_rows[..., : 3 * cols]
     swapped = narrow_blocks(lambda n: at(qkv_rows, n))
-    qkv_grad = in_order(swapped).reshape(narrow, shard, 3, cols)
-    qkv_grad = qkv_grad.transpose(2, 1, 0, 3).reshape(3, shard, width).astype(f32)
+    qkv_grad = place_qkv(me, swapped)
     back_sums = jnp.sum(back.astype(f32), axis=0)
     input_grad, again_grad, ashift_grad = made["pulled"]
     input_grad = input_grad.reshape(batch, tokens, width)
@@ -1247,7 +1308,7 @@
     slices = jnp.concatenate([v.reshape(wide, -1) for v in slices], axis=1)
     placed = jnp.zeros((narrow * wide, slices.shape[1]), f32)
     placed = lax.dynamic_update_slice_in_dim(placed, slices, me_n * wide, 0)
-    vectors = cube_scatter(hold(jnp.concatenate([fulls, placed], axis=1), swapped[1]))
+    vectors = cube_scatter(jnp.concatenate([fulls, placed], axis=1), swapped[1])
 
     def vector(k):
         return vectors[k * shard : (k + 1) * shard]

time: 873 us -> 844 us (0.967)
  waiting for transfers between devices: 412 us -> 378 us
  local copies, waits for them, and re-layouts: 114 us -> 95.1 us
  starting transfers between devices: 89.9 us -> 106 us
    ppermute x16, waiting for transfers between devices: 119 us -> 83.8 us  [ring_step(): lax.ppermute(value, WIDE, [(order[i], order[(i + by) % size]) for i in ra...]
    ppermute x62, starting transfers between devices: 50.9 us -> 66.2 us  [flip(): return lax.ppermute(value, axis, [(i, i ^ bits) for i in range(size)])]
    all_to_all x4, waiting for transfers between devices: 29.9 us -> 43.9 us  [wide_swap(): return lax.all_to_all(parts, WIDE, split_axis=0, concat_axis=0, tiled=True)]
    ppermute x62, waiting for transfers between devices: 262 us -> 250 us  [flip(): return lax.ppermute(value, axis, [(i, i ^ bits) for i in range(size)])]
    unnamed x142 -> x173, local copies, waits for them, and re-layouts: 54.6 us -> 50 us
    pallas_call x1 -> x3, Pallas kernels: 18.3 us -> 22.1 us  [the longest x1 18.3 us: feed_forward(): pl.pallas_call(ff_kernel, grid=(inner // step,), out_shape=(jax.ShapeDtyp...]
  transfers between devices with their start and end apart: 87 -> 87, of which waited for: 52 -> 53; matrix products, arithmetic and copies ran while one was open for 22% -> 20% of each run, Pallas kernels for 8% -> 9%
where the time goes in v5:
time: 844 us; the launch traced here: 835 us
  waiting for transfers between devices  378 us (45%)
  Pallas kernels  127 us (15%)
  starting transfers between devices  106 us (13%)
  local copies, waits for them, and re-layouts  95.1 us (11%)
  other arithmetic  67.8 us (8%)
  matrix products  44.3 us (5%)
  between operations  15.7 us (2%)
    ppermute x62, waiting for transfers between devices, flip(): return lax.ppermute(value, axis, [(i, i ^ bits) for i in range(size)])  250 us
    ppermute x16, waiting for transfers between devices, ring_step(): lax.ppermute(value, WIDE, [(order[i], order[(i + by) % size]) for i in ra...  83.8 us
    ppermute x62, starting transfers between devices, flip(): return lax.ppermute(value, axis, [(i, i ^ bits) for i in range(size)])  66.2 us
    unnamed x173, local copies, waits for them, and re-layouts  50 us
    all_to_all x4, waiting for transfers between devices, wide_swap(): return lax.all_to_all(parts, WIDE, split_axis=0, concat_axis=0, tiled=True)  43.9 us
    dot_general x3, matrix products, outer_sum(): lax.dot_general(left, right, (((0,), (0,)), ((), ())), preferred_element_...  32.1 us
    pallas_call x4, Pallas kernels, times_parts(): pl.pallas_call(times_parts_kernel, grid=(narrow,), out_shape=jax.ShapeDty...  27.5 us
    ppermute x16, starting transfers between devices, ring_step(): lax.ppermute(value, WIDE, [(order[i], order[(i + by) % size]) for i in ra...  21.7 us
  transfers between devices with their start and end apart: 87, of which 53 were waited for; matrix products, arithmetic and copies ran while one was open for 20% of the time, Pallas kernels for 9%

profile of v5, /device:TPU:0, one launch (start us, length us, event | category | flops | bytes accessed | tf_op | source)
XLA Modules:
  0.0 834.5 jit_solution(15167592451214781712)
XLA Ops:
  26.7 3.6 collective-permute-done.4
  36.8 3.3 broadcast_in_dim.71
  41.0 20.8 %collective-permute-done.11 = bf16[4,64,1536]{2,1,0:T(8,128)(2,1)} collective-permute-done((bf16[4,64,1536]{2,1,0:T(8,128)(2,1)}, bf16[4,64,1536]{2,1,0:T(8,128)(2,1)}, u32[]{:S(2)}, u32[]{:S(2)}) %collective-permute-start.11) | collective-permute-done | bytes 786464 | tf_op jit(solution)/shard_map/ppermute | solution.py:542
  61.8 5.9 collective-permute-start.13
  67.7 3.4 collective-permute-done.12
  76.1 11.8 %collective-permute-done.13 = bf16[4,64,1536]{2,1,0:T(8,128)(2,1)S(1)} collective-permute-done((bf16[4,64,1536]{2,1,0:T(8,128)(2,1)}, bf16[4,64,1536]{2,1,0:T(8,128)(2,1)S(1)}, u32[]{:S(2)}, u32[]{:S(2)}) %collective-permute-start.13) | collective-permute-done | bytes 786464 | tf_op jit(solution)/shard_map/ppermute | solution.py:542
  91.9 13.2 %collective-permute-done.15 = bf16[4,64,1536]{2,1,0:T(8,128)(2,1)S(1)} collective-permute-done((bf16[4,64,1536]{2,1,0:T(8,128)(2,1)S(1)}, bf16[4,64,1536]{2,1,0:T(8,128)(2,1)S(1)}, u32[]{:S(2)}, u32[]{:S(2)}) %collective-permute-start.15) | collective-permute-done | bytes 786464 | tf_op jit(solution)/shard_map/ppermute | solution.py:542
  109.5 3.8 collective-permute-done.17
  116.3 11.5 %project_parts.1 = bf16[8,3,4,128,128]{4,3,2,1,0:T(8,128)(2,1)} custom-call(bf16[256,2048]{1,0:T(8,128)(2,1)S(1)} %fusion.32.refs_0_.refs_8_.refs_9_.refs_10_.refs_11_, bf16[256,2048]{1,0:T(8,128)(2,1)S(1)} %collective-permute-done.5.refs_1_.refs_0_.refs_2_.refs_3_, bf16[256,2048]{1,0:T(8,128)(2,1)S(1)} %collective-permute-done.6.refs_2_.refs_12_.refs_13_.refs_14_.refs_15_, ...), custom_call_target="tpu_custom_call" | custom-call | tf_op jit(solution)/shard_map/project_parts/pallas_call | solution.py:697
  127.8 4.6 all-to-all-start
  138.4 3.3 reshape.422.segc_ref
  141.7 30.5 %collective-permute-done.19 = bf16[4,64,1024]{2,1,0:T(8,128)(2,1)} collective-permute-done((bf16[4,64,1024]{2,1,0:T(8,128)(2,1)}, bf16[4,64,1024]{2,1,0:T(8,128)(2,1)}, u32[]{:S(2)}, u32[]{:S(2)}) %collective-permute-start.19) | collective-permute-done | bytes 524320 | tf_op jit(solution)/shard_map/ppermute | solution.py:379
  176.3 4.7 collective-permute-done.20
  181.0 6.8 collective-permute-done.21
  189.1 10.9 %all-to-all-done.parts_ref = bf16[8,3,4,128,128]{4,3,2,1,0:T(8,128)(2,1)} async-done(((bf16[8,3,4,128,128]{4,3,2,1,0:T(8,128)(2,1)}), bf16[8,3,4,128,128]{4,3,2,1,0:T(8,128)(2,1)}, u32[]{:S(2)}, u32[]{:S(2)}) %all-to-all-start) | async-done | bytes 3145760 | tf_op jit(solution)/shard_map/all_to_all | solution.py:605
  201.6 8.2 attend_fwd.1
  213.3 4.2 all-to-all-start.1
  220.7 23.8 %collective-permute-done.24 = bf16[256,2048]{1,0:T(8,128)(2,1)} collective-permute-done((bf16[256,2048]{1,0:T(8,128)(2,1)}, bf16[256,2048]{1,0:T(8,128)(2,1)}, u32[]{:S(2)}, u32[]{:S(2)}) %collective-permute-start.24) | collective-permute-done | bytes 1048608 | tf_op jit(solution)/shard_map/ppermute | solution.py:379
  263.5 6.3 all-to-all-done.1.parts_ref
  269.9 5.9 unproject.1
  281.6 3.3 collective-permute-start.29
  294.7 14.0 %collective-permute-done.29 = bf16[256,2048]{1,0:T(8,128)(2,1)} collective-permute-done((bf16[256,2048]{1,0:T(8,128)(2,1)}, bf16[256,2048]{1,0:T(8,128)(2,1)}, u32[]{:S(2)}, u32[]{:S(2)}) %collective-permute-start.29) | collective-permute-done | bytes 1048608 | tf_op jit(solution)/shard_map/ppermute | solution.py:379
  308.7 3.5 fusion.37
  320.1 22.4 %collective-permute-done.35 = bf16[256,2048]{1,0:T(8,128)(2,1)S(1)} collective-permute-done((bf16[256,2048]{1,0:T(8,128)(2,1)S(1)}, bf16[256,2048]{1,0:T(8,128)(2,1)S(1)}, u32[]{:S(2)}, u32[]{:S(2)}) %collective-permute-start.35) | collective-permute-done | bytes 1048608 | tf_op jit(solution)/shard_map/ppermute | solution.py:379
  351.9 5.4 collective-permute-done.36
  370.9 18.3 %feed_forward.1 = (bf16[2048,1024]{1,0:T(8,128)(2,1)S(1)}, f32[2048,1024]{1,0:T(8,128)}) custom-call(bf16[2048,2048]{1,0:T(8,128)(2,1)} %constant_dynamic-update-slice_fusion.10.rows_ref, bf16[4,4,128,1024]{3,2,1,0:T(8,128)(2,1)} %bitcast.221, bf16[4,4,128,1024]{3,2,1,0:T(8,128)(2,1)} %bitcast.222, bf16[4,4,128,1024]{3,2,1,0:T(8,128)(2,1)} %bitcast.223, ...), custom_call_target="tpu_custom_call" | custom-call | tf_op jit(solution)/shard_map/feed_forward/pallas_call | solution.py:981
  391.2 12.8 %convolution_convert_fusion = bf16[1024,2048]{1,0:T(8,128)(2,1)} fusion(bf16[2048,1024]{1,0:T(8,128)(2,1)S(1)} %get-tuple-element.95, bf16[2048,2048]{1,0:T(8,128)(2,1)} %constant_dynamic-update-slice_fusion.2.rows_ref), kind=kOutput, calls=%fused_computation.9 | convolution fusion | flops 8592031744 | bytes 16777216 | tf_op jit(solution)/shard_map/dot_general | solution.py:46
  404.0 14.6 %pull_back.1 = (bf16[2048,1024]{1,0:T(8,128)(2,1)S(1)}, f32[1,1024]{1,0:T(1,128)S(1)}) custom-call(bf16[2048,2048]{1,0:T(8,128)(2,1)} %constant_dynamic-update-slice_fusion.2.rows_ref, bf16[1024,2048]{1,0:T(8,128)(2,1)} %all-gather.7.cloned.1.call-done.weight_ref, f32[2048,1024]{1,0:T(8,128)} %get-tuple-element.90.slope_ref), custom_call_target="tpu_custom_call" | custom-call | tf_op jit(solution)/shard_map/pull_back/pallas_call | solution.py:1022
  420.7 7.4 times_parts.4
  428.6 7.8 times_parts.5
  436.4 3.9 convert_add_fusion.11
  447.0 9.2 %collective-permute-done.43 = bf16[256,1024]{1,0:T(8,128)(2,1)} collective-permute-done((bf16[256,1024]{1,0:T(8,128)(2,1)}, bf16[256,1024]{1,0:T(8,128)(2,1)}, u32[]{:S(2)}, u32[]{:S(2)}) %collective-permute-start.43) | collective-permute-done | bytes 524320 | tf_op jit(solution)/shard_map/ppermute | solution.py:379
  460.0 12.9 %convolution_convert_fusion.3 = bf16[2048,1024]{1,0:T(8,128)(2,1)} fusion(bf16[2048,2048]{1,0:T(8,128)(2,1)} %constant_dynamic-update-slice_fusion.10.rows_ref, bf16[2048,1024]{1,0:T(8,128)(2,1)S(1)} %copy-done.5), kind=kOutput, calls=%fused_computation.12 | convolution fusion | flops 8592031744 | bytes 16777216 | tf_op jit(solution)/shard_map/dot_general | solution.py:46
  472.9 9.0 %collective-permute-done.44 = bf16[256,2048]{1,0:T(8,128)(2,1)S(1)} collective-permute-done((bf16[256,2048]{1,0:T(8,128)(2,1)S(1)}, bf16[256,2048]{1,0:T(8,128)(2,1)S(1)}, u32[]{:S(2)}, u32[]{:S(2)}) %collective-permute-start.44) | collective-permute-done | bytes 1048608 | tf_op jit(solution)/shard_map/ppermute | solution.py:379
  491.4 6.1 convolution_convert_fusion.1
  497.5 6.1 convolution_convert_fusion.2
  503.6 10.4 %collective-permute-done.48.refs_2_ = bf16[256,2048]{1,0:T(8,128)(2,1)S(1)} collective-permute-done((bf16[256,2048]{1,0:T(8,128)(2,1)S(1)}, bf16[256,2048]{1,0:T(8,128)(2,1)S(1)}, u32[]{:S(2)}, u32[]{:S(2)}) %collective-permute-start.48) | collective-permute-done | bytes 1048608 | tf_op jit(solution)/shard_map/ppermute | solution.py:379
  516.6 5.2 project.1
  523.0 7.3 collective-permute-done.50
  530.3 6.1 convert_add_fusion.7
  537.8 4.2 all-to-all-start.2
  546.6 7.7 collective-permute-done.51
  562.8 6.3 fusion.8.refs_17_
  569.2 10.9 %collective-permute-done.52 = bf16[256,2048]{1,0:T(8,128)(2,1)} collective-permute-done((bf16[256,2048]{1,0:T(8,128)(2,1)}, bf16[256,2048]{1,0:T(8,128)(2,1)}, u32[]{:S(2)}, u32[]{:S(2)}) %collective-permute-start.52) | collective-permute-done | bytes 1048608 | tf_op jit(solution)/shard_map/ppermute | solution.py:379
  580.1 7.6 collective-permute-done.54
  587.6 4.1 fusion.22
  591.7 5.2 all-to-all-done.2.do_ref
  600.1 17.5 %attend_bwd.1 = bf16[8,3,4,128,128]{4,3,2,1,0:T(8,128)(2,1)} custom-call(s32[2]{0:T(128)S(1)} %pad_add_fusion.me_ref, s32[8,512,1]{2,1,0:T(8,128)S(1)} %copy-done.3, s32[1,4096]{1,0:T(1,128)S(1)} %fusion.59.segr_ref, f32[8,512,1]{2,1,0:T(8,128)S(1)} %copy-done.13, bf16[8,3,4,128,128]{4,3,2,1,0:T(8,128)(2,1)} %all-to-all-done.parts_ref, ...), custom_call_target="tpu_custom_call" | custom-call | tf_op jit(solution)/shard_map/attend_bwd/pallas_call | solution.py:945
  617.6 4.5 all-to-all-start.3
  627.9 5.6 collective-permute-done.56
  634.5 3.8 collective-permute-done.57
  640.3 26.5 %collective-permute-done.58.other_ref = bf16[4,64,1024]{2,1,0:T(8,128)(2,1)S(1)} collective-permute-done((bf16[4,64,1024]{2,1,0:T(8,128)(2,1)S(1)}, bf16[4,64,1024]{2,1,0:T(8,128)(2,1)S(1)}, u32[]{:S(2)}, u32[]{:S(2)}) %collective-permute-start.58) | collective-permute-done | bytes 524320 | tf_op jit(solution)/shard_map/ppermute | solution.py:379
  668.9 21.4 %all-to-all-done.3.parts_ref = bf16[8,3,4,128,128]{4,3,2,1,0:T(8,128)(2,1)} async-done(((bf16[8,3,4,128,128]{4,3,2,1,0:T(8,128)(2,1)}), bf16[8,3,4,128,128]{4,3,2,1,0:T(8,128)(2,1)}, u32[]{:S(2)}, u32[]{:S(2)}) %all-to-all-start.3) | async-done | bytes 3145760 | tf_op jit(solution)/shard_map/all_to_all | solution.py:605
  694.4 11.8 %wide_outer.1 = bf16[8,4,64,2048]{3,2,1,0:T(8,128)(2,1)} custom-call(bf16[256,2048]{1,0:T(8,128)(2,1)S(1)} %collective-permute-done.5.refs_1_.refs_0_.refs_2_.refs_3_, bf16[256,2048]{1,0:T(8,128)(2,1)S(1)} %collective-permute-done.5.refs_1_.refs_0_.refs_2_.refs_3_, bf16[256,2048]{1,0:T(8,128)(2,1)S(1)} %collective-permute-done.5.refs_1_.refs_0_.refs_2_.refs_3_, ...), custom_call_target="tpu_custom_call" | custom-call | tf_op jit(solution)/shard_map/wide_outer/pallas_call | solution.py:765
  710.8 6.0 times_parts.6
  725.7 6.3 times_parts.7
  734.6 4.5 collective-permute-start.63
  743.8 3.9 collective-permute-done.66
  755.1 8.2 collective-permute-done.63
  770.7 5.3 collective-permute-done.68
  776.9 3.6 fusion.11
  785.0 4.6 collective-permute-start.65
  789.7 12.7 %collective-permute-done.70 = bf16[4,64,2048]{2,1,0:T(8,128)(2,1)} collective-permute-done((bf16[4,64,2048]{2,1,0:T(8,128)(2,1)}, bf16[4,64,2048]{2,1,0:T(8,128)(2,1)}, u32[]{:S(2)}, u32[]{:S(2)}) %collective-permute-start.70) | collective-permute-done | bytes 1048608 | tf_op jit(solution)/shard_map/ppermute | solution.py:542
  813.7 3.6 collective-permute-start.76
  (473 shorter events, 250.6 us)
Async XLA Ops:
  7.3 109.0 %all-gather.5.cloned.1.call-start = ((), (), s32[]{:S(2)}) async-start(), calls=%async_computation.6 | async-start | bytes 2359296 | tf_op jit(solution)/shard_map/all_gather | solution.py:609
  9.6 22.2 %collective-permute-start.10 = (bf16[64,1536]{1,0:T(8,128)(2,1)S(1)}, bf16[64,1536]{1,0:T(8,128)(2,1)S(1)}, u32[]{:S(2)}, u32[]{:S(2)}) collective-permute-start(bf16[64,1536]{1,0:T(8,128)(2,1)S(1)} %pad_maximum_fusion.13), channel_id=1, source_target_pairs={{0,8},{8,0},{16,24},{24,16},{1,9},{9,1},{17,25},{25,17},{2,10},{10... | collective-permute-start | bytes 589832 | tf_op jit(solution)/shard_map/ppermute | solution.py:379
  10.1 21.7 %collective-permute-start.8 = (bf16[64,1536]{1,0:T(8,128)(2,1)S(1)}, bf16[64,1536]{1,0:T(8,128)(2,1)S(1)}, u32[]{:S(2)}, u32[]{:S(2)}) collective-permute-start(bf16[64,1536]{1,0:T(8,128)(2,1)S(1)} %pad_maximum_fusion.11), channel_id=1, source_target_pairs={{0,24},{8,16},{16,8},{24,0},{1,25},{9,17},{17,9},{25,1},{2,26},{10... | collective-permute-start | bytes 589832 | tf_op jit(solution)/shard_map/ppermute | solution.py:379
  14.6 17.2 %collective-permute-start.9 = (bf16[64,1536]{1,0:T(8,128)(2,1)S(1)}, bf16[64,1536]{1,0:T(8,128)(2,1)S(1)}, u32[]{:S(2)}, u32[]{:S(2)}) collective-permute-start(bf16[64,1536]{1,0:T(8,128)(2,1)S(1)} %pad_maximum_fusion.12), channel_id=1, source_target_pairs={{0,16},{8,24},{16,0},{24,8},{1,17},{9,25},{17,1},{25,9},{2,18},{10... | collective-permute-start | bytes 589832 | tf_op jit(solution)/shard_map/ppermute | solution.py:379
  33.1 28.7 %collective-permute-start.11 = (bf16[4,64,1536]{2,1,0:T(8,128)(2,1)}, bf16[4,64,1536]{2,1,0:T(8,128)(2,1)}, u32[]{:S(2)}, u32[]{:S(2)}) collective-permute-start(bf16[4,64,1536]{2,1,0:T(8,128)(2,1)} %pad_maximum_fusion.8), channel_id=1, source_target_pairs={{0,2},{2,4},{4,6},{6,7},{7,5},{5,3},{3,1},{1,0},{8,10},{10,12},{12... | collective-permute-start | bytes 2359304 | tf_op jit(solution)/shard_map/ppermute | solution.py:542
  34.6 36.4 %collective-permute-start.12 = (bf16[4,64,1536]{2,1,0:T(8,128)(2,1)}, bf16[4,64,1536]{2,1,0:T(8,128)(2,1)}, u32[]{:S(2)}, u32[]{:S(2)}) collective-permute-start(bf16[4,64,1536]{2,1,0:T(8,128)(2,1)} %pad_maximum_fusion.8), channel_id=1, source_target_pairs={{0,1},{2,0},{4,2},{6,4},{7,6},{5,7},{3,5},{1,3},{8,9},{10,8},{12,1... | collective-permute-start | bytes 2359304 | tf_op jit(solution)/shard_map/ppermute | solution.py:542
  35.6 40.5 %collective-permute-start.6 = (bf16[256,2048]{1,0:T(8,128)(2,1)S(1)}, bf16[256,2048]{1,0:T(8,128)(2,1)S(1)}, u32[]{:S(2)}, u32[]{:S(2)}) collective-permute-start(bf16[256,2048]{1,0:T(8,128)(2,1)S(1)} %fusion.32.refs_0_.refs_8_.refs_9_.refs_10_.refs_11_), channel_id=1, source_target_pairs={{0,16},{8,24},{16,0},{24,8},{1,17},{9,25},{17,1},{25,9},{2,18},{10... | collective-permute-start | bytes 3145736 | tf_op jit(solution)/shard_map/ppermute | solution.py:379
  35.9 80.4 %collective-permute-start.5 = (bf16[256,2048]{1,0:T(8,128)(2,1)S(1)}, bf16[256,2048]{1,0:T(8,128)(2,1)S(1)}, u32[]{:S(2)}, u32[]{:S(2)}) collective-permute-start(bf16[256,2048]{1,0:T(8,128)(2,1)S(1)} %fusion.32.refs_0_.refs_8_.refs_9_.refs_10_.refs_11_), channel_id=1, source_target_pairs={{0,8},{8,0},{16,24},{24,16},{1,9},{9,1},{17,25},{25,17},{2,10},{10... | collective-permute-start | bytes 3145736 | tf_op jit(solution)/shard_map/ppermute | solution.py:379
  61.8 26.2 %collective-permute-start.13 = (bf16[4,64,1536]{2,1,0:T(8,128)(2,1)}, bf16[4,64,1536]{2,1,0:T(8,128)(2,1)S(1)}, u32[]{:S(2)}, u32[]{:S(2)}) collective-permute-start(bf16[4,64,1536]{2,1,0:T(8,128)(2,1)} %collective-permute-done.11), channel_id=1, source_target_pairs={{0,2},{2,4},{4,6},{6,7},{7,5},{5,3},{3,1},{1,0},{8,10},{10,12},{12... | collective-permute-start | bytes 2359304 | tf_op jit(solution)/shard_map/ppermute | solution.py:542
  71.1 18.0 %collective-permute-start.14 = (bf16[4,64,1536]{2,1,0:T(8,128)(2,1)}, bf16[4,64,1536]{2,1,0:T(8,128)(2,1)S(1)}, u32[]{:S(2)}, u32[]{:S(2)}) collective-permute-start(bf16[4,64,1536]{2,1,0:T(8,128)(2,1)} %collective-permute-done.12), channel_id=1, source_target_pairs={{0,1},{2,0},{4,2},{6,4},{7,6},{5,7},{3,5},{1,3},{8,9},{10,8},{12,1... | collective-permute-start | bytes 2359304 | tf_op jit(solution)/shard_map/ppermute | solution.py:542
  76.1 40.1 %collective-permute-start.7 = (bf16[256,2048]{1,0:T(8,128)(2,1)S(1)}, bf16[256,2048]{1,0:T(8,128)(2,1)}, u32[]{:S(2)}, u32[]{:S(2)}) collective-permute-start(bf16[256,2048]{1,0:T(8,128)(2,1)S(1)} %collective-permute-done.6.refs_2_.refs_12_.refs_13_.refs_14_.refs_15_), channel_id=1, source_target_pairs={{0,8},{8,0},{16,24},{24,16},{1,9},{9,1},{17,25},{25,17},{2,10},{10... | collective-permute-start | bytes 3145736 | tf_op jit(solution)/shard_map/ppermute | solution.py:379
  88.0 17.2 %collective-permute-start.15 = (bf16[4,64,1536]{2,1,0:T(8,128)(2,1)S(1)}, bf16[4,64,1536]{2,1,0:T(8,128)(2,1)S(1)}, u32[]{:S(2)}, u32[]{:S(2)}) collective-permute-start(bf16[4,64,1536]{2,1,0:T(8,128)(2,1)S(1)} %collective-permute-done.13), channel_id=1, source_target_pairs={{0,2},{2,4},{4,6},{6,7},{7,5},{5,3},{3,1},{1,0},{8,10},{10,12},{12... | collective-permute-start | bytes 2359304 | tf_op jit(solution)/shard_map/ppermute | solution.py:542
  89.1 17.9 %collective-permute-start.16 = (bf16[4,64,1536]{2,1,0:T(8,128)(2,1)S(1)}, bf16[4,64,1536]{2,1,0:T(8,128)(2,1)S(1)}, u32[]{:S(2)}, u32[]{:S(2)}) collective-permute-start(bf16[4,64,1536]{2,1,0:T(8,128)(2,1)S(1)} %collective-permute-done.14), channel_id=1, source_target_pairs={{0,1},{2,0},{4,2},{6,4},{7,6},{5,7},{3,5},{1,3},{8,9},{10,8},{12,1... | collective-permute-start | bytes 2359304 | tf_op jit(solution)/shard_map/ppermute | solution.py:542
  127.8 72.2 %all-to-all-start = ((bf16[8,3,4,128,128]{4,3,2,1,0:T(8,128)(2,1)}), bf16[8,3,4,128,128]{4,3,2,1,0:T(8,128)(2,1)}, u32[]{:S(2)}, u32[]{:S(2)}) async-start(bf16[8,3,4,128,128]{4,3,2,1,0:T(8,128)(2,1)} %project_parts.1), calls=%async_computation | async-start | bytes 6291456 | tf_op jit(solution)/shard_map/all_to_all | solution.py:605
  132.4 179.8 %all-gather.9.cloned.1.call-start = ((), (), s32[]{:S(2)}) async-start(), calls=%async_computation.10 | async-start | bytes 5242880 | tf_op jit(solution)/shard_map/all_gather | solution.py:515
  136.4 35.7 %collective-permute-start.19 = (bf16[4,64,1024]{2,1,0:T(8,128)(2,1)}, bf16[4,64,1024]{2,1,0:T(8,128)(2,1)}, u32[]{:S(2)}, u32[]{:S(2)}) collective-permute-start(bf16[4,64,1024]{2,1,0:T(8,128)(2,1)} %slice_bitcast_fusion.9), channel_id=1, source_target_pairs={{0,1},{1,0},{2,3},{3,2},{4,5},{5,4},{6,7},{7,6},{8,9},{9,8},{10,11... | collective-permute-start | bytes 1572872 | tf_op jit(solution)/shard_map/ppermute | solution.py:379
  173.6 14.2 %collective-permute-start.21 = (bf16[2,64,1024]{2,1,0:T(8,128)(2,1)S(1)}, bf16[2,64,1024]{2,1,0:T(8,128)(2,1)S(1)}, u32[]{:S(2)}, u32[]{:S(2)}) collective-permute-start(bf16[2,64,1024]{2,1,0:T(8,128)(2,1)S(1)} %get-tuple-element.173), channel_id=1, source_target_pairs={{0,16},{8,24},{16,0},{24,8},{1,17},{9,25},{17,1},{25,9},{2,18},{10... | collective-permute-start | bytes 786440 | tf_op jit(solution)/shard_map/ppermute | solution.py:379
  176.3 11.5 %collective-permute-start.22 = (bf16[2,64,1024]{2,1,0:T(8,128)(2,1)S(1)}, bf16[2,64,1024]{2,1,0:T(8,128)(2,1)S(1)}, u32[]{:S(2)}, u32[]{:S(2)}) collective-permute-start(bf16[2,64,1024]{2,1,0:T(8,128)(2,1)S(1)} %get-tuple-element.171), channel_id=1, source_target_pairs={{0,8},{8,0},{16,24},{24,16},{1,9},{9,1},{17,25},{25,17},{2,10},{10... | collective-permute-start | bytes 786440 | tf_op jit(solution)/shard_map/ppermute | solution.py:379
  212.0 32.4 %collective-permute-start.24 = (bf16[256,2048]{1,0:T(8,128)(2,1)}, bf16[256,2048]{1,0:T(8,128)(2,1)}, u32[]{:S(2)}, u32[]{:S(2)}) collective-permute-start(bf16[256,2048]{1,0:T(8,128)(2,1)} %bitcast.227), channel_id=1, source_target_pairs={{0,1},{1,0},{2,3},{3,2},{4,5},{5,4},{6,7},{7,6},{8,9},{9,8},{10,11... | collective-permute-start | bytes 3145736 | tf_op jit(solution)/shard_map/ppermute | solution.py:379
  213.3 56.5 %all-to-all-start.1 = ((bf16[8,1,4,128,128]{4,3,2,1,0:T(8,128)(2,1)}), bf16[8,1,4,128,128]{4,3,2,1,0:T(8,128)(2,1)}, u32[]{:S(2)}, u32[]{:S(2)}) async-start(bf16[8,1,4,128,128]{4,3,2,1,0:T(8,128)(2,1)} %copy-done.15), calls=%async_computation.1 | async-start | bytes 2097152 | tf_op jit(solution)/shard_map/all_to_all | solution.py:605
  217.6 186.4 %all-gather.7.cloned.1.call-start = ((), (), s32[]{:S(2)}) async-start(), calls=%async_computation.7 | async-start | bytes 5242880 | tf_op jit(solution)/shard_map/all_gather | solution.py:515
  218.1 32.4 %collective-permute-start.23 = (bf16[256,2048]{1,0:T(8,128)(2,1)}, bf16[256,2048]{1,0:T(8,128)(2,1)}, u32[]{:S(2)}, u32[]{:S(2)}) collective-permute-start(bf16[256,2048]{1,0:T(8,128)(2,1)} %bitcast.228), channel_id=1, source_target_pairs={{0,16},{8,24},{16,0},{24,8},{1,17},{9,25},{17,1},{25,9},{2,18},{10... | collective-permute-start | bytes 3145736 | tf_op jit(solution)/shard_map/ppermute | solution.py:379
  245.5 12.6 %collective-permute-start.25 = (bf16[256,1024]{1,0:T(8,128)(2,1)S(1)}, bf16[256,1024]{1,0:T(8,128)(2,1)S(1)}, u32[]{:S(2)}, u32[]{:S(2)}) collective-permute-start(bf16[256,1024]{1,0:T(8,128)(2,1)S(1)} %slice.336), channel_id=1, source_target_pairs={{0,16},{8,24},{16,0},{24,8},{1,17},{9,25},{17,1},{25,9},{2,18},{10... | collective-permute-start | bytes 1572872 | tf_op jit(solution)/shard_map/ppermute | solution.py:379
  251.6 10.8 %collective-permute-start.26 = (bf16[256,1024]{1,0:T(8,128)(2,1)S(1)}, bf16[256,1024]{1,0:T(8,128)(2,1)S(1)}, u32[]{:S(2)}, u32[]{:S(2)}) collective-permute-start(bf16[256,1024]{1,0:T(8,128)(2,1)S(1)} %slice.337), channel_id=1, source_target_pairs={{0,1},{1,0},{2,3},{3,2},{4,5},{5,4},{6,7},{7,6},{8,9},{9,8},{10,11... | collective-permute-start | bytes 1572872 | tf_op jit(solution)/shard_map/ppermute | solution.py:379
  276.4 11.0 %collective-permute-start.31 = (bf16[256,2048]{1,0:T(8,128)(2,1)}, bf16[256,2048]{1,0:T(8,128)(2,1)}, u32[]{:S(2)}, u32[]{:S(2)}) collective-permute-start(bf16[256,2048]{1,0:T(8,128)(2,1)} %collective-permute-done.23), channel_id=1, source_target_pairs={{0,8},{8,0},{16,24},{24,16},{1,9},{9,1},{17,25},{25,17},{2,10},{10... | collective-permute-start | bytes 3145736 | tf_op jit(solution)/shard_map/ppermute | solution.py:379
  276.5 15.8 %collective-permute-start.33 = (bf16[256,2048]{1,0:T(8,128)(2,1)}, bf16[256,2048]{1,0:T(8,128)(2,1)}, u32[]{:S(2)}, u32[]{:S(2)}) collective-permute-start(bf16[256,2048]{1,0:T(8,128)(2,1)} %get-tuple-element.85), channel_id=1, source_target_pairs={{0,8},{8,0},{16,24},{24,16},{1,9},{9,1},{17,25},{25,17},{2,10},{10... | collective-permute-start | bytes 3145736 | tf_op jit(solution)/shard_map/ppermute | solution.py:379
  276.9 12.9 %collective-permute-start.32 = (bf16[256,2048]{1,0:T(8,128)(2,1)}, bf16[256,2048]{1,0:T(8,128)(2,1)}, u32[]{:S(2)}, u32[]{:S(2)}) collective-permute-start(bf16[256,2048]{1,0:T(8,128)(2,1)} %collective-permute-done.24), channel_id=1, source_target_pairs={{0,8},{8,0},{16,24},{24,16},{1,9},{9,1},{17,25},{25,17},{2,10},{10... | collective-permute-start | bytes 3145736 | tf_op jit(solution)/shard_map/ppermute | solution.py:379
  278.6 16.1 %collective-permute-start.27 = (bf16[256,2048]{1,0:T(8,128)(2,1)}, bf16[256,2048]{1,0:T(8,128)(2,1)}, u32[]{:S(2)}, u32[]{:S(2)}) collective-permute-start(bf16[256,2048]{1,0:T(8,128)(2,1)} %get-tuple-element.78), channel_id=1, source_target_pairs={{0,8},{8,0},{16,24},{24,16},{1,9},{9,1},{17,25},{25,17},{2,10},{10... | collective-permute-start | bytes 3145736 | tf_op jit(solution)/shard_map/ppermute | solution.py:379
  281.6 27.1 %collective-permute-start.29 = (bf16[256,2048]{1,0:T(8,128)(2,1)}, bf16[256,2048]{1,0:T(8,128)(2,1)}, u32[]{:S(2)}, u32[]{:S(2)}) collective-permute-start(bf16[256,2048]{1,0:T(8,128)(2,1)} %add_convert_fusion.2), channel_id=1, source_target_pairs={{0,16},{8,24},{16,0},{24,8},{1,17},{9,25},{17,1},{25,9},{2,18},{10... | collective-permute-start | bytes 3145736 | tf_op jit(solution)/shard_map/ppermute | solution.py:379
  314.0 208.9 %reduce-scatter.3.cloned.1.call-start = ((), (), s32[]{:S(2)}) async-start(), calls=%async_computation.8 | async-start | bytes 5242880 | tf_op jit(solution)/shard_map/reduce_scatter | solution.py:520
  317.7 24.7 %collective-permute-start.35 = (bf16[256,2048]{1,0:T(8,128)(2,1)S(1)}, bf16[256,2048]{1,0:T(8,128)(2,1)S(1)}, u32[]{:S(2)}, u32[]{:S(2)}) collective-permute-start(bf16[256,2048]{1,0:T(8,128)(2,1)S(1)} %get-tuple-element.137), channel_id=1, source_target_pairs={{0,1},{1,0},{2,3},{3,2},{4,5},{5,4},{6,7},{7,6},{8,9},{9,8},{10,11... | collective-permute-start | bytes 3145736 | tf_op jit(solution)/shard_map/ppermute | solution.py:379
  318.3 27.4 %collective-permute-start.34 = (bf16[256,2048]{1,0:T(8,128)(2,1)S(1)}, bf16[256,2048]{1,0:T(8,128)(2,1)S(1)}, u32[]{:S(2)}, u32[]{:S(2)}) collective-permute-start(bf16[256,2048]{1,0:T(8,128)(2,1)S(1)} %get-tuple-element.137), channel_id=1, source_target_pairs={{0,16},{8,24},{16,0},{24,8},{1,17},{9,25},{17,1},{25,9},{2,18},{10... | collective-permute-start | bytes 3145736 | tf_op jit(solution)/shard_map/ppermute | solution.py:379
  344.2 13.0 %collective-permute-start.36 = (bf16[256,1024]{1,0:T(8,128)(2,1)}, bf16[256,1024]{1,0:T(8,128)(2,1)}, u32[]{:S(2)}, u32[]{:S(2)}) collective-permute-start(bf16[256,1024]{1,0:T(8,128)(2,1)} %slice.344), channel_id=1, source_target_pairs={{0,16},{8,24},{16,0},{24,8},{1,17},{9,25},{17,1},{25,9},{2,18},{10... | collective-permute-start | bytes 1572872 | tf_op jit(solution)/shard_map/ppermute | solution.py:379
  347.5 12.5 %collective-permute-start.37 = (bf16[256,1024]{1,0:T(8,128)(2,1)}, bf16[256,1024]{1,0:T(8,128)(2,1)}, u32[]{:S(2)}, u32[]{:S(2)}) collective-permute-start(bf16[256,1024]{1,0:T(8,128)(2,1)} %slice.345), channel_id=1, source_target_pairs={{0,1},{1,0},{2,3},{3,2},{4,5},{5,4},{6,7},{7,6},{8,9},{9,8},{10,11... | collective-permute-start | bytes 1572872 | tf_op jit(solution)/shard_map/ppermute | solution.py:379
  348.7 17.6 %collective-permute-start.38 = (bf16[256,2048]{1,0:T(8,128)(2,1)}, bf16[256,2048]{1,0:T(8,128)(2,1)S(1)}, u32[]{:S(2)}, u32[]{:S(2)}) collective-permute-start(bf16[256,2048]{1,0:T(8,128)(2,1)} %copy-done.49), channel_id=1, source_target_pairs={{0,8},{8,0},{16,24},{24,16},{1,9},{9,1},{17,25},{25,17},{2,10},{10... | collective-permute-start | bytes 3145736 | tf_op jit(solution)/shard_map/ppermute | solution.py:379
  348.8 18.7 %collective-permute-start.39 = (bf16[256,2048]{1,0:T(8,128)(2,1)}, bf16[256,2048]{1,0:T(8,128)(2,1)S(1)}, u32[]{:S(2)}, u32[]{:S(2)}) collective-permute-start(bf16[256,2048]{1,0:T(8,128)(2,1)} %copy-done.43), channel_id=1, source_target_pairs={{0,8},{8,0},{16,24},{24,16},{1,9},{9,1},{17,25},{25,17},{2,10},{10... | collective-permute-start | bytes 3145736 | tf_op jit(solution)/shard_map/ppermute | solution.py:379
  349.3 19.3 %collective-permute-start.40 = (bf16[256,2048]{1,0:T(8,128)(2,1)}, bf16[256,2048]{1,0:T(8,128)(2,1)S(1)}, u32[]{:S(2)}, u32[]{:S(2)}) collective-permute-start(bf16[256,2048]{1,0:T(8,128)(2,1)} %copy-done.41), channel_id=1, source_target_pairs={{0,8},{8,0},{16,24},{24,16},{1,9},{9,1},{17,25},{25,17},{2,10},{10... | collective-permute-start | bytes 3145736 | tf_op jit(solution)/shard_map/ppermute | solution.py:379
  442.1 14.2 %collective-permute-start.43 = (bf16[256,1024]{1,0:T(8,128)(2,1)}, bf16[256,1024]{1,0:T(8,128)(2,1)}, u32[]{:S(2)}, u32[]{:S(2)}) collective-permute-start(bf16[256,1024]{1,0:T(8,128)(2,1)} %get-tuple-element.166), channel_id=1, source_target_pairs={{0,1},{1,0},{2,3},{3,2},{4,5},{5,4},{6,7},{7,6},{8,9},{9,8},{10,11... | collective-permute-start | bytes 1572872 | tf_op jit(solution)/shard_map/ppermute | solution.py:379
  443.8 178.3 %reduce-scatter.5.cloned.1.call-start = ((), (), s32[]{:S(2)}) async-start(), calls=%async_computation.9 | async-start | bytes 5242880 | tf_op jit(solution)/shard_map/reduce_scatter | solution.py:520
  445.4 13.9 %collective-permute-start.45 = (bf16[256,1024]{1,0:T(8,128)(2,1)}, bf16[256,1024]{1,0:T(8,128)(2,1)S(1)}, u32[]{:S(2)}, u32[]{:S(2)}) collective-permute-start(bf16[256,1024]{1,0:T(8,128)(2,1)} %get-tuple-element.167), channel_id=1, source_target_pairs={{0,16},{8,24},{16,0},{24,8},{1,17},{9,25},{17,1},{25,9},{2,18},{10... | collective-permute-start | bytes 1572872 | tf_op jit(solution)/shard_map/ppermute | solution.py:379
  457.6 24.3 %collective-permute-start.44 = (bf16[256,2048]{1,0:T(8,128)(2,1)S(1)}, bf16[256,2048]{1,0:T(8,128)(2,1)S(1)}, u32[]{:S(2)}, u32[]{:S(2)}) collective-permute-start(bf16[256,2048]{1,0:T(8,128)(2,1)S(1)} %pad_maximum_fusion.2), channel_id=1, source_target_pairs={{0,16},{8,24},{16,0},{24,8},{1,17},{9,25},{17,1},{25,9},{2,18},{10... | collective-permute-start | bytes 3145736 | tf_op jit(solution)/shard_map/ppermute | solution.py:379
  459.5 24.1 %collective-permute-start.46 = (bf16[256,2048]{1,0:T(8,128)(2,1)S(1)}, bf16[256,2048]{1,0:T(8,128)(2,1)S(1)}, u32[]{:S(2)}, u32[]{:S(2)}) collective-permute-start(bf16[256,2048]{1,0:T(8,128)(2,1)S(1)} %pad_maximum_fusion.3), channel_id=1, source_target_pairs={{0,1},{1,0},{2,3},{3,2},{4,5},{5,4},{6,7},{7,6},{8,9},{9,8},{10,11... | collective-permute-start | bytes 3145736 | tf_op jit(solution)/shard_map/ppermute | solution.py:379
  488.4 25.6 %collective-permute-start.48 = (bf16[256,2048]{1,0:T(8,128)(2,1)S(1)}, bf16[256,2048]{1,0:T(8,128)(2,1)S(1)}, u32[]{:S(2)}, u32[]{:S(2)}) collective-permute-start(bf16[256,2048]{1,0:T(8,128)(2,1)S(1)} %get-tuple-element.130.refs_0_), channel_id=1, source_target_pairs={{0,16},{8,24},{16,0},{24,8},{1,17},{9,25},{17,1},{25,9},{2,18},{10... | collective-permute-start | bytes 3145736 | tf_op jit(solution)/shard_map/ppermute | solution.py:379
  537.4 16.8 %collective-permute-start.51 = (bf16[256,1024]{1,0:T(8,128)(2,1)}, bf16[256,1024]{1,0:T(8,128)(2,1)}, u32[]{:S(2)}, u32[]{:S(2)}) collective-permute-start(bf16[256,1024]{1,0:T(8,128)(2,1)} %get-tuple-element.164), channel_id=1, source_target_pairs={{0,1},{1,0},{2,3},{3,2},{4,5},{5,4},{6,7},{7,6},{8,9},{9,8},{10,11... | collective-permute-start | bytes 1572872 | tf_op jit(solution)/shard_map/ppermute | solution.py:379
  537.8 59.1 %all-to-all-start.2 = ((bf16[8,1,4,128,128]{4,3,2,1,0:T(8,128)(2,1)}), bf16[8,1,4,128,128]{4,3,2,1,0:T(8,128)(2,1)}, u32[]{:S(2)}, u32[]{:S(2)}) async-start(bf16[8,1,4,128,128]{4,3,2,1,0:T(8,128)(2,1)} %copy-done.11), calls=%async_computation.2 | async-start | bytes 2097152 | tf_op jit(solution)/shard_map/all_to_all | solution.py:605
  543.5 14.8 %collective-permute-start.53 = (bf16[256,1024]{1,0:T(8,128)(2,1)}, bf16[256,1024]{1,0:T(8,128)(2,1)S(1)}, u32[]{:S(2)}, u32[]{:S(2)}) collective-permute-start(bf16[256,1024]{1,0:T(8,128)(2,1)} %get-tuple-element.165), channel_id=1, source_target_pairs={{0,16},{8,24},{16,0},{24,8},{1,17},{9,25},{17,1},{25,9},{2,18},{10... | collective-permute-start | bytes 1572872 | tf_op jit(solution)/shard_map/ppermute | solution.py:379
  556.6 23.4 %collective-permute-start.52 = (bf16[256,2048]{1,0:T(8,128)(2,1)}, bf16[256,2048]{1,0:T(8,128)(2,1)}, u32[]{:S(2)}, u32[]{:S(2)}) collective-permute-start(bf16[256,2048]{1,0:T(8,128)(2,1)} %pad_maximum_fusion.4), channel_id=1, source_target_pairs={{0,16},{8,24},{16,0},{24,8},{1,17},{9,25},{17,1},{25,9},{2,18},{10... | collective-permute-start | bytes 3145736 | tf_op jit(solution)/shard_map/ppermute | solution.py:379
  559.6 28.0 %collective-permute-start.54 = (bf16[256,2048]{1,0:T(8,128)(2,1)}, bf16[256,2048]{1,0:T(8,128)(2,1)}, u32[]{:S(2)}, u32[]{:S(2)}) collective-permute-start(bf16[256,2048]{1,0:T(8,128)(2,1)} %pad_maximum_fusion.5), channel_id=1, source_target_pairs={{0,1},{1,0},{2,3},{3,2},{4,5},{5,4},{6,7},{7,6},{8,9},{9,8},{10,11... | collective-permute-start | bytes 3145736 | tf_op jit(solution)/shard_map/ppermute | solution.py:379
  617.6 72.7 %all-to-all-start.3 = ((bf16[8,3,4,128,128]{4,3,2,1,0:T(8,128)(2,1)}), bf16[8,3,4,128,128]{4,3,2,1,0:T(8,128)(2,1)}, u32[]{:S(2)}, u32[]{:S(2)}) async-start(bf16[8,3,4,128,128]{4,3,2,1,0:T(8,128)(2,1)} %attend_bwd.1), calls=%async_computation.3 | async-start | bytes 6291456 | tf_op jit(solution)/shard_map/all_to_all | solution.py:605
  624.1 9.4 %collective-permute-start.56 = (bf16[2,64,1024]{2,1,0:T(8,128)(2,1)}, bf16[2,64,1024]{2,1,0:T(8,128)(2,1)}, u32[]{:S(2)}, u32[]{:S(2)}) collective-permute-start(bf16[2,64,1024]{2,1,0:T(8,128)(2,1)} %get-tuple-element.163), channel_id=1, source_target_pairs={{0,16},{8,24},{16,0},{24,8},{1,17},{9,25},{17,1},{25,9},{2,18},{10... | collective-permute-start | bytes 786440 | tf_op jit(solution)/shard_map/ppermute | solution.py:379
  625.8 12.5 %collective-permute-start.57 = (bf16[2,64,1024]{2,1,0:T(8,128)(2,1)S(1)}, bf16[2,64,1024]{2,1,0:T(8,128)(2,1)S(1)}, u32[]{:S(2)}, u32[]{:S(2)}) collective-permute-start(bf16[2,64,1024]{2,1,0:T(8,128)(2,1)S(1)} %get-tuple-element.162), channel_id=1, source_target_pairs={{0,24},{8,16},{16,8},{24,0},{1,25},{9,17},{17,9},{25,1},{2,26},{10... | collective-permute-start | bytes 786440 | tf_op jit(solution)/shard_map/ppermute | solution.py:379
  638.4 28.5 %collective-permute-start.58 = (bf16[4,64,1024]{2,1,0:T(8,128)(2,1)S(1)}, bf16[4,64,1024]{2,1,0:T(8,128)(2,1)S(1)}, u32[]{:S(2)}, u32[]{:S(2)}) collective-permute-start(bf16[4,64,1024]{2,1,0:T(8,128)(2,1)S(1)} %pad_maximum_fusion.10), channel_id=1, source_target_pairs={{0,1},{1,0},{2,3},{3,2},{4,5},{5,4},{6,7},{7,6},{8,9},{9,8},{10,11... | collective-permute-start | bytes 1572872 | tf_op jit(solution)/shard_map/ppermute | solution.py:379
  708.7 13.4 %collective-permute-start.59 = (bf16[4,64,1024]{2,1,0:T(8,128)(2,1)S(1)}, bf16[4,64,1024]{2,1,0:T(8,128)(2,1)S(1)}, u32[]{:S(2)}, u32[]{:S(2)}) collective-permute-start(bf16[4,64,1024]{2,1,0:T(8,128)(2,1)S(1)} %get-tuple-element.106), channel_id=1, source_target_pairs={{0,2},{2,4},{4,6},{6,7},{7,5},{5,3},{3,1},{1,0},{8,10},{10,12},{12... | collective-permute-start | bytes 1572872 | tf_op jit(solution)/shard_map/ppermute | solution.py:542
  708.8 12.1 %collective-permute-start.60 = (bf16[4,64,1024]{2,1,0:T(8,128)(2,1)S(1)}, bf16[4,64,1024]{2,1,0:T(8,128)(2,1)S(1)}, u32[]{:S(2)}, u32[]{:S(2)}) collective-permute-start(bf16[4,64,1024]{2,1,0:T(8,128)(2,1)S(1)} %get-tuple-element.107), channel_id=1, source_target_pairs={{0,1},{2,0},{4,2},{6,4},{7,6},{5,7},{3,5},{1,3},{8,9},{10,8},{12,1... | collective-permute-start | bytes 1572872 | tf_op jit(solution)/shard_map/ppermute | solution.py:542
  718.2 13.8 %collective-permute-start.62 = (bf16[256,2048]{1,0:T(8,128)(2,1)S(1)}, bf16[256,2048]{1,0:T(8,128)(2,1)S(1)}, u32[]{:S(2)}, u32[]{:S(2)}) collective-permute-start(bf16[256,2048]{1,0:T(8,128)(2,1)S(1)} %get-tuple-element.154), channel_id=1, source_target_pairs={{0,8},{8,0},{16,24},{24,16},{1,9},{9,1},{17,25},{25,17},{2,10},{10... | collective-permute-start | bytes 3145736 | tf_op jit(solution)/shard_map/ppermute | solution.py:379
  723.4 24.3 %collective-permute-start.66 = (bf16[4,64,2048]{2,1,0:T(8,128)(2,1)}, bf16[4,64,2048]{2,1,0:T(8,128)(2,1)}, u32[]{:S(2)}, u32[]{:S(2)}) collective-permute-start(bf16[4,64,2048]{2,1,0:T(8,128)(2,1)} %pad_maximum_fusion.6), channel_id=1, source_target_pairs={{0,2},{2,4},{4,6},{6,7},{7,5},{5,3},{3,1},{1,0},{8,10},{10,12},{12... | collective-permute-start | bytes 3145736 | tf_op jit(solution)/shard_map/ppermute | solution.py:542
  725.6 24.3 %collective-permute-start.67 = (bf16[4,64,2048]{2,1,0:T(8,128)(2,1)}, bf16[4,64,2048]{2,1,0:T(8,128)(2,1)}, u32[]{:S(2)}, u32[]{:S(2)}) collective-permute-start(bf16[4,64,2048]{2,1,0:T(8,128)(2,1)} %pad_maximum_fusion.7), channel_id=1, source_target_pairs={{0,1},{2,0},{4,2},{6,4},{7,6},{5,7},{3,5},{1,3},{8,9},{10,8},{12,1... | collective-permute-start | bytes 3145736 | tf_op jit(solution)/shard_map/ppermute | solution.py:542
  725.7 29.4 %collective-permute-start.61 = (bf16[256,2048]{1,0:T(8,128)(2,1)}, bf16[256,2048]{1,0:T(8,128)(2,1)}, u32[]{:S(2)}, u32[]{:S(2)}) collective-permute-start(bf16[256,2048]{1,0:T(8,128)(2,1)} %get-tuple-element.153), channel_id=1, source_target_pairs={{0,8},{8,0},{16,24},{24,16},{1,9},{9,1},{17,25},{25,17},{2,10},{10... | collective-permute-start | bytes 3145736 | tf_op jit(solution)/shard_map/ppermute | solution.py:379
  734.6 28.6 %collective-permute-start.63 = (bf16[256,2048]{1,0:T(8,128)(2,1)}, bf16[256,2048]{1,0:T(8,128)(2,1)}, u32[]{:S(2)}, u32[]{:S(2)}) collective-permute-start(bf16[256,2048]{1,0:T(8,128)(2,1)} %add_convert_fusion), channel_id=1, source_target_pairs={{0,16},{8,24},{16,0},{24,8},{1,17},{9,25},{17,1},{25,9},{2,18},{10... | collective-permute-start | bytes 3145736 | tf_op jit(solution)/shard_map/ppermute | solution.py:379
  753.0 23.1 %collective-permute-start.68 = (bf16[4,64,2048]{2,1,0:T(8,128)(2,1)S(1)}, bf16[4,64,2048]{2,1,0:T(8,128)(2,1)S(1)}, u32[]{:S(2)}, u32[]{:S(2)}) collective-permute-start(bf16[4,64,2048]{2,1,0:T(8,128)(2,1)S(1)} %get-tuple-element.113), channel_id=1, source_target_pairs={{0,2},{2,4},{4,6},{6,7},{7,5},{5,3},{3,1},{1,0},{8,10},{10,12},{12... | collective-permute-start | bytes 3145736 | tf_op jit(solution)/shard_map/ppermute | solution.py:542
  754.4 22.4 %collective-permute-start.69 = (bf16[4,64,2048]{2,1,0:T(8,128)(2,1)S(1)}, bf16[4,64,2048]{2,1,0:T(8,128)(2,1)S(1)}, u32[]{:S(2)}, u32[]{:S(2)}) collective-permute-start(bf16[4,64,2048]{2,1,0:T(8,128)(2,1)S(1)} %get-tuple-element.114), channel_id=1, source_target_pairs={{0,1},{2,0},{4,2},{6,4},{7,6},{5,7},{3,5},{1,3},{8,9},{10,8},{12,1... | collective-permute-start | bytes 3145736 | tf_op jit(solution)/shard_map/ppermute | solution.py:542
  780.5 21.8 %collective-permute-start.70 = (bf16[4,64,2048]{2,1,0:T(8,128)(2,1)}, bf16[4,64,2048]{2,1,0:T(8,128)(2,1)}, u32[]{:S(2)}, u32[]{:S(2)}) collective-permute-start(bf16[4,64,2048]{2,1,0:T(8,128)(2,1)} %get-tuple-element.115), channel_id=1, source_target_pairs={{0,2},{2,4},{4,6},{6,7},{7,5},{5,3},{3,1},{1,0},{8,10},{10,12},{12... | collective-permute-start | bytes 3145736 | tf_op jit(solution)/shard_map/ppermute | solution.py:542
  782.1 21.5 %collective-permute-start.71 = (bf16[4,64,2048]{2,1,0:T(8,128)(2,1)}, bf16[4,64,2048]{2,1,0:T(8,128)(2,1)}, u32[]{:S(2)}, u32[]{:S(2)}) collective-permute-start(bf16[4,64,2048]{2,1,0:T(8,128)(2,1)} %get-tuple-element.116), channel_id=1, source_target_pairs={{0,1},{2,0},{4,2},{6,4},{7,6},{5,7},{3,5},{1,3},{8,9},{10,8},{12,1... | collective-permute-start | bytes 3145736 | tf_op jit(solution)/shard_map/ppermute | solution.py:542
  785.0 21.2 %collective-permute-start.65 = (f32[2,2,2,768]{3,2,1,0:T(2,128)S(1)}, f32[2,2,2,768]{3,2,1,0:T(2,128)S(1)}, u32[]{:S(2)}, u32[]{:S(2)}) collective-permute-start(f32[2,2,2,768]{3,2,1,0:T(2,128)S(1)} %dynamic-slice_bitcast_fusion.13), channel_id=1, source_target_pairs={{0,16},{8,24},{16,0},{24,8},{1,17},{9,25},{17,1},{25,9},{2,18},{10... | collective-permute-start | bytes 73736 | tf_op jit(solution)/shard_map/ppermute | solution.py:379
  (103 other events, 754.3 us)
Sparse Core Ops, SparseCore 0:
  15.3 58.8 all-gather.4
  212.2 98.4 all-gather.8
  314.1 80.1 all-gather.6
  444.0 74.0 reduce-scatter.2
  523.1 91.4 reduce-scatter.4

commit v6 on v5

--- a/solution.py
+++ b/solution.py
@@ -488,7 +488,7 @@
     return near + [flip(part, NARROW, 1) for part in near]
 
 
-def fold(far, near, made=None):
+def fold_first(far, near):
     f32, bf16 = jnp.float32, jnp.bfloat16
     width = far.shape[-1]
     half = width // 2
@@ -500,6 +500,11 @@
     last = flip(both[:, half:], NARROW, 2).astype(f32)
     over_x = jnp.concatenate([over_x[:, :half] + first, over_x[:, half:]], axis=1).astype(bf16)
     over_y = jnp.concatenate([over_y[:, :half], over_y[:, half:] + last], axis=1).astype(bf16)
+    return own, over_x, over_y
+
+
+def fold_last(own, over_x, over_y, made=None):
+    f32 = jnp.float32
     last = flip(over_x, NARROW, 2)
     if made is not None:
         last = hold(last, made(over_x))
@@ -544,61 +549,77 @@
     )
 
 
-def ring_gather(shard):
+def ring_gather(shard, chunks):
     wide = lax.axis_size(WIDE)
     here = ring_position(wide)
-    middle = shard.shape[-1] // 2
     full = jnp.zeros((wide,) + shard.shape, shard.dtype)
-
-    def put(full, piece, position):
-        return lax.dynamic_update_slice_in_dim(
-            full, piece[None], ring_at(position + wide, wide), 0
-        )
-
-    full = put(full, shard, here)
-    ahead = behind = shard
+    zero = jnp.int32(0)
+
+    def put(full, piece, position, column):
+        where = (ring_at(position + wide, wide).astype(jnp.int32), zero, zero, jnp.int32(column))
+        return lax.dynamic_update_slice(full, piece[None], where)
+
+    full = put(full, shard, here, 0)
+    step = shard.shape[-1] // chunks
+    middle = step // 2
+    ahead = [shard[..., c * step : (c + 1) * step] for c in range(chunks)]
+    behind = list(ahead)
     for k in range(1, wide // 2):
-        ahead, behind = ring_step(ahead, 1), ring_step(behind, -1)
-        full = put(put(full, ahead, here - k), behind, here + k)
-    ahead = ring_step(ahead[..., :middle], 1)
-    behind = ring_step(behind[..., middle:], -1)
-    return put(full, jnp.concatenate([ahead, behind], axis=-1), here + wide // 2)
-
-
-def ring_scatter(full, beside):
+        for c in range(chunks):
+            ahead[c], behind[c] = ring_step(ahead[c], 1), ring_step(behind[c], -1)
+        for c in range(chunks):
+            full = put(full, ahead[c], here - k, c * step)
+            full = put(full, behind[c], here + k, c * step)
+    for c in range(chunks):
+        left = ring_step(ahead[c][..., :middle], 1)
+        right = ring_step(behind[c][..., middle:], -1)
+        full = put(full, left, here + wide // 2, c * step)
+        full = put(full, right, here + wide // 2, c * step + middle)
+    return full
+
+
+def ring_scatter(full, beside, chunks):
     wide = lax.axis_size(WIDE)
     here = ring_position(wide)
     bf16, f32 = jnp.bfloat16, jnp.float32
-    middle = full.shape[-1] // 2
-
-    def local(position):
-        return at(full, ring_at(position + wide, wide))
-
-    far = local(here + wide // 2)
-    ahead, behind = lax.optimization_barrier((far[..., :middle], far[..., middle:]))
-    event = ahead
-    stage = 0
-    for k in range(wide // 2 - 1, -1, -1):
-        ahead, behind = ring_step(ahead, 1).astype(f32), ring_step(behind, -1).astype(f32)
+    step = full.shape[-1] // chunks
+    middle = step // 2
+
+    def local(position, c):
+        return at(full, ring_at(position + wide, wide))[..., c * step : (c + 1) * step]
+
+    sent = []
+    for c in range(chunks):
+        far = local(here + wide // 2, c)
+        sent.append(lax.optimization_barrier((far[..., :middle], far[..., middle:])))
+    event = sent[0][0]
+    for stage, k in enumerate(range(wide // 2 - 1, -1, -1)):
+        came = [
+            (ring_step(sent[c][0], 1).astype(f32), ring_step(sent[c][1], -1).astype(f32))
+            for c in range(chunks)
+        ]
         values = beside(stage, event)
-        stage += 1
         if k == 0:
             break
-        to_ahead, to_behind = local(here + k).astype(f32), local(here - k).astype(f32)
-        if k == wide // 2 - 1:
-            to_ahead = jnp.concatenate(
-                [to_ahead[..., :middle] + ahead, to_ahead[..., middle:]], axis=-1
-            )
-            to_behind = jnp.concatenate(
-                [to_behind[..., :middle], to_behind[..., middle:] + behind], axis=-1
-            )
-        else:
-            to_ahead, to_behind = to_ahead + ahead, to_behind + behind
-        ahead, behind = lax.optimization_barrier(
-            (to_ahead.astype(bf16), to_behind.astype(bf16)) + values
-        )[:2]
-        event = ahead
-    return local(here).astype(f32) + ahead + behind
+        sent = []
+        for c in range(chunks):
+            ahead, behind = came[c]
+            to_ahead, to_behind = local(here + k, c).astype(f32), local(here - k, c).astype(f32)
+            if k == wide // 2 - 1:
+                to_ahead = jnp.concatenate(
+                    [to_ahead[..., :middle] + ahead, to_ahead[..., middle:]], axis=-1
+                )
+                to_behind = jnp.concatenate(
+                    [to_behind[..., :middle], to_behind[..., middle:] + behind], axis=-1
+                )
+            else:
+                to_ahead, to_behind = to_ahead + ahead, to_behind + behind
+            terms = (to_ahead.astype(bf16), to_behind.astype(bf16)) + (values if c == 0 else ())
+            sent.append(lax.optimization_barrier(terms)[:2])
+        event = sent[0][0]
+    return [
+        (local(here, c).astype(f32) + came[c][0] + came[c][1]).astype(bf16) for c in range(chunks)
+    ]
 
 
 def wide_swap(parts):
@@ -739,46 +760,64 @@
     )(rows, weight)
 
 
-def wide_outer_kernel(*refs):
-    lefts, (right_ref, extra_ref, out_ref) = refs[:-3], refs[-3:]
+def wide_outer_kernel(*refs, heads, order):
+    lefts, (parts_ref, extra_ref, out_ref, rows_ref) = refs[:-4], refs[-4:]
     pair, narrow, shard, total = out_ref.shape
-    width = right_ref.shape[1]
+    width = rows_ref.shape[1]
     more = total - width
+
+    @pl.when(pl.program_id(0) == 0)
+    def _():
+        tokens = parts_ref.shape[3]
+        row = 0
+        for j in order:
+            for b in range(parts_ref.shape[0] // heads):
+                rows_ref[row : row + tokens] = row_block(parts_ref, j, b, heads)
+                row += tokens
+
     for n in range(narrow):
         left = jnp.concatenate([ref[...] for ref in lefts[n::narrow]], axis=0)
         acc = lax.dot_general(
-            left, right_ref[...], CONTRACT_FIRST, preferred_element_type=jnp.float32
+            left, rows_ref[...], CONTRACT_FIRST, preferred_element_type=jnp.float32
         )
         for y in range(pair):
             out_ref[y, n, :, :width] = acc[y * shard : (y + 1) * shard].astype(jnp.bfloat16)
-        for y in range(pair):
             out_ref[y, n, :, width:] = extra_ref[
                 y * shard : (y + 1) * shard, n * more : (n + 1) * more
             ]
 
 
-def wide_outer(lefts, right, extra, wide):
-    shard, narrow, width = extra.shape[0] // wide, 4, right.shape[1]
+def wide_outer(lefts, parts, extra, wide, heads, order):
+    narrow = len(lefts)
+    units, count, blocks, tokens, head_dim = parts.shape
+    shard, width = extra.shape[0] // wide, count * heads * head_dim
     more = extra.shape[1] // narrow
     block = lefts[0].shape[0]
+    rows = blocks * tokens * units // heads
     deep = wide // 2
     return pl.pallas_call(
-        wide_outer_kernel,
+        functools.partial(wide_outer_kernel, heads=heads, order=order),
         grid=(deep,),
-        out_shape=jax.ShapeDtypeStruct((wide, narrow, shard, width + more), jnp.bfloat16),
+        out_shape=(
+            jax.ShapeDtypeStruct((wide, narrow, shard, width + more), jnp.bfloat16),
+            jax.ShapeDtypeStruct((rows, width), jnp.bfloat16),
+        ),
         in_specs=[
             pl.BlockSpec((block, 2 * shard), lambda i, n=n: (0, n * deep + i))
             for _ in lefts
             for n in range(narrow)
         ]
         + [
-            resident(right.shape),
+            resident(parts.shape),
             pl.BlockSpec((2 * shard, extra.shape[1]), lambda i: (i, 0)),
         ],
-        out_specs=pl.BlockSpec((2, narrow, shard, width + more), lambda i: (i, 0, 0, 0)),
+        out_specs=(
+            pl.BlockSpec((2, narrow, shard, width + more), lambda i: (i, 0, 0, 0)),
+            pl.BlockSpec((rows, width), lambda i: (0, 0)),
+        ),
         compiler_params=BIG,
         name="wide_outer",
-    )(*[left for left in lefts for _ in range(narrow)], right, extra)
+    )(*[left for left in lefts for _ in range(narrow)], parts, extra)
 
 
 def row_block(parts_ref, j, b, heads):
@@ -824,29 +863,6 @@
         name="unproject",
     )(parts, weight)
     return results[:blocks], results[blocks].reshape(blocks * step, inner)
-
-
-def join_kernel(parts_ref, rows_ref, *, heads, order):
-    units, tokens = parts_ref.shape[0], parts_ref.shape[3]
-    row = 0
-    for j in order:
-        for b in range(units // heads):
-            rows_ref[row : row + tokens] = row_block(parts_ref, j, b, heads)
-            row += tokens
-
-
-def join(parts, heads, order):
-    units, count, blocks, tokens, head_dim = parts.shape
-    return pl.pallas_call(
-        functools.partial(join_kernel, heads=heads, order=order),
-        out_shape=jax.ShapeDtypeStruct(
-            (blocks * tokens * units // heads, count * heads * head_dim), jnp.bfloat16
-        ),
-        in_specs=vmem_specs(1),
-        out_specs=vmem_specs(1)[0],
-        compiler_params=BIG,
-        name="join",
-    )(parts)
 
 
 def mask_of(segc_ref, segr_ref, i, lo):
@@ -956,7 +972,7 @@
 
 
 def ff_kernel(rows_ref, *refs):
-    weights, (bias_ref, hidden_ref, slope_ref) = refs[:-3], refs[-3:]
+    weights, (bias_ref, right_ref, hidden_ref, slope_ref, outer_ref) = refs[:-5], refs[-5:]
     step = 256
     depth = rows_ref.shape[1] // len(weights)
     for r in range(0, rows_ref.shape[0], step):
@@ -972,10 +988,13 @@
         slope_ref[r : r + step] = below + x * (
             jnp.exp(-0.5 * x * x) * (1.0 / math.sqrt(2.0 * math.pi))
         )
-
-
-def feed_forward(rows, weight, bias):
-    count = rows.shape[0]
+    outer_ref[...] = lax.dot_general(
+        hidden_ref[...], right_ref[...], CONTRACT_FIRST, preferred_element_type=jnp.float32
+    ).astype(jnp.bfloat16)
+
+
+def feed_forward(rows, weight, bias, right):
+    count, width = right.shape
     deep, narrow, shard, inner = weight.shape
     step = 256
     return pl.pallas_call(
@@ -984,19 +1003,21 @@
         out_shape=(
             jax.ShapeDtypeStruct((count, inner), jnp.bfloat16),
             jax.ShapeDtypeStruct((count, inner), jnp.float32),
+            jax.ShapeDtypeStruct((inner, width), jnp.bfloat16),
         ),
         in_specs=[resident(rows.shape)]
         + [
             pl.BlockSpec((deep, 1, shard, step), lambda i, n=n: (0, n, 0, i)) for n in range(narrow)
         ]
-        + [pl.BlockSpec((1, step), lambda i: (0, i))],
+        + [pl.BlockSpec((1, step), lambda i: (0, i)), resident(right.shape)],
         out_specs=(
             pl.BlockSpec((count, step), lambda i: (0, i)),
             pl.BlockSpec((count, step), lambda i: (0, i)),
+            pl.BlockSpec((step, width), lambda i: (i, 0)),
         ),
         compiler_params=BIG,
         name="feed_forward",
-    )(rows, *[weight] * narrow, bias.reshape(1, -1))
+    )(rows, *[weight] * narrow, bias.reshape(1, -1), right)
 
 
 def pull_kernel(rows_ref, weight_ref, slope_ref, grad_ref, sum_ref):
@@ -1165,7 +1186,7 @@
 
     out_w = wide_gather(out_weight, 0)
     qkv_shard = narrow_swap(qkv_block)
-    attn_parts = ring_gather(qkv_shard)
+    attn_parts = ring_gather(qkv_shard, 1)
 
     smalls = [
         attn_gain, attn_shift, out_bias, mlp_gain, mlp_shift, down_bias, query_bias, value_bias, up_bias
@@ -1214,9 +1235,7 @@
 
     second_norm = spread(normalize(middle, gain_mlp, shift_mlp).astype(bf16))
     second_norm = jnp.concatenate(second_norm, axis=0)
-    hidden, slope = feed_forward(second_norm, up_parts, ubias)
-    down_grad = outer_sum(hidden, cotan).astype(bf16)
-    slope = hold(slope, down_grad)
+    hidden, slope, down_grad = feed_forward(second_norm, up_parts, ubias, cotan)
     down_grad = z_scatter(down_grad, 0)
     inner_grad, ubias_grad = pull_back(cotan, down_w, slope)
     split = inner_grad.shape[0] // 2
@@ -1228,7 +1247,7 @@
         up_made.append(outer_sum(second_norm, hold(inner_grad, event)).astype(bf16))
         return up_made[0]
 
-    second_grad = fold(far, near, make_up_grad)
+    second_grad = fold_last(*fold_first(far, near), make_up_grad)
     mlp_pull = jax.vjp(normalize, middle, gain_mlp, shift_mlp)[1]
     middle_part, mgain_grad, mshift_grad = mlp_pull(second_grad)
     middle_grad = cotan_own.astype(f32) + middle_part
@@ -1250,10 +1269,12 @@
     no_bias = jnp.zeros((cols,), f32)
     sent = project(branch, out_w, no_bias, wide, 1, heads, tokens, True)
     out_grad = outer_sum(hold(mixed, sent), jnp.concatenate(branch, axis=0)).astype(bf16)
-    output = middle + fold(*hold_all(out_made, sent)) + dbias
+    own, over_x, over_y = fold_first(*hold_all(out_made, sent))
+    dout, over_x, over_y = hold_all((wide_swap(sent), over_x, over_y), out_grad)
+    output = middle + fold_last(own, over_x, over_y) + dbias
     block_output = output.astype(bf16).reshape(batch, tokens, width)
-    dout = hold(wide_swap(sent), out_grad, block_output)
     unit_grads = attend_bwd(me, segc, segr, lse, qkv, dout)
+    unit_grads = hold(unit_grads, block_output)
     grads = wide_swap(unit_grads)
     up_rows = hold(up_grad, unit_grads).reshape(narrow, 2, shard, ff_local)
     up_sent = up_rows
@@ -1264,8 +1285,9 @@
     down_grad = down_grad.astype(f32)
     grads = hold(grads, up_back)
     order = (1, 3, 0, 2)
-    back = join(grads, heads, order)
-    sums = wide_outer([first_norm[j] for j in order], back, out_grad, wide)
+    sums, back = wide_outer(
+        [first_norm[j] for j in order], grads, out_grad, wide, heads, order
+    )
     made = {}
 
     def beside(stage, event):
@@ -1286,7 +1308,7 @@
             return made["pulled"] + (down_grad,)
         return ()
 
-    qkv_rows = ring_scatter(sums, beside).astype(bf16)
+    qkv_rows = jnp.concatenate(ring_scatter(sums, beside, 1), axis=-1)
     out_grad = qkv_rows[..., 3 * cols :].transpose(1, 0, 2).reshape(shard, width)
     qkv_rows = qkv_rows[..., : 3 * cols]
     swapped = narrow_blocks(lambda n: at(qkv_rows, n))

time: 844 us -> 834 us (0.988)
  matrix products: 44.3 us -> 29 us
  waiting for transfers between devices: 378 us -> 392 us
  starting transfers between devices: 106 us -> 95.9 us
  Pallas kernels: 127 us -> 137 us
    all_to_all x4, waiting for transfers between devices: 43.9 us -> 61.7 us  [wide_swap(): return lax.all_to_all(parts, WIDE, split_axis=0, concat_axis=0, tiled=True)]
    dot_general x3 -> x2, matrix products: 32.1 us -> 17 us  [outer_sum(): lax.dot_general(left, right, (((0,), (0,)), ((), ())), preferred_element_...]
    pallas_call x1, Pallas kernels: 18.3 us -> 29.8 us  [feed_forward(): pl.pallas_call(ff_kernel, grid=(inner // step,), out_shape=(jax.ShapeDtyp...]
    ppermute x62, waiting for transfers between devices: 250 us -> 239 us  [flip(): return lax.ppermute(value, axis, [(i, i ^ bits) for i in range(size)])]
    ppermute x62, starting transfers between devices: 66.2 us -> 56.2 us  [flip(): return lax.ppermute(value, axis, [(i, i ^ bits) for i in range(size)])]
    unnamed x173 -> x177, local copies, waits for them, and re-layouts: 50 us -> 48.9 us
  transfers between devices with their start and end apart: 87 -> 87, of which waited for: 53 -> 55; matrix products, arithmetic and copies ran while one was open for 20% -> 18% of each run, Pallas kernels for 9% -> 10%
where the time goes in v6:
time: 834 us; the launch traced here: 825 us
  waiting for transfers between devices  392 us (47%)
  Pallas kernels  137 us (16%)
  starting transfers between devices  95.9 us (11%)
  local copies, waits for them, and re-layouts  92 us (11%)
  other arithmetic  63.9 us (8%)
  matrix products  29 us (3%)
  between operations  15.7 us (2%)
    ppermute x62, waiting for transfers between devices, flip(): return lax.ppermute(value, axis, [(i, i ^ bits) for i in range(size)])  239 us
    ppermute x16, waiting for transfers between devices, ring_step(): lax.ppermute(value, WIDE, [(order[i], order[(i + by) % size]) for i in ra...  90.9 us
    all_to_all x4, waiting for transfers between devices, wide_swap(): return lax.all_to_all(parts, WIDE, split_axis=0, concat_axis=0, tiled=True)  61.7 us
    ppermute x62, starting transfers between devices, flip(): return lax.ppermute(value, axis, [(i, i ^ bits) for i in range(size)])  56.2 us
    unnamed x177, local copies, waits for them, and re-layouts  48.9 us
    pallas_call x1, Pallas kernels, feed_forward(): pl.pallas_call(ff_kernel, grid=(inner // step,), out_shape=(jax.ShapeDtyp...  29.8 us
    pallas_call x4, Pallas kernels, times_parts(): pl.pallas_call(times_parts_kernel, grid=(narrow,), out_shape=jax.ShapeDty...  26.9 us
    ppermute x16, starting transfers between devices, ring_step(): lax.ppermute(value, WIDE, [(order[i], order[(i + by) % size]) for i in ra...  21.4 us
  transfers between devices with their start and end apart: 87, of which 55 were waited for; matrix products, arithmetic and copies ran while one was open for 18% of the time, Pallas kernels for 10%

profile of v6, /device:TPU:0, one launch (start us, length us, event | category | flops | bytes accessed | tf_op | source)
XLA Modules:
  0.0 824.8 jit_solution(7066651411166497068)
XLA Ops:
  26.7 3.6 collective-permute-done.4
  36.8 3.4 broadcast_in_dim.74
  41.1 20.7 %collective-permute-done.11 = bf16[4,64,1536]{2,1,0:T(8,128)(2,1)} collective-permute-done((bf16[4,64,1536]{2,1,0:T(8,128)(2,1)}, bf16[4,64,1536]{2,1,0:T(8,128)(2,1)}, u32[]{:S(2)}, u32[]{:S(2)}) %collective-permute-start.11) | collective-permute-done | bytes 786464 | tf_op jit(solution)/shard_map/ppermute | solution.py:547
  61.8 5.9 collective-permute-start.13
  67.7 3.4 collective-permute-done.12
  76.1 12.0 %collective-permute-done.13 = bf16[4,64,1536]{2,1,0:T(8,128)(2,1)S(1)} collective-permute-done((bf16[4,64,1536]{2,1,0:T(8,128)(2,1)}, bf16[4,64,1536]{2,1,0:T(8,128)(2,1)S(1)}, u32[]{:S(2)}, u32[]{:S(2)}) %collective-permute-start.13) | collective-permute-done | bytes 786464 | tf_op jit(solution)/shard_map/ppermute | solution.py:547
  92.0 13.6 %collective-permute-done.15 = bf16[4,64,1536]{2,1,0:T(8,128)(2,1)S(1)} collective-permute-done((bf16[4,64,1536]{2,1,0:T(8,128)(2,1)S(1)}, bf16[4,64,1536]{2,1,0:T(8,128)(2,1)S(1)}, u32[]{:S(2)}, u32[]{:S(2)}) %collective-permute-start.15) | collective-permute-done | bytes 786464 | tf_op jit(solution)/shard_map/ppermute | solution.py:547
  109.7 3.9 collective-permute-done.17
  116.2 11.6 %project_parts.1 = bf16[8,3,4,128,128]{4,3,2,1,0:T(8,128)(2,1)} custom-call(bf16[256,2048]{1,0:T(8,128)(2,1)S(1)} %fusion.32.refs_0_.refs_8_.refs_9_.refs_10_.refs_11_, bf16[256,2048]{1,0:T(8,128)(2,1)S(1)} %collective-permute-done.5.refs_1_.refs_0_.refs_2_.refs_3_, bf16[256,2048]{1,0:T(8,128)(2,1)S(1)} %collective-permute-done.6.refs_2_.refs_12_.refs_13_.refs_14_.refs_15_, ...), custom_call_target="tpu_custom_call" | custom-call | tf_op jit(solution)/shard_map/project_parts/pallas_call | solution.py:718
  127.7 4.6 all-to-all-start
  138.3 3.3 reshape.422.segc_ref
  141.6 30.5 %collective-permute-done.19 = bf16[4,64,1024]{2,1,0:T(8,128)(2,1)} collective-permute-done((bf16[4,64,1024]{2,1,0:T(8,128)(2,1)}, bf16[4,64,1024]{2,1,0:T(8,128)(2,1)}, u32[]{:S(2)}, u32[]{:S(2)}) %collective-permute-start.19) | collective-permute-done | bytes 524320 | tf_op jit(solution)/shard_map/ppermute | solution.py:379
  176.5 4.2 collective-permute-done.20
  180.7 7.0 collective-permute-done.21
  189.1 10.9 %all-to-all-done.parts_ref = bf16[8,3,4,128,128]{4,3,2,1,0:T(8,128)(2,1)} async-done(((bf16[8,3,4,128,128]{4,3,2,1,0:T(8,128)(2,1)}), bf16[8,3,4,128,128]{4,3,2,1,0:T(8,128)(2,1)}, u32[]{:S(2)}, u32[]{:S(2)}) %all-to-all-start) | async-done | bytes 3145760 | tf_op jit(solution)/shard_map/all_to_all | solution.py:626
  201.5 8.2 attend_fwd.1
  213.4 4.2 all-to-all-start.1
  218.1 2.9 collective-permute-start.23
  221.0 23.5 %collective-permute-done.24 = bf16[256,2048]{1,0:T(8,128)(2,1)} collective-permute-done((bf16[256,2048]{1,0:T(8,128)(2,1)}, bf16[256,2048]{1,0:T(8,128)(2,1)}, u32[]{:S(2)}, u32[]{:S(2)}) %collective-permute-start.24) | collective-permute-done | bytes 1048608 | tf_op jit(solution)/shard_map/ppermute | solution.py:379
  245.5 2.9 collective-permute-start.25
  259.5 3.1 collective-permute-done.26
  263.7 5.9 all-to-all-done.1.parts_ref
  269.7 5.9 unproject.1
  281.2 3.9 collective-permute-start.29
  294.7 14.3 %collective-permute-done.29 = bf16[256,2048]{1,0:T(8,128)(2,1)} collective-permute-done((bf16[256,2048]{1,0:T(8,128)(2,1)}, bf16[256,2048]{1,0:T(8,128)(2,1)}, u32[]{:S(2)}, u32[]{:S(2)}) %collective-permute-start.29) | collective-permute-done | bytes 1048608 | tf_op jit(solution)/shard_map/ppermute | solution.py:379
  308.9 3.6 fusion.37
  320.5 22.4 %collective-permute-done.35 = bf16[256,2048]{1,0:T(8,128)(2,1)S(1)} collective-permute-done((bf16[256,2048]{1,0:T(8,128)(2,1)S(1)}, bf16[256,2048]{1,0:T(8,128)(2,1)S(1)}, u32[]{:S(2)}, u32[]{:S(2)}) %collective-permute-start.35) | collective-permute-done | bytes 1048608 | tf_op jit(solution)/shard_map/ppermute | solution.py:379
  352.3 5.4 collective-permute-done.36
  371.2 29.8 %feed_forward.1 = (bf16[2048,1024]{1,0:T(8,128)(2,1)S(1)}, f32[2048,1024]{1,0:T(8,128)}, bf16[1024,2048]{1,0:T(8,128)(2,1)}) custom-call(bf16[2048,2048]{1,0:T(8,128)(2,1)} %constant_dynamic-update-slice_fusion.10.rows_ref, bf16[4,4,128,1024]{3,2,1,0:T(8,128)(2,1)} %bitcast.219, bf16[4,4,128,1024]{3,2,1,0:T(8,128)(2,1)} %bitcast.220, ...), custom_call_target="tpu_custom_call" | custom-call | tf_op jit(solution)/shard_map/feed_forward/pallas_call | solution.py:1000
  403.0 14.6 %pull_back.1 = (bf16[2048,1024]{1,0:T(8,128)(2,1)S(1)}, f32[1,1024]{1,0:T(1,128)S(1)}) custom-call(bf16[2048,2048]{1,0:T(8,128)(2,1)} %constant_dynamic-update-slice_fusion.2.refs_5_.rows_ref, bf16[1024,2048]{1,0:T(8,128)(2,1)} %all-gather.7.cloned.1.call-done.weight_ref, f32[2048,1024]{1,0:T(8,128)} %get-tuple-element.94.slope_ref), custom_call_target="tpu_custom_call" | custom-call | tf_op jit(solution)/shard_map/pull_back/pallas_call | solution.py:1043
  419.6 7.4 times_parts.4
  427.5 7.4 times_parts.5
  434.9 3.8 convert_add_fusion.11
  445.4 9.2 %collective-permute-done.43 = bf16[256,1024]{1,0:T(8,128)(2,1)} collective-permute-done((bf16[256,1024]{1,0:T(8,128)(2,1)}, bf16[256,1024]{1,0:T(8,128)(2,1)}, u32[]{:S(2)}, u32[]{:S(2)}) %collective-permute-start.43) | collective-permute-done | bytes 524320 | tf_op jit(solution)/shard_map/ppermute | solution.py:379
  458.5 13.3 %convolution_convert_fusion.2 = bf16[2048,1024]{1,0:T(8,128)(2,1)} fusion(bf16[2048,2048]{1,0:T(8,128)(2,1)} %constant_dynamic-update-slice_fusion.10.rows_ref, bf16[2048,1024]{1,0:T(8,128)(2,1)S(1)} %copy-done.4), kind=kOutput, calls=%fused_computation.11 | convolution fusion | flops 8592031744 | bytes 16777216 | tf_op jit(solution)/shard_map/dot_general | solution.py:46
  471.8 8.6 %collective-permute-done.44 = bf16[256,2048]{1,0:T(8,128)(2,1)S(1)} collective-permute-done((bf16[256,2048]{1,0:T(8,128)(2,1)S(1)}, bf16[256,2048]{1,0:T(8,128)(2,1)S(1)}, u32[]{:S(2)}, u32[]{:S(2)}) %collective-permute-start.44) | collective-permute-done | bytes 1048608 | tf_op jit(solution)/shard_map/ppermute | solution.py:379
  489.8 6.0 convolution_convert_fusion
  495.8 6.0 convolution_convert_fusion.1
  501.8 10.6 %collective-permute-done.48.refs_2_ = bf16[256,2048]{1,0:T(8,128)(2,1)S(1)} collective-permute-done((bf16[256,2048]{1,0:T(8,128)(2,1)S(1)}, bf16[256,2048]{1,0:T(8,128)(2,1)S(1)}, u32[]{:S(2)}, u32[]{:S(2)}) %collective-permute-start.48) | collective-permute-done | bytes 1048608 | tf_op jit(solution)/shard_map/ppermute | solution.py:379
  515.1 5.2 project.1
  521.4 4.2 all-to-all-start.2
  525.7 3.1 collective-permute-done.50
  528.8 4.3 convert_add_fusion.5
  534.6 3.7 fusion.8.refs_17_
  539.3 7.9 collective-permute-done.52
  548.4 8.4 %collective-permute-done.51 = bf16[256,1024]{1,0:T(8,128)(2,1)S(1)} collective-permute-done((bf16[256,1024]{1,0:T(8,128)(2,1)S(1)}, bf16[256,1024]{1,0:T(8,128)(2,1)S(1)}, u32[]{:S(2)}, u32[]{:S(2)}) %collective-permute-start.51) | collective-permute-done | bytes 524320 | tf_op jit(solution)/shard_map/ppermute | solution.py:379
  558.0 21.7 %all-to-all-done.2.do_ref = bf16[8,1,4,128,128]{4,3,2,1,0:T(8,128)(2,1)} async-done(((bf16[8,1,4,128,128]{4,3,2,1,0:T(8,128)(2,1)}), bf16[8,1,4,128,128]{4,3,2,1,0:T(8,128)(2,1)}, u32[]{:S(2)}, u32[]{:S(2)}) %all-to-all-start.2) | async-done | bytes 1048608 | tf_op jit(solution)/shard_map/all_to_all | solution.py:626
  585.4 17.7 %attend_bwd.1 = bf16[8,3,4,128,128]{4,3,2,1,0:T(8,128)(2,1)} custom-call(s32[2]{0:T(128)S(1)} %pad_add_fusion.me_ref, s32[8,512,1]{2,1,0:T(8,128)S(1)} %copy-done.2, s32[1,4096]{1,0:T(1,128)S(1)} %fusion.58.segr_ref, f32[8,512,1]{2,1,0:T(8,128)S(1)} %copy-done.13, bf16[8,3,4,128,128]{4,3,2,1,0:T(8,128)(2,1)} %all-to-all-done.parts_ref, ...), custom_call_target="tpu_custom_call" | custom-call | tf_op jit(solution)/shard_map/attend_bwd/pallas_call | solution.py:961
  605.5 4.0 fusion.22
  609.6 4.5 all-to-all-start.3
  619.9 5.6 collective-permute-done.56
  626.4 3.8 collective-permute-done.57
  632.3 28.3 %collective-permute-done.58.other_ref = bf16[4,64,1024]{2,1,0:T(8,128)(2,1)S(1)} collective-permute-done((bf16[4,64,1024]{2,1,0:T(8,128)(2,1)S(1)}, bf16[4,64,1024]{2,1,0:T(8,128)(2,1)S(1)}, u32[]{:S(2)}, u32[]{:S(2)}) %collective-permute-start.58) | collective-permute-done | bytes 524320 | tf_op jit(solution)/shard_map/ppermute | solution.py:379
  662.6 23.3 %all-to-all-done.3.refs_16_ = bf16[8,3,4,128,128]{4,3,2,1,0:T(8,128)(2,1)} async-done(((bf16[8,3,4,128,128]{4,3,2,1,0:T(8,128)(2,1)}), bf16[8,3,4,128,128]{4,3,2,1,0:T(8,128)(2,1)}, u32[]{:S(2)}, u32[]{:S(2)}) %all-to-all-start.3) | async-done | bytes 3145760 | tf_op jit(solution)/shard_map/all_to_all | solution.py:626
  685.9 12.2 %wide_outer.1 = (bf16[8,4,64,2048]{3,2,1,0:T(8,128)(2,1)}, bf16[1024,1536]{1,0:T(8,128)(2,1)}) custom-call(bf16[256,2048]{1,0:T(8,128)(2,1)S(1)} %collective-permute-done.5.refs_1_.refs_0_.refs_2_.refs_3_, bf16[256,2048]{1,0:T(8,128)(2,1)S(1)} %collective-permute-done.5.refs_1_.refs_0_.refs_2_.refs_3_, ...), custom_call_target="tpu_custom_call" | custom-call | tf_op jit(solution)/shard_map/wide_outer/pallas_call | solution.py:798
  702.7 6.0 times_parts.6
  710.2 3.8 collective-permute-done.60
  718.7 6.0 times_parts.7
  733.5 7.3 collective-permute-done.66
  740.8 3.1 fusion.12
  746.2 7.1 collective-permute-done.63
  760.8 6.3 collective-permute-done.68
  769.0 3.7 fusion.11
  778.8 16.5 %collective-permute-done.70 = bf16[4,64,2048]{2,1,0:T(8,128)(2,1)} collective-permute-done((bf16[4,64,2048]{2,1,0:T(8,128)(2,1)}, bf16[4,64,2048]{2,1,0:T(8,128)(2,1)}, u32[]{:S(2)}, u32[]{:S(2)}) %collective-permute-start.70) | collective-permute-done | bytes 1048608 | tf_op jit(solution)/shard_map/ppermute | solution.py:547
  (476 shorter events, 229.9 us)
Async XLA Ops:
  7.3 108.8 %all-gather.5.cloned.1.call-start = ((), (), s32[]{:S(2)}) async-start(), calls=%async_computation.6 | async-start | bytes 2359296 | tf_op jit(solution)/shard_map/all_gather | solution.py:630
  9.6 22.2 %collective-permute-start.10 = (bf16[64,1536]{1,0:T(8,128)(2,1)S(1)}, bf16[64,1536]{1,0:T(8,128)(2,1)S(1)}, u32[]{:S(2)}, u32[]{:S(2)}) collective-permute-start(bf16[64,1536]{1,0:T(8,128)(2,1)S(1)} %pad_maximum_fusion.13), channel_id=1, source_target_pairs={{0,8},{8,0},{16,24},{24,16},{1,9},{9,1},{17,25},{25,17},{2,10},{10... | collective-permute-start | bytes 589832 | tf_op jit(solution)/shard_map/ppermute | solution.py:379
  10.1 21.7 %collective-permute-start.8 = (bf16[64,1536]{1,0:T(8,128)(2,1)S(1)}, bf16[64,1536]{1,0:T(8,128)(2,1)S(1)}, u32[]{:S(2)}, u32[]{:S(2)}) collective-permute-start(bf16[64,1536]{1,0:T(8,128)(2,1)S(1)} %pad_maximum_fusion.11), channel_id=1, source_target_pairs={{0,24},{8,16},{16,8},{24,0},{1,25},{9,17},{17,9},{25,1},{2,26},{10... | collective-permute-start | bytes 589832 | tf_op jit(solution)/shard_map/ppermute | solution.py:379
  14.6 17.2 %collective-permute-start.9 = (bf16[64,1536]{1,0:T(8,128)(2,1)S(1)}, bf16[64,1536]{1,0:T(8,128)(2,1)S(1)}, u32[]{:S(2)}, u32[]{:S(2)}) collective-permute-start(bf16[64,1536]{1,0:T(8,128)(2,1)S(1)} %pad_maximum_fusion.12), channel_id=1, source_target_pairs={{0,16},{8,24},{16,0},{24,8},{1,17},{9,25},{17,1},{25,9},{2,18},{10... | collective-permute-start | bytes 589832 | tf_op jit(solution)/shard_map/ppermute | solution.py:379
  33.1 28.7 %collective-permute-start.11 = (bf16[4,64,1536]{2,1,0:T(8,128)(2,1)}, bf16[4,64,1536]{2,1,0:T(8,128)(2,1)}, u32[]{:S(2)}, u32[]{:S(2)}) collective-permute-start(bf16[4,64,1536]{2,1,0:T(8,128)(2,1)} %pad_maximum_fusion.8), channel_id=1, source_target_pairs={{0,2},{2,4},{4,6},{6,7},{7,5},{5,3},{3,1},{1,0},{8,10},{10,12},{12... | collective-permute-start | bytes 2359304 | tf_op jit(solution)/shard_map/ppermute | solution.py:547
  34.6 36.4 %collective-permute-start.12 = (bf16[4,64,1536]{2,1,0:T(8,128)(2,1)}, bf16[4,64,1536]{2,1,0:T(8,128)(2,1)}, u32[]{:S(2)}, u32[]{:S(2)}) collective-permute-start(bf16[4,64,1536]{2,1,0:T(8,128)(2,1)} %pad_maximum_fusion.8), channel_id=1, source_target_pairs={{0,1},{2,0},{4,2},{6,4},{7,6},{5,7},{3,5},{1,3},{8,9},{10,8},{12,1... | collective-permute-start | bytes 2359304 | tf_op jit(solution)/shard_map/ppermute | solution.py:547
  35.6 40.5 %collective-permute-start.6 = (bf16[256,2048]{1,0:T(8,128)(2,1)S(1)}, bf16[256,2048]{1,0:T(8,128)(2,1)S(1)}, u32[]{:S(2)}, u32[]{:S(2)}) collective-permute-start(bf16[256,2048]{1,0:T(8,128)(2,1)S(1)} %fusion.32.refs_0_.refs_8_.refs_9_.refs_10_.refs_11_), channel_id=1, source_target_pairs={{0,16},{8,24},{16,0},{24,8},{1,17},{9,25},{17,1},{25,9},{2,18},{10... | collective-permute-start | bytes 3145736 | tf_op jit(solution)/shard_map/ppermute | solution.py:379
  35.9 80.3 %collective-permute-start.5 = (bf16[256,2048]{1,0:T(8,128)(2,1)S(1)}, bf16[256,2048]{1,0:T(8,128)(2,1)S(1)}, u32[]{:S(2)}, u32[]{:S(2)}) collective-permute-start(bf16[256,2048]{1,0:T(8,128)(2,1)S(1)} %fusion.32.refs_0_.refs_8_.refs_9_.refs_10_.refs_11_), channel_id=1, source_target_pairs={{0,8},{8,0},{16,24},{24,16},{1,9},{9,1},{17,25},{25,17},{2,10},{10... | collective-permute-start | bytes 3145736 | tf_op jit(solution)/shard_map/ppermute | solution.py:379
  61.8 26.3 %collective-permute-start.13 = (bf16[4,64,1536]{2,1,0:T(8,128)(2,1)}, bf16[4,64,1536]{2,1,0:T(8,128)(2,1)S(1)}, u32[]{:S(2)}, u32[]{:S(2)}) collective-permute-start(bf16[4,64,1536]{2,1,0:T(8,128)(2,1)} %collective-permute-done.11), channel_id=1, source_target_pairs={{0,2},{2,4},{4,6},{6,7},{7,5},{5,3},{3,1},{1,0},{8,10},{10,12},{12... | collective-permute-start | bytes 2359304 | tf_op jit(solution)/shard_map/ppermute | solution.py:547
  71.1 18.0 %collective-permute-start.14 = (bf16[4,64,1536]{2,1,0:T(8,128)(2,1)}, bf16[4,64,1536]{2,1,0:T(8,128)(2,1)S(1)}, u32[]{:S(2)}, u32[]{:S(2)}) collective-permute-start(bf16[4,64,1536]{2,1,0:T(8,128)(2,1)} %collective-permute-done.12), channel_id=1, source_target_pairs={{0,1},{2,0},{4,2},{6,4},{7,6},{5,7},{3,5},{1,3},{8,9},{10,8},{12,1... | collective-permute-start | bytes 2359304 | tf_op jit(solution)/shard_map/ppermute | solution.py:547
  76.1 40.1 %collective-permute-start.7 = (bf16[256,2048]{1,0:T(8,128)(2,1)S(1)}, bf16[256,2048]{1,0:T(8,128)(2,1)}, u32[]{:S(2)}, u32[]{:S(2)}) collective-permute-start(bf16[256,2048]{1,0:T(8,128)(2,1)S(1)} %collective-permute-done.6.refs_2_.refs_12_.refs_13_.refs_14_.refs_15_), channel_id=1, source_target_pairs={{0,8},{8,0},{16,24},{24,16},{1,9},{9,1},{17,25},{25,17},{2,10},{10... | collective-permute-start | bytes 3145736 | tf_op jit(solution)/shard_map/ppermute | solution.py:379
  88.1 17.5 %collective-permute-start.15 = (bf16[4,64,1536]{2,1,0:T(8,128)(2,1)S(1)}, bf16[4,64,1536]{2,1,0:T(8,128)(2,1)S(1)}, u32[]{:S(2)}, u32[]{:S(2)}) collective-permute-start(bf16[4,64,1536]{2,1,0:T(8,128)(2,1)S(1)} %collective-permute-done.13), channel_id=1, source_target_pairs={{0,2},{2,4},{4,6},{6,7},{7,5},{5,3},{3,1},{1,0},{8,10},{10,12},{12... | collective-permute-start | bytes 2359304 | tf_op jit(solution)/shard_map/ppermute | solution.py:547
  89.1 17.9 %collective-permute-start.16 = (bf16[4,64,1536]{2,1,0:T(8,128)(2,1)S(1)}, bf16[4,64,1536]{2,1,0:T(8,128)(2,1)S(1)}, u32[]{:S(2)}, u32[]{:S(2)}) collective-permute-start(bf16[4,64,1536]{2,1,0:T(8,128)(2,1)S(1)} %collective-permute-done.14), channel_id=1, source_target_pairs={{0,1},{2,0},{4,2},{6,4},{7,6},{5,7},{3,5},{1,3},{8,9},{10,8},{12,1... | collective-permute-start | bytes 2359304 | tf_op jit(solution)/shard_map/ppermute | solution.py:547
  127.7 72.2 %all-to-all-start = ((bf16[8,3,4,128,128]{4,3,2,1,0:T(8,128)(2,1)}), bf16[8,3,4,128,128]{4,3,2,1,0:T(8,128)(2,1)}, u32[]{:S(2)}, u32[]{:S(2)}) async-start(bf16[8,3,4,128,128]{4,3,2,1,0:T(8,128)(2,1)} %project_parts.1), calls=%async_computation | async-start | bytes 6291456 | tf_op jit(solution)/shard_map/all_to_all | solution.py:626
  132.3 180.2 %all-gather.9.cloned.1.call-start = ((), (), s32[]{:S(2)}) async-start(), calls=%async_computation.10 | async-start | bytes 5242880 | tf_op jit(solution)/shard_map/all_gather | solution.py:520
  136.3 35.8 %collective-permute-start.19 = (bf16[4,64,1024]{2,1,0:T(8,128)(2,1)}, bf16[4,64,1024]{2,1,0:T(8,128)(2,1)}, u32[]{:S(2)}, u32[]{:S(2)}) collective-permute-start(bf16[4,64,1024]{2,1,0:T(8,128)(2,1)} %slice_bitcast_fusion.9), channel_id=1, source_target_pairs={{0,1},{1,0},{2,3},{3,2},{4,5},{5,4},{6,7},{7,6},{8,9},{9,8},{10,11... | collective-permute-start | bytes 1572872 | tf_op jit(solution)/shard_map/ppermute | solution.py:379
  173.5 14.2 %collective-permute-start.21 = (bf16[2,64,1024]{2,1,0:T(8,128)(2,1)S(1)}, bf16[2,64,1024]{2,1,0:T(8,128)(2,1)S(1)}, u32[]{:S(2)}, u32[]{:S(2)}) collective-permute-start(bf16[2,64,1024]{2,1,0:T(8,128)(2,1)S(1)} %get-tuple-element.183), channel_id=1, source_target_pairs={{0,16},{8,24},{16,0},{24,8},{1,17},{9,25},{17,1},{25,9},{2,18},{10... | collective-permute-start | bytes 786440 | tf_op jit(solution)/shard_map/ppermute | solution.py:379
  176.4 11.3 %collective-permute-start.22 = (bf16[2,64,1024]{2,1,0:T(8,128)(2,1)S(1)}, bf16[2,64,1024]{2,1,0:T(8,128)(2,1)S(1)}, u32[]{:S(2)}, u32[]{:S(2)}) collective-permute-start(bf16[2,64,1024]{2,1,0:T(8,128)(2,1)S(1)} %get-tuple-element.181), channel_id=1, source_target_pairs={{0,8},{8,0},{16,24},{24,16},{1,9},{9,1},{17,25},{25,17},{2,10},{10... | collective-permute-start | bytes 786440 | tf_op jit(solution)/shard_map/ppermute | solution.py:379
  212.0 32.4 %collective-permute-start.24 = (bf16[256,2048]{1,0:T(8,128)(2,1)}, bf16[256,2048]{1,0:T(8,128)(2,1)}, u32[]{:S(2)}, u32[]{:S(2)}) collective-permute-start(bf16[256,2048]{1,0:T(8,128)(2,1)} %bitcast.225), channel_id=1, source_target_pairs={{0,1},{1,0},{2,3},{3,2},{4,5},{5,4},{6,7},{7,6},{8,9},{9,8},{10,11... | collective-permute-start | bytes 3145736 | tf_op jit(solution)/shard_map/ppermute | solution.py:379
  213.4 56.3 %all-to-all-start.1 = ((bf16[8,1,4,128,128]{4,3,2,1,0:T(8,128)(2,1)}), bf16[8,1,4,128,128]{4,3,2,1,0:T(8,128)(2,1)}, u32[]{:S(2)}, u32[]{:S(2)}) async-start(bf16[8,1,4,128,128]{4,3,2,1,0:T(8,128)(2,1)} %copy-done.15), calls=%async_computation.1 | async-start | bytes 2097152 | tf_op jit(solution)/shard_map/all_to_all | solution.py:626
  217.6 185.4 %all-gather.7.cloned.1.call-start = ((), (), s32[]{:S(2)}) async-start(), calls=%async_computation.7 | async-start | bytes 5242880 | tf_op jit(solution)/shard_map/all_gather | solution.py:520
  218.1 32.7 %collective-permute-start.23 = (bf16[256,2048]{1,0:T(8,128)(2,1)}, bf16[256,2048]{1,0:T(8,128)(2,1)}, u32[]{:S(2)}, u32[]{:S(2)}) collective-permute-start(bf16[256,2048]{1,0:T(8,128)(2,1)} %bitcast.226), channel_id=1, source_target_pairs={{0,16},{8,24},{16,0},{24,8},{1,17},{9,25},{17,1},{25,9},{2,18},{10... | collective-permute-start | bytes 3145736 | tf_op jit(solution)/shard_map/ppermute | solution.py:379
  245.5 12.8 %collective-permute-start.25 = (bf16[256,1024]{1,0:T(8,128)(2,1)S(1)}, bf16[256,1024]{1,0:T(8,128)(2,1)S(1)}, u32[]{:S(2)}, u32[]{:S(2)}) collective-permute-start(bf16[256,1024]{1,0:T(8,128)(2,1)S(1)} %slice.336), channel_id=1, source_target_pairs={{0,16},{8,24},{16,0},{24,8},{1,17},{9,25},{17,1},{25,9},{2,18},{10... | collective-permute-start | bytes 1572872 | tf_op jit(solution)/shard_map/ppermute | solution.py:379
  251.9 10.7 %collective-permute-start.26 = (bf16[256,1024]{1,0:T(8,128)(2,1)S(1)}, bf16[256,1024]{1,0:T(8,128)(2,1)S(1)}, u32[]{:S(2)}, u32[]{:S(2)}) collective-permute-start(bf16[256,1024]{1,0:T(8,128)(2,1)S(1)} %slice.337), channel_id=1, source_target_pairs={{0,1},{1,0},{2,3},{3,2},{4,5},{5,4},{6,7},{7,6},{8,9},{9,8},{10,11... | collective-permute-start | bytes 1572872 | tf_op jit(solution)/shard_map/ppermute | solution.py:379
  276.1 11.5 %collective-permute-start.31 = (bf16[256,2048]{1,0:T(8,128)(2,1)}, bf16[256,2048]{1,0:T(8,128)(2,1)}, u32[]{:S(2)}, u32[]{:S(2)}) collective-permute-start(bf16[256,2048]{1,0:T(8,128)(2,1)} %collective-permute-done.23), channel_id=1, source_target_pairs={{0,8},{8,0},{16,24},{24,16},{1,9},{9,1},{17,25},{25,17},{2,10},{10... | collective-permute-start | bytes 3145736 | tf_op jit(solution)/shard_map/ppermute | solution.py:379
  276.2 16.2 %collective-permute-start.33 = (bf16[256,2048]{1,0:T(8,128)(2,1)}, bf16[256,2048]{1,0:T(8,128)(2,1)}, u32[]{:S(2)}, u32[]{:S(2)}) collective-permute-start(bf16[256,2048]{1,0:T(8,128)(2,1)} %get-tuple-element.90), channel_id=1, source_target_pairs={{0,8},{8,0},{16,24},{24,16},{1,9},{9,1},{17,25},{25,17},{2,10},{10... | collective-permute-start | bytes 3145736 | tf_op jit(solution)/shard_map/ppermute | solution.py:379
  276.6 13.3 %collective-permute-start.32 = (bf16[256,2048]{1,0:T(8,128)(2,1)}, bf16[256,2048]{1,0:T(8,128)(2,1)}, u32[]{:S(2)}, u32[]{:S(2)}) collective-permute-start(bf16[256,2048]{1,0:T(8,128)(2,1)} %collective-permute-done.24), channel_id=1, source_target_pairs={{0,8},{8,0},{16,24},{24,16},{1,9},{9,1},{17,25},{25,17},{2,10},{10... | collective-permute-start | bytes 3145736 | tf_op jit(solution)/shard_map/ppermute | solution.py:379
  278.2 16.4 %collective-permute-start.27 = (bf16[256,2048]{1,0:T(8,128)(2,1)}, bf16[256,2048]{1,0:T(8,128)(2,1)}, u32[]{:S(2)}, u32[]{:S(2)}) collective-permute-start(bf16[256,2048]{1,0:T(8,128)(2,1)} %get-tuple-element.83), channel_id=1, source_target_pairs={{0,8},{8,0},{16,24},{24,16},{1,9},{9,1},{17,25},{25,17},{2,10},{10... | collective-permute-start | bytes 3145736 | tf_op jit(solution)/shard_map/ppermute | solution.py:379
  281.2 27.7 %collective-permute-start.29 = (bf16[256,2048]{1,0:T(8,128)(2,1)}, bf16[256,2048]{1,0:T(8,128)(2,1)}, u32[]{:S(2)}, u32[]{:S(2)}) collective-permute-start(bf16[256,2048]{1,0:T(8,128)(2,1)} %add_convert_fusion.2), channel_id=1, source_target_pairs={{0,16},{8,24},{16,0},{24,8},{1,17},{9,25},{17,1},{25,9},{2,18},{10... | collective-permute-start | bytes 3145736 | tf_op jit(solution)/shard_map/ppermute | solution.py:379
  312.5 208.9 %reduce-scatter.3.cloned.1.call-start = ((), (), s32[]{:S(2)}) async-start(), calls=%async_computation.8 | async-start | bytes 5242880 | tf_op jit(solution)/shard_map/reduce_scatter | solution.py:525
  318.2 24.7 %collective-permute-start.35 = (bf16[256,2048]{1,0:T(8,128)(2,1)S(1)}, bf16[256,2048]{1,0:T(8,128)(2,1)S(1)}, u32[]{:S(2)}, u32[]{:S(2)}) collective-permute-start(bf16[256,2048]{1,0:T(8,128)(2,1)S(1)} %get-tuple-element.147), channel_id=1, source_target_pairs={{0,1},{1,0},{2,3},{3,2},{4,5},{5,4},{6,7},{7,6},{8,9},{9,8},{10,11... | collective-permute-start | bytes 3145736 | tf_op jit(solution)/shard_map/ppermute | solution.py:379
  318.8 27.4 %collective-permute-start.34 = (bf16[256,2048]{1,0:T(8,128)(2,1)S(1)}, bf16[256,2048]{1,0:T(8,128)(2,1)S(1)}, u32[]{:S(2)}, u32[]{:S(2)}) collective-permute-start(bf16[256,2048]{1,0:T(8,128)(2,1)S(1)} %get-tuple-element.147), channel_id=1, source_target_pairs={{0,16},{8,24},{16,0},{24,8},{1,17},{9,25},{17,1},{25,9},{2,18},{10... | collective-permute-start | bytes 3145736 | tf_op jit(solution)/shard_map/ppermute | solution.py:379
  344.7 13.0 %collective-permute-start.36 = (bf16[256,1024]{1,0:T(8,128)(2,1)}, bf16[256,1024]{1,0:T(8,128)(2,1)}, u32[]{:S(2)}, u32[]{:S(2)}) collective-permute-start(bf16[256,1024]{1,0:T(8,128)(2,1)} %slice.344), channel_id=1, source_target_pairs={{0,16},{8,24},{16,0},{24,8},{1,17},{9,25},{17,1},{25,9},{2,18},{10... | collective-permute-start | bytes 1572872 | tf_op jit(solution)/shard_map/ppermute | solution.py:379
  348.0 12.5 %collective-permute-start.37 = (bf16[256,1024]{1,0:T(8,128)(2,1)}, bf16[256,1024]{1,0:T(8,128)(2,1)}, u32[]{:S(2)}, u32[]{:S(2)}) collective-permute-start(bf16[256,1024]{1,0:T(8,128)(2,1)} %slice.345), channel_id=1, source_target_pairs={{0,1},{1,0},{2,3},{3,2},{4,5},{5,4},{6,7},{7,6},{8,9},{9,8},{10,11... | collective-permute-start | bytes 1572872 | tf_op jit(solution)/shard_map/ppermute | solution.py:379
  349.2 17.6 %collective-permute-start.38 = (bf16[256,2048]{1,0:T(8,128)(2,1)}, bf16[256,2048]{1,0:T(8,128)(2,1)S(1)}, u32[]{:S(2)}, u32[]{:S(2)}) collective-permute-start(bf16[256,2048]{1,0:T(8,128)(2,1)} %copy-done.51), channel_id=1, source_target_pairs={{0,8},{8,0},{16,24},{24,16},{1,9},{9,1},{17,25},{25,17},{2,10},{10... | collective-permute-start | bytes 3145736 | tf_op jit(solution)/shard_map/ppermute | solution.py:379
  349.3 18.7 %collective-permute-start.39 = (bf16[256,2048]{1,0:T(8,128)(2,1)}, bf16[256,2048]{1,0:T(8,128)(2,1)S(1)}, u32[]{:S(2)}, u32[]{:S(2)}) collective-permute-start(bf16[256,2048]{1,0:T(8,128)(2,1)} %copy-done.45), channel_id=1, source_target_pairs={{0,8},{8,0},{16,24},{24,16},{1,9},{9,1},{17,25},{25,17},{2,10},{10... | collective-permute-start | bytes 3145736 | tf_op jit(solution)/shard_map/ppermute | solution.py:379
  349.8 19.2 %collective-permute-start.40 = (bf16[256,2048]{1,0:T(8,128)(2,1)}, bf16[256,2048]{1,0:T(8,128)(2,1)S(1)}, u32[]{:S(2)}, u32[]{:S(2)}) collective-permute-start(bf16[256,2048]{1,0:T(8,128)(2,1)} %copy-done.43), channel_id=1, source_target_pairs={{0,8},{8,0},{16,24},{24,16},{1,9},{9,1},{17,25},{25,17},{2,10},{10... | collective-permute-start | bytes 3145736 | tf_op jit(solution)/shard_map/ppermute | solution.py:379
  440.5 14.2 %collective-permute-start.43 = (bf16[256,1024]{1,0:T(8,128)(2,1)}, bf16[256,1024]{1,0:T(8,128)(2,1)}, u32[]{:S(2)}, u32[]{:S(2)}) collective-permute-start(bf16[256,1024]{1,0:T(8,128)(2,1)} %get-tuple-element.176), channel_id=1, source_target_pairs={{0,1},{1,0},{2,3},{3,2},{4,5},{5,4},{6,7},{7,6},{8,9},{9,8},{10,11... | collective-permute-start | bytes 1572872 | tf_op jit(solution)/shard_map/ppermute | solution.py:379
  442.3 171.8 %reduce-scatter.5.cloned.1.call-start = ((), (), s32[]{:S(2)}) async-start(), calls=%async_computation.9 | async-start | bytes 5242880 | tf_op jit(solution)/shard_map/reduce_scatter | solution.py:525
  443.8 13.9 %collective-permute-start.45 = (bf16[256,1024]{1,0:T(8,128)(2,1)}, bf16[256,1024]{1,0:T(8,128)(2,1)S(1)}, u32[]{:S(2)}, u32[]{:S(2)}) collective-permute-start(bf16[256,1024]{1,0:T(8,128)(2,1)} %get-tuple-element.177), channel_id=1, source_target_pairs={{0,16},{8,24},{16,0},{24,8},{1,17},{9,25},{17,1},{25,9},{2,18},{10... | collective-permute-start | bytes 1572872 | tf_op jit(solution)/shard_map/ppermute | solution.py:379
  456.0 24.3 %collective-permute-start.44 = (bf16[256,2048]{1,0:T(8,128)(2,1)S(1)}, bf16[256,2048]{1,0:T(8,128)(2,1)S(1)}, u32[]{:S(2)}, u32[]{:S(2)}) collective-permute-start(bf16[256,2048]{1,0:T(8,128)(2,1)S(1)} %pad_maximum_fusion.2), channel_id=1, source_target_pairs={{0,16},{8,24},{16,0},{24,8},{1,17},{9,25},{17,1},{25,9},{2,18},{10... | collective-permute-start | bytes 3145736 | tf_op jit(solution)/shard_map/ppermute | solution.py:379
  457.9 24.1 %collective-permute-start.46 = (bf16[256,2048]{1,0:T(8,128)(2,1)S(1)}, bf16[256,2048]{1,0:T(8,128)(2,1)S(1)}, u32[]{:S(2)}, u32[]{:S(2)}) collective-permute-start(bf16[256,2048]{1,0:T(8,128)(2,1)S(1)} %pad_maximum_fusion.3), channel_id=1, source_target_pairs={{0,1},{1,0},{2,3},{3,2},{4,5},{5,4},{6,7},{7,6},{8,9},{9,8},{10,11... | collective-permute-start | bytes 3145736 | tf_op jit(solution)/shard_map/ppermute | solution.py:379
  486.8 25.6 %collective-permute-start.48 = (bf16[256,2048]{1,0:T(8,128)(2,1)S(1)}, bf16[256,2048]{1,0:T(8,128)(2,1)S(1)}, u32[]{:S(2)}, u32[]{:S(2)}) collective-permute-start(bf16[256,2048]{1,0:T(8,128)(2,1)S(1)} %get-tuple-element.140.refs_0_), channel_id=1, source_target_pairs={{0,16},{8,24},{16,0},{24,8},{1,17},{9,25},{17,1},{25,9},{2,18},{10... | collective-permute-start | bytes 3145736 | tf_op jit(solution)/shard_map/ppermute | solution.py:379
  521.4 58.3 %all-to-all-start.2 = ((bf16[8,1,4,128,128]{4,3,2,1,0:T(8,128)(2,1)}), bf16[8,1,4,128,128]{4,3,2,1,0:T(8,128)(2,1)}, u32[]{:S(2)}, u32[]{:S(2)}) async-start(bf16[8,1,4,128,128]{4,3,2,1,0:T(8,128)(2,1)} %copy-done.11), calls=%async_computation.2 | async-start | bytes 2097152 | tf_op jit(solution)/shard_map/all_to_all | solution.py:626
  533.1 14.0 %collective-permute-start.52 = (bf16[256,1024]{1,0:T(8,128)(2,1)S(1)}, bf16[256,1024]{1,0:T(8,128)(2,1)S(1)}, u32[]{:S(2)}, u32[]{:S(2)}) collective-permute-start(bf16[256,1024]{1,0:T(8,128)(2,1)S(1)} %get-tuple-element.174), channel_id=1, source_target_pairs={{0,16},{8,24},{16,0},{24,8},{1,17},{9,25},{17,1},{25,9},{2,18},{10... | collective-permute-start | bytes 1572872 | tf_op jit(solution)/shard_map/ppermute | solution.py:379
  538.4 18.4 %collective-permute-start.51 = (bf16[256,1024]{1,0:T(8,128)(2,1)S(1)}, bf16[256,1024]{1,0:T(8,128)(2,1)S(1)}, u32[]{:S(2)}, u32[]{:S(2)}) collective-permute-start(bf16[256,1024]{1,0:T(8,128)(2,1)S(1)} %get-tuple-element.175), channel_id=1, source_target_pairs={{0,1},{1,0},{2,3},{3,2},{4,5},{5,4},{6,7},{7,6},{8,9},{9,8},{10,11... | collective-permute-start | bytes 1572872 | tf_op jit(solution)/shard_map/ppermute | solution.py:379
  579.7 25.5 %collective-permute-start.53 = (bf16[256,2048]{1,0:T(8,128)(2,1)}, bf16[256,2048]{1,0:T(8,128)(2,1)}, u32[]{:S(2)}, u32[]{:S(2)}) collective-permute-start(bf16[256,2048]{1,0:T(8,128)(2,1)} %pad_maximum_fusion.4), channel_id=1, source_target_pairs={{0,16},{8,24},{16,0},{24,8},{1,17},{9,25},{17,1},{25,9},{2,18},{10... | collective-permute-start | bytes 3145736 | tf_op jit(solution)/shard_map/ppermute | solution.py:379
  580.6 24.9 %collective-permute-start.54 = (bf16[256,2048]{1,0:T(8,128)(2,1)}, bf16[256,2048]{1,0:T(8,128)(2,1)}, u32[]{:S(2)}, u32[]{:S(2)}) collective-permute-start(bf16[256,2048]{1,0:T(8,128)(2,1)} %pad_maximum_fusion.5), channel_id=1, source_target_pairs={{0,1},{1,0},{2,3},{3,2},{4,5},{5,4},{6,7},{7,6},{8,9},{9,8},{10,11... | collective-permute-start | bytes 3145736 | tf_op jit(solution)/shard_map/ppermute | solution.py:379
  609.6 76.3 %all-to-all-start.3 = ((bf16[8,3,4,128,128]{4,3,2,1,0:T(8,128)(2,1)}), bf16[8,3,4,128,128]{4,3,2,1,0:T(8,128)(2,1)}, u32[]{:S(2)}, u32[]{:S(2)}) async-start(bf16[8,3,4,128,128]{4,3,2,1,0:T(8,128)(2,1)} %attend_bwd.1), calls=%async_computation.3 | async-start | bytes 6291456 | tf_op jit(solution)/shard_map/all_to_all | solution.py:626
  616.0 9.4 %collective-permute-start.56 = (bf16[2,64,1024]{2,1,0:T(8,128)(2,1)}, bf16[2,64,1024]{2,1,0:T(8,128)(2,1)}, u32[]{:S(2)}, u32[]{:S(2)}) collective-permute-start(bf16[2,64,1024]{2,1,0:T(8,128)(2,1)} %get-tuple-element.173), channel_id=1, source_target_pairs={{0,16},{8,24},{16,0},{24,8},{1,17},{9,25},{17,1},{25,9},{2,18},{10... | collective-permute-start | bytes 786440 | tf_op jit(solution)/shard_map/ppermute | solution.py:379
  617.5 12.7 %collective-permute-start.57 = (bf16[2,64,1024]{2,1,0:T(8,128)(2,1)S(1)}, bf16[2,64,1024]{2,1,0:T(8,128)(2,1)S(1)}, u32[]{:S(2)}, u32[]{:S(2)}) collective-permute-start(bf16[2,64,1024]{2,1,0:T(8,128)(2,1)S(1)} %get-tuple-element.172), channel_id=1, source_target_pairs={{0,24},{8,16},{16,8},{24,0},{1,25},{9,17},{17,9},{25,1},{2,26},{10... | collective-permute-start | bytes 786440 | tf_op jit(solution)/shard_map/ppermute | solution.py:379
  630.3 30.3 %collective-permute-start.58 = (bf16[4,64,1024]{2,1,0:T(8,128)(2,1)S(1)}, bf16[4,64,1024]{2,1,0:T(8,128)(2,1)S(1)}, u32[]{:S(2)}, u32[]{:S(2)}) collective-permute-start(bf16[4,64,1024]{2,1,0:T(8,128)(2,1)S(1)} %pad_maximum_fusion.10), channel_id=1, source_target_pairs={{0,1},{1,0},{2,3},{3,2},{4,5},{5,4},{6,7},{7,6},{8,9},{9,8},{10,11... | collective-permute-start | bytes 1572872 | tf_op jit(solution)/shard_map/ppermute | solution.py:379
  700.6 13.3 %collective-permute-start.60 = (bf16[4,64,1024]{2,1,0:T(8,128)(2,1)S(1)}, bf16[4,64,1024]{2,1,0:T(8,128)(2,1)S(1)}, u32[]{:S(2)}, u32[]{:S(2)}) collective-permute-start(bf16[4,64,1024]{2,1,0:T(8,128)(2,1)S(1)} %get-tuple-element.117), channel_id=1, source_target_pairs={{0,1},{2,0},{4,2},{6,4},{7,6},{5,7},{3,5},{1,3},{8,9},{10,8},{12,1... | collective-permute-start | bytes 1572872 | tf_op jit(solution)/shard_map/ppermute | solution.py:547
  702.0 13.4 %collective-permute-start.59 = (bf16[4,64,1024]{2,1,0:T(8,128)(2,1)S(1)}, bf16[4,64,1024]{2,1,0:T(8,128)(2,1)S(1)}, u32[]{:S(2)}, u32[]{:S(2)}) collective-permute-start(bf16[4,64,1024]{2,1,0:T(8,128)(2,1)S(1)} %get-tuple-element.116), channel_id=1, source_target_pairs={{0,2},{2,4},{4,6},{6,7},{7,5},{5,3},{3,1},{1,0},{8,10},{10,12},{12... | collective-permute-start | bytes 1572872 | tf_op jit(solution)/shard_map/ppermute | solution.py:547
  710.1 14.7 %collective-permute-start.62 = (bf16[256,2048]{1,0:T(8,128)(2,1)S(1)}, bf16[256,2048]{1,0:T(8,128)(2,1)S(1)}, u32[]{:S(2)}, u32[]{:S(2)}) collective-permute-start(bf16[256,2048]{1,0:T(8,128)(2,1)S(1)} %get-tuple-element.164), channel_id=1, source_target_pairs={{0,8},{8,0},{16,24},{24,16},{1,9},{9,1},{17,25},{25,17},{2,10},{10... | collective-permute-start | bytes 3145736 | tf_op jit(solution)/shard_map/ppermute | solution.py:379
  716.6 24.2 %collective-permute-start.66 = (bf16[4,64,2048]{2,1,0:T(8,128)(2,1)}, bf16[4,64,2048]{2,1,0:T(8,128)(2,1)}, u32[]{:S(2)}, u32[]{:S(2)}) collective-permute-start(bf16[4,64,2048]{2,1,0:T(8,128)(2,1)} %pad_maximum_fusion.6), channel_id=1, source_target_pairs={{0,2},{2,4},{4,6},{6,7},{7,5},{5,3},{3,1},{1,0},{8,10},{10,12},{12... | collective-permute-start | bytes 3145736 | tf_op jit(solution)/shard_map/ppermute | solution.py:547
  716.9 23.9 %collective-permute-start.67 = (bf16[4,64,2048]{2,1,0:T(8,128)(2,1)}, bf16[4,64,2048]{2,1,0:T(8,128)(2,1)}, u32[]{:S(2)}, u32[]{:S(2)}) collective-permute-start(bf16[4,64,2048]{2,1,0:T(8,128)(2,1)} %pad_maximum_fusion.7), channel_id=1, source_target_pairs={{0,1},{2,0},{4,2},{6,4},{7,6},{5,7},{3,5},{1,3},{8,9},{10,8},{12,1... | collective-permute-start | bytes 3145736 | tf_op jit(solution)/shard_map/ppermute | solution.py:547
  718.7 27.6 %collective-permute-start.61 = (bf16[256,2048]{1,0:T(8,128)(2,1)}, bf16[256,2048]{1,0:T(8,128)(2,1)}, u32[]{:S(2)}, u32[]{:S(2)}) collective-permute-start(bf16[256,2048]{1,0:T(8,128)(2,1)} %get-tuple-element.163), channel_id=1, source_target_pairs={{0,8},{8,0},{16,24},{24,16},{1,9},{9,1},{17,25},{25,17},{2,10},{10... | collective-permute-start | bytes 3145736 | tf_op jit(solution)/shard_map/ppermute | solution.py:379
  727.4 25.9 %collective-permute-start.63 = (bf16[256,2048]{1,0:T(8,128)(2,1)}, bf16[256,2048]{1,0:T(8,128)(2,1)}, u32[]{:S(2)}, u32[]{:S(2)}) collective-permute-start(bf16[256,2048]{1,0:T(8,128)(2,1)} %add_convert_fusion), channel_id=1, source_target_pairs={{0,16},{8,24},{16,0},{24,8},{1,17},{9,25},{17,1},{25,9},{2,18},{10... | collective-permute-start | bytes 3145736 | tf_op jit(solution)/shard_map/ppermute | solution.py:379
  743.9 23.1 %collective-permute-start.68 = (bf16[4,64,2048]{2,1,0:T(8,128)(2,1)S(1)}, bf16[4,64,2048]{2,1,0:T(8,128)(2,1)S(1)}, u32[]{:S(2)}, u32[]{:S(2)}) collective-permute-start(bf16[4,64,2048]{2,1,0:T(8,128)(2,1)S(1)} %get-tuple-element.123), channel_id=1, source_target_pairs={{0,2},{2,4},{4,6},{6,7},{7,5},{5,3},{3,1},{1,0},{8,10},{10,12},{12... | collective-permute-start | bytes 3145736 | tf_op jit(solution)/shard_map/ppermute | solution.py:547
  745.6 23.4 %collective-permute-start.69 = (bf16[4,64,2048]{2,1,0:T(8,128)(2,1)S(1)}, bf16[4,64,2048]{2,1,0:T(8,128)(2,1)S(1)}, u32[]{:S(2)}, u32[]{:S(2)}) collective-permute-start(bf16[4,64,2048]{2,1,0:T(8,128)(2,1)S(1)} %get-tuple-element.124), channel_id=1, source_target_pairs={{0,1},{2,0},{4,2},{6,4},{7,6},{5,7},{3,5},{1,3},{8,9},{10,8},{12,1... | collective-permute-start | bytes 3145736 | tf_op jit(solution)/shard_map/ppermute | solution.py:547
  772.7 22.6 %collective-permute-start.70 = (bf16[4,64,2048]{2,1,0:T(8,128)(2,1)}, bf16[4,64,2048]{2,1,0:T(8,128)(2,1)}, u32[]{:S(2)}, u32[]{:S(2)}) collective-permute-start(bf16[4,64,2048]{2,1,0:T(8,128)(2,1)} %get-tuple-element.125), channel_id=1, source_target_pairs={{0,2},{2,4},{4,6},{6,7},{7,5},{5,3},{3,1},{1,0},{8,10},{10,12},{12... | collective-permute-start | bytes 3145736 | tf_op jit(solution)/shard_map/ppermute | solution.py:547
  773.8 22.0 %collective-permute-start.71 = (bf16[4,64,2048]{2,1,0:T(8,128)(2,1)}, bf16[4,64,2048]{2,1,0:T(8,128)(2,1)}, u32[]{:S(2)}, u32[]{:S(2)}) collective-permute-start(bf16[4,64,2048]{2,1,0:T(8,128)(2,1)} %get-tuple-element.126), channel_id=1, source_target_pairs={{0,1},{2,0},{4,2},{6,4},{7,6},{5,7},{3,5},{1,3},{8,9},{10,8},{12,1... | collective-permute-start | bytes 3145736 | tf_op jit(solution)/shard_map/ppermute | solution.py:547
  777.3 21.2 %collective-permute-start.65 = (f32[2,2,2,768]{3,2,1,0:T(2,128)S(1)}, f32[2,2,2,768]{3,2,1,0:T(2,128)S(1)}, u32[]{:S(2)}, u32[]{:S(2)}) collective-permute-start(f32[2,2,2,768]{3,2,1,0:T(2,128)S(1)} %dynamic-slice_bitcast_fusion.13), channel_id=1, source_target_pairs={{0,16},{8,24},{16,0},{24,8},{1,17},{9,25},{17,1},{25,9},{2,18},{10... | collective-permute-start | bytes 73736 | tf_op jit(solution)/shard_map/ppermute | solution.py:379
  (105 other events, 755.0 us)
Sparse Core Ops, SparseCore 0:
  15.3 58.8 all-gather.4
  212.2 98.4 all-gather.8
  312.6 80.5 all-gather.6
  442.4 73.9 reduce-scatter.2
  521.5 91.3 reduce-scatter.4

commit v7 on v6

--- a/solution.py
+++ b/solution.py
@@ -761,10 +761,8 @@
 
 
 def wide_outer_kernel(*refs, heads, order):
-    lefts, (parts_ref, extra_ref, out_ref, rows_ref) = refs[:-4], refs[-4:]
-    pair, narrow, shard, total = out_ref.shape
-    width = rows_ref.shape[1]
-    more = total - width
+    lefts, (parts_ref, out_ref, rows_ref) = refs[:-3], refs[-3:]
+    pair, narrow, shard, _ = out_ref.shape
 
     @pl.when(pl.program_id(0) == 0)
     def _():
@@ -781,17 +779,13 @@
             left, rows_ref[...], CONTRACT_FIRST, preferred_element_type=jnp.float32
         )
         for y in range(pair):
-            out_ref[y, n, :, :width] = acc[y * shard : (y + 1) * shard].astype(jnp.bfloat16)
-            out_ref[y, n, :, width:] = extra_ref[
-                y * shard : (y + 1) * shard, n * more : (n + 1) * more
-            ]
-
-
-def wide_outer(lefts, parts, extra, wide, heads, order):
+            out_ref[y, n] = acc[y * shard : (y + 1) * shard].astype(jnp.bfloat16)
+
+
+def wide_outer(lefts, parts, wide, heads, order):
     narrow = len(lefts)
     units, count, blocks, tokens, head_dim = parts.shape
-    shard, width = extra.shape[0] // wide, count * heads * head_dim
-    more = extra.shape[1] // narrow
+    shard, width = lefts[0].shape[1] // (wide * narrow), count * heads * head_dim
     block = lefts[0].shape[0]
     rows = blocks * tokens * units // heads
     deep = wide // 2
@@ -799,7 +793,7 @@
         functools.partial(wide_outer_kernel, heads=heads, order=order),
         grid=(deep,),
         out_shape=(
-            jax.ShapeDtypeStruct((wide, narrow, shard, width + more), jnp.bfloat16),
+            jax.ShapeDtypeStruct((wide, narrow, shard, width), jnp.bfloat16),
             jax.ShapeDtypeStruct((rows, width), jnp.bfloat16),
         ),
         in_specs=[
@@ -807,17 +801,14 @@
             for _ in lefts
             for n in range(narrow)
         ]
-        + [
-            resident(parts.shape),
-            pl.BlockSpec((2 * shard, extra.shape[1]), lambda i: (i, 0)),
-        ],
+        + [resident(parts.shape)],
         out_specs=(
-            pl.BlockSpec((2, narrow, shard, width + more), lambda i: (i, 0, 0, 0)),
+            pl.BlockSpec((2, narrow, shard, width), lambda i: (i, 0, 0, 0)),
             pl.BlockSpec((rows, width), lambda i: (0, 0)),
         ),
         compiler_params=BIG,
         name="wide_outer",
-    )(*[left for left in lefts for _ in range(narrow)], parts, extra)
+    )(*[left for left in lefts for _ in range(narrow)], parts)
 
 
 def row_block(parts_ref, j, b, heads):
@@ -1286,7 +1277,7 @@
     grads = hold(grads, up_back)
     order = (1, 3, 0, 2)
     sums, back = wide_outer(
-        [first_norm[j] for j in order], grads, out_grad, wide, heads, order
+        [first_norm[j] for j in order], grads, wide, heads, order
     )
     made = {}
 
@@ -1309,8 +1300,7 @@
         return ()
 
     qkv_rows = jnp.concatenate(ring_scatter(sums, beside, 1), axis=-1)
-    out_grad = qkv_rows[..., 3 * cols :].transpose(1, 0, 2).reshape(shard, width)
-    qkv_rows = qkv_rows[..., : 3 * cols]
+    out_grad = wide_scatter(hold(out_grad, back), 0)
     swapped = narrow_blocks(lambda n: at(qkv_rows, n))
     qkv_grad = place_qkv(me, swapped)
     back_sums = jnp.sum(back.astype(f32), axis=0)

time: 834 us -> 832 us (level)
    unnamed x177 -> x181, local copies, waits for them, and re-layouts: 48.9 us -> 47.3 us
  transfers between devices with their start and end apart: 87 -> 88, of which waited for: 55 -> 57; matrix products, arithmetic and copies ran while one was open for 18% -> 19% of each run, Pallas kernels for 10% -> 10%
where the time goes in v7:
time: 832 us; the launch traced here: 822 us
  waiting for transfers between devices  387 us (47%)
  Pallas kernels  137 us (16%)
  starting transfers between devices  96.3 us (12%)
  local copies, waits for them, and re-layouts  92.6 us (11%)
  other arithmetic  64.2 us (8%)
  matrix products  29.1 us (3%)
  between operations  16.1 us (2%)
    ppermute x62, waiting for transfers between devices, flip(): return lax.ppermute(value, axis, [(i, i ^ bits) for i in range(size)])  236 us
    ppermute x16, waiting for transfers between devices, ring_step(): lax.ppermute(value, WIDE, [(order[i], order[(i + by) % size]) for i in ra...  90.3 us
    all_to_all x4, waiting for transfers between devices, wide_swap(): return lax.all_to_all(parts, WIDE, split_axis=0, concat_axis=0, tiled=True)  56.7 us
    ppermute x62, starting transfers between devices, flip(): return lax.ppermute(value, axis, [(i, i ^ bits) for i in range(size)])  56.6 us
    unnamed x181, local copies, waits for them, and re-layouts  47.3 us
    pallas_call x1, Pallas kernels, feed_forward(): pl.pallas_call(ff_kernel, grid=(inner // step,), out_shape=(jax.ShapeDtyp...  30.1 us
    pallas_call x4, Pallas kernels, times_parts(): pl.pallas_call(times_parts_kernel, grid=(narrow,), out_shape=jax.ShapeDty...  26.9 us
    ppermute x16, starting transfers between devices, ring_step(): lax.ppermute(value, WIDE, [(order[i], order[(i + by) % size]) for i in ra...  21.3 us
  transfers between devices with their start and end apart: 88, of which 57 were waited for; matrix products, arithmetic and copies ran while one was open for 19% of the time, Pallas kernels for 10%

profile of v7, /device:TPU:0, one launch (start us, length us, event | category | flops | bytes accessed | tf_op | source)
XLA Modules:
  0.0 822.4 jit_solution(15788314542265615801)
XLA Ops:
  26.7 3.6 collective-permute-done.4
  36.8 3.3 broadcast_in_dim.74
  41.0 20.8 %collective-permute-done.11 = bf16[4,64,1536]{2,1,0:T(8,128)(2,1)} collective-permute-done((bf16[4,64,1536]{2,1,0:T(8,128)(2,1)}, bf16[4,64,1536]{2,1,0:T(8,128)(2,1)}, u32[]{:S(2)}, u32[]{:S(2)}) %collective-permute-start.11) | collective-permute-done | bytes 786464 | tf_op jit(solution)/shard_map/ppermute | solution.py:547
  61.8 5.9 collective-permute-start.13
  67.7 3.4 collective-permute-done.12
  76.2 11.9 %collective-permute-done.13 = bf16[4,64,1536]{2,1,0:T(8,128)(2,1)S(1)} collective-permute-done((bf16[4,64,1536]{2,1,0:T(8,128)(2,1)}, bf16[4,64,1536]{2,1,0:T(8,128)(2,1)S(1)}, u32[]{:S(2)}, u32[]{:S(2)}) %collective-permute-start.13) | collective-permute-done | bytes 786464 | tf_op jit(solution)/shard_map/ppermute | solution.py:547
  91.9 13.4 %collective-permute-done.15 = bf16[4,64,1536]{2,1,0:T(8,128)(2,1)S(1)} collective-permute-done((bf16[4,64,1536]{2,1,0:T(8,128)(2,1)S(1)}, bf16[4,64,1536]{2,1,0:T(8,128)(2,1)S(1)}, u32[]{:S(2)}, u32[]{:S(2)}) %collective-permute-start.15) | collective-permute-done | bytes 786464 | tf_op jit(solution)/shard_map/ppermute | solution.py:547
  109.6 3.8 collective-permute-done.17
  116.1 11.5 %project_parts.1 = bf16[8,3,4,128,128]{4,3,2,1,0:T(8,128)(2,1)} custom-call(bf16[256,2048]{1,0:T(8,128)(2,1)S(1)} %fusion.26.refs_0_.refs_8_.refs_9_.refs_10_.refs_11_, bf16[256,2048]{1,0:T(8,128)(2,1)S(1)} %collective-permute-done.5.refs_1_.refs_0_.refs_2_.refs_3_, bf16[256,2048]{1,0:T(8,128)(2,1)S(1)} %collective-permute-done.6.refs_2_.refs_12_.refs_13_.refs_14_.refs_15_, ...), custom_call_target="tpu_custom_call" | custom-call | tf_op jit(solution)/shard_map/project_parts/pallas_call | solution.py:718
  127.6 4.6 all-to-all-start
  138.2 3.3 reshape.418.segc_ref
  141.5 30.5 %collective-permute-done.19 = bf16[4,64,1024]{2,1,0:T(8,128)(2,1)} collective-permute-done((bf16[4,64,1024]{2,1,0:T(8,128)(2,1)}, bf16[4,64,1024]{2,1,0:T(8,128)(2,1)}, u32[]{:S(2)}, u32[]{:S(2)}) %collective-permute-start.19) | collective-permute-done | bytes 524320 | tf_op jit(solution)/shard_map/ppermute | solution.py:379
  176.4 4.2 collective-permute-done.20
  180.6 7.1 collective-permute-done.21
  188.9 10.9 %all-to-all-done.parts_ref = bf16[8,3,4,128,128]{4,3,2,1,0:T(8,128)(2,1)} async-done(((bf16[8,3,4,128,128]{4,3,2,1,0:T(8,128)(2,1)}), bf16[8,3,4,128,128]{4,3,2,1,0:T(8,128)(2,1)}, u32[]{:S(2)}, u32[]{:S(2)}) %all-to-all-start) | async-done | bytes 3145760 | tf_op jit(solution)/shard_map/all_to_all | solution.py:626
  201.4 8.2 attend_fwd.1
  213.2 4.2 all-to-all-start.1
  217.9 3.0 collective-permute-start.23
  220.9 23.4 %collective-permute-done.24 = bf16[256,2048]{1,0:T(8,128)(2,1)} collective-permute-done((bf16[256,2048]{1,0:T(8,128)(2,1)}, bf16[256,2048]{1,0:T(8,128)(2,1)}, u32[]{:S(2)}, u32[]{:S(2)}) %collective-permute-start.24) | collective-permute-done | bytes 1048608 | tf_op jit(solution)/shard_map/ppermute | solution.py:379
  245.4 3.0 collective-permute-start.25
  259.4 3.1 collective-permute-done.26
  263.6 5.9 all-to-all-done.1.parts_ref
  269.5 5.9 unproject.1
  281.1 3.9 collective-permute-start.29
  294.6 14.2 %collective-permute-done.29 = bf16[256,2048]{1,0:T(8,128)(2,1)} collective-permute-done((bf16[256,2048]{1,0:T(8,128)(2,1)}, bf16[256,2048]{1,0:T(8,128)(2,1)}, u32[]{:S(2)}, u32[]{:S(2)}) %collective-permute-start.29) | collective-permute-done | bytes 1048608 | tf_op jit(solution)/shard_map/ppermute | solution.py:379
  308.8 3.6 fusion.31
  320.4 22.4 %collective-permute-done.35 = bf16[256,2048]{1,0:T(8,128)(2,1)S(1)} collective-permute-done((bf16[256,2048]{1,0:T(8,128)(2,1)S(1)}, bf16[256,2048]{1,0:T(8,128)(2,1)S(1)}, u32[]{:S(2)}, u32[]{:S(2)}) %collective-permute-start.35) | collective-permute-done | bytes 1048608 | tf_op jit(solution)/shard_map/ppermute | solution.py:379
  352.2 5.4 collective-permute-done.36
  371.2 30.1 %feed_forward.1 = (bf16[2048,1024]{1,0:T(8,128)(2,1)S(1)}, f32[2048,1024]{1,0:T(8,128)}, bf16[1024,2048]{1,0:T(8,128)(2,1)}) custom-call(bf16[2048,2048]{1,0:T(8,128)(2,1)} %constant_dynamic-update-slice_fusion.10.rows_ref, bf16[4,4,128,1024]{3,2,1,0:T(8,128)(2,1)} %bitcast.215, bf16[4,4,128,1024]{3,2,1,0:T(8,128)(2,1)} %bitcast.216, ...), custom_call_target="tpu_custom_call" | custom-call | tf_op jit(solution)/shard_map/feed_forward/pallas_call | solution.py:991
  403.2 14.6 %pull_back.1 = (bf16[2048,1024]{1,0:T(8,128)(2,1)S(1)}, f32[1,1024]{1,0:T(1,128)S(1)}) custom-call(bf16[2048,2048]{1,0:T(8,128)(2,1)} %constant_dynamic-update-slice_fusion.2.refs_5_.rows_ref, bf16[1024,2048]{1,0:T(8,128)(2,1)} %all-gather.7.cloned.1.call-done.weight_ref, f32[2048,1024]{1,0:T(8,128)} %get-tuple-element.95.slope_ref), custom_call_target="tpu_custom_call" | custom-call | tf_op jit(solution)/shard_map/pull_back/pallas_call | solution.py:1034
  419.9 7.4 times_parts.4
  427.9 7.4 times_parts.5
  435.3 3.9 convert_add_fusion.6
  445.9 9.3 %collective-permute-done.43 = bf16[256,1024]{1,0:T(8,128)(2,1)} collective-permute-done((bf16[256,1024]{1,0:T(8,128)(2,1)}, bf16[256,1024]{1,0:T(8,128)(2,1)}, u32[]{:S(2)}, u32[]{:S(2)}) %collective-permute-start.43) | collective-permute-done | bytes 524320 | tf_op jit(solution)/shard_map/ppermute | solution.py:379
  458.9 13.3 %convolution_convert_fusion.2 = bf16[2048,1024]{1,0:T(8,128)(2,1)} fusion(bf16[2048,2048]{1,0:T(8,128)(2,1)} %constant_dynamic-update-slice_fusion.10.rows_ref, bf16[2048,1024]{1,0:T(8,128)(2,1)S(1)} %copy-done.4), kind=kOutput, calls=%fused_computation.11 | convolution fusion | flops 8592031744 | bytes 16777216 | tf_op jit(solution)/shard_map/dot_general | solution.py:46
  472.1 8.6 %collective-permute-done.44 = bf16[256,2048]{1,0:T(8,128)(2,1)S(1)} collective-permute-done((bf16[256,2048]{1,0:T(8,128)(2,1)S(1)}, bf16[256,2048]{1,0:T(8,128)(2,1)S(1)}, u32[]{:S(2)}, u32[]{:S(2)}) %collective-permute-start.44) | collective-permute-done | bytes 1048608 | tf_op jit(solution)/shard_map/ppermute | solution.py:379
  490.2 6.1 convolution_convert_fusion
  496.3 6.0 convolution_convert_fusion.1
  502.3 10.6 %collective-permute-done.48.refs_2_ = bf16[256,2048]{1,0:T(8,128)(2,1)S(1)} collective-permute-done((bf16[256,2048]{1,0:T(8,128)(2,1)S(1)}, bf16[256,2048]{1,0:T(8,128)(2,1)S(1)}, u32[]{:S(2)}, u32[]{:S(2)}) %collective-permute-start.48) | collective-permute-done | bytes 1048608 | tf_op jit(solution)/shard_map/ppermute | solution.py:379
  515.5 5.2 project.1
  521.9 4.3 all-to-all-start.2
  526.1 3.1 collective-permute-done.50
  529.2 6.4 convert_add_fusion
  537.6 3.7 fusion.8
  545.3 5.6 collective-permute-done.52
  553.2 9.1 %collective-permute-done.51 = bf16[256,1024]{1,0:T(8,128)(2,1)S(1)} collective-permute-done((bf16[256,1024]{1,0:T(8,128)(2,1)}, bf16[256,1024]{1,0:T(8,128)(2,1)S(1)}, u32[]{:S(2)}, u32[]{:S(2)}) %collective-permute-start.51) | collective-permute-done | bytes 524320 | tf_op jit(solution)/shard_map/ppermute | solution.py:379
  563.5 16.7 %all-to-all-done.2.do_ref = bf16[8,1,4,128,128]{4,3,2,1,0:T(8,128)(2,1)} async-done(((bf16[8,1,4,128,128]{4,3,2,1,0:T(8,128)(2,1)}), bf16[8,1,4,128,128]{4,3,2,1,0:T(8,128)(2,1)}, u32[]{:S(2)}, u32[]{:S(2)}) %all-to-all-start.2) | async-done | bytes 1048608 | tf_op jit(solution)/shard_map/all_to_all | solution.py:626
  585.9 17.7 %attend_bwd.1 = bf16[8,3,4,128,128]{4,3,2,1,0:T(8,128)(2,1)} custom-call(s32[2]{0:T(128)S(1)} %pad_add_fusion.me_ref, s32[8,512,1]{2,1,0:T(8,128)S(1)} %copy-done.2, s32[1,4096]{1,0:T(1,128)S(1)} %fusion.58.segr_ref, f32[8,512,1]{2,1,0:T(8,128)S(1)} %copy-done.13, bf16[8,3,4,128,128]{4,3,2,1,0:T(8,128)(2,1)} %all-to-all-done.parts_ref, ...), custom_call_target="tpu_custom_call" | custom-call | tf_op jit(solution)/shard_map/attend_bwd/pallas_call | solution.py:952
  606.0 4.0 fusion.16
  610.1 4.5 all-to-all-start.3
  620.4 5.6 collective-permute-done.56
  627.0 3.8 collective-permute-done.57
  632.8 28.3 %collective-permute-done.58.other_ref = bf16[4,64,1024]{2,1,0:T(8,128)(2,1)S(1)} collective-permute-done((bf16[4,64,1024]{2,1,0:T(8,128)(2,1)S(1)}, bf16[4,64,1024]{2,1,0:T(8,128)(2,1)S(1)}, u32[]{:S(2)}, u32[]{:S(2)}) %collective-permute-start.58) | collective-permute-done | bytes 524320 | tf_op jit(solution)/shard_map/ppermute | solution.py:379
  663.1 23.2 %all-to-all-done.3.refs_16_ = bf16[8,3,4,128,128]{4,3,2,1,0:T(8,128)(2,1)} async-done(((bf16[8,3,4,128,128]{4,3,2,1,0:T(8,128)(2,1)}), bf16[8,3,4,128,128]{4,3,2,1,0:T(8,128)(2,1)}, u32[]{:S(2)}, u32[]{:S(2)}) %all-to-all-start.3) | async-done | bytes 3145760 | tf_op jit(solution)/shard_map/all_to_all | solution.py:626
  686.4 12.3 %wide_outer.1 = (bf16[8,4,64,1536]{3,2,1,0:T(8,128)(2,1)}, bf16[1024,1536]{1,0:T(8,128)(2,1)}) custom-call(bf16[256,2048]{1,0:T(8,128)(2,1)S(1)} %collective-permute-done.5.refs_1_.refs_0_.refs_2_.refs_3_, bf16[256,2048]{1,0:T(8,128)(2,1)S(1)} %collective-permute-done.5.refs_1_.refs_0_.refs_2_.refs_3_, ...), custom_call_target="tpu_custom_call" | custom-call | tf_op jit(solution)/shard_map/wide_outer/pallas_call | solution.py:792
  702.7 6.1 times_parts.6
  716.5 6.0 times_parts.7
  722.6 8.3 %collective-permute-done.66 = bf16[4,64,1536]{2,1,0:T(8,128)(2,1)S(1)} collective-permute-done((bf16[4,64,1536]{2,1,0:T(8,128)(2,1)S(1)}, bf16[4,64,1536]{2,1,0:T(8,128)(2,1)S(1)}, u32[]{:S(2)}, u32[]{:S(2)}) %collective-permute-start.66) | collective-permute-done | bytes 786464 | tf_op jit(solution)/shard_map/ppermute | solution.py:547
  744.1 7.1 collective-permute-done.68
  754.4 5.3 collective-permute-done.63
  772.8 15.8 %collective-permute-done.70 = bf16[4,64,1536]{2,1,0:T(8,128)(2,1)S(1)} collective-permute-done((bf16[4,64,1536]{2,1,0:T(8,128)(2,1)S(1)}, bf16[4,64,1536]{2,1,0:T(8,128)(2,1)S(1)}, u32[]{:S(2)}, u32[]{:S(2)}) %collective-permute-start.70) | collective-permute-done | bytes 786464 | tf_op jit(solution)/shard_map/ppermute | solution.py:547
  793.4 3.1 collective-permute-done.73
  801.8 3.0 collective-permute-done.76.refs_2_
  809.4 4.0 reduce-scatter.8.cloned.1.call-done
  (481 shorter events, 232.9 us)
Async XLA Ops:
  7.3 108.8 %all-gather.5.cloned.1.call-start = ((), (), s32[]{:S(2)}) async-start(), calls=%async_computation.7 | async-start | bytes 2359296 | tf_op jit(solution)/shard_map/all_gather | solution.py:630
  9.6 22.2 %collective-permute-start.10 = (bf16[64,1536]{1,0:T(8,128)(2,1)S(1)}, bf16[64,1536]{1,0:T(8,128)(2,1)S(1)}, u32[]{:S(2)}, u32[]{:S(2)}) collective-permute-start(bf16[64,1536]{1,0:T(8,128)(2,1)S(1)} %pad_maximum_fusion.13), channel_id=1, source_target_pairs={{0,8},{8,0},{16,24},{24,16},{1,9},{9,1},{17,25},{25,17},{2,10},{10... | collective-permute-start | bytes 589832 | tf_op jit(solution)/shard_map/ppermute | solution.py:379
  10.1 21.7 %collective-permute-start.8 = (bf16[64,1536]{1,0:T(8,128)(2,1)S(1)}, bf16[64,1536]{1,0:T(8,128)(2,1)S(1)}, u32[]{:S(2)}, u32[]{:S(2)}) collective-permute-start(bf16[64,1536]{1,0:T(8,128)(2,1)S(1)} %pad_maximum_fusion.11), channel_id=1, source_target_pairs={{0,24},{8,16},{16,8},{24,0},{1,25},{9,17},{17,9},{25,1},{2,26},{10... | collective-permute-start | bytes 589832 | tf_op jit(solution)/shard_map/ppermute | solution.py:379
  14.6 17.2 %collective-permute-start.9 = (bf16[64,1536]{1,0:T(8,128)(2,1)S(1)}, bf16[64,1536]{1,0:T(8,128)(2,1)S(1)}, u32[]{:S(2)}, u32[]{:S(2)}) collective-permute-start(bf16[64,1536]{1,0:T(8,128)(2,1)S(1)} %pad_maximum_fusion.12), channel_id=1, source_target_pairs={{0,16},{8,24},{16,0},{24,8},{1,17},{9,25},{17,1},{25,9},{2,18},{10... | collective-permute-start | bytes 589832 | tf_op jit(solution)/shard_map/ppermute | solution.py:379
  33.1 28.7 %collective-permute-start.11 = (bf16[4,64,1536]{2,1,0:T(8,128)(2,1)}, bf16[4,64,1536]{2,1,0:T(8,128)(2,1)}, u32[]{:S(2)}, u32[]{:S(2)}) collective-permute-start(bf16[4,64,1536]{2,1,0:T(8,128)(2,1)} %pad_maximum_fusion.6), channel_id=1, source_target_pairs={{0,2},{2,4},{4,6},{6,7},{7,5},{5,3},{3,1},{1,0},{8,10},{10,12},{12... | collective-permute-start | bytes 2359304 | tf_op jit(solution)/shard_map/ppermute | solution.py:547
  34.6 36.4 %collective-permute-start.12 = (bf16[4,64,1536]{2,1,0:T(8,128)(2,1)}, bf16[4,64,1536]{2,1,0:T(8,128)(2,1)}, u32[]{:S(2)}, u32[]{:S(2)}) collective-permute-start(bf16[4,64,1536]{2,1,0:T(8,128)(2,1)} %pad_maximum_fusion.6), channel_id=1, source_target_pairs={{0,1},{2,0},{4,2},{6,4},{7,6},{5,7},{3,5},{1,3},{8,9},{10,8},{12,1... | collective-permute-start | bytes 2359304 | tf_op jit(solution)/shard_map/ppermute | solution.py:547
  35.6 40.6 %collective-permute-start.6 = (bf16[256,2048]{1,0:T(8,128)(2,1)S(1)}, bf16[256,2048]{1,0:T(8,128)(2,1)S(1)}, u32[]{:S(2)}, u32[]{:S(2)}) collective-permute-start(bf16[256,2048]{1,0:T(8,128)(2,1)S(1)} %fusion.26.refs_0_.refs_8_.refs_9_.refs_10_.refs_11_), channel_id=1, source_target_pairs={{0,16},{8,24},{16,0},{24,8},{1,17},{9,25},{17,1},{25,9},{2,18},{10... | collective-permute-start | bytes 3145736 | tf_op jit(solution)/shard_map/ppermute | solution.py:379
  35.9 80.3 %collective-permute-start.5 = (bf16[256,2048]{1,0:T(8,128)(2,1)S(1)}, bf16[256,2048]{1,0:T(8,128)(2,1)S(1)}, u32[]{:S(2)}, u32[]{:S(2)}) collective-permute-start(bf16[256,2048]{1,0:T(8,128)(2,1)S(1)} %fusion.26.refs_0_.refs_8_.refs_9_.refs_10_.refs_11_), channel_id=1, source_target_pairs={{0,8},{8,0},{16,24},{24,16},{1,9},{9,1},{17,25},{25,17},{2,10},{10... | collective-permute-start | bytes 3145736 | tf_op jit(solution)/shard_map/ppermute | solution.py:379
  61.8 26.2 %collective-permute-start.13 = (bf16[4,64,1536]{2,1,0:T(8,128)(2,1)}, bf16[4,64,1536]{2,1,0:T(8,128)(2,1)S(1)}, u32[]{:S(2)}, u32[]{:S(2)}) collective-permute-start(bf16[4,64,1536]{2,1,0:T(8,128)(2,1)} %collective-permute-done.11), channel_id=1, source_target_pairs={{0,2},{2,4},{4,6},{6,7},{7,5},{5,3},{3,1},{1,0},{8,10},{10,12},{12... | collective-permute-start | bytes 2359304 | tf_op jit(solution)/shard_map/ppermute | solution.py:547
  71.1 18.0 %collective-permute-start.14 = (bf16[4,64,1536]{2,1,0:T(8,128)(2,1)}, bf16[4,64,1536]{2,1,0:T(8,128)(2,1)S(1)}, u32[]{:S(2)}, u32[]{:S(2)}) collective-permute-start(bf16[4,64,1536]{2,1,0:T(8,128)(2,1)} %collective-permute-done.12), channel_id=1, source_target_pairs={{0,1},{2,0},{4,2},{6,4},{7,6},{5,7},{3,5},{1,3},{8,9},{10,8},{12,1... | collective-permute-start | bytes 2359304 | tf_op jit(solution)/shard_map/ppermute | solution.py:547
  76.2 40.0 %collective-permute-start.7 = (bf16[256,2048]{1,0:T(8,128)(2,1)S(1)}, bf16[256,2048]{1,0:T(8,128)(2,1)}, u32[]{:S(2)}, u32[]{:S(2)}) collective-permute-start(bf16[256,2048]{1,0:T(8,128)(2,1)S(1)} %collective-permute-done.6.refs_2_.refs_12_.refs_13_.refs_14_.refs_15_), channel_id=1, source_target_pairs={{0,8},{8,0},{16,24},{24,16},{1,9},{9,1},{17,25},{25,17},{2,10},{10... | collective-permute-start | bytes 3145736 | tf_op jit(solution)/shard_map/ppermute | solution.py:379
  88.0 17.3 %collective-permute-start.15 = (bf16[4,64,1536]{2,1,0:T(8,128)(2,1)S(1)}, bf16[4,64,1536]{2,1,0:T(8,128)(2,1)S(1)}, u32[]{:S(2)}, u32[]{:S(2)}) collective-permute-start(bf16[4,64,1536]{2,1,0:T(8,128)(2,1)S(1)} %collective-permute-done.13), channel_id=1, source_target_pairs={{0,2},{2,4},{4,6},{6,7},{7,5},{5,3},{3,1},{1,0},{8,10},{10,12},{12... | collective-permute-start | bytes 2359304 | tf_op jit(solution)/shard_map/ppermute | solution.py:547
  89.1 17.9 %collective-permute-start.16 = (bf16[4,64,1536]{2,1,0:T(8,128)(2,1)S(1)}, bf16[4,64,1536]{2,1,0:T(8,128)(2,1)S(1)}, u32[]{:S(2)}, u32[]{:S(2)}) collective-permute-start(bf16[4,64,1536]{2,1,0:T(8,128)(2,1)S(1)} %collective-permute-done.14), channel_id=1, source_target_pairs={{0,1},{2,0},{4,2},{6,4},{7,6},{5,7},{3,5},{1,3},{8,9},{10,8},{12,1... | collective-permute-start | bytes 2359304 | tf_op jit(solution)/shard_map/ppermute | solution.py:547
  127.6 72.2 %all-to-all-start = ((bf16[8,3,4,128,128]{4,3,2,1,0:T(8,128)(2,1)}), bf16[8,3,4,128,128]{4,3,2,1,0:T(8,128)(2,1)}, u32[]{:S(2)}, u32[]{:S(2)}) async-start(bf16[8,3,4,128,128]{4,3,2,1,0:T(8,128)(2,1)} %project_parts.1), calls=%async_computation | async-start | bytes 6291456 | tf_op jit(solution)/shard_map/all_to_all | solution.py:626
  132.3 180.1 %all-gather.9.cloned.1.call-start = ((), (), s32[]{:S(2)}) async-start(), calls=%async_computation.12 | async-start | bytes 5242880 | tf_op jit(solution)/shard_map/all_gather | solution.py:520
  136.3 35.7 %collective-permute-start.19 = (bf16[4,64,1024]{2,1,0:T(8,128)(2,1)}, bf16[4,64,1024]{2,1,0:T(8,128)(2,1)}, u32[]{:S(2)}, u32[]{:S(2)}) collective-permute-start(bf16[4,64,1024]{2,1,0:T(8,128)(2,1)} %slice_bitcast_fusion.9), channel_id=1, source_target_pairs={{0,1},{1,0},{2,3},{3,2},{4,5},{5,4},{6,7},{7,6},{8,9},{9,8},{10,11... | collective-permute-start | bytes 1572872 | tf_op jit(solution)/shard_map/ppermute | solution.py:379
  173.5 14.2 %collective-permute-start.21 = (bf16[2,64,1024]{2,1,0:T(8,128)(2,1)S(1)}, bf16[2,64,1024]{2,1,0:T(8,128)(2,1)S(1)}, u32[]{:S(2)}, u32[]{:S(2)}) collective-permute-start(bf16[2,64,1024]{2,1,0:T(8,128)(2,1)S(1)} %get-tuple-element.183), channel_id=1, source_target_pairs={{0,16},{8,24},{16,0},{24,8},{1,17},{9,25},{17,1},{25,9},{2,18},{10... | collective-permute-start | bytes 786440 | tf_op jit(solution)/shard_map/ppermute | solution.py:379
  176.4 11.3 %collective-permute-start.22 = (bf16[2,64,1024]{2,1,0:T(8,128)(2,1)S(1)}, bf16[2,64,1024]{2,1,0:T(8,128)(2,1)S(1)}, u32[]{:S(2)}, u32[]{:S(2)}) collective-permute-start(bf16[2,64,1024]{2,1,0:T(8,128)(2,1)S(1)} %get-tuple-element.181), channel_id=1, source_target_pairs={{0,8},{8,0},{16,24},{24,16},{1,9},{9,1},{17,25},{25,17},{2,10},{10... | collective-permute-start | bytes 786440 | tf_op jit(solution)/shard_map/ppermute | solution.py:379
  211.9 32.4 %collective-permute-start.24 = (bf16[256,2048]{1,0:T(8,128)(2,1)}, bf16[256,2048]{1,0:T(8,128)(2,1)}, u32[]{:S(2)}, u32[]{:S(2)}) collective-permute-start(bf16[256,2048]{1,0:T(8,128)(2,1)} %bitcast.221), channel_id=1, source_target_pairs={{0,1},{1,0},{2,3},{3,2},{4,5},{5,4},{6,7},{7,6},{8,9},{9,8},{10,11... | collective-permute-start | bytes 3145736 | tf_op jit(solution)/shard_map/ppermute | solution.py:379
  213.2 56.3 %all-to-all-start.1 = ((bf16[8,1,4,128,128]{4,3,2,1,0:T(8,128)(2,1)}), bf16[8,1,4,128,128]{4,3,2,1,0:T(8,128)(2,1)}, u32[]{:S(2)}, u32[]{:S(2)}) async-start(bf16[8,1,4,128,128]{4,3,2,1,0:T(8,128)(2,1)} %copy-done.15), calls=%async_computation.1 | async-start | bytes 2097152 | tf_op jit(solution)/shard_map/all_to_all | solution.py:626
  217.5 185.8 %all-gather.7.cloned.1.call-start = ((), (), s32[]{:S(2)}) async-start(), calls=%async_computation.8 | async-start | bytes 5242880 | tf_op jit(solution)/shard_map/all_gather | solution.py:520
  217.9 32.8 %collective-permute-start.23 = (bf16[256,2048]{1,0:T(8,128)(2,1)}, bf16[256,2048]{1,0:T(8,128)(2,1)}, u32[]{:S(2)}, u32[]{:S(2)}) collective-permute-start(bf16[256,2048]{1,0:T(8,128)(2,1)} %bitcast.222), channel_id=1, source_target_pairs={{0,16},{8,24},{16,0},{24,8},{1,17},{9,25},{17,1},{25,9},{2,18},{10... | collective-permute-start | bytes 3145736 | tf_op jit(solution)/shard_map/ppermute | solution.py:379
  245.4 12.8 %collective-permute-start.25 = (bf16[256,1024]{1,0:T(8,128)(2,1)S(1)}, bf16[256,1024]{1,0:T(8,128)(2,1)S(1)}, u32[]{:S(2)}, u32[]{:S(2)}) collective-permute-start(bf16[256,1024]{1,0:T(8,128)(2,1)S(1)} %slice.328), channel_id=1, source_target_pairs={{0,16},{8,24},{16,0},{24,8},{1,17},{9,25},{17,1},{25,9},{2,18},{10... | collective-permute-start | bytes 1572872 | tf_op jit(solution)/shard_map/ppermute | solution.py:379
  251.8 10.7 %collective-permute-start.26 = (bf16[256,1024]{1,0:T(8,128)(2,1)S(1)}, bf16[256,1024]{1,0:T(8,128)(2,1)S(1)}, u32[]{:S(2)}, u32[]{:S(2)}) collective-permute-start(bf16[256,1024]{1,0:T(8,128)(2,1)S(1)} %slice.329), channel_id=1, source_target_pairs={{0,1},{1,0},{2,3},{3,2},{4,5},{5,4},{6,7},{7,6},{8,9},{9,8},{10,11... | collective-permute-start | bytes 1572872 | tf_op jit(solution)/shard_map/ppermute | solution.py:379
  276.0 11.5 %collective-permute-start.31 = (bf16[256,2048]{1,0:T(8,128)(2,1)}, bf16[256,2048]{1,0:T(8,128)(2,1)}, u32[]{:S(2)}, u32[]{:S(2)}) collective-permute-start(bf16[256,2048]{1,0:T(8,128)(2,1)} %collective-permute-done.23), channel_id=1, source_target_pairs={{0,8},{8,0},{16,24},{24,16},{1,9},{9,1},{17,25},{25,17},{2,10},{10... | collective-permute-start | bytes 3145736 | tf_op jit(solution)/shard_map/ppermute | solution.py:379
  276.0 16.3 %collective-permute-start.33 = (bf16[256,2048]{1,0:T(8,128)(2,1)}, bf16[256,2048]{1,0:T(8,128)(2,1)}, u32[]{:S(2)}, u32[]{:S(2)}) collective-permute-start(bf16[256,2048]{1,0:T(8,128)(2,1)} %get-tuple-element.91), channel_id=1, source_target_pairs={{0,8},{8,0},{16,24},{24,16},{1,9},{9,1},{17,25},{25,17},{2,10},{10... | collective-permute-start | bytes 3145736 | tf_op jit(solution)/shard_map/ppermute | solution.py:379
  276.5 13.4 %collective-permute-start.32 = (bf16[256,2048]{1,0:T(8,128)(2,1)}, bf16[256,2048]{1,0:T(8,128)(2,1)}, u32[]{:S(2)}, u32[]{:S(2)}) collective-permute-start(bf16[256,2048]{1,0:T(8,128)(2,1)} %collective-permute-done.24), channel_id=1, source_target_pairs={{0,8},{8,0},{16,24},{24,16},{1,9},{9,1},{17,25},{25,17},{2,10},{10... | collective-permute-start | bytes 3145736 | tf_op jit(solution)/shard_map/ppermute | solution.py:379
  278.1 16.5 %collective-permute-start.27 = (bf16[256,2048]{1,0:T(8,128)(2,1)}, bf16[256,2048]{1,0:T(8,128)(2,1)}, u32[]{:S(2)}, u32[]{:S(2)}) collective-permute-start(bf16[256,2048]{1,0:T(8,128)(2,1)} %get-tuple-element.84), channel_id=1, source_target_pairs={{0,8},{8,0},{16,24},{24,16},{1,9},{9,1},{17,25},{25,17},{2,10},{10... | collective-permute-start | bytes 3145736 | tf_op jit(solution)/shard_map/ppermute | solution.py:379
  281.1 27.7 %collective-permute-start.29 = (bf16[256,2048]{1,0:T(8,128)(2,1)}, bf16[256,2048]{1,0:T(8,128)(2,1)}, u32[]{:S(2)}, u32[]{:S(2)}) collective-permute-start(bf16[256,2048]{1,0:T(8,128)(2,1)} %add_convert_fusion.2), channel_id=1, source_target_pairs={{0,16},{8,24},{16,0},{24,8},{1,17},{9,25},{17,1},{25,9},{2,18},{10... | collective-permute-start | bytes 3145736 | tf_op jit(solution)/shard_map/ppermute | solution.py:379
  312.4 209.4 %reduce-scatter.4.cloned.1.call-start = ((), (), s32[]{:S(2)}) async-start(), calls=%async_computation.9 | async-start | bytes 5242880 | tf_op jit(solution)/shard_map/reduce_scatter | solution.py:525
  318.1 24.7 %collective-permute-start.35 = (bf16[256,2048]{1,0:T(8,128)(2,1)S(1)}, bf16[256,2048]{1,0:T(8,128)(2,1)S(1)}, u32[]{:S(2)}, u32[]{:S(2)}) collective-permute-start(bf16[256,2048]{1,0:T(8,128)(2,1)S(1)} %get-tuple-element.149), channel_id=1, source_target_pairs={{0,1},{1,0},{2,3},{3,2},{4,5},{5,4},{6,7},{7,6},{8,9},{9,8},{10,11... | collective-permute-start | bytes 3145736 | tf_op jit(solution)/shard_map/ppermute | solution.py:379
  318.7 27.4 %collective-permute-start.34 = (bf16[256,2048]{1,0:T(8,128)(2,1)S(1)}, bf16[256,2048]{1,0:T(8,128)(2,1)S(1)}, u32[]{:S(2)}, u32[]{:S(2)}) collective-permute-start(bf16[256,2048]{1,0:T(8,128)(2,1)S(1)} %get-tuple-element.149), channel_id=1, source_target_pairs={{0,16},{8,24},{16,0},{24,8},{1,17},{9,25},{17,1},{25,9},{2,18},{10... | collective-permute-start | bytes 3145736 | tf_op jit(solution)/shard_map/ppermute | solution.py:379
  344.6 13.0 %collective-permute-start.36 = (bf16[256,1024]{1,0:T(8,128)(2,1)}, bf16[256,1024]{1,0:T(8,128)(2,1)}, u32[]{:S(2)}, u32[]{:S(2)}) collective-permute-start(bf16[256,1024]{1,0:T(8,128)(2,1)} %slice.336), channel_id=1, source_target_pairs={{0,16},{8,24},{16,0},{24,8},{1,17},{9,25},{17,1},{25,9},{2,18},{10... | collective-permute-start | bytes 1572872 | tf_op jit(solution)/shard_map/ppermute | solution.py:379
  347.9 12.5 %collective-permute-start.37 = (bf16[256,1024]{1,0:T(8,128)(2,1)}, bf16[256,1024]{1,0:T(8,128)(2,1)}, u32[]{:S(2)}, u32[]{:S(2)}) collective-permute-start(bf16[256,1024]{1,0:T(8,128)(2,1)} %slice.337), channel_id=1, source_target_pairs={{0,1},{1,0},{2,3},{3,2},{4,5},{5,4},{6,7},{7,6},{8,9},{9,8},{10,11... | collective-permute-start | bytes 1572872 | tf_op jit(solution)/shard_map/ppermute | solution.py:379
  349.1 17.6 %collective-permute-start.38 = (bf16[256,2048]{1,0:T(8,128)(2,1)}, bf16[256,2048]{1,0:T(8,128)(2,1)S(1)}, u32[]{:S(2)}, u32[]{:S(2)}) collective-permute-start(bf16[256,2048]{1,0:T(8,128)(2,1)} %copy-done.53), channel_id=1, source_target_pairs={{0,8},{8,0},{16,24},{24,16},{1,9},{9,1},{17,25},{25,17},{2,10},{10... | collective-permute-start | bytes 3145736 | tf_op jit(solution)/shard_map/ppermute | solution.py:379
  349.1 18.7 %collective-permute-start.39 = (bf16[256,2048]{1,0:T(8,128)(2,1)}, bf16[256,2048]{1,0:T(8,128)(2,1)S(1)}, u32[]{:S(2)}, u32[]{:S(2)}) collective-permute-start(bf16[256,2048]{1,0:T(8,128)(2,1)} %copy-done.47), channel_id=1, source_target_pairs={{0,8},{8,0},{16,24},{24,16},{1,9},{9,1},{17,25},{25,17},{2,10},{10... | collective-permute-start | bytes 3145736 | tf_op jit(solution)/shard_map/ppermute | solution.py:379
  349.7 19.3 %collective-permute-start.40 = (bf16[256,2048]{1,0:T(8,128)(2,1)}, bf16[256,2048]{1,0:T(8,128)(2,1)S(1)}, u32[]{:S(2)}, u32[]{:S(2)}) collective-permute-start(bf16[256,2048]{1,0:T(8,128)(2,1)} %copy-done.45), channel_id=1, source_target_pairs={{0,8},{8,0},{16,24},{24,16},{1,9},{9,1},{17,25},{25,17},{2,10},{10... | collective-permute-start | bytes 3145736 | tf_op jit(solution)/shard_map/ppermute | solution.py:379
  440.9 14.2 %collective-permute-start.43 = (bf16[256,1024]{1,0:T(8,128)(2,1)}, bf16[256,1024]{1,0:T(8,128)(2,1)}, u32[]{:S(2)}, u32[]{:S(2)}) collective-permute-start(bf16[256,1024]{1,0:T(8,128)(2,1)} %get-tuple-element.176), channel_id=1, source_target_pairs={{0,1},{1,0},{2,3},{3,2},{4,5},{5,4},{6,7},{7,6},{8,9},{9,8},{10,11... | collective-permute-start | bytes 1572872 | tf_op jit(solution)/shard_map/ppermute | solution.py:379
  442.7 171.9 %reduce-scatter.6.cloned.1.call-start = ((), (), s32[]{:S(2)}) async-start(), calls=%async_computation.10 | async-start | bytes 5242880 | tf_op jit(solution)/shard_map/reduce_scatter | solution.py:525
  444.2 13.9 %collective-permute-start.45 = (bf16[256,1024]{1,0:T(8,128)(2,1)}, bf16[256,1024]{1,0:T(8,128)(2,1)S(1)}, u32[]{:S(2)}, u32[]{:S(2)}) collective-permute-start(bf16[256,1024]{1,0:T(8,128)(2,1)} %get-tuple-element.177), channel_id=1, source_target_pairs={{0,16},{8,24},{16,0},{24,8},{1,17},{9,25},{17,1},{25,9},{2,18},{10... | collective-permute-start | bytes 1572872 | tf_op jit(solution)/shard_map/ppermute | solution.py:379
  456.4 24.3 %collective-permute-start.44 = (bf16[256,2048]{1,0:T(8,128)(2,1)S(1)}, bf16[256,2048]{1,0:T(8,128)(2,1)S(1)}, u32[]{:S(2)}, u32[]{:S(2)}) collective-permute-start(bf16[256,2048]{1,0:T(8,128)(2,1)S(1)} %pad_maximum_fusion.2), channel_id=1, source_target_pairs={{0,16},{8,24},{16,0},{24,8},{1,17},{9,25},{17,1},{25,9},{2,18},{10... | collective-permute-start | bytes 3145736 | tf_op jit(solution)/shard_map/ppermute | solution.py:379
  458.3 24.1 %collective-permute-start.46 = (bf16[256,2048]{1,0:T(8,128)(2,1)S(1)}, bf16[256,2048]{1,0:T(8,128)(2,1)S(1)}, u32[]{:S(2)}, u32[]{:S(2)}) collective-permute-start(bf16[256,2048]{1,0:T(8,128)(2,1)S(1)} %pad_maximum_fusion.3), channel_id=1, source_target_pairs={{0,1},{1,0},{2,3},{3,2},{4,5},{5,4},{6,7},{7,6},{8,9},{9,8},{10,11... | collective-permute-start | bytes 3145736 | tf_op jit(solution)/shard_map/ppermute | solution.py:379
  487.3 25.6 %collective-permute-start.48 = (bf16[256,2048]{1,0:T(8,128)(2,1)S(1)}, bf16[256,2048]{1,0:T(8,128)(2,1)S(1)}, u32[]{:S(2)}, u32[]{:S(2)}) collective-permute-start(bf16[256,2048]{1,0:T(8,128)(2,1)S(1)} %get-tuple-element.142.refs_0_), channel_id=1, source_target_pairs={{0,16},{8,24},{16,0},{24,8},{1,17},{9,25},{17,1},{25,9},{2,18},{10... | collective-permute-start | bytes 3145736 | tf_op jit(solution)/shard_map/ppermute | solution.py:379
  521.9 58.3 %all-to-all-start.2 = ((bf16[8,1,4,128,128]{4,3,2,1,0:T(8,128)(2,1)}), bf16[8,1,4,128,128]{4,3,2,1,0:T(8,128)(2,1)}, u32[]{:S(2)}, u32[]{:S(2)}) async-start(bf16[8,1,4,128,128]{4,3,2,1,0:T(8,128)(2,1)} %copy-done.11), calls=%async_computation.2 | async-start | bytes 2097152 | tf_op jit(solution)/shard_map/all_to_all | solution.py:626
  536.6 14.3 %collective-permute-start.52 = (bf16[256,1024]{1,0:T(8,128)(2,1)}, bf16[256,1024]{1,0:T(8,128)(2,1)}, u32[]{:S(2)}, u32[]{:S(2)}) collective-permute-start(bf16[256,1024]{1,0:T(8,128)(2,1)} %get-tuple-element.174), channel_id=1, source_target_pairs={{0,16},{8,24},{16,0},{24,8},{1,17},{9,25},{17,1},{25,9},{2,18},{10... | collective-permute-start | bytes 1572872 | tf_op jit(solution)/shard_map/ppermute | solution.py:379
  542.7 19.6 %collective-permute-start.51 = (bf16[256,1024]{1,0:T(8,128)(2,1)}, bf16[256,1024]{1,0:T(8,128)(2,1)S(1)}, u32[]{:S(2)}, u32[]{:S(2)}) collective-permute-start(bf16[256,1024]{1,0:T(8,128)(2,1)} %get-tuple-element.175), channel_id=1, source_target_pairs={{0,1},{1,0},{2,3},{3,2},{4,5},{5,4},{6,7},{7,6},{8,9},{9,8},{10,11... | collective-permute-start | bytes 1572872 | tf_op jit(solution)/shard_map/ppermute | solution.py:379
  580.2 25.5 %collective-permute-start.53 = (bf16[256,2048]{1,0:T(8,128)(2,1)}, bf16[256,2048]{1,0:T(8,128)(2,1)}, u32[]{:S(2)}, u32[]{:S(2)}) collective-permute-start(bf16[256,2048]{1,0:T(8,128)(2,1)} %pad_maximum_fusion.4), channel_id=1, source_target_pairs={{0,16},{8,24},{16,0},{24,8},{1,17},{9,25},{17,1},{25,9},{2,18},{10... | collective-permute-start | bytes 3145736 | tf_op jit(solution)/shard_map/ppermute | solution.py:379
  581.1 24.9 %collective-permute-start.54 = (bf16[256,2048]{1,0:T(8,128)(2,1)}, bf16[256,2048]{1,0:T(8,128)(2,1)}, u32[]{:S(2)}, u32[]{:S(2)}) collective-permute-start(bf16[256,2048]{1,0:T(8,128)(2,1)} %pad_maximum_fusion.5), channel_id=1, source_target_pairs={{0,1},{1,0},{2,3},{3,2},{4,5},{5,4},{6,7},{7,6},{8,9},{9,8},{10,11... | collective-permute-start | bytes 3145736 | tf_op jit(solution)/shard_map/ppermute | solution.py:379
  610.1 76.3 %all-to-all-start.3 = ((bf16[8,3,4,128,128]{4,3,2,1,0:T(8,128)(2,1)}), bf16[8,3,4,128,128]{4,3,2,1,0:T(8,128)(2,1)}, u32[]{:S(2)}, u32[]{:S(2)}) async-start(bf16[8,3,4,128,128]{4,3,2,1,0:T(8,128)(2,1)} %attend_bwd.1), calls=%async_computation.3 | async-start | bytes 6291456 | tf_op jit(solution)/shard_map/all_to_all | solution.py:626
  614.6 198.8 %reduce-scatter.8.cloned.1.call-start = ((), (), s32[]{:S(2)}) async-start(), calls=%async_computation.11 | async-start | bytes 2359296 | tf_op jit(solution)/shard_map/reduce_scatter | solution.py:634
  618.0 12.7 %collective-permute-start.57 = (bf16[2,64,1024]{2,1,0:T(8,128)(2,1)S(1)}, bf16[2,64,1024]{2,1,0:T(8,128)(2,1)S(1)}, u32[]{:S(2)}, u32[]{:S(2)}) collective-permute-start(bf16[2,64,1024]{2,1,0:T(8,128)(2,1)S(1)} %get-tuple-element.172), channel_id=1, source_target_pairs={{0,24},{8,16},{16,8},{24,0},{1,25},{9,17},{17,9},{25,1},{2,26},{10... | collective-permute-start | bytes 786440 | tf_op jit(solution)/shard_map/ppermute | solution.py:379
  630.8 30.3 %collective-permute-start.58 = (bf16[4,64,1024]{2,1,0:T(8,128)(2,1)S(1)}, bf16[4,64,1024]{2,1,0:T(8,128)(2,1)S(1)}, u32[]{:S(2)}, u32[]{:S(2)}) collective-permute-start(bf16[4,64,1024]{2,1,0:T(8,128)(2,1)S(1)} %pad_maximum_fusion.10), channel_id=1, source_target_pairs={{0,1},{1,0},{2,3},{3,2},{4,5},{5,4},{6,7},{7,6},{8,9},{9,8},{10,11... | collective-permute-start | bytes 1572872 | tf_op jit(solution)/shard_map/ppermute | solution.py:379
  700.5 10.5 %collective-permute-start.60 = (bf16[4,64,768]{2,1,0:T(8,128)(2,1)S(1)}, bf16[4,64,768]{2,1,0:T(8,128)(2,1)S(1)}, u32[]{:S(2)}, u32[]{:S(2)}) collective-permute-start(bf16[4,64,768]{2,1,0:T(8,128)(2,1)S(1)} %get-tuple-element.118), channel_id=1, source_target_pairs={{0,1},{2,0},{4,2},{6,4},{7,6},{5,7},{3,5},{1,3},{8,9},{10,8},{12,1... | collective-permute-start | bytes 1179656 | tf_op jit(solution)/shard_map/ppermute | solution.py:547
  701.9 10.6 %collective-permute-start.59 = (bf16[4,64,768]{2,1,0:T(8,128)(2,1)S(1)}, bf16[4,64,768]{2,1,0:T(8,128)(2,1)S(1)}, u32[]{:S(2)}, u32[]{:S(2)}) collective-permute-start(bf16[4,64,768]{2,1,0:T(8,128)(2,1)S(1)} %get-tuple-element.117), channel_id=1, source_target_pairs={{0,2},{2,4},{4,6},{6,7},{7,5},{5,3},{3,1},{1,0},{8,10},{10,12},{12... | collective-permute-start | bytes 1179656 | tf_op jit(solution)/shard_map/ppermute | solution.py:547
  712.7 18.1 %collective-permute-start.66 = (bf16[4,64,1536]{2,1,0:T(8,128)(2,1)S(1)}, bf16[4,64,1536]{2,1,0:T(8,128)(2,1)S(1)}, u32[]{:S(2)}, u32[]{:S(2)}) collective-permute-start(bf16[4,64,1536]{2,1,0:T(8,128)(2,1)S(1)} %pad_maximum_fusion.7), channel_id=1, source_target_pairs={{0,2},{2,4},{4,6},{6,7},{7,5},{5,3},{3,1},{1,0},{8,10},{10,12},{12... | collective-permute-start | bytes 2359304 | tf_op jit(solution)/shard_map/ppermute | solution.py:547
  713.0 17.9 %collective-permute-start.67 = (bf16[4,64,1536]{2,1,0:T(8,128)(2,1)S(1)}, bf16[4,64,1536]{2,1,0:T(8,128)(2,1)S(1)}, u32[]{:S(2)}, u32[]{:S(2)}) collective-permute-start(bf16[4,64,1536]{2,1,0:T(8,128)(2,1)S(1)} %pad_maximum_fusion.8), channel_id=1, source_target_pairs={{0,1},{2,0},{4,2},{6,4},{7,6},{5,7},{3,5},{1,3},{8,9},{10,8},{12,1... | collective-permute-start | bytes 2359304 | tf_op jit(solution)/shard_map/ppermute | solution.py:547
  716.0 19.9 %collective-permute-start.62 = (bf16[256,2048]{1,0:T(8,128)(2,1)S(1)}, bf16[256,2048]{1,0:T(8,128)(2,1)S(1)}, u32[]{:S(2)}, u32[]{:S(2)}) collective-permute-start(bf16[256,2048]{1,0:T(8,128)(2,1)S(1)} %get-tuple-element.166), channel_id=1, source_target_pairs={{0,8},{8,0},{16,24},{24,16},{1,9},{9,1},{17,25},{25,17},{2,10},{10... | collective-permute-start | bytes 3145736 | tf_op jit(solution)/shard_map/ppermute | solution.py:379
  716.0 38.4 %collective-permute-start.61 = (bf16[256,2048]{1,0:T(8,128)(2,1)}, bf16[256,2048]{1,0:T(8,128)(2,1)}, u32[]{:S(2)}, u32[]{:S(2)}) collective-permute-start(bf16[256,2048]{1,0:T(8,128)(2,1)} %get-tuple-element.165), channel_id=1, source_target_pairs={{0,8},{8,0},{16,24},{24,16},{1,9},{9,1},{17,25},{25,17},{2,10},{10... | collective-permute-start | bytes 3145736 | tf_op jit(solution)/shard_map/ppermute | solution.py:379
  733.8 17.4 %collective-permute-start.68 = (bf16[4,64,1536]{2,1,0:T(8,128)(2,1)}, bf16[4,64,1536]{2,1,0:T(8,128)(2,1)}, u32[]{:S(2)}, u32[]{:S(2)}) collective-permute-start(bf16[4,64,1536]{2,1,0:T(8,128)(2,1)} %get-tuple-element.124), channel_id=1, source_target_pairs={{0,2},{2,4},{4,6},{6,7},{7,5},{5,3},{3,1},{1,0},{8,10},{10,12},{12... | collective-permute-start | bytes 2359304 | tf_op jit(solution)/shard_map/ppermute | solution.py:547
  734.3 17.8 %collective-permute-start.69 = (bf16[4,64,1536]{2,1,0:T(8,128)(2,1)}, bf16[4,64,1536]{2,1,0:T(8,128)(2,1)}, u32[]{:S(2)}, u32[]{:S(2)}) collective-permute-start(bf16[4,64,1536]{2,1,0:T(8,128)(2,1)} %get-tuple-element.125), channel_id=1, source_target_pairs={{0,1},{2,0},{4,2},{6,4},{7,6},{5,7},{3,5},{1,3},{8,9},{10,8},{12,1... | collective-permute-start | bytes 2359304 | tf_op jit(solution)/shard_map/ppermute | solution.py:547
  737.3 22.5 %collective-permute-start.63 = (bf16[256,2048]{1,0:T(8,128)(2,1)}, bf16[256,2048]{1,0:T(8,128)(2,1)}, u32[]{:S(2)}, u32[]{:S(2)}) collective-permute-start(bf16[256,2048]{1,0:T(8,128)(2,1)} %add_convert_fusion), channel_id=1, source_target_pairs={{0,16},{8,24},{16,0},{24,8},{1,17},{9,25},{17,1},{25,9},{2,18},{10... | collective-permute-start | bytes 3145736 | tf_op jit(solution)/shard_map/ppermute | solution.py:379
  767.3 21.4 %collective-permute-start.70 = (bf16[4,64,1536]{2,1,0:T(8,128)(2,1)S(1)}, bf16[4,64,1536]{2,1,0:T(8,128)(2,1)S(1)}, u32[]{:S(2)}, u32[]{:S(2)}) collective-permute-start(bf16[4,64,1536]{2,1,0:T(8,128)(2,1)S(1)} %get-tuple-element.126), channel_id=1, source_target_pairs={{0,2},{2,4},{4,6},{6,7},{7,5},{5,3},{3,1},{1,0},{8,10},{10,12},{12... | collective-permute-start | bytes 2359304 | tf_op jit(solution)/shard_map/ppermute | solution.py:547
  767.9 21.0 %collective-permute-start.71 = (bf16[4,64,1536]{2,1,0:T(8,128)(2,1)S(1)}, bf16[4,64,1536]{2,1,0:T(8,128)(2,1)S(1)}, u32[]{:S(2)}, u32[]{:S(2)}) collective-permute-start(bf16[4,64,1536]{2,1,0:T(8,128)(2,1)S(1)} %get-tuple-element.127), channel_id=1, source_target_pairs={{0,1},{2,0},{4,2},{6,4},{7,6},{5,7},{3,5},{1,3},{8,9},{10,8},{12,1... | collective-permute-start | bytes 2359304 | tf_op jit(solution)/shard_map/ppermute | solution.py:547
  771.3 19.1 %collective-permute-start.65 = (f32[2,2,2,768]{3,2,1,0:T(2,128)S(1)}, f32[2,2,2,768]{3,2,1,0:T(2,128)S(1)}, u32[]{:S(2)}, u32[]{:S(2)}) collective-permute-start(f32[2,2,2,768]{3,2,1,0:T(2,128)S(1)} %dynamic-slice_bitcast_fusion.13), channel_id=1, source_target_pairs={{0,16},{8,24},{16,0},{24,8},{1,17},{9,25},{17,1},{25,9},{2,18},{10... | collective-permute-start | bytes 73736 | tf_op jit(solution)/shard_map/ppermute | solution.py:379
  (108 other events, 781.3 us)
Sparse Core Ops, SparseCore 0:
  15.3 58.8 all-gather.4
  212.1 98.4 all-gather.8
  312.5 80.5 all-gather.6
  442.8 73.9 reduce-scatter.3
  522.0 91.3 reduce-scatter.5
  743.7 69.6 reduce-scatter.7
